TPU v7x, 32 devices: a whole 2x2x4 slice. The times are simulated.
32 devices in a mesh: groups: 2 (over x), space: 16 (over z, y, core).
Axes of the slice: x: 2, y: 2, z: 4, core: 2. Of those that a mesh axis runs over, the one named last changes fastest.
Arguments:
- mol_feats: bfloat16 [8192, 512], P(('groups', 'space')), parts along dimension 0, may hold values from -6 to 6
- w_src: bfloat16 [512, 512], replicated, may hold values from -0.25 to 0.25
- w_dst: bfloat16 [512, 512], replicated, may hold values from -0.25 to 0.25
- w_out: bfloat16 [512, 529], replicated, may hold values from -0.25 to 0.25
- grad_blocks: bfloat16 [16, 32, 128, 529], P('space', 'groups'), parts along dimension 1, may hold values from -6 to 6
- edge_src: int32 [65536], P(('groups', 'space')), parts along dimension 0, may hold values from 0 to 255
- edge_dst: int32 [65536], P(('groups', 'space')), parts along dimension 0, may hold values from 0 to 383
- edge_live: int32 [65536], P(('groups', 'space')), parts along dimension 0, may hold values from 0 to 1, as said below
Outputs:
- feature_grad: float32 [8192, 512], P(('groups', 'space')), parts along dimension 0
- src_weight_grad: float32 [1024, 512], P(('groups', 'space')), parts along dimension 0
- dst_weight_grad: float32 [1024, 512], P(('groups', 'space')), parts along dimension 0
- out_weight_grad: float32 [1024, 529], P(('groups', 'space')), parts along dimension 0
There are 2 independent parts, one for each index of `groups`. A program takes and returns all parts, laid end to end along the dimension named above; an argument that names none is the same for every part. Nothing has to cross between parts.
Inputs may be any that keep to these rules, and one draw needn't show every extreme that they name: `edge_live`: on every slab the live slots of each owner come first among its 128 slots, and the slab's own blocks fill all 128 of theirs. Any other owner has at most 64 live slots for a slab, and on every slab some other owner has exactly 64. `edge_dst`: index into the slab's molecules extended by 64 molecules of the slab below (first) and 64 of the slab above (last), periodic.
All inputs are finite; a program needn't handle non-finite values.
Results may differ from a plain program's by a relative error of at most 0.0029.
Values may be sent and summed in bfloat16 or wider, within the bound.
No kernel may reach another device: no remote copies, remote signals or barrier semaphores. Data moves between devices by JAX's collectives and lax.ppermute only.
A program may use at most 64 MiB of HBM per device.

v0:
```python
import jax
import jax.numpy as jnp
from jax import lax
from jax.sharding import PartitionSpec as P


def passed_along(block, axis, distance):
    devices = range(lax.axis_size(axis))
    route = [((i - distance) % len(devices), i) for i in devices]
    return lax.ppermute(block, axis, route)


def extended_2(cells, sides, width):
    for axis, dim in sides:
        count = lax.axis_size(axis)
        head = lax.slice_in_dim(cells, 0, width, axis=dim)
        tail = lax.slice_in_dim(cells, cells.shape[dim] - width, cells.shape[dim], axis=dim)
        cells = jnp.concatenate(
            [
                lax.ppermute(tail, axis, [(i, (i + 1) % count) for i in range(count)]),
                cells,
                lax.ppermute(head, axis, [((i + 1) % count, i) for i in range(count)]),
            ],
            axis=dim,
        )
    return cells


def settle_rims(wide_sum, reach):
    mols = wide_sum.shape[0] - 2 * reach
    lower = wide_sum[:reach]
    upper = wide_sum[reach + mols :]
    from_above = passed_along(lower, "space", -1)
    from_below = passed_along(upper, "space", 1)
    middle = wide_sum[reach : reach + mols]
    middle = middle.at[:reach].add(from_below)
    return middle.at[mols - reach :].add(from_above)


def column_term(left, right, factor):
    product = lax.dot_general(
        left,
        right,
        (((0,), (0,)), ((), ())),
        precision=lax.Precision.HIGHEST,
        preferred_element_type=jnp.float32,
    )
    return factor * product


def on_device(mol_feats, w_src, w_dst, w_out, grad_blocks, edge_src, edge_dst, edge_live):
    mols = mol_feats.shape[0]
    entries = w_out.shape[1]
    reach = mols // 4
    highest = lax.Precision.HIGHEST
    transposed = (((1,), (1,)), ((), ()))
    extended = extended_2(mol_feats, (("space", 0),), reach)
    proj_src = jnp.dot(mol_feats, w_src, preferred_element_type=jnp.float32)
    proj_dst = jnp.dot(extended, w_dst, preferred_element_type=jnp.float32)
    arrived = lax.all_to_all(grad_blocks, "space", split_axis=1, concat_axis=0, tiled=True)
    blocks = arrived.reshape(-1, entries)
    blocks = jnp.where(edge_live[:, None] > 0, blocks, jnp.zeros_like(blocks))
    pre = proj_src[edge_src] + proj_dst[edge_dst]
    sigma = jax.nn.sigmoid(pre)
    hidden = (pre * sigma).astype(jnp.bfloat16)
    grad_hidden = lax.dot_general(blocks, w_out, transposed, preferred_element_type=jnp.float32)
    grad_pre = (grad_hidden * sigma * (1.0 + pre * (1.0 - sigma))).astype(jnp.bfloat16)
    grad_wide = lax.optimization_barrier(grad_pre).astype(jnp.float32)
    src_sum = jax.ops.segment_sum(grad_wide, edge_src, num_segments=mols)
    dst_wide = jax.ops.segment_sum(grad_wide, edge_dst, num_segments=mols + 2 * reach)
    dst_total = settle_rims(dst_wide, reach)
    feature_grad = jnp.dot(src_sum, w_src.astype(jnp.float32).T, precision=highest) + jnp.dot(
        dst_total, w_dst.astype(jnp.float32).T, precision=highest
    )
    factor = float(edge_src.shape[0] * lax.axis_size("space")) ** (-0.5)
    feats_wide = mol_feats.astype(jnp.float32)
    ext_wide = extended.astype(jnp.float32)
    src_weight_grad = lax.psum_scatter(
        column_term(feats_wide, src_sum, factor), "space", scatter_dimension=0, tiled=True
    )
    dst_weight_grad = lax.psum_scatter(
        column_term(ext_wide, dst_wide, factor), "space", scatter_dimension=0, tiled=True
    )
    product = lax.dot_general(
        hidden, blocks, (((0,), (0,)), ((), ())), preferred_element_type=jnp.float32
    )
    out_weight_grad = lax.psum_scatter(factor * product, "space", scatter_dimension=0, tiled=True)
    return (feature_grad, src_weight_grad, dst_weight_grad, out_weight_grad)


def solution(mesh):
    placed = (
        P(("groups", "space"), None),
        P(),
        P(),
        P(),
        P("space", "groups", None, None),
        P(("groups", "space")),
        P(("groups", "space")),
        P(("groups", "space")),
    )
    return jax.shard_map(
        on_device,
        mesh=mesh,
        in_specs=placed,
        out_specs=(
            P(("groups", "space"), None),
            P(("groups", "space"), None),
            P(("groups", "space"), None),
            P(("groups", "space"), None),
        ),
        check_vma=False,
    )
```

profile of v0, /device:TPU:0, one launch (start us, length us, event | category | flops | bytes accessed | tf_op | source)
XLA Modules:
  0.0 292.4 jit_solution(4587517296089946174)
XLA Ops:
  7.2 3.7 %copy.15 = bf16[1,16,128,529]{2,3,0,1:T(8,128)(2,1)} copy(bf16[1,16,128,529]{2,1,3,0:T(8,128)(2,1)} %param.16) | data formatting | bytes 4333568 | tf_op args[4]
  10.9 7.4 %all-to-all-start = ((bf16[1,16,128,529]{2,3,0,1:T(8,128)(2,1)}), bf16[1,16,128,529]{2,3,0,1:T(8,128)(2,1)S(1)}, u32[]{:S(2)}, u32[]{:S(2)}) async-start(bf16[1,16,128,529]{2,3,0,1:T(8,128)(2,1)} %copy.15), calls=%async_computation | async-start | bytes 4390912 | tf_op jit(solution)/shard_map/all_to_all | solution.py:60
  18.3 0.7 fusion.20
  19.0 4.4 %collective-permute-start.1 = (bf16[64,512]{1,0:T(8,128)(2,1)}, bf16[64,512]{1,0:T(8,128)(2,1)}, u32[]{:S(2)}, u32[]{:S(2)}) collective-permute-start(bf16[64,512]{1,0:T(8,128)(2,1)} %get-tuple-element.42), channel_id=1, source_target_pairs={{1,0},{2,1},{3,2},{4,3},{5,4},{6,5},{7,6},{8,7},{9,8},{10,9},{11,1... | collective-permute-start | bytes 196616 | tf_op jit(solution)/shard_map/ppermute | solution.py:22
  23.4 1.3 fusion.21
  24.8 0.6 broadcast_compare_fusion
  25.3 8.9 %gather_fusion = f32[2048,512]{1,0:T(8,128)} fusion(f32[256,512]{1,0:T(8,128)S(1)} %fusion.21, s32[2048]{0:T(1024)S(1)} %get-tuple-element.44), kind=kCustom, calls=%fused_computation | custom fusion | bytes 8396800 | tf_op jit(solution)/shard_map/gather | solution.py:63
  34.2 26.3 %collective-permute-done = bf16[64,512]{1,0:T(8,128)(2,1)} collective-permute-done((bf16[64,512]{1,0:T(8,128)(2,1)}, bf16[64,512]{1,0:T(8,128)(2,1)}, u32[]{:S(2)}, u32[]{:S(2)}) %collective-permute-start) | collective-permute-done | bytes 65568 | tf_op jit(solution)/shard_map/ppermute | solution.py:20
  60.5 0.8 constant_dynamic-update-slice_fusion.2
  61.4 0.8 constant_dynamic-update-slice_fusion
  62.3 0.7 copy-done.8
  63.0 1.4 fusion.22
  64.4 9.0 %gather_fusion.1 = f32[2048,512]{1,0:T(8,128)} fusion(f32[384,512]{1,0:T(8,128)S(1)} %fusion.22, s32[2048]{0:T(1024)S(1)} %get-tuple-element.45), kind=kCustom, calls=%fused_computation.1 | custom fusion | bytes 8396800 | tf_op jit(solution)/shard_map/gather | solution.py:63
  73.7 0.4 pad.6
  74.1 0.6 copy.20
  74.7 1.4 copy-done.5
  76.5 1.5 copy-done.3
  77.9 3.1 %multiply_convert_fusion.1 = bf16[2048,512]{1,0:T(8,128)(2,1)S(1)} fusion(bf16[512,529]{0,1:T(8,128)(2,1)S(1)} %copy-done, bf16[2048,529]{0,1:T(8,128)(2,1)S(1)} %bitcast.26, pred[2048]{0:T(1024)(128)(4,1)S(1)} %copy-done.12, f32[2048,512]{1,0:T(8,128)S(1)} %copy-done.2, f32[2048,512]{1,0:T(8,128)S(1)} %copy-done.3), kind=kOutput, calls=%fused_computation.9 | convolution fusion | flops 1120962560 | bytes 13196288 | tf_op jit(solution)/shard_map/dot_general | solution.py:66
  81.0 13.2 %scatter_custom_fusion.1 = f32[384,512]{1,0:T(8,128)S(1)} fusion(s32[2048]{0:T(1024)} %param.18, bf16[2048,512]{1,0:T(8,128)(2,1)S(1)} %multiply_convert_fusion.1, f32[]{:T(128)} %constant.64.clone.1), kind=kCustom, calls=%fused_computation.4 | custom fusion | flops 2097152 | bytes 2884096 | tf_op jit(solution)/shard_map/scatter-add | solution.py:70
  94.2 3.0 %convolution_multiply_fusion = f32[512,512]{1,0:T(8,128)} fusion(bf16[384,512]{1,0:T(8,128)(2,1)} %copy-done.8, f32[384,512]{1,0:T(8,128)S(1)} %scatter_custom_fusion.1), kind=kOutput, calls=%fused_computation.16 | convolution fusion | flops 1208221696 | bytes 2228224 | tf_op jit(solution)/shard_map/dot_general | solution.py:41
  97.3 13.7 %scatter_custom_fusion = f32[256,512]{1,0:T(8,128)} fusion(s32[2048]{0:T(1024)} %param.17, bf16[2048,512]{1,0:T(8,128)(2,1)S(1)} %multiply_convert_fusion.1, f32[]{:T(128)} %constant.64.clone.1), kind=kCustom, calls=%fused_computation.6 | custom fusion | flops 2097152 | bytes 2621952 | tf_op jit(solution)/shard_map/scatter-add | solution.py:69
  111.0 1.7 fusion.7
  112.8 1.3 copy.18
  114.2 7.8 %fusion.6 = f32[512,529]{1,0:T(8,128)} fusion(bf16[2048,529]{0,1:T(8,128)(2,1)} %bitcast.27, pred[2048]{0:T(1024)(128)(4,1)S(1)} %copy-done.12, f32[2048,512]{1,0:T(8,128)} %gather_fusion, f32[2048,512]{1,0:T(8,128)} %gather_fusion.1), kind=kOutput, calls=%fused_computation.15 | convolution fusion | flops 1117039104 | bytes 11640832 | tf_op jit(solution)/shard_map/dot_general | solution.py:84
  122.2 0.6 fusion.23
  122.8 4.5 %collective-permute-start.3 = (f32[64,512]{1,0:T(8,128)S(1)}, f32[64,512]{1,0:T(8,128)S(1)}, u32[]{:S(2)}, u32[]{:S(2)}) collective-permute-start(f32[64,512]{1,0:T(8,128)S(1)} %get-tuple-element.40), channel_id=1, source_target_pairs={{1,0},{2,1},{3,2},{4,3},{5,4},{6,5},{7,6},{8,7},{9,8},{10,9},{11,1... | collective-permute-start | bytes 393224 | tf_op jit(solution)/shard_map/ppermute | solution.py:10
  127.3 1.9 collective-permute-done.2
  129.3 0.6 collective-permute-done.3
  129.9 1.4 convolution_add_fusion
  131.3 31.8 %reduce-scatter.6.cloned.1.call-done = f32[32,512]{1,0:T(8,128)} async-done(((f32[512,512]{1,0:T(8,128)}), f32[32,512]{1,0:T(8,128)}) %reduce-scatter.6.cloned.1.call-update) | async-done | bytes 65552 | tf_op jit(solution)/shard_map/reduce_scatter | solution.py:81
  163.1 61.0 %reduce-scatter.10.cloned.1.call-done = f32[32,512]{1,0:T(8,128)} async-done(((f32[512,512]{1,0:T(8,128)}), f32[32,512]{1,0:T(8,128)}) %reduce-scatter.10.cloned.1.call-update) | async-done | bytes 65552
  224.2 61.7 %reduce-scatter.8.cloned.1.call-done = f32[32,529]{1,0:T(8,128)} async-done(((f32[512,529]{1,0:T(8,128)}), f32[32,529]{1,0:T(8,128)}) %reduce-scatter.8.cloned.1.call-update) | async-done | bytes 67728 | tf_op jit(solution)/shard_map/reduce_scatter | solution.py:87
  (40 shorter events, 1.1 us)
Async XLA Ops:
  7.2 68.9 %copy-start = (bf16[512,529]{0,1:T(8,128)(2,1)S(1)}, bf16[512,529]{0,1:T(8,128)(2,1)}, u32[]{:S(2)}) copy-start(bf16[512,529]{0,1:T(8,128)(2,1)} %param.15) | copy-start | bytes 1625092
  7.2 11.1 %copy-start.4 = (bf16[256,512]{1,0:T(8,128)(2,1)S(1)}, bf16[256,512]{1,0:T(8,128)(2,1)}, u32[]{:S(2)}) copy-start(bf16[256,512]{1,0:T(8,128)(2,1)} %param.12) | copy-start | bytes 786436
  7.2 16.2 %copy-start.10 = (s32[2048]{0:T(1024)S(1)}, s32[2048]{0:T(1024)}, u32[]{:S(2)}) copy-start(s32[2048]{0:T(1024)} %param.18) | copy-start | bytes 24580
  7.2 16.2 %copy-start.11 = (s32[2048]{0:T(1024)S(1)}, s32[2048]{0:T(1024)}, u32[]{:S(2)}) copy-start(s32[2048]{0:T(1024)} %param.17) | copy-start | bytes 24580
  7.2 17.5 %copy-start.9 = (s32[2048]{0:T(1024)S(1)}, s32[2048]{0:T(1024)}, u32[]{:S(2)}) copy-start(s32[2048]{0:T(1024)} %param.19) | copy-start | bytes 24580
  10.9 62.5 %all-to-all-start = ((bf16[1,16,128,529]{2,3,0,1:T(8,128)(2,1)}), bf16[1,16,128,529]{2,3,0,1:T(8,128)(2,1)S(1)}, u32[]{:S(2)}, u32[]{:S(2)}) async-start(bf16[1,16,128,529]{2,3,0,1:T(8,128)(2,1)} %copy.15), calls=%async_computation | async-start | bytes 4390912 | tf_op jit(solution)/shard_map/all_to_all | solution.py:60
  18.3 144.8 %reduce-scatter.6.cloned.1.call-start = ((), (), s32[]{:S(2)}) async-start(), calls=%async_computation.4 | async-start | bytes 1114112 | tf_op jit(solution)/shard_map/reduce_scatter | solution.py:81
  19.0 42.4 %collective-permute-start.1 = (bf16[64,512]{1,0:T(8,128)(2,1)}, bf16[64,512]{1,0:T(8,128)(2,1)}, u32[]{:S(2)}, u32[]{:S(2)}) collective-permute-start(bf16[64,512]{1,0:T(8,128)(2,1)} %get-tuple-element.42), channel_id=1, source_target_pairs={{1,0},{2,1},{3,2},{4,3},{5,4},{6,5},{7,6},{8,7},{9,8},{10,9},{11,1... | collective-permute-start | bytes 196616 | tf_op jit(solution)/shard_map/ppermute | solution.py:22
  23.4 37.2 %collective-permute-start = (bf16[64,512]{1,0:T(8,128)(2,1)}, bf16[64,512]{1,0:T(8,128)(2,1)}, u32[]{:S(2)}, u32[]{:S(2)}) collective-permute-start(bf16[64,512]{1,0:T(8,128)(2,1)} %get-tuple-element.43), channel_id=1, source_target_pairs={{0,1},{1,2},{2,3},{3,4},{4,5},{5,6},{6,7},{7,8},{8,9},{9,10},{10,1... | collective-permute-start | bytes 196616 | tf_op jit(solution)/shard_map/ppermute | solution.py:20
  62.3 0.7 copy-start.8
  73.7 2.8 copy-start.2
  73.7 4.3 %copy-start.3 = (f32[2048,512]{1,0:T(8,128)S(1)}, f32[2048,512]{1,0:T(8,128)}, u32[]{:S(2)}) copy-start(f32[2048,512]{1,0:T(8,128)} %gather_fusion.1) | copy-start | bytes 12582916
  73.7 4.2 %copy-start.12 = (pred[2048]{0:T(1024)(128)(4,1)S(1)}, pred[2048]{0:T(1024)(128)(4,1)}, u32[]{:S(2)}) copy-start(pred[2048]{0:T(1024)(128)(4,1)} %broadcast_compare_fusion) | copy-start | bytes 6148
  74.7 1.4 copy-start.5
  97.3 126.9 %reduce-scatter.10.cloned.1.call-start = ((), (), s32[]{:S(2)}) async-start(), calls=%async_computation.6 | async-start | bytes 1114112
  114.2 8.0 %copy-start.1 = (f32[256,512]{1,0:T(8,128)S(1)}, f32[256,512]{1,0:T(8,128)}, u32[]{:S(2)}) copy-start(f32[256,512]{1,0:T(8,128)} %scatter_custom_fusion) | copy-start | bytes 1572868
  114.2 8.0 %copy-start.6 = (bf16[512,512]{1,0:T(8,128)(2,1)S(1)}, bf16[512,512]{1,0:T(8,128)(2,1)}, u32[]{:S(2)}) copy-start(bf16[512,512]{1,0:T(8,128)(2,1)} %param.13) | copy-start | bytes 1572868
  114.2 171.7 %reduce-scatter.8.cloned.1.call-start = ((), (), s32[]{:S(2)}) async-start(), calls=%async_computation.5 | async-start | bytes 1392640 | tf_op jit(solution)/shard_map/reduce_scatter | solution.py:87
  122.0 7.8 %copy-start.7 = (bf16[512,512]{1,0:T(8,128)(2,1)S(1)}, bf16[512,512]{1,0:T(8,128)(2,1)}, u32[]{:S(2)}) copy-start(bf16[512,512]{1,0:T(8,128)(2,1)} %param.14) | copy-start | bytes 1572868
  122.1 7.1 %collective-permute-start.2 = (f32[64,512]{1,0:T(8,128)S(1)}, f32[64,512]{1,0:T(8,128)S(1)}, u32[]{:S(2)}, u32[]{:S(2)}) collective-permute-start(f32[64,512]{1,0:T(8,128)S(1)} %get-tuple-element.41), channel_id=1, source_target_pairs={{15,0},{0,1},{1,2},{2,3},{3,4},{4,5},{5,6},{6,7},{7,8},{8,9},{9,10... | collective-permute-start | bytes 393224 | tf_op jit(solution)/shard_map/ppermute | solution.py:10
  122.8 7.0 %collective-permute-start.3 = (f32[64,512]{1,0:T(8,128)S(1)}, f32[64,512]{1,0:T(8,128)S(1)}, u32[]{:S(2)}, u32[]{:S(2)}) collective-permute-start(f32[64,512]{1,0:T(8,128)S(1)} %get-tuple-element.40), channel_id=1, source_target_pairs={{1,0},{2,1},{3,2},{4,3},{5,4},{6,5},{7,6},{8,7},{9,8},{10,9},{11,1... | collective-permute-start | bytes 393224 | tf_op jit(solution)/shard_map/ppermute | solution.py:10
Sparse Core Ops, SparseCore 0:
  97.4 65.6 reduce-scatter.5
  167.7 56.3 reduce-scatter.9
  228.4 57.4 reduce-scatter.7
where the time goes:
time: 293 us; the launch traced here: 292 us
  waiting for transfers between devices  183 us (62%)
  local copies, waits for them, and re-layouts  30.6 us (10%)
  other arithmetic  27.5 us (9%)
  matrix products  20.5 us (7%)
  starting transfers between devices  16.4 us (6%)
  between operations  14 us (5%)
    reduce_scatter x1, waiting for transfers between devices, on_device(): lax.psum_scatter(factor * product, 'space', scatter_dimension=0, tiled=True)  61.7 us
    unnamed x4, waiting for transfers between devices  61.1 us
    reduce_scatter x1, waiting for transfers between devices, on_device(): lax.psum_scatter(column_term(ext_wide, dst_wide, factor), 'space', scatte...  31.8 us
    ppermute x1, waiting for transfers between devices, extended_2(): lax.ppermute(tail, axis, [(i, (i + 1) % count) for i in range(count)])  26.3 us
    gather x2, local copies, waits for them, and re-layouts, on_device(): pre = proj_src[edge_src] + proj_dst[edge_dst]  17.9 us
    scatter-add x1, other arithmetic, on_device(): src_sum = jax.ops.segment_sum(grad_wide, edge_src, num_segments=mols)  13.7 us
    scatter-add x1, other arithmetic, on_device(): jax.ops.segment_sum(grad_wide, edge_dst, num_segments=mols + 2 * reach)  13.2 us
    unnamed x32, local copies, waits for them, and re-layouts  10.9 us
  transfers between devices with their start and end apart: 8, of which 6 were waited for; matrix products, arithmetic and copies ran while one was open for 17% of the time, Pallas kernels for 0%

commit v1 on v0

v1 whole, which is shorter than its diff:
```python
import functools

import jax
import jax.numpy as jnp
from jax import lax
from jax.experimental import pallas as pl
from jax.experimental.pallas import tpu as pltpu
from jax.sharding import PartitionSpec as P

F32 = jnp.float32
BF16 = jnp.bfloat16
LANES = 128
PACK = 16
NN = (((1,), (0,)), ((), ()))
NT = (((1,), (1,)), ((), ()))


def mm(left, right, dims=NN):
    return lax.dot_general(left, right, dims, preferred_element_type=F32)


def halves(x):
    high = x.astype(BF16)
    return high, (x - high.astype(F32)).astype(BF16)


def round_up(x, to):
    return -(-x // to) * to


def vmem(count):
    return [pl.BlockSpec(memory_space=pltpu.VMEM)] * count


def pack_kernel(rows, half, me_ref, g_ref, out_ref, own_ref, late_ref):
    entries, slabs, cap = g_ref.shape
    groups = LANES // half
    size = PACK * slabs
    to = lax.broadcasted_iota(jnp.int32, (size, size), 0)
    source = lax.broadcasted_iota(jnp.int32, (size, size), 1)
    perm = jnp.where((to % PACK) * slabs + to // PACK == source, 1.0, 0.0).astype(BF16)
    for block in range(rows // PACK):
        early, late = [], []
        for group in range(groups):
            first = group * rows + block * PACK
            valid = max(0, min(PACK, entries - first))
            parts = []
            if valid:
                parts.append(g_ref[first : first + valid])
            if valid < PACK:
                parts.append(jnp.zeros((PACK - valid, slabs, cap), BF16))
            tile = parts[0] if len(parts) == 1 else jnp.concatenate(parts, axis=0)
            tile = tile.reshape(size, cap)
            early.append(tile[:, :half])
            late.append(tile[:, half:])
        both = jnp.concatenate(early + late, axis=1)
        moved = mm(perm, both).astype(BF16).reshape(slabs, PACK, 2 * LANES)
        here = pl.ds(block * PACK, PACK)
        out_ref[:, here, :] = moved[:, :, :LANES]
        late_ref[:, here, :] = moved[:, :, LANES:]
    own_ref[...] = late_ref[me_ref[0]]


def slot_rows(ref, me, half):
    slabs, cap = ref.shape
    per = LANES // half
    rows = []
    for tile in range(slabs // per):
        rows.append(jnp.concatenate([ref[tile * per + k : tile * per + k + 1, :half] for k in range(per)], axis=1))
    own = ref[pl.ds(me, 1), :][:, half:]
    rows.append(jnp.concatenate([own, jnp.full((1, LANES - half), -1, jnp.int32)], axis=1))
    return rows


def edge_kernel(
    half, me_ref, feats_ref, below_ref, above_ref, w_src_ref, w_dst_ref, src_ref, dst_ref, live_ref,
    onehot_ref, hidden_ref, slope_ref,
):
    me = me_ref[0]
    mols = feats_ref.shape[0]
    reach = below_ref.shape[0]
    wide = mols + 2 * reach
    feats = feats_ref[...]
    ext = jnp.concatenate([feats, below_ref[...], above_ref[...]], axis=0)
    proj_src = mm(feats, w_src_ref[...])
    proj_dst = mm(ext, w_dst_ref[...])
    proj = jnp.concatenate([proj_src, proj_dst], axis=0).T
    high, low = halves(proj)
    mol_src = lax.broadcasted_iota(jnp.int32, (mols, LANES), 0)
    mol_dst = lax.broadcasted_iota(jnp.int32, (wide, LANES), 0)
    lists = [slot_rows(ref, me, half) for ref in (src_ref, dst_ref, live_ref)]
    for tile, (src, dst, live) in enumerate(zip(*lists)):
        src = jnp.where(live > 0, src, -1)
        moved = jnp.where(dst < reach, dst + mols, jnp.where(dst < reach + mols, dst - reach, dst))
        dst = jnp.where(live > 0, moved, -1)
        one_src = jnp.where(mol_src == src, 1.0, 0.0).astype(BF16)
        one_dst = jnp.where(mol_dst == dst, 1.0, 0.0).astype(BF16)
        onehot = jnp.concatenate([one_src, one_dst], axis=0)
        here = pl.ds(tile * LANES, LANES)
        onehot_ref[:, here] = onehot
        pre = mm(high, onehot) + mm(low, onehot)
        sigma = 1.0 / (1.0 + jnp.exp(-pre))
        hidden_ref[:, here] = (pre * sigma).astype(BF16)
        slope_ref[:, here] = sigma * (1.0 + pre * (1.0 - sigma))


def grad_kernel(
    half, factor, came_ref, own_ref, onehot_ref, hidden_ref, slope_ref, w_out_ref, ext_ref, w_src_ref, w_dst_ref,
    terms_ref, feature_ref, rims_ref, g_ref,
):
    slabs, rows, _ = came_ref.shape
    groups = LANES // half
    mols = feature_ref.shape[0]
    width = w_src_ref.shape[0]
    for tile in range(slabs // groups + 1):
        if tile < slabs // groups:
            chunks = [came_ref[tile * groups + k] for k in range(groups)]
        else:
            chunks = [own_ref[...]] + [jnp.zeros((rows, LANES), BF16)] * (groups - 1)
        for group in range(groups):
            lanes = slice(group * half, (group + 1) * half)
            g_ref[group * rows : (group + 1) * rows, tile * LANES : (tile + 1) * LANES] = jnp.concatenate(
                [chunk[:, lanes] for chunk in chunks], axis=1
            )
    g = g_ref[...]
    dpre = (mm(w_out_ref[...], g) * slope_ref[...]).astype(BF16)
    sums = mm(onehot_ref[...], dpre, NT)
    rims_ref[...] = sums[2 * mols :]
    high, low = halves(sums)
    feats = ext_ref[:, :mols]
    terms_ref[:, :width] = (factor * (mm(feats, high[:mols]) + mm(feats, low[:mols]))).astype(BF16)
    ext = ext_ref[...]
    terms_ref[:, width : 2 * width] = (factor * (mm(ext, high[mols:]) + mm(ext, low[mols:]))).astype(BF16)
    out_term = factor * mm(hidden_ref[...], g, NT)
    padding = terms_ref.shape[1] - 2 * width - out_term.shape[1]
    if padding:
        out_term = jnp.concatenate([out_term, jnp.zeros((out_term.shape[0], padding), F32)], axis=1)
    terms_ref[:, 2 * width :] = out_term.astype(BF16)
    w_src = w_src_ref[...]
    w_dst = w_dst_ref[...]
    feature_ref[...] = (
        mm(high[:mols], w_src, NT)
        + mm(low[:mols], w_src, NT)
        + mm(high[mols : 2 * mols], w_dst, NT)
        + mm(low[mols : 2 * mols], w_dst, NT)
    )


def rim_kernel(part_ref, from_below_ref, from_above_ref, w_dst_ref, out_ref):
    mols = part_ref.shape[0]
    reach = from_below_ref.shape[0]
    rims = jnp.concatenate([from_below_ref[...], from_above_ref[...]], axis=0)
    high, low = halves(rims)
    w_dst = w_dst_ref[...]
    grad = mm(high, w_dst, NT) + mm(low, w_dst, NT)
    out_ref[:reach] = part_ref[:reach] + grad[:reach]
    out_ref[reach : mols - reach] = part_ref[reach : mols - reach]
    out_ref[mols - reach :] = part_ref[mols - reach :] + grad[reach:]


def total_kernel(terms_ref, src_ref, dst_ref, out_ref):
    width = src_ref.shape[1]
    total = terms_ref[0].astype(F32)
    for slab in range(1, terms_ref.shape[0]):
        total = total + terms_ref[slab].astype(F32)
    src_ref[...] = total[:, :width]
    dst_ref[...] = total[:, width : 2 * width]
    out_ref[...] = total[:, 2 * width : 2 * width + out_ref.shape[1]]


def on_device(mol_feats, w_src, w_dst, w_out, grad_blocks, edge_src, edge_dst, edge_live):
    slabs = lax.axis_size("space")
    mols, width = mol_feats.shape
    entries = w_out.shape[1]
    cap = grad_blocks.shape[2]
    half = cap // 2
    reach = mols // 4
    groups = LANES // half
    rows = round_up(pl.cdiv(entries, groups), PACK)
    slots = (slabs // groups + 1) * LANES
    factor = float(edge_src.shape[0] * slabs) ** (-0.5)
    me = lax.axis_index("space").astype(jnp.int32).reshape(1)
    smem = pl.BlockSpec(memory_space=pltpu.SMEM)
    big = pltpu.CompilerParams(vmem_limit_bytes=48 * 1024 * 1024)
    up = [(i, (i + 1) % slabs) for i in range(slabs)]
    down = [((i + 1) % slabs, i) for i in range(slabs)]

    below = lax.ppermute(mol_feats[mols - reach :], "space", up)
    above = lax.ppermute(mol_feats[:reach], "space", down)

    packed, own = pl.pallas_call(
        functools.partial(pack_kernel, rows, half),
        out_shape=(
            jax.ShapeDtypeStruct((slabs, rows, LANES), BF16),
            jax.ShapeDtypeStruct((rows, LANES), BF16),
        ),
        in_specs=[smem] + vmem(1),
        out_specs=tuple(vmem(2)),
        scratch_shapes=[pltpu.VMEM((slabs, rows, LANES), BF16)],
        compiler_params=big,
        name="pack",
    )(me, jnp.transpose(grad_blocks[0], (2, 0, 1)))
    came = lax.all_to_all(packed, "space", split_axis=0, concat_axis=0, tiled=True)

    onehot, hidden, slope = pl.pallas_call(
        functools.partial(edge_kernel, half),
        out_shape=(
            jax.ShapeDtypeStruct((2 * mols + 2 * reach, slots), BF16),
            jax.ShapeDtypeStruct((width, slots), BF16),
            jax.ShapeDtypeStruct((width, slots), F32),
        ),
        in_specs=[smem] + vmem(8),
        out_specs=tuple(vmem(3)),
        compiler_params=big,
        name="edges",
        cost_estimate=pl.CostEstimate(
            flops=2 * width * slots * 2 * (2 * mols + 2 * reach), bytes_accessed=8 * 1024 * 1024,
            transcendentals=width * slots,
        ),
    )(
        me, mol_feats, below, above, w_src, w_dst,
        edge_src.reshape(slabs, cap), edge_dst.reshape(slabs, cap), edge_live.reshape(slabs, cap),
    )

    ext = jnp.concatenate([mol_feats, below, above], axis=0).T
    w_out_wide = jnp.pad(w_out, ((0, 0), (0, groups * rows - entries)))
    terms, feature_part, rims = pl.pallas_call(
        functools.partial(grad_kernel, half, factor),
        out_shape=(
            jax.ShapeDtypeStruct((width, 2 * width + round_up(groups * rows, LANES)), BF16),
            jax.ShapeDtypeStruct((mols, width), F32),
            jax.ShapeDtypeStruct((2 * reach, width), F32),
        ),
        in_specs=vmem(9),
        out_specs=tuple(vmem(3)),
        scratch_shapes=[pltpu.VMEM((groups * rows, slots), BF16)],
        compiler_params=big,
        name="grads",
    )(came, own, onehot, hidden, slope, w_out_wide, ext, w_src, w_dst)

    from_above = lax.ppermute(rims[:reach], "space", down)
    from_below = lax.ppermute(rims[reach:], "space", up)
    spread = lax.all_to_all(
        terms.reshape(slabs, width // slabs, -1), "space", split_axis=0, concat_axis=0, tiled=True
    )
    feature_grad = pl.pallas_call(
        rim_kernel,
        out_shape=jax.ShapeDtypeStruct((mols, width), F32),
        in_specs=vmem(4),
        out_specs=vmem(1)[0],
        compiler_params=big,
        name="rims",
    )(feature_part, from_below, from_above, w_dst)
    part = width // slabs
    src_grad, dst_grad, out_grad = pl.pallas_call(
        total_kernel,
        out_shape=(
            jax.ShapeDtypeStruct((part, width), F32),
            jax.ShapeDtypeStruct((part, width), F32),
            jax.ShapeDtypeStruct((part, entries), F32),
        ),
        in_specs=vmem(1),
        out_specs=tuple(vmem(3)),
        compiler_params=big,
        name="totals",
    )(spread)
    return (feature_grad, src_grad, dst_grad, out_grad)


def solution(mesh):
    placed = (
        P(("groups", "space"), None),
        P(),
        P(),
        P(),
        P("space", "groups", None, None),
        P(("groups", "space")),
        P(("groups", "space")),
        P(("groups", "space")),
    )
    return jax.shard_map(
        on_device,
        mesh=mesh,
        in_specs=placed,
        out_specs=(
            P(("groups", "space"), None),
            P(("groups", "space"), None),
            P(("groups", "space"), None),
            P(("groups", "space"), None),
        ),
        check_vma=False,
    )
```

time: 293 us -> 109 us (0.37)
  the two profiles are of different devices: /device:TPU:0 before, /device:TPU:15 now
where the time goes in v1:
time: 109 us; the launch traced here: 108 us
  waiting for transfers between devices  58.5 us (54%)
  Pallas kernels  16.8 us (15%)
  starting transfers between devices  16 us (15%)
  local copies, waits for them, and re-layouts  15.2 us (14%)
  other arithmetic  1.19 us (1%)
    ppermute x1, waiting for transfers between devices, on_device(): from_above = lax.ppermute(rims[:reach], 'space', down)  37.6 us
    ppermute x1, waiting for transfers between devices, on_device(): above = lax.ppermute(mol_feats[:reach], 'space', down)  20.9 us
    unnamed x36, local copies, waits for them, and re-layouts  11.8 us
    pallas_call x1, Pallas kernels, on_device(): pl.pallas_call(functools.partial(grad_kernel, half, factor), out_shape=(j...  7.38 us
    all_to_all x1, starting transfers between devices, on_device(): lax.all_to_all(packed, 'space', split_axis=0, concat_axis=0, tiled=True)  6.55 us
    pallas_call x1, Pallas kernels, on_device(): pl.pallas_call(functools.partial(edge_kernel, half), out_shape=(jax.Shape...  5.43 us
    all_to_all x1, starting transfers between devices, on_device(): lax.all_to_all(terms.reshape(slabs, width // slabs, -1), 'space', split_a...  4.1 us
    ppermute x1, starting transfers between devices, on_device(): from_below = lax.ppermute(rims[reach:], 'space', up)  2.28 us
  transfers between devices with their start and end apart: 6, of which 2 were waited for; matrix products, arithmetic and copies ran while one was open for 6% of the time, Pallas kernels for 6%

profile of v1, /device:TPU:15, one launch (start us, length us, event | category | flops | bytes accessed | tf_op | source)
XLA Modules:
  0.0 108.4 jit_solution(16996892705889207292)
XLA Ops:
  0.6 1.6 %copy-done = bf16[1,16,128,529]{2,1,3,0:T(8,128)(2,1)S(1)} copy-done((bf16[1,16,128,529]{2,1,3,0:T(8,128)(2,1)S(1)}, bf16[1,16,128,529]{2,1,3,0:T(8,128)(2,1)}, u32[]{:S(2)}) %copy-start) | copy-done | bytes 2166808
  2.2 1.9 %pack.1 = (bf16[16,272,128]{2,1,0:T(8,128)(2,1)}, bf16[272,128]{1,0:T(8,128)(2,1)S(1)}) custom-call(s32[1]{0:T(128)} %bitcast.me_ref, bf16[529,16,128]{2,1,0:T(8,128)(2,1)S(1)} %bitcast.10), custom_call_target="tpu_custom_call" | custom-call | tf_op jit(solution)/shard_map/pack/pallas_call | solution.py:191
  4.1 6.6 %all-to-all-start = ((bf16[16,272,128]{2,1,0:T(8,128)(2,1)}), bf16[16,272,128]{2,1,0:T(8,128)(2,1)S(1)}, u32[]{:S(2)}, u32[]{:S(2)}) async-start(bf16[16,272,128]{2,1,0:T(8,128)(2,1)} %get-tuple-element.15), calls=%async_computation | async-start | bytes 2228224 | tf_op jit(solution)/shard_map/all_to_all | solution.py:203
  10.7 0.1 copy.12
  10.8 0.0 copy-start.14
  10.8 0.7 fusion.1
  11.6 0.4 collective-permute-start.1
  11.9 2.3 %collective-permute-start = (bf16[64,512]{0,1:T(8,128)(2,1)S(1)}, bf16[64,512]{0,1:T(8,128)(2,1)S(1)}, u32[]{:S(2)}, u32[]{:S(2)}) collective-permute-start(bf16[64,512]{0,1:T(8,128)(2,1)S(1)} %get-tuple-element.29), channel_id=1, source_target_pairs={{0,1},{1,2},{2,3},{3,4},{4,5},{5,6},{6,7},{7,8},{8,9},{9,10},{10,1... | collective-permute-start | bytes 196616 | tf_op jit(solution)/shard_map/ppermute | solution.py:188
  14.2 2.1 %copy.16 = bf16[512,529]{1,0:T(8,128)(2,1)} copy(bf16[512,529]{0,1:T(8,128)(2,1)} %param.11) | data formatting | bytes 1083392 | tf_op args[3]
  16.4 1.1 %pad.4.w_out_ref = bf16[512,544]{1,0:T(8,128)(2,1)S(1)} pad(bf16[512,529]{1,0:T(8,128)(2,1)} %copy.16, bf16[]{:T(256)} %constant.6.clone.1), padding=0_0x0_15 | pad | bytes 1098754 | tf_op jit(solution)/shard_map/jit(_pad)/pad | solution.py:226
  17.5 20.9 %collective-permute-done.1 = bf16[64,512]{0,1:T(8,128)(2,1)S(1)} collective-permute-done((bf16[64,512]{0,1:T(8,128)(2,1)}, bf16[64,512]{0,1:T(8,128)(2,1)S(1)}, u32[]{:S(2)}, u32[]{:S(2)}) %collective-permute-start.1) | collective-permute-done | bytes 65568 | tf_op jit(solution)/shard_map/ppermute | solution.py:189
  38.4 0.7 copy.15.above_ref
  39.1 0.6 copy-done.16
  39.8 0.7 copy.14.below_ref
  40.5 1.2 %maximum_bitcast_fusion.ext_ref = bf16[512,384]{1,0:T(8,128)(2,1)S(1)} fusion(bf16[64,512]{0,1:T(8,128)(2,1)} %copy-done.15, bf16[64,512]{0,1:T(8,128)(2,1)} %copy-done.16, bf16[256,512]{0,1:T(8,128)(2,1)} %copy-done.14), kind=kLoop, calls=%fused_computation | loop fusion | flops 1179648 | bytes 786432 | tf_op jit(solution)/shard_map/transpose | solution.py:225
  41.7 0.0 copy-start.9
  41.7 0.8 copy-done.9
  42.6 0.8 copy-done.10
  43.4 0.7 copy-done.12
  44.1 0.7 copy-done.13
  44.8 5.4 %edges.1 = (bf16[640,1152]{1,0:T(8,128)(2,1)S(1)}, bf16[512,1152]{1,0:T(8,128)(2,1)S(1)}, f32[512,1152]{1,0:T(8,128)}) custom-call(s32[1]{0:T(128)} %bitcast.me_ref, bf16[256,512]{1,0:T(8,128)(2,1)S(1)} %copy-done.8, bf16[64,512]{1,0:T(8,128)(2,1)S(1)} %copy-done.10, bf16[64,512]{1,0:T(8,128)(2,1)S(1)} %copy-done.9, bf16[512,512]{1,0:T(8,128)(2,1)S(1)} %copy-done.5, ...), custom_call_target="tpu_custom_call" | custom-call | flops 1509949440 | bytes 8388608 | tf_op jit(solution)/shard_map/edges/pallas_call | solution.py:205
  50.2 1.2 %copy-done.2 = bf16[640,1152]{1,0:T(8,128)(2,1)} copy-done((bf16[640,1152]{1,0:T(8,128)(2,1)}, bf16[640,1152]{1,0:T(8,128)(2,1)S(1)}, u32[]{:S(2)}) %copy-start.2) | copy-done | bytes 1474584
  51.4 1.0 copy-done.3
  52.4 1.3 %copy-done.4 = bf16[512,1152]{1,0:T(8,128)(2,1)S(1)} copy-done((bf16[512,1152]{1,0:T(8,128)(2,1)S(1)}, bf16[512,1152]{1,0:T(8,128)(2,1)}, u32[]{:S(2)}) %copy-start.4) | copy-done | bytes 1179672
  53.7 7.4 %grads.1 = (bf16[512,1664]{1,0:T(8,128)(2,1)}, f32[256,512]{1,0:T(8,128)S(1)}, f32[128,512]{1,0:T(8,128)S(1)}) custom-call(bf16[16,272,128]{2,1,0:T(8,128)(2,1)S(1)} %all-to-all-done.came_ref, bf16[272,128]{1,0:T(8,128)(2,1)S(1)} %get-tuple-element.16.own_ref, bf16[640,1152]{1,0:T(8,128)(2,1)} %copy-done.2, bf16[512,1152]{1,0:T(8,128)(2,1)S(1)} %copy-done.4, ...), custom_call_target="tpu_custom_call" | custom-call | tf_op jit(solution)/shard_map/grads/pallas_call | solution.py:227
  61.0 0.8 copy-done.6
  61.8 4.1 %all-to-all-start.1 = ((bf16[16,32,1664]{2,1,0:T(8,128)(2,1)}), bf16[16,32,1664]{2,1,0:T(8,128)(2,1)S(1)}, u32[]{:S(2)}, u32[]{:S(2)}) async-start(bf16[16,32,1664]{2,1,0:T(8,128)(2,1)} %bitcast.14), calls=%async_computation.1 | async-start | bytes 3407872 | tf_op jit(solution)/shard_map/all_to_all | solution.py:243
  66.0 0.4 collective-permute-start.3
  66.4 2.3 %collective-permute-start.2 = (f32[64,512]{1,0:T(8,128)S(1)}, f32[64,512]{1,0:T(8,128)S(1)}, u32[]{:S(2)}, u32[]{:S(2)}) collective-permute-start(f32[64,512]{1,0:T(8,128)S(1)} %get-tuple-element.27), channel_id=1, source_target_pairs={{0,1},{1,2},{2,3},{3,4},{4,5},{5,6},{6,7},{7,8},{8,9},{9,10},{10,1... | collective-permute-start | bytes 393224 | tf_op jit(solution)/shard_map/ppermute | solution.py:242
  68.7 37.6 %collective-permute-done.3.from_above_ref = f32[64,512]{1,0:T(8,128)S(1)} collective-permute-done((f32[64,512]{1,0:T(8,128)S(1)}, f32[64,512]{1,0:T(8,128)S(1)}, u32[]{:S(2)}, u32[]{:S(2)}) %collective-permute-start.3) | collective-permute-done | bytes 131104 | tf_op jit(solution)/shard_map/ppermute | solution.py:241
  106.3 1.3 %rims.1 = f32[256,512]{1,0:T(8,128)} custom-call(f32[256,512]{1,0:T(8,128)S(1)} %copy-done.7, f32[64,512]{1,0:T(8,128)S(1)} %collective-permute-done.2.from_below_ref, f32[64,512]{1,0:T(8,128)S(1)} %collective-permute-done.3.from_above_ref, bf16[512,512]{1,0:T(8,128)(2,1)S(1)} %copy-done.1), custom_call_target="tpu_custom_call" | custom-call | tf_op jit(solution)/shard_map/rims/pallas_call | solution.py:246
  107.6 0.9 totals.1
  (27 shorter events, 0.1 us)
Async XLA Ops:
  0.6 1.6 %copy-start = (bf16[1,16,128,529]{2,1,3,0:T(8,128)(2,1)S(1)}, bf16[1,16,128,529]{2,1,3,0:T(8,128)(2,1)}, u32[]{:S(2)}) copy-start(bf16[1,16,128,529]{2,1,3,0:T(8,128)(2,1)} %param.12) | copy-start | bytes 6500356
  2.2 8.4 %copy-start.8 = (bf16[256,512]{1,0:T(8,128)(2,1)S(1)}, bf16[256,512]{1,0:T(8,128)(2,1)}, u32[]{:S(2)}) copy-start(bf16[256,512]{1,0:T(8,128)(2,1)} %feats_ref.1) | copy-start | bytes 786436
  4.1 48.3 %all-to-all-start = ((bf16[16,272,128]{2,1,0:T(8,128)(2,1)}), bf16[16,272,128]{2,1,0:T(8,128)(2,1)S(1)}, u32[]{:S(2)}, u32[]{:S(2)}) async-start(bf16[16,272,128]{2,1,0:T(8,128)(2,1)} %get-tuple-element.15), calls=%async_computation | async-start | bytes 2228224 | tf_op jit(solution)/shard_map/all_to_all | solution.py:203
  10.8 3.4 %copy-start.14 = (bf16[256,512]{0,1:T(8,128)(2,1)}, bf16[256,512]{0,1:T(8,128)(2,1)S(1)}, u32[]{:S(2)}) copy-start(bf16[256,512]{0,1:T(8,128)(2,1)S(1)} %copy.12) | copy-start | bytes 786436
  11.6 26.8 %collective-permute-start.1 = (bf16[64,512]{0,1:T(8,128)(2,1)}, bf16[64,512]{0,1:T(8,128)(2,1)S(1)}, u32[]{:S(2)}, u32[]{:S(2)}) collective-permute-start(bf16[64,512]{0,1:T(8,128)(2,1)} %get-tuple-element.28), channel_id=1, source_target_pairs={{1,0},{2,1},{3,2},{4,3},{5,4},{6,5},{7,6},{8,7},{9,8},{10,9},{11,1... | collective-permute-start | bytes 196616 | tf_op jit(solution)/shard_map/ppermute | solution.py:189
  11.9 29.8 %copy-start.1 = (bf16[512,512]{1,0:T(8,128)(2,1)S(1)}, bf16[512,512]{1,0:T(8,128)(2,1)}, u32[]{:S(2)}) copy-start(bf16[512,512]{1,0:T(8,128)(2,1)} %w_dst_ref.5) | copy-start | bytes 1572868
  11.9 29.8 %copy-start.5 = (bf16[512,512]{1,0:T(8,128)(2,1)S(1)}, bf16[512,512]{1,0:T(8,128)(2,1)}, u32[]{:S(2)}) copy-start(bf16[512,512]{1,0:T(8,128)(2,1)} %w_src_ref.3) | copy-start | bytes 1572868
  11.9 29.8 %copy-start.11 = (s32[2048]{0:T(1024)S(1)}, s32[2048]{0:T(1024)}, u32[]{:S(2)}) copy-start(s32[2048]{0:T(1024)} %param.13) | copy-start | bytes 24580
  11.9 27.2 %collective-permute-start = (bf16[64,512]{0,1:T(8,128)(2,1)S(1)}, bf16[64,512]{0,1:T(8,128)(2,1)S(1)}, u32[]{:S(2)}, u32[]{:S(2)}) collective-permute-start(bf16[64,512]{0,1:T(8,128)(2,1)S(1)} %get-tuple-element.29), channel_id=1, source_target_pairs={{0,1},{1,2},{2,3},{3,4},{4,5},{5,6},{6,7},{7,8},{8,9},{9,10},{10,1... | collective-permute-start | bytes 196616 | tf_op jit(solution)/shard_map/ppermute | solution.py:188
  38.4 0.7 copy-start.15
  39.1 0.6 copy-start.16
  41.7 0.8 copy-start.9
  42.6 0.8 copy-start.10
  43.4 0.7 copy-start.12
  44.1 0.7 copy-start.13
  50.2 1.2 %copy-start.2 = (bf16[640,1152]{1,0:T(8,128)(2,1)}, bf16[640,1152]{1,0:T(8,128)(2,1)S(1)}, u32[]{:S(2)}) copy-start(bf16[640,1152]{1,0:T(8,128)(2,1)S(1)} %get-tuple-element.17.onehot_ref) | copy-start | bytes 4423684
  51.4 1.0 copy-start.3
  52.4 1.3 %copy-start.4 = (bf16[512,1152]{1,0:T(8,128)(2,1)S(1)}, bf16[512,1152]{1,0:T(8,128)(2,1)}, u32[]{:S(2)}) copy-start(bf16[512,1152]{1,0:T(8,128)(2,1)} %copy-done.3) | copy-start | bytes 3538948
  61.0 0.8 copy-start.6
  61.8 44.5 %copy-start.7 = (f32[256,512]{1,0:T(8,128)S(1)}, f32[256,512]{1,0:T(8,128)}, u32[]{:S(2)}) copy-start(f32[256,512]{1,0:T(8,128)} %copy-done.6) | copy-start | bytes 1572868
  61.8 45.7 %all-to-all-start.1 = ((bf16[16,32,1664]{2,1,0:T(8,128)(2,1)}), bf16[16,32,1664]{2,1,0:T(8,128)(2,1)S(1)}, u32[]{:S(2)}, u32[]{:S(2)}) async-start(bf16[16,32,1664]{2,1,0:T(8,128)(2,1)} %bitcast.14), calls=%async_computation.1 | async-start | bytes 3407872 | tf_op jit(solution)/shard_map/all_to_all | solution.py:243
  66.0 40.3 %collective-permute-start.3 = (f32[64,512]{1,0:T(8,128)S(1)}, f32[64,512]{1,0:T(8,128)S(1)}, u32[]{:S(2)}, u32[]{:S(2)}) collective-permute-start(f32[64,512]{1,0:T(8,128)S(1)} %get-tuple-element.26), channel_id=1, source_target_pairs={{1,0},{2,1},{3,2},{4,3},{5,4},{6,5},{7,6},{8,7},{9,8},{10,9},{11,1... | collective-permute-start | bytes 393224 | tf_op jit(solution)/shard_map/ppermute | solution.py:241
  66.4 39.9 %collective-permute-start.2 = (f32[64,512]{1,0:T(8,128)S(1)}, f32[64,512]{1,0:T(8,128)S(1)}, u32[]{:S(2)}, u32[]{:S(2)}) collective-permute-start(f32[64,512]{1,0:T(8,128)S(1)} %get-tuple-element.27), channel_id=1, source_target_pairs={{0,1},{1,2},{2,3},{3,4},{4,5},{5,6},{6,7},{7,8},{8,9},{9,10},{10,1... | collective-permute-start | bytes 393224 | tf_op jit(solution)/shard_map/ppermute | solution.py:242

commit v2 on v1

--- a/solution.py
+++ b/solution.py
@@ -74,7 +74,7 @@
 
 def edge_kernel(
     half, me_ref, feats_ref, below_ref, above_ref, w_src_ref, w_dst_ref, src_ref, dst_ref, live_ref,
-    onehot_ref, hidden_ref, slope_ref,
+    onehot_ref, hidden_ref, slope_ref, ext_ref,
 ):
     me = me_ref[0]
     mols = feats_ref.shape[0]
@@ -82,6 +82,7 @@
     wide = mols + 2 * reach
     feats = feats_ref[...]
     ext = jnp.concatenate([feats, below_ref[...], above_ref[...]], axis=0)
+    ext_ref[...] = ext.T
     proj_src = mm(feats, w_src_ref[...])
     proj_dst = mm(ext, w_dst_ref[...])
     proj = jnp.concatenate([proj_src, proj_dst], axis=0).T
@@ -104,10 +105,34 @@
         slope_ref[:, here] = sigma * (1.0 + pre * (1.0 - sigma))
 
 
+def halve(terms, odd, keep_ref, send_ref, first):
+    count, rows, _ = keep_ref.shape
+    lanes = slice(first, first + terms.shape[-1])
+    pairs = terms.reshape(count, 2, rows, terms.shape[-1])
+    even_part, odd_part = pairs[:, 0], pairs[:, 1]
+    keep_ref[:, :, lanes] = jnp.where(odd > 0, odd_part, even_part)
+    send_ref[:, :, lanes] = jnp.where(odd > 0, even_part, odd_part).astype(BF16)
+
+
+def fold_kernel(bit, me_ref, keep_ref, came_ref, next_ref, send_ref):
+    odd = (me_ref[0] >> bit) % 2
+    halve(keep_ref[...] + came_ref[...].astype(F32), odd, next_ref, send_ref, 0)
+
+
+def direct_kernel(bit, me_ref, keep_ref, came_ref, own_ref, *rest):
+    *send_refs, total_ref = rest
+    mine = me_ref[0] >> bit
+    total_ref[...] = keep_ref[...] + came_ref[...].astype(F32)
+    own_ref[...] = total_ref[mine]
+    for step, send_ref in enumerate(send_refs):
+        send_ref[...] = total_ref[mine ^ (step + 1)].astype(BF16)
+
+
 def grad_kernel(
-    half, factor, came_ref, own_ref, onehot_ref, hidden_ref, slope_ref, w_out_ref, ext_ref, w_src_ref, w_dst_ref,
-    terms_ref, feature_ref, rims_ref, g_ref,
+    half, factor, me_ref, came_ref, own_ref, onehot_ref, hidden_ref, slope_ref, w_out_ref, ext_ref, w_src_ref, w_dst_ref,
+    keep_ref, send_ref, feature_ref, rims_ref, g_ref,
 ):
+    odd = me_ref[0] % 2
     slabs, rows, _ = came_ref.shape
     groups = LANES // half
     mols = feature_ref.shape[0]
@@ -128,14 +153,14 @@
     rims_ref[...] = sums[2 * mols :]
     high, low = halves(sums)
     feats = ext_ref[:, :mols]
-    terms_ref[:, :width] = (factor * (mm(feats, high[:mols]) + mm(feats, low[:mols]))).astype(BF16)
     ext = ext_ref[...]
-    terms_ref[:, width : 2 * width] = (factor * (mm(ext, high[mols:]) + mm(ext, low[mols:]))).astype(BF16)
+    halve(factor * (mm(feats, high[:mols]) + mm(feats, low[:mols])), odd, keep_ref, send_ref, 0)
+    halve(factor * (mm(ext, high[mols:]) + mm(ext, low[mols:])), odd, keep_ref, send_ref, width)
     out_term = factor * mm(hidden_ref[...], g, NT)
-    padding = terms_ref.shape[1] - 2 * width - out_term.shape[1]
+    padding = keep_ref.shape[2] - 2 * width - out_term.shape[1]
     if padding:
         out_term = jnp.concatenate([out_term, jnp.zeros((out_term.shape[0], padding), F32)], axis=1)
-    terms_ref[:, 2 * width :] = out_term.astype(BF16)
+    halve(out_term, odd, keep_ref, send_ref, 2 * width)
     w_src = w_src_ref[...]
     w_dst = w_dst_ref[...]
     feature_ref[...] = (
@@ -158,14 +183,19 @@
     out_ref[mols - reach :] = part_ref[mols - reach :] + grad[reach:]
 
 
-def total_kernel(terms_ref, src_ref, dst_ref, out_ref):
+def total_kernel(own_ref, *rest):
+    *came_refs, src_ref, dst_ref, out_ref = rest
     width = src_ref.shape[1]
-    total = terms_ref[0].astype(F32)
-    for slab in range(1, terms_ref.shape[0]):
-        total = total + terms_ref[slab].astype(F32)
+    total = own_ref[...]
+    for came_ref in came_refs:
+        total = total + came_ref[...].astype(F32)
     src_ref[...] = total[:, :width]
     dst_ref[...] = total[:, width : 2 * width]
     out_ref[...] = total[:, 2 * width : 2 * width + out_ref.shape[1]]
+
+
+def swap(block, bit, slabs):
+    return lax.ppermute(block, "space", [(i, i ^ (1 << bit)) for i in range(slabs)])
 
 
 def on_device(mol_feats, w_src, w_dst, w_out, grad_blocks, edge_src, edge_dst, edge_live):
@@ -181,7 +211,7 @@
     factor = float(edge_src.shape[0] * slabs) ** (-0.5)
     me = lax.axis_index("space").astype(jnp.int32).reshape(1)
     smem = pl.BlockSpec(memory_space=pltpu.SMEM)
-    big = pltpu.CompilerParams(vmem_limit_bytes=48 * 1024 * 1024)
+    big = pltpu.CompilerParams(vmem_limit_bytes=24 * 1024 * 1024)
     up = [(i, (i + 1) % slabs) for i in range(slabs)]
     down = [((i + 1) % slabs, i) for i in range(slabs)]
 
@@ -200,17 +230,19 @@
         compiler_params=big,
         name="pack",
     )(me, jnp.transpose(grad_blocks[0], (2, 0, 1)))
+    packed, below, above = lax.optimization_barrier((packed, below, above))
     came = lax.all_to_all(packed, "space", split_axis=0, concat_axis=0, tiled=True)
 
-    onehot, hidden, slope = pl.pallas_call(
+    onehot, hidden, slope, ext = pl.pallas_call(
         functools.partial(edge_kernel, half),
         out_shape=(
             jax.ShapeDtypeStruct((2 * mols + 2 * reach, slots), BF16),
             jax.ShapeDtypeStruct((width, slots), BF16),
             jax.ShapeDtypeStruct((width, slots), F32),
+            jax.ShapeDtypeStruct((width, mols + 2 * reach), BF16),
         ),
         in_specs=[smem] + vmem(8),
-        out_specs=tuple(vmem(3)),
+        out_specs=tuple(vmem(4)),
         compiler_params=big,
         name="edges",
         cost_estimate=pl.CostEstimate(
@@ -222,27 +254,57 @@
         edge_src.reshape(slabs, cap), edge_dst.reshape(slabs, cap), edge_live.reshape(slabs, cap),
     )
 
-    ext = jnp.concatenate([mol_feats, below, above], axis=0).T
     w_out_wide = jnp.pad(w_out, ((0, 0), (0, groups * rows - entries)))
-    terms, feature_part, rims = pl.pallas_call(
+    part = width // slabs
+    lanes = 2 * width + round_up(groups * rows, LANES)
+    bits = 2
+    rest = slabs >> bits
+
+    def chunks(count, dtype):
+        return jax.ShapeDtypeStruct((count, part, lanes), dtype)
+
+    keep, send, feature_part, rims = pl.pallas_call(
         functools.partial(grad_kernel, half, factor),
         out_shape=(
-            jax.ShapeDtypeStruct((width, 2 * width + round_up(groups * rows, LANES)), BF16),
+            chunks(slabs // 2, F32),
+            chunks(slabs // 2, BF16),
             jax.ShapeDtypeStruct((mols, width), F32),
             jax.ShapeDtypeStruct((2 * reach, width), F32),
         ),
-        in_specs=vmem(9),
-        out_specs=tuple(vmem(3)),
+        in_specs=[smem] + vmem(9),
+        out_specs=tuple(vmem(4)),
         scratch_shapes=[pltpu.VMEM((groups * rows, slots), BF16)],
         compiler_params=big,
         name="grads",
-    )(came, own, onehot, hidden, slope, w_out_wide, ext, w_src, w_dst)
-
+    )(me, came, own, onehot, hidden, slope, w_out_wide, ext, w_src, w_dst)
+
+    crossed = swap(send, 0, slabs)
     from_above = lax.ppermute(rims[:reach], "space", down)
     from_below = lax.ppermute(rims[reach:], "space", up)
-    spread = lax.all_to_all(
-        terms.reshape(slabs, width // slabs, -1), "space", split_axis=0, concat_axis=0, tiled=True
-    )
+    for bit in range(1, bits):
+        keep, send = pl.pallas_call(
+            functools.partial(fold_kernel, bit),
+            out_shape=(chunks(keep.shape[0] // 2, F32), chunks(keep.shape[0] // 2, BF16)),
+            in_specs=[smem] + vmem(2),
+            out_specs=tuple(vmem(2)),
+            compiler_params=big,
+            name="fold",
+        )(me, keep, crossed)
+        crossed = swap(send, bit, slabs)
+    one = jax.ShapeDtypeStruct((part, lanes), BF16)
+    own_term, *sends = pl.pallas_call(
+        functools.partial(direct_kernel, bits),
+        out_shape=(jax.ShapeDtypeStruct((part, lanes), F32),) + (one,) * (rest - 1),
+        in_specs=[smem] + vmem(2),
+        out_specs=tuple(vmem(rest)),
+        scratch_shapes=[pltpu.VMEM((rest, part, lanes), F32)],
+        compiler_params=big,
+        name="direct",
+    )(me, keep, crossed)
+    cames = [
+        lax.ppermute(block, "space", [(i, i ^ ((step + 1) << bits)) for i in range(slabs)])
+        for step, block in enumerate(sends)
+    ]
     feature_grad = pl.pallas_call(
         rim_kernel,
         out_shape=jax.ShapeDtypeStruct((mols, width), F32),
@@ -251,7 +313,6 @@
         compiler_params=big,
         name="rims",
     )(feature_part, from_below, from_above, w_dst)
-    part = width // slabs
     src_grad, dst_grad, out_grad = pl.pallas_call(
         total_kernel,
         out_shape=(
@@ -259,11 +320,11 @@
             jax.ShapeDtypeStruct((part, width), F32),
             jax.ShapeDtypeStruct((part, entries), F32),
         ),
-        in_specs=vmem(1),
+        in_specs=vmem(rest),
         out_specs=tuple(vmem(3)),
         compiler_params=big,
         name="totals",
-    )(spread)
+    )(own_term, *cames)
     return (feature_grad, src_grad, dst_grad, out_grad)
 
 

time: 109 us -> 84 us (0.77)
  the two profiles are of different devices: /device:TPU:15 before, /device:TPU:0 now
where the time goes in v2:
time: 84 us; the launch traced here: 83.3 us
  waiting for transfers between devices  30 us (36%)
  starting transfers between devices  21.4 us (25%)
  local copies, waits for them, and re-layouts  18.2 us (22%)
  Pallas kernels  12.9 us (15%)
    unnamed x39, local copies, waits for them, and re-layouts  17.2 us
    all_to_all x1, waiting for transfers between devices, on_device(): lax.all_to_all(packed, 'space', split_axis=0, concat_axis=0, tiled=True)  10.5 us
    ppermute x2, waiting for transfers between devices, swap(): lax.ppermute(block, 'space', [(i, i ^ 1 << bit) for i in range(slabs)])  10.4 us
    ppermute x3, waiting for transfers between devices, on_device(): lax.ppermute(block, 'space', [(i, i ^ step + 1 << bits) for i in range(sl...  6.75 us
    ppermute x3, starting transfers between devices, on_device(): lax.ppermute(block, 'space', [(i, i ^ step + 1 << bits) for i in range(sl...  5.99 us
    ppermute x1, starting transfers between devices, on_device(): above = lax.ppermute(mol_feats[:reach], 'space', down)  5.5 us
    pallas_call x1, Pallas kernels, on_device(): pl.pallas_call(functools.partial(grad_kernel, half, factor), out_shape=(c...  4.69 us
    pallas_call x1, Pallas kernels, on_device(): pl.pallas_call(functools.partial(edge_kernel, half), out_shape=(jax.Shape...  4.02 us
  transfers between devices with their start and end apart: 10, of which 5 were waited for; matrix products, arithmetic and copies ran while one was open for 0% of the time, Pallas kernels for 9%

profile of v2, /device:TPU:0, one launch (start us, length us, event | category | flops | bytes accessed | tf_op | source)
XLA Modules:
  0.0 83.3 jit_solution(2988931481306152535)
XLA Ops:
  0.6 0.9 %fusion.1 = (bf16[64,512]{1,0:T(8,128)(2,1)S(1)}, bf16[64,512]{1,0:T(8,128)(2,1)S(1)}) fusion(bf16[256,512]{1,0:T(8,128)(2,1)} %feats_ref.1), kind=kLoop, calls=%fused_computation.1 | loop fusion | bytes 262144 | tf_op jit(solution)/shard_map/slice | solution.py:219
  1.5 5.5 %collective-permute-start.1 = (bf16[64,512]{1,0:T(8,128)(2,1)S(1)}, bf16[64,512]{1,0:T(8,128)(2,1)S(1)}, u32[]{:S(2)}, u32[]{:S(2)}) collective-permute-start(bf16[64,512]{1,0:T(8,128)(2,1)S(1)} %get-tuple-element.50), channel_id=1, source_target_pairs={{1,0},{2,1},{3,2},{4,3},{5,4},{6,5},{7,6},{8,7},{9,8},{10,9},{11,1... | collective-permute-start | bytes 196616 | tf_op jit(solution)/shard_map/ppermute | solution.py:219
  7.0 1.6 %copy-done.2 = bf16[1,16,128,529]{2,1,3,0:T(8,128)(2,1)S(1)} copy-done((bf16[1,16,128,529]{2,1,3,0:T(8,128)(2,1)S(1)}, bf16[1,16,128,529]{2,1,3,0:T(8,128)(2,1)}, u32[]{:S(2)}) %copy-start.2) | copy-done | bytes 2166808
  8.6 1.9 %pack.1 = (bf16[16,272,128]{2,1,0:T(8,128)(2,1)}, bf16[272,128]{1,0:T(8,128)(2,1)S(1)}) custom-call(s32[1]{0:T(128)} %bitcast.me_ref, bf16[529,16,128]{2,1,0:T(8,128)(2,1)S(1)} %bitcast.7), custom_call_target="tpu_custom_call" | custom-call | tf_op jit(solution)/shard_map/pack/pallas_call | solution.py:221
  11.1 2.3 %collective-permute-done.below_ref = bf16[64,512]{1,0:T(8,128)(2,1)S(1)} collective-permute-done((bf16[64,512]{1,0:T(8,128)(2,1)S(1)}, bf16[64,512]{1,0:T(8,128)(2,1)S(1)}, u32[]{:S(2)}, u32[]{:S(2)}) %collective-permute-start) | collective-permute-done | bytes 65568 | tf_op jit(solution)/shard_map/ppermute | solution.py:218
  14.0 3.7 %all-to-all-start = ((bf16[16,272,128]{2,1,0:T(8,128)(2,1)}), bf16[16,272,128]{2,1,0:T(8,128)(2,1)S(1)}, u32[]{:S(2)}, u32[]{:S(2)}) async-start(bf16[16,272,128]{2,1,0:T(8,128)(2,1)} %get-tuple-element.27), calls=%async_computation | async-start | bytes 2228224 | tf_op jit(solution)/shard_map/all_to_all | solution.py:234
  18.8 1.0 %copy-done.6 = bf16[512,512]{1,0:T(8,128)(2,1)S(1)} copy-done((bf16[512,512]{1,0:T(8,128)(2,1)S(1)}, bf16[512,512]{1,0:T(8,128)(2,1)}, u32[]{:S(2)}) %copy-start.6) | copy-done | bytes 524312
  19.8 0.9 %copy-done.10 = bf16[256,512]{1,0:T(8,128)(2,1)S(1)} copy-done((bf16[256,512]{1,0:T(8,128)(2,1)S(1)}, bf16[256,512]{1,0:T(8,128)(2,1)}, u32[]{:S(2)}) %copy-start.10) | copy-done | bytes 262168
  20.8 0.8 %copy-done.12 = bf16[64,512]{1,0:T(8,128)(2,1)S(1)} copy-done((bf16[64,512]{1,0:T(8,128)(2,1)S(1)}, bf16[64,512]{1,0:T(8,128)(2,1)}, u32[]{:S(2)}) %copy-start.12) | copy-done | bytes 65560
  21.6 0.8 %copy-done.14 = bf16[64,512]{1,0:T(8,128)(2,1)S(1)} copy-done((bf16[64,512]{1,0:T(8,128)(2,1)S(1)}, bf16[64,512]{1,0:T(8,128)(2,1)}, u32[]{:S(2)}) %copy-start.14) | copy-done | bytes 65560
  22.5 0.7 copy-done.16
  23.9 4.0 %edges.1 = (bf16[640,1152]{1,0:T(8,128)(2,1)S(1)}, bf16[512,1152]{1,0:T(8,128)(2,1)S(1)}, f32[512,1152]{1,0:T(8,128)S(1)}, bf16[512,384]{1,0:T(8,128)(2,1)S(1)}) custom-call(s32[1]{0:T(128)} %bitcast.me_ref, bf16[256,512]{1,0:T(8,128)(2,1)S(1)} %copy-done.10, bf16[64,512]{1,0:T(8,128)(2,1)S(1)} %copy-done.14, bf16[64,512]{1,0:T(8,128)(2,1)S(1)} %copy-done.12, ...), custom_call_target="tpu_custom_call" | custom-call | flops 1509949440 | bytes 8388608 | tf_op jit(solution)/shard_map/edges/pallas_call | solution.py:236
  27.9 1.4 %copy-done = f32[512,1152]{1,0:T(8,128)} copy-done((f32[512,1152]{1,0:T(8,128)}, f32[512,1152]{1,0:T(8,128)S(1)}, u32[]{:S(2)}) %copy-start) | copy-done | bytes 2359320
  29.3 1.1 %copy-done.4 = bf16[640,1152]{1,0:T(8,128)(2,1)} copy-done((bf16[640,1152]{1,0:T(8,128)(2,1)}, bf16[640,1152]{1,0:T(8,128)(2,1)S(1)}, u32[]{:S(2)}) %copy-start.4) | copy-done | bytes 1474584
  30.4 0.7 copy-done.8
  31.2 10.5 %all-to-all-done.came_ref = bf16[16,272,128]{2,1,0:T(8,128)(2,1)S(1)} async-done(((bf16[16,272,128]{2,1,0:T(8,128)(2,1)}), bf16[16,272,128]{2,1,0:T(8,128)(2,1)S(1)}, u32[]{:S(2)}, u32[]{:S(2)}) %all-to-all-start) | async-done | bytes 1114144 | tf_op jit(solution)/shard_map/all_to_all | solution.py:234
  41.7 1.7 %copy-done.1 = f32[512,1152]{1,0:T(8,128)S(1)} copy-done((f32[512,1152]{1,0:T(8,128)S(1)}, f32[512,1152]{1,0:T(8,128)}, u32[]{:S(2)}) %copy-start.1) | copy-done | bytes 2359320
  43.4 1.4 %copy-done.5 = bf16[640,1152]{1,0:T(8,128)(2,1)S(1)} copy-done((bf16[640,1152]{1,0:T(8,128)(2,1)S(1)}, bf16[640,1152]{1,0:T(8,128)(2,1)}, u32[]{:S(2)}) %copy-start.5) | copy-done | bytes 1474584
  44.8 1.0 %copy-done.7 = bf16[512,512]{1,0:T(8,128)(2,1)S(1)} copy-done((bf16[512,512]{1,0:T(8,128)(2,1)S(1)}, bf16[512,512]{1,0:T(8,128)(2,1)}, u32[]{:S(2)}) %copy-start.7) | copy-done | bytes 524312
  45.8 1.0 %copy-done.9 = bf16[512,384]{1,0:T(8,128)(2,1)S(1)} copy-done((bf16[512,384]{1,0:T(8,128)(2,1)S(1)}, bf16[512,384]{1,0:T(8,128)(2,1)}, u32[]{:S(2)}) %copy-start.9) | copy-done | bytes 393240
  46.8 4.7 %grads.1 = (f32[8,32,1664]{2,1,0:T(8,128)S(1)}, bf16[8,32,1664]{2,1,0:T(8,128)(2,1)S(1)}, f32[256,512]{1,0:T(8,128)S(1)}, f32[128,512]{1,0:T(8,128)S(1)}) custom-call(s32[1]{0:T(128)} %bitcast.me_ref, bf16[16,272,128]{2,1,0:T(8,128)(2,1)S(1)} %all-to-all-done.came_ref, bf16[272,128]{1,0:T(8,128)(2,1)S(1)} %get-tuple-element.28.own_ref, ...), custom_call_target="tpu_custom_call" | custom-call | tf_op jit(solution)/shard_map/grads/pallas_call | solution.py:266
  51.5 0.8 collective-permute-start.4
  52.3 2.0 %collective-permute-done.4.came_ref = bf16[8,32,1664]{2,1,0:T(8,128)(2,1)S(1)} collective-permute-done((bf16[8,32,1664]{2,1,0:T(8,128)(2,1)S(1)}, bf16[8,32,1664]{2,1,0:T(8,128)(2,1)S(1)}, u32[]{:S(2)}, u32[]{:S(2)}) %collective-permute-start.4) | collective-permute-done | bytes 852000 | tf_op jit(solution)/shard_map/ppermute | solution.py:198
  54.5 2.1 %collective-permute-start.5 = (bf16[4,32,1664]{2,1,0:T(8,128)(2,1)S(1)}, bf16[4,32,1664]{2,1,0:T(8,128)(2,1)S(1)}, u32[]{:S(2)}, u32[]{:S(2)}) collective-permute-start(bf16[4,32,1664]{2,1,0:T(8,128)(2,1)S(1)} %get-tuple-element.40), channel_id=1, source_target_pairs={{0,2},{1,3},{2,0},{3,1},{4,6},{5,7},{6,4},{7,5},{8,10},{9,11},{10,... | collective-permute-start | bytes 1277960 | tf_op jit(solution)/shard_map/ppermute | solution.py:198
  56.7 3.3 %collective-permute-start.3 = (f32[64,512]{1,0:T(8,128)S(1)}, f32[64,512]{1,0:T(8,128)S(1)}, u32[]{:S(2)}, u32[]{:S(2)}) collective-permute-start(f32[64,512]{1,0:T(8,128)S(1)} %get-tuple-element.48), channel_id=1, source_target_pairs={{1,0},{2,1},{3,2},{4,3},{5,4},{6,5},{7,6},{8,7},{9,8},{10,9},{11,1... | collective-permute-start | bytes 393224 | tf_op jit(solution)/shard_map/ppermute | solution.py:282
  60.0 8.4 %collective-permute-done.5.came_ref = bf16[4,32,1664]{2,1,0:T(8,128)(2,1)S(1)} collective-permute-done((bf16[4,32,1664]{2,1,0:T(8,128)(2,1)S(1)}, bf16[4,32,1664]{2,1,0:T(8,128)(2,1)S(1)}, u32[]{:S(2)}, u32[]{:S(2)}) %collective-permute-start.5) | collective-permute-done | bytes 426016 | tf_op jit(solution)/shard_map/ppermute | solution.py:198
  68.6 3.3 %collective-permute-start.6 = (bf16[32,1664]{1,0:T(8,128)(2,1)S(1)}, bf16[32,1664]{1,0:T(8,128)(2,1)S(1)}, u32[]{:S(2)}, u32[]{:S(2)}) collective-permute-start(bf16[32,1664]{1,0:T(8,128)(2,1)S(1)} %get-tuple-element.42), channel_id=1, source_target_pairs={{0,4},{1,5},{2,6},{3,7},{4,0},{5,1},{6,2},{7,3},{8,12},{9,13},{10,... | collective-permute-start | bytes 319496 | tf_op jit(solution)/shard_map/ppermute | solution.py:305
  71.9 1.3 %collective-permute-start.7 = (bf16[32,1664]{1,0:T(8,128)(2,1)S(1)}, bf16[32,1664]{1,0:T(8,128)(2,1)S(1)}, u32[]{:S(2)}, u32[]{:S(2)}) collective-permute-start(bf16[32,1664]{1,0:T(8,128)(2,1)S(1)} %get-tuple-element.43), channel_id=1, source_target_pairs={{0,8},{1,9},{2,10},{3,11},{4,12},{5,13},{6,14},{7,15},{8,0},{9,1},... | collective-permute-start | bytes 319496 | tf_op jit(solution)/shard_map/ppermute | solution.py:305
  73.2 1.4 %collective-permute-start.8 = (bf16[32,1664]{1,0:T(8,128)(2,1)S(1)}, bf16[32,1664]{1,0:T(8,128)(2,1)S(1)}, u32[]{:S(2)}, u32[]{:S(2)}) collective-permute-start(bf16[32,1664]{1,0:T(8,128)(2,1)S(1)} %get-tuple-element.44), channel_id=1, source_target_pairs={{0,12},{1,13},{2,14},{3,15},{4,8},{5,9},{6,10},{7,11},{8,4},{9,5},... | collective-permute-start | bytes 319496 | tf_op jit(solution)/shard_map/ppermute | solution.py:305
  74.6 1.3 %rims.1 = f32[256,512]{1,0:T(8,128)} custom-call(f32[256,512]{1,0:T(8,128)S(1)} %get-tuple-element.35.part_ref, f32[64,512]{1,0:T(8,128)S(1)} %collective-permute-done.2.from_below_ref, f32[64,512]{1,0:T(8,128)S(1)} %collective-permute-done.3.from_above_ref, bf16[512,512]{1,0:T(8,128)(2,1)S(1)} %copy-done.3), custom_call_target="tpu_custom_call" | custom-call | tf_op jit(solution)/shard_map/rims/pallas_call | solution.py:308
  75.8 6.7 %collective-permute-done.7.rest_1_ = bf16[32,1664]{1,0:T(8,128)(2,1)S(1)} collective-permute-done((bf16[32,1664]{1,0:T(8,128)(2,1)S(1)}, bf16[32,1664]{1,0:T(8,128)(2,1)S(1)}, u32[]{:S(2)}, u32[]{:S(2)}) %collective-permute-start.7) | collective-permute-done | bytes 106528 | tf_op jit(solution)/shard_map/ppermute | solution.py:305
  82.6 0.7 totals.1
  (37 shorter events, 3.4 us)
Async XLA Ops:
  1.5 9.0 %collective-permute-start.1 = (bf16[64,512]{1,0:T(8,128)(2,1)S(1)}, bf16[64,512]{1,0:T(8,128)(2,1)S(1)}, u32[]{:S(2)}, u32[]{:S(2)}) collective-permute-start(bf16[64,512]{1,0:T(8,128)(2,1)S(1)} %get-tuple-element.50), channel_id=1, source_target_pairs={{1,0},{2,1},{3,2},{4,3},{5,4},{6,5},{7,6},{8,7},{9,8},{10,9},{11,1... | collective-permute-start | bytes 196616 | tf_op jit(solution)/shard_map/ppermute | solution.py:219
  7.0 6.4 %collective-permute-start = (bf16[64,512]{1,0:T(8,128)(2,1)S(1)}, bf16[64,512]{1,0:T(8,128)(2,1)S(1)}, u32[]{:S(2)}, u32[]{:S(2)}) collective-permute-start(bf16[64,512]{1,0:T(8,128)(2,1)S(1)} %get-tuple-element.51), channel_id=1, source_target_pairs={{0,1},{1,2},{2,3},{3,4},{4,5},{5,6},{6,7},{7,8},{8,9},{9,10},{10,1... | collective-permute-start | bytes 196616 | tf_op jit(solution)/shard_map/ppermute | solution.py:218
  7.0 1.6 %copy-start.2 = (bf16[1,16,128,529]{2,1,3,0:T(8,128)(2,1)S(1)}, bf16[1,16,128,529]{2,1,3,0:T(8,128)(2,1)}, u32[]{:S(2)}) copy-start(bf16[1,16,128,529]{2,1,3,0:T(8,128)(2,1)} %param.12) | copy-start | bytes 6500356
  10.5 7.2 %copy-start.18 = (bf16[512,529]{0,1:T(8,128)(2,1)S(1)}, bf16[512,529]{0,1:T(8,128)(2,1)}, u32[]{:S(2)}) copy-start(bf16[512,529]{0,1:T(8,128)(2,1)} %param.11) | copy-start | bytes 1625092
  10.5 0.6 copy-start.11
  13.4 0.6 copy-start.13
  14.0 27.7 %all-to-all-start = ((bf16[16,272,128]{2,1,0:T(8,128)(2,1)}), bf16[16,272,128]{2,1,0:T(8,128)(2,1)S(1)}, u32[]{:S(2)}, u32[]{:S(2)}) async-start(bf16[16,272,128]{2,1,0:T(8,128)(2,1)} %get-tuple-element.27), calls=%async_computation | async-start | bytes 2228224 | tf_op jit(solution)/shard_map/all_to_all | solution.py:234
  17.7 1.0 %copy-start.3 = (bf16[512,512]{1,0:T(8,128)(2,1)S(1)}, bf16[512,512]{1,0:T(8,128)(2,1)}, u32[]{:S(2)}) copy-start(bf16[512,512]{1,0:T(8,128)(2,1)} %w_dst_ref.5) | copy-start | bytes 1572868
  17.8 1.0 %copy-start.15 = (s32[2048]{0:T(1024)S(1)}, s32[2048]{0:T(1024)}, u32[]{:S(2)}) copy-start(s32[2048]{0:T(1024)} %param.13) | copy-start | bytes 24580
  18.8 1.0 %copy-start.6 = (bf16[512,512]{1,0:T(8,128)(2,1)S(1)}, bf16[512,512]{1,0:T(8,128)(2,1)}, u32[]{:S(2)}) copy-start(bf16[512,512]{1,0:T(8,128)(2,1)} %w_src_ref.3) | copy-start | bytes 1572868
  19.8 0.9 %copy-start.10 = (bf16[256,512]{1,0:T(8,128)(2,1)S(1)}, bf16[256,512]{1,0:T(8,128)(2,1)}, u32[]{:S(2)}) copy-start(bf16[256,512]{1,0:T(8,128)(2,1)} %feats_ref.1) | copy-start | bytes 786436
  20.8 0.8 %copy-start.12 = (bf16[64,512]{1,0:T(8,128)(2,1)S(1)}, bf16[64,512]{1,0:T(8,128)(2,1)}, u32[]{:S(2)}) copy-start(bf16[64,512]{1,0:T(8,128)(2,1)} %copy-done.11) | copy-start | bytes 196612
  21.6 0.8 %copy-start.14 = (bf16[64,512]{1,0:T(8,128)(2,1)S(1)}, bf16[64,512]{1,0:T(8,128)(2,1)}, u32[]{:S(2)}) copy-start(bf16[64,512]{1,0:T(8,128)(2,1)} %copy-done.13) | copy-start | bytes 196612
  22.5 0.7 copy-start.16
  23.2 0.7 copy-start.17
  27.9 1.4 %copy-start = (f32[512,1152]{1,0:T(8,128)}, f32[512,1152]{1,0:T(8,128)S(1)}, u32[]{:S(2)}) copy-start(f32[512,1152]{1,0:T(8,128)S(1)} %get-tuple-element.33.slope_ref) | copy-start | bytes 7077892
  29.3 1.1 %copy-start.4 = (bf16[640,1152]{1,0:T(8,128)(2,1)}, bf16[640,1152]{1,0:T(8,128)(2,1)S(1)}, u32[]{:S(2)}) copy-start(bf16[640,1152]{1,0:T(8,128)(2,1)S(1)} %get-tuple-element.31.onehot_ref) | copy-start | bytes 4423684
  30.4 0.7 copy-start.8
  41.7 1.7 %copy-start.1 = (f32[512,1152]{1,0:T(8,128)S(1)}, f32[512,1152]{1,0:T(8,128)}, u32[]{:S(2)}) copy-start(f32[512,1152]{1,0:T(8,128)} %copy-done) | copy-start | bytes 7077892
  43.4 1.4 %copy-start.5 = (bf16[640,1152]{1,0:T(8,128)(2,1)S(1)}, bf16[640,1152]{1,0:T(8,128)(2,1)}, u32[]{:S(2)}) copy-start(bf16[640,1152]{1,0:T(8,128)(2,1)} %copy-done.4) | copy-start | bytes 4423684
  44.8 1.0 %copy-start.7 = (bf16[512,512]{1,0:T(8,128)(2,1)S(1)}, bf16[512,512]{1,0:T(8,128)(2,1)}, u32[]{:S(2)}) copy-start(bf16[512,512]{1,0:T(8,128)(2,1)} %w_src_ref.3) | copy-start | bytes 1572868
  45.8 1.0 %copy-start.9 = (bf16[512,384]{1,0:T(8,128)(2,1)S(1)}, bf16[512,384]{1,0:T(8,128)(2,1)}, u32[]{:S(2)}) copy-start(bf16[512,384]{1,0:T(8,128)(2,1)} %copy-done.8) | copy-start | bytes 1179652
  51.5 2.8 %collective-permute-start.4 = (bf16[8,32,1664]{2,1,0:T(8,128)(2,1)S(1)}, bf16[8,32,1664]{2,1,0:T(8,128)(2,1)S(1)}, u32[]{:S(2)}, u32[]{:S(2)}) collective-permute-start(bf16[8,32,1664]{2,1,0:T(8,128)(2,1)S(1)} %get-tuple-element.38), channel_id=1, source_target_pairs={{0,1},{1,0},{2,3},{3,2},{4,5},{5,4},{6,7},{7,6},{8,9},{9,8},{10,11... | collective-permute-start | bytes 2555912 | tf_op jit(solution)/shard_map/ppermute | solution.py:198
  54.5 13.9 %collective-permute-start.5 = (bf16[4,32,1664]{2,1,0:T(8,128)(2,1)S(1)}, bf16[4,32,1664]{2,1,0:T(8,128)(2,1)S(1)}, u32[]{:S(2)}, u32[]{:S(2)}) collective-permute-start(bf16[4,32,1664]{2,1,0:T(8,128)(2,1)S(1)} %get-tuple-element.40), channel_id=1, source_target_pairs={{0,2},{1,3},{2,0},{3,1},{4,6},{5,7},{6,4},{7,5},{8,10},{9,11},{10,... | collective-permute-start | bytes 1277960 | tf_op jit(solution)/shard_map/ppermute | solution.py:198
  56.7 17.9 %collective-permute-start.3 = (f32[64,512]{1,0:T(8,128)S(1)}, f32[64,512]{1,0:T(8,128)S(1)}, u32[]{:S(2)}, u32[]{:S(2)}) collective-permute-start(f32[64,512]{1,0:T(8,128)S(1)} %get-tuple-element.48), channel_id=1, source_target_pairs={{1,0},{2,1},{3,2},{4,3},{5,4},{6,5},{7,6},{8,7},{9,8},{10,9},{11,1... | collective-permute-start | bytes 393224 | tf_op jit(solution)/shard_map/ppermute | solution.py:282
  60.0 14.6 %collective-permute-start.2 = (f32[64,512]{1,0:T(8,128)S(1)}, f32[64,512]{1,0:T(8,128)S(1)}, u32[]{:S(2)}, u32[]{:S(2)}) collective-permute-start(f32[64,512]{1,0:T(8,128)S(1)} %get-tuple-element.49), channel_id=1, source_target_pairs={{0,1},{1,2},{2,3},{3,4},{4,5},{5,6},{6,7},{7,8},{8,9},{9,10},{10,1... | collective-permute-start | bytes 393224 | tf_op jit(solution)/shard_map/ppermute | solution.py:283
  68.6 7.3 %collective-permute-start.6 = (bf16[32,1664]{1,0:T(8,128)(2,1)S(1)}, bf16[32,1664]{1,0:T(8,128)(2,1)S(1)}, u32[]{:S(2)}, u32[]{:S(2)}) collective-permute-start(bf16[32,1664]{1,0:T(8,128)(2,1)S(1)} %get-tuple-element.42), channel_id=1, source_target_pairs={{0,4},{1,5},{2,6},{3,7},{4,0},{5,1},{6,2},{7,3},{8,12},{9,13},{10,... | collective-permute-start | bytes 319496 | tf_op jit(solution)/shard_map/ppermute | solution.py:305
  71.9 10.7 %collective-permute-start.7 = (bf16[32,1664]{1,0:T(8,128)(2,1)S(1)}, bf16[32,1664]{1,0:T(8,128)(2,1)S(1)}, u32[]{:S(2)}, u32[]{:S(2)}) collective-permute-start(bf16[32,1664]{1,0:T(8,128)(2,1)S(1)} %get-tuple-element.43), channel_id=1, source_target_pairs={{0,8},{1,9},{2,10},{3,11},{4,12},{5,13},{6,14},{7,15},{8,0},{9,1},... | collective-permute-start | bytes 319496 | tf_op jit(solution)/shard_map/ppermute | solution.py:305
  73.2 9.4 %collective-permute-start.8 = (bf16[32,1664]{1,0:T(8,128)(2,1)S(1)}, bf16[32,1664]{1,0:T(8,128)(2,1)S(1)}, u32[]{:S(2)}, u32[]{:S(2)}) collective-permute-start(bf16[32,1664]{1,0:T(8,128)(2,1)S(1)} %get-tuple-element.44), channel_id=1, source_target_pairs={{0,12},{1,13},{2,14},{3,15},{4,8},{5,9},{6,10},{7,11},{8,4},{9,5},... | collective-permute-start | bytes 319496 | tf_op jit(solution)/shard_map/ppermute | solution.py:305

commit v3 on v1

v3 whole, which is shorter than its diff:
```python
import functools

import jax
import jax.numpy as jnp
from jax import lax
from jax.experimental import pallas as pl
from jax.experimental.pallas import tpu as pltpu
from jax.sharding import PartitionSpec as P

F32 = jnp.float32
BF16 = jnp.bfloat16
LANES = 128
PACK = 16
NN = (((1,), (0,)), ((), ()))
NT = (((1,), (1,)), ((), ()))


def mm(left, right, dims=NN):
    return lax.dot_general(left, right, dims, preferred_element_type=F32)


def halves(x):
    high = x.astype(BF16)
    return high, (x - high.astype(F32)).astype(BF16)


def round_up(x, to):
    return -(-x // to) * to


def vmem(count):
    return [pl.BlockSpec(memory_space=pltpu.VMEM)] * count


def pack_kernel(rows, half, me_ref, feats_ref, g_ref, out_ref, own_ref, low_ref, top_ref, late_ref, here_ref, sems, rim_sems):
    entries, slabs, cap = g_ref.shape
    mols = feats_ref.shape[0]
    reach = low_ref.shape[0]
    groups = LANES // half
    blocks = rows // PACK
    count = sems.shape[0]
    stages = []
    for stage in range(count):
        begin, end = stage * blocks // count, (stage + 1) * blocks // count
        copies = []
        for group in range(groups):
            first = min(entries, group * rows + begin * PACK)
            last = min(entries, group * rows + end * PACK)
            if first < last:
                copies.append(
                    pltpu.make_async_copy(g_ref.at[first:last], here_ref.at[first:last], sems.at[stage, group])
                )
        stages.append((begin, end, copies))
        for copy in copies:
            copy.start()
    rims = [
        pltpu.make_async_copy(feats_ref.at[:reach], low_ref, rim_sems.at[0]),
        pltpu.make_async_copy(feats_ref.at[mols - reach :], top_ref, rim_sems.at[1]),
    ]
    for copy in rims:
        copy.start()
    size = PACK * slabs
    to = lax.broadcasted_iota(jnp.int32, (size, size), 0)
    source = lax.broadcasted_iota(jnp.int32, (size, size), 1)
    perm = jnp.where((to % PACK) * slabs + to // PACK == source, 1.0, 0.0).astype(BF16)
    for begin, end, copies in stages:
        for copy in copies:
            copy.wait()
        for block in range(begin, end):
            early, late = [], []
            for group in range(groups):
                first = group * rows + block * PACK
                valid = max(0, min(PACK, entries - first))
                tiles = []
                if valid:
                    tiles.append(here_ref[first : first + valid])
                if valid < PACK:
                    tiles.append(jnp.zeros((PACK - valid, slabs, cap), BF16))
                tile = tiles[0] if len(tiles) == 1 else jnp.concatenate(tiles, axis=0)
                tile = tile.reshape(size, cap)
                early.append(tile[:, :half])
                late.append(tile[:, half:])
            both = jnp.concatenate(early + late, axis=1)
            moved = mm(perm, both).astype(BF16).reshape(slabs, PACK, 2 * LANES)
            here = pl.ds(block * PACK, PACK)
            out_ref[:, here, :] = moved[:, :, :LANES]
            late_ref[:, here, :] = moved[:, :, LANES:]
    own_ref[...] = late_ref[me_ref[0]]
    for copy in rims:
        copy.wait()


def unpack(half, came_ref, own_ref, g_ref):
    slabs, rows, _ = came_ref.shape
    groups = LANES // half
    for tile in range(slabs // groups + 1):
        if tile < slabs // groups:
            chunks = [came_ref[tile * groups + k] for k in range(groups)]
        else:
            chunks = [own_ref[...]] + [jnp.zeros((rows, LANES), BF16)] * (groups - 1)
        for group in range(groups):
            lanes = slice(group * half, (group + 1) * half)
            g_ref[group * rows : (group + 1) * rows, tile * LANES : (tile + 1) * LANES] = jnp.concatenate(
                [chunk[:, lanes] for chunk in chunks], axis=1
            )


def slot_rows(ref, me, half):
    slabs, cap = ref.shape
    per = LANES // half
    rows = []
    for tile in range(slabs // per):
        rows.append(jnp.concatenate([ref[tile * per + k : tile * per + k + 1, :half] for k in range(per)], axis=1))
    own = ref[pl.ds(me, 1), :][:, half:]
    rows.append(jnp.concatenate([own, jnp.full((1, LANES - half), -1, jnp.int32)], axis=1))
    return rows


def edge_kernel(
    half, me_ref, feats_ref, below_ref, above_ref, w_src_ref, w_dst_ref, src_ref, dst_ref, live_ref,
    onehot_ref, hidden_ref, slope_ref, ext_ref,
):
    me = me_ref[0]
    mols = feats_ref.shape[0]
    reach = below_ref.shape[0]
    wide = mols + 2 * reach
    feats = feats_ref[...]
    ext = jnp.concatenate([feats, below_ref[...], above_ref[...]], axis=0)
    ext_ref[...] = ext.T
    proj_src = mm(feats, w_src_ref[...])
    proj_dst = mm(ext, w_dst_ref[...])
    proj = jnp.concatenate([proj_src, proj_dst], axis=0).T
    high, low = halves(proj)
    mol_src = lax.broadcasted_iota(jnp.int32, (mols, LANES), 0)
    mol_dst = lax.broadcasted_iota(jnp.int32, (wide, LANES), 0)
    lists = [slot_rows(ref, me, half) for ref in (src_ref, dst_ref, live_ref)]
    for tile, (src, dst, live) in enumerate(zip(*lists)):
        src = jnp.where(live > 0, src, -1)
        moved = jnp.where(dst < reach, dst + mols, jnp.where(dst < reach + mols, dst - reach, dst))
        dst = jnp.where(live > 0, moved, -1)
        one_src = jnp.where(mol_src == src, 1.0, 0.0).astype(BF16)
        one_dst = jnp.where(mol_dst == dst, 1.0, 0.0).astype(BF16)
        onehot = jnp.concatenate([one_src, one_dst], axis=0)
        here = pl.ds(tile * LANES, LANES)
        onehot_ref[:, here] = onehot
        pre = mm(high, onehot) + mm(low, onehot)
        sigma = 1.0 / (1.0 + jnp.exp(-pre))
        hidden_ref[:, here] = (pre * sigma).astype(BF16)
        slope_ref[:, here] = sigma * (1.0 + pre * (1.0 - sigma))


def halve(terms, odd, place, keep_ref, send_ref, first):
    count, rows, _ = keep_ref.shape
    width = terms.shape[-1]
    lanes = slice(first, first + width)
    inner = 1 << place
    pairs = terms.reshape(count // inner, 2, inner, rows, width)
    even_part = pairs[:, 0].reshape(count, rows, width)
    odd_part = pairs[:, 1].reshape(count, rows, width)
    keep_ref[:, :, lanes] = jnp.where(odd > 0, odd_part, even_part)
    send_ref[:, :, lanes] = jnp.where(odd > 0, even_part, odd_part).astype(BF16)


def fold_kernel(bit, place, me_ref, keep_ref, came_ref, next_ref, send_ref):
    odd = (me_ref[0] >> bit) % 2
    halve(keep_ref[...] + came_ref[...].astype(F32), odd, place, next_ref, send_ref, 0)


def close_kernel(keep_ref, came_ref, send_ref):
    send_ref[...] = (keep_ref[...] + came_ref[...].astype(F32)).astype(BF16)


def grad_kernel(
    half, factor, me_ref, came_ref, own_ref, w_out_ref, slope_hbm, onehot_hbm, ext_hbm,
    keep_ref, send_ref, sums_ref, lower_ref, upper_ref, g_ref, slope_ref, onehot_ref, ext_ref, sems,
):
    odd = me_ref[0] % 2
    width = w_out_ref.shape[0]
    slots = g_ref.shape[1]
    inside = sums_ref.shape[0]
    mols = inside // 2
    step = slots // 3
    tiles = []
    for tile in range(3):
        lanes = pl.ds(tile * step, step)
        copies = [
            pltpu.make_async_copy(slope_hbm.at[:, lanes], slope_ref.at[:, lanes], sems.at[tile, 0]),
            pltpu.make_async_copy(onehot_hbm.at[:, lanes], onehot_ref.at[:, lanes], sems.at[tile, 1]),
        ]
        for copy in copies:
            copy.start()
        tiles.append(copies)
    ext_copy = pltpu.make_async_copy(ext_hbm, ext_ref, sems.at[3, 0])
    ext_copy.start()
    unpack(half, came_ref, own_ref, g_ref)
    sums = None
    for tile, copies in enumerate(tiles):
        lanes = slice(tile * step, (tile + 1) * step)
        dh = mm(w_out_ref[...], g_ref[:, lanes])
        for copy in copies:
            copy.wait()
        dpre = (dh * slope_ref[:, lanes]).astype(BF16)
        term = mm(onehot_ref[:, lanes], dpre, NT)
        sums = term if sums is None else sums + term
    reach = lower_ref.shape[0]
    lower_ref[...] = sums[inside : inside + reach]
    upper_ref[...] = sums[inside + reach :]
    sums_ref[...] = sums[:inside]
    high, low = halves(sums)
    ext_copy.wait()
    feats = ext_ref[:, :mols]
    ext = ext_ref[...]
    halve(factor * (mm(feats, high[:mols]) + mm(feats, low[:mols])), odd, 0, keep_ref, send_ref, 0)
    halve(factor * (mm(ext, high[mols:]) + mm(ext, low[mols:])), odd, 0, keep_ref, send_ref, width)


def outer_kernel(factor, me_ref, hidden_ref, g_ref, keep_ref, send_ref):
    term = factor * mm(hidden_ref[...], g_ref[...], NT)
    padding = keep_ref.shape[2] - term.shape[1]
    if padding > 0:
        term = jnp.concatenate([term, jnp.zeros((term.shape[0], padding), F32)], axis=1)
    halve(term, me_ref[0] % 2, 0, keep_ref, send_ref, 0)


def rim_kernel(sums_ref, from_below_ref, from_above_ref, w_src_ref, w_dst_ref, out_ref):
    mols = out_ref.shape[0]
    reach = from_below_ref.shape[0]
    src = sums_ref[:mols]
    dst = sums_ref[mols:]
    dst = jnp.concatenate(
        [dst[:reach] + from_below_ref[...], dst[reach : mols - reach], dst[mols - reach :] + from_above_ref[...]], axis=0
    )
    w_src = w_src_ref[...]
    w_dst = w_dst_ref[...]
    src_high, src_low = halves(src)
    dst_high, dst_low = halves(dst)
    out_ref[...] = mm(src_high, w_src, NT) + mm(src_low, w_src, NT) + mm(dst_high, w_dst, NT) + mm(dst_low, w_dst, NT)


def total_kernel(*refs):
    *refs, src_ref, dst_ref, out_ref = refs
    count = len(refs) // 2
    width = src_ref.shape[1]
    totals = []
    for piece in (refs[:count], refs[count:]):
        terms = [ref[slab].astype(F32) for ref in piece for slab in range(ref.shape[0])]
        totals.append(functools.reduce(jnp.add, terms))
    sides, outer = totals
    src_ref[...] = sides[:, :width]
    dst_ref[...] = sides[:, width:]
    out_ref[...] = outer[:, : out_ref.shape[1]]


def in_hbm(x):
    return pltpu.with_memory_space_constraint(x, pltpu.HBM)


def swap(block, bit, slabs):
    return lax.ppermute(block, "space", [(i, i ^ (1 << bit)) for i in range(slabs)])


def on_device(mol_feats, w_src, w_dst, w_out, grad_blocks, edge_src, edge_dst, edge_live):
    slabs = lax.axis_size("space")
    mols, width = mol_feats.shape
    entries = w_out.shape[1]
    cap = grad_blocks.shape[2]
    half = cap // 2
    reach = mols // 4
    groups = LANES // half
    slots = (slabs // groups + 1) * LANES
    bits = slabs.bit_length() - 1
    if 3 <= bits <= 4:
        late_bits = tuple((bit, 0) for bit in range(3, bits))
        paths = (((0, 0), (1, 0), (2, 0)) + late_bits, ((0, 0), (2, 1), (1, 0)) + late_bits)
    else:
        paths = (tuple((bit, 0) for bit in range(min(bits, 2))),) * 2
    rest = slabs >> len(paths[0])
    part = width // slabs
    factor = float(edge_src.shape[0] * slabs) ** (-0.5)
    me = lax.axis_index("space").astype(jnp.int32).reshape(1)
    smem = pl.BlockSpec(memory_space=pltpu.SMEM)
    hbm = pl.BlockSpec(memory_space=pltpu.HBM)
    big = pltpu.CompilerParams(vmem_limit_bytes=24 * 1024 * 1024)
    up = [(i, (i + 1) % slabs) for i in range(slabs)]
    down = [((i + 1) % slabs, i) for i in range(slabs)]

    rows = round_up(pl.cdiv(entries, groups), PACK)
    stages = 4
    packed, own, low, top = pl.pallas_call(
        functools.partial(pack_kernel, rows, half),
        out_shape=(
            jax.ShapeDtypeStruct((slabs, rows, LANES), BF16),
            jax.ShapeDtypeStruct((rows, LANES), BF16),
            jax.ShapeDtypeStruct((reach, width), BF16),
            jax.ShapeDtypeStruct((reach, width), BF16),
        ),
        in_specs=[smem, hbm, hbm],
        out_specs=tuple(vmem(4)),
        scratch_shapes=[
            pltpu.VMEM((slabs, rows, LANES), BF16),
            pltpu.VMEM((entries, slabs, cap), BF16),
            pltpu.SemaphoreType.DMA((stages, groups)),
            pltpu.SemaphoreType.DMA((2,)),
        ],
        compiler_params=big,
        name="pack",
    )(me, in_hbm(mol_feats), in_hbm(jnp.transpose(grad_blocks[0], (2, 0, 1))))
    below = lax.ppermute(top, "space", up)
    above = lax.ppermute(low, "space", down)
    came = lax.all_to_all(packed, "space", split_axis=0, concat_axis=0, tiled=True)

    onehot, hidden, slope, ext = pl.pallas_call(
        functools.partial(edge_kernel, half),
        out_shape=(
            jax.ShapeDtypeStruct((2 * mols + 2 * reach, slots), BF16),
            jax.ShapeDtypeStruct((width, slots), BF16),
            jax.ShapeDtypeStruct((width, slots), F32),
            jax.ShapeDtypeStruct((width, mols + 2 * reach), BF16),
        ),
        in_specs=[smem] + vmem(8),
        out_specs=tuple(vmem(4)),
        compiler_params=big,
        name="edges",
        cost_estimate=pl.CostEstimate(
            flops=40 * width * slots * 2 * (2 * mols + 2 * reach), bytes_accessed=8 * 1024 * 1024,
            transcendentals=width * slots,
        ),
    )(
        me, mol_feats, below, above, w_src, w_dst,
        edge_src.reshape(slabs, cap), edge_dst.reshape(slabs, cap), edge_live.reshape(slabs, cap),
    )

    def chunks(count, lanes, dtype):
        return jax.ShapeDtypeStruct((count, part, lanes), dtype)

    entries_wide = groups * rows
    w_out_wide = jnp.pad(w_out, ((0, 0), (0, entries_wide - entries)))
    wide = mols + 2 * reach
    keep, send, sums, lower, upper, g = pl.pallas_call(
        functools.partial(grad_kernel, half, factor),
        out_shape=(
            chunks(slabs // 2, 2 * width, F32),
            chunks(slabs // 2, 2 * width, BF16),
            jax.ShapeDtypeStruct((2 * mols, width), F32),
            jax.ShapeDtypeStruct((reach, width), F32),
            jax.ShapeDtypeStruct((reach, width), F32),
            jax.ShapeDtypeStruct((entries_wide, slots), BF16),
        ),
        in_specs=[smem] + vmem(3) + [hbm] * 3,
        out_specs=tuple(vmem(6)),
        scratch_shapes=[
            pltpu.VMEM((width, slots), F32),
            pltpu.VMEM((mols + wide, slots), BF16),
            pltpu.VMEM((width, wide), BF16),
            pltpu.SemaphoreType.DMA((4, 2)),
        ],
        compiler_params=big,
        name="grads",
    )(me, came, own, w_out_wide, in_hbm(slope), in_hbm(onehot), in_hbm(ext))
    lanes = round_up(entries_wide, LANES)
    keep_o, send_o = pl.pallas_call(
        functools.partial(outer_kernel, factor),
        out_shape=(chunks(slabs // 2, lanes, F32), chunks(slabs // 2, lanes, BF16)),
        in_specs=[smem] + vmem(2),
        out_specs=tuple(vmem(2)),
        compiler_params=big,
        name="outer",
        cost_estimate=pl.CostEstimate(
            flops=40 * width * slots * entries_wide, bytes_accessed=4 * 1024 * 1024, transcendentals=0
        ),
    )(me, hidden, g)

    def fold(bit, place, keep, crossed):
        shape = (keep.shape[0] // 2, keep.shape[2])
        return pl.pallas_call(
            functools.partial(fold_kernel, bit, place),
            out_shape=(chunks(*shape, F32), chunks(*shape, BF16)),
            in_specs=[smem] + vmem(2),
            out_specs=tuple(vmem(2)),
            compiler_params=big,
            name="fold",
        )(me, keep, crossed)

    def close(keep, crossed):
        if rest == 1:
            return [keep, crossed]
        sends = pl.pallas_call(
            close_kernel,
            out_shape=chunks(rest, keep.shape[2], BF16),
            in_specs=vmem(2),
            out_specs=vmem(1)[0],
            compiler_params=big,
            name="close",
        )(keep, crossed)
        same = [[low + rank * (slabs // rest) for rank in range(rest)] for low in range(slabs // rest)]
        return [
            lax.all_to_all(sends, "space", split_axis=0, concat_axis=0, tiled=True, axis_index_groups=same)
        ]

    from_above = lax.ppermute(lower, "space", down)
    from_below = lax.ppermute(upper, "space", up)
    crossed = swap(send, 0, slabs)
    crossed_o = swap(send_o, 0, slabs)
    keep, crossed, from_above, from_below = lax.optimization_barrier((keep, crossed, from_above, from_below))
    for (bit, place), (bit_o, place_o) in zip(paths[0][1:], paths[1][1:]):
        keep, send = fold(bit, place, keep, crossed)
        crossed = swap(send, bit, slabs)
        keep_o, crossed_o, _ = lax.optimization_barrier((keep_o, crossed_o, send))
        keep_o, send_o = fold(bit_o, place_o, keep_o, crossed_o)
        crossed_o = swap(send_o, bit_o, slabs)
    terms = close(keep, crossed)
    terms_o = close(keep_o, crossed_o)
    feature_grad = pl.pallas_call(
        rim_kernel,
        out_shape=jax.ShapeDtypeStruct((mols, width), F32),
        in_specs=vmem(5),
        out_specs=vmem(1)[0],
        compiler_params=big,
        name="rims",
        cost_estimate=pl.CostEstimate(flops=2 * width * slots * width * 40, bytes_accessed=4 * 1024 * 1024, transcendentals=0),
    )(sums, from_below, from_above, w_src, w_dst)
    src_grad, dst_grad, out_grad = pl.pallas_call(
        total_kernel,
        out_shape=(
            jax.ShapeDtypeStruct((part, width), F32),
            jax.ShapeDtypeStruct((part, width), F32),
            jax.ShapeDtypeStruct((part, entries), F32),
        ),
        in_specs=vmem(len(terms) + len(terms_o)),
        out_specs=tuple(vmem(3)),
        compiler_params=big,
        name="totals",
    )(*terms, *terms_o)
    return (feature_grad, src_grad, dst_grad, out_grad)


def solution(mesh):
    placed = (
        P(("groups", "space"), None),
        P(),
        P(),
        P(),
        P("space", "groups", None, None),
        P(("groups", "space")),
        P(("groups", "space")),
        P(("groups", "space")),
    )
    return jax.shard_map(
        on_device,
        mesh=mesh,
        in_specs=placed,
        out_specs=(
            P(("groups", "space"), None),
            P(("groups", "space"), None),
            P(("groups", "space"), None),
            P(("groups", "space"), None),
        ),
        check_vma=False,
    )
```

time: 109 us -> 77.3 us (0.71)
  the two profiles are of different devices: /device:TPU:15 before, /device:TPU:0 now
where the time goes in v3:
time: 77.3 us; the launch traced here: 77 us
  waiting for transfers between devices  31.1 us (40%)
  starting transfers between devices  21.3 us (28%)
  Pallas kernels  17.1 us (22%)
  local copies, waits for them, and re-layouts  6.6 us (9%)
  between operations  0.9 us (1%)
    all_to_all x1, waiting for transfers between devices, on_device(): lax.all_to_all(packed, 'space', split_axis=0, concat_axis=0, tiled=True)  13.2 us
    ppermute x8, waiting for transfers between devices, swap(): lax.ppermute(block, 'space', [(i, i ^ 1 << bit) for i in range(slabs)])  10.7 us
    ppermute x8, starting transfers between devices, swap(): lax.ppermute(block, 'space', [(i, i ^ 1 << bit) for i in range(slabs)])  6.57 us
    unnamed x25, local copies, waits for them, and re-layouts  5.45 us
    ppermute x1, starting transfers between devices, on_device(): from_above = lax.ppermute(lower, 'space', down)  5.45 us
    pallas_call x1, Pallas kernels, on_device(): pl.pallas_call(functools.partial(grad_kernel, half, factor), out_shape=(c...  5.41 us
    ppermute x1, starting transfers between devices, on_device(): above = lax.ppermute(low, 'space', down)  5.06 us
    ppermute x1, waiting for transfers between devices, on_device(): from_below = lax.ppermute(upper, 'space', up)  4.69 us
  transfers between devices with their start and end apart: 13, of which 6 were waited for; matrix products, arithmetic and copies ran while one was open for 3% of the time, Pallas kernels for 9%

profile of v3, /device:TPU:0, one launch (start us, length us, event | category | flops | bytes accessed | tf_op | source)
XLA Modules:
  0.0 77.0 jit_solution(3341170601627176142)
XLA Ops:
  0.6 3.8 %pack.1 = (bf16[16,272,128]{2,1,0:T(8,128)(2,1)}, bf16[272,128]{1,0:T(8,128)(2,1)S(1)}, bf16[64,512]{1,0:T(8,128)(2,1)S(1)}, bf16[64,512]{1,0:T(8,128)(2,1)S(1)}) custom-call(s32[1]{0:T(128)} %bitcast.me_ref, bf16[256,512]{1,0:T(8,128)(2,1)} %feats_ref.3, bf16[529,16,128]{2,1,0:T(8,128)(2,1)} %bitcast.10), custom_call_target="tpu_custom_call" | custom-call | tf_op jit(solution)/shard_map/pack/pallas_call | solution.py:289
  4.5 0.5 collective-permute-start
  5.0 5.1 %collective-permute-start.1 = (bf16[64,512]{1,0:T(8,128)(2,1)S(1)}, bf16[64,512]{1,0:T(8,128)(2,1)S(1)}, u32[]{:S(2)}, u32[]{:S(2)}) collective-permute-start(bf16[64,512]{1,0:T(8,128)(2,1)S(1)} %get-tuple-element.48), channel_id=1, source_target_pairs={{1,0},{2,1},{3,2},{4,3},{5,4},{6,5},{7,6},{8,7},{9,8},{10,9},{11,1... | collective-permute-start | bytes 196616 | tf_op jit(solution)/shard_map/ppermute | solution.py:309
  10.0 3.7 %all-to-all-start = ((bf16[16,272,128]{2,1,0:T(8,128)(2,1)}), bf16[16,272,128]{2,1,0:T(8,128)(2,1)S(1)}, u32[]{:S(2)}, u32[]{:S(2)}) async-start(bf16[16,272,128]{2,1,0:T(8,128)(2,1)} %get-tuple-element.45), calls=%async_computation | async-start | bytes 2228224 | tf_op jit(solution)/shard_map/all_to_all | solution.py:310
  13.8 1.1 %copy.12 = bf16[512,529]{1,0:T(8,128)(2,1)} copy(bf16[512,529]{0,1:T(8,128)(2,1)S(1)} %copy-done.11) | data formatting | bytes 1083392 | tf_op args[3]
  14.9 1.1 %pad.4.w_out_ref = bf16[512,544]{1,0:T(8,128)(2,1)S(1)} pad(bf16[512,529]{1,0:T(8,128)(2,1)} %copy.12, bf16[]{:T(256)} %constant.6.clone.1), padding=0_0x0_15 | pad | bytes 1098754 | tf_op jit(solution)/shard_map/jit(_pad)/pad | solution.py:337
  16.1 4.0 %edges.1 = (bf16[640,1152]{1,0:T(8,128)(2,1)S(1)}, bf16[512,1152]{1,0:T(8,128)(2,1)S(1)}, f32[512,1152]{1,0:T(8,128)S(1)}, bf16[512,384]{1,0:T(8,128)(2,1)S(1)}) custom-call(s32[1]{0:T(128)} %bitcast.me_ref, bf16[256,512]{1,0:T(8,128)(2,1)S(1)} %copy-done.3, bf16[64,512]{1,0:T(8,128)(2,1)S(1)} %collective-permute-done.below_ref, ...), custom_call_target="tpu_custom_call" | custom-call | flops 30198988800 | bytes 8388608 | tf_op jit(solution)/shard_map/edges/pallas_call | solution.py:312
  20.2 1.4 %copy-done = f32[512,1152]{1,0:T(8,128)} copy-done((f32[512,1152]{1,0:T(8,128)}, f32[512,1152]{1,0:T(8,128)S(1)}, u32[]{:S(2)}) %copy-start) | copy-done | bytes 2359320
  21.6 1.1 %copy-done.1 = bf16[640,1152]{1,0:T(8,128)(2,1)} copy-done((bf16[640,1152]{1,0:T(8,128)(2,1)}, bf16[640,1152]{1,0:T(8,128)(2,1)S(1)}, u32[]{:S(2)}) %copy-start.1) | copy-done | bytes 1474584
  22.7 0.7 copy-done.2
  23.5 1.0 %copy-done.9 = bf16[512,1152]{1,0:T(8,128)(2,1)} copy-done((bf16[512,1152]{1,0:T(8,128)(2,1)}, bf16[512,1152]{1,0:T(8,128)(2,1)S(1)}, u32[]{:S(2)}) %copy-start.9) | copy-done | bytes 1179672
  24.5 13.2 %all-to-all-done.came_ref = bf16[16,272,128]{2,1,0:T(8,128)(2,1)S(1)} async-done(((bf16[16,272,128]{2,1,0:T(8,128)(2,1)}), bf16[16,272,128]{2,1,0:T(8,128)(2,1)S(1)}, u32[]{:S(2)}, u32[]{:S(2)}) %all-to-all-start) | async-done | bytes 1114144 | tf_op jit(solution)/shard_map/all_to_all | solution.py:310
  37.7 5.4 %grads.1 = (f32[8,32,1024]{2,1,0:T(8,128)S(1)}, bf16[8,32,1024]{2,1,0:T(8,128)(2,1)S(1)}, f32[512,512]{1,0:T(8,128)S(1)}, f32[64,512]{1,0:T(8,128)S(1)}, f32[64,...) custom-call(s32[1]{0:T(128)} %bitcast.me_ref, bf16[16,272,128]{2,1,0:T(8,128)(2,1)S(1)} %all-to-all-done.came_ref, ...), custom_call_target="tpu_custom_call" | custom-call | tf_op jit(solution)/shard_map/grads/pallas_call | solution.py:339
  43.1 0.8 %collective-permute-start.2 = (bf16[8,32,1024]{2,1,0:T(8,128)(2,1)S(1)}, bf16[8,32,1024]{2,1,0:T(8,128)(2,1)S(1)}, u32[]{:S(2)}, u32[]{:S(2)}) collective-permute-start(bf16[8,32,1024]{2,1,0:T(8,128)(2,1)S(1)} %get-tuple-element.54), channel_id=1, source_target_pairs={{0,1},{1,0},{2,3},{3,2},{4,5},{5,4},{6,7},{7,6},{8,9},{9,8},{10,11... | collective-permute-start | bytes 1572872 | tf_op jit(solution)/shard_map/ppermute | solution.py:259
  43.9 1.2 %outer.1 = (f32[8,32,640]{2,1,0:T(8,128)S(1)}, bf16[8,32,640]{2,1,0:T(8,128)(2,1)S(1)}) custom-call(s32[1]{0:T(128)} %bitcast.me_ref, bf16[512,1152]{1,0:T(8,128)(2,1)S(1)} %copy-done.10, bf16[544,1152]{1,0:T(8,128)(2,1)S(1)} %get-tuple-element.68.g_ref), custom_call_target="tpu_custom_call" | custom-call | flops 12834570240 | bytes 4194304 | tf_op jit(solution)/shard_map/outer/pallas_call | solution.py:361
  45.1 0.1 collective-permute-start.8
  45.2 5.5 %collective-permute-start.3 = (f32[64,512]{1,0:T(8,128)S(1)}, f32[64,512]{1,0:T(8,128)S(1)}, u32[]{:S(2)}, u32[]{:S(2)}) collective-permute-start(f32[64,512]{1,0:T(8,128)S(1)} %get-tuple-element.55), channel_id=1, source_target_pairs={{1,0},{2,1},{3,2},{4,3},{5,4},{6,5},{7,6},{8,7},{9,8},{10,9},{11,1... | collective-permute-start | bytes 393224 | tf_op jit(solution)/shard_map/ppermute | solution.py:400
  50.7 2.5 %collective-permute-done.3.from_above_ref = f32[64,512]{1,0:T(8,128)S(1)} collective-permute-done((f32[64,512]{1,0:T(8,128)S(1)}, f32[64,512]{1,0:T(8,128)S(1)}, u32[]{:S(2)}, u32[]{:S(2)}) %collective-permute-start.3) | collective-permute-done | bytes 131104 | tf_op jit(solution)/shard_map/ppermute | solution.py:400
  53.2 4.7 %collective-permute-done.4.from_below_ref = f32[64,512]{1,0:T(8,128)S(1)} collective-permute-done((f32[64,512]{1,0:T(8,128)S(1)}, f32[64,512]{1,0:T(8,128)S(1)}, u32[]{:S(2)}, u32[]{:S(2)}) %collective-permute-start.4) | collective-permute-done | bytes 131104 | tf_op jit(solution)/shard_map/ppermute | solution.py:401
  57.9 0.2 fold.6
  58.0 0.1 collective-permute-start.5
  58.1 0.1 fold.9
  58.2 0.1 collective-permute-start.9
  58.3 6.2 %collective-permute-done.5.came_ref = bf16[4,32,1024]{2,1,0:T(8,128)(2,1)S(1)} collective-permute-done((bf16[4,32,1024]{2,1,0:T(8,128)(2,1)S(1)}, bf16[4,32,1024]{2,1,0:T(8,128)(2,1)S(1)}, u32[]{:S(2)}, u32[]{:S(2)}) %collective-permute-start.5) | collective-permute-done | bytes 262176 | tf_op jit(solution)/shard_map/ppermute | solution.py:259
  64.5 0.1 collective-permute-start.6
  64.7 2.4 %collective-permute-start.10 = (bf16[2,32,640]{2,1,0:T(8,128)(2,1)S(1)}, bf16[2,32,640]{2,1,0:T(8,128)(2,1)S(1)}, u32[]{:S(2)}, u32[]{:S(2)}) collective-permute-start(bf16[2,32,640]{2,1,0:T(8,128)(2,1)S(1)} %get-tuple-element.78), channel_id=1, source_target_pairs={{0,2},{1,3},{2,0},{3,1},{4,6},{5,7},{6,4},{7,5},{8,10},{9,11},{10,... | collective-permute-start | bytes 245768 | tf_op jit(solution)/shard_map/ppermute | solution.py:259
  67.1 2.5 %collective-permute-done.6.came_ref = bf16[2,32,1024]{2,1,0:T(8,128)(2,1)S(1)} collective-permute-done((bf16[2,32,1024]{2,1,0:T(8,128)(2,1)S(1)}, bf16[2,32,1024]{2,1,0:T(8,128)(2,1)S(1)}, u32[]{:S(2)}, u32[]{:S(2)}) %collective-permute-start.6) | collective-permute-done | bytes 131104 | tf_op jit(solution)/shard_map/ppermute | solution.py:259
  69.6 0.3 collective-permute-start.7
  69.9 2.8 %collective-permute-start.11 = (bf16[1,32,640]{2,1,0:T(8,128)(2,1)S(1)}, bf16[1,32,640]{2,1,0:T(8,128)(2,1)S(1)}, u32[]{:S(2)}, u32[]{:S(2)}) collective-permute-start(bf16[1,32,640]{2,1,0:T(8,128)(2,1)S(1)} %get-tuple-element.82), channel_id=1, source_target_pairs={{0,8},{1,9},{2,10},{3,11},{4,12},{5,13},{6,14},{7,15},{8,0},{9,1},... | collective-permute-start | bytes 122888 | tf_op jit(solution)/shard_map/ppermute | solution.py:259
  72.7 1.6 %rims.1 = f32[256,512]{1,0:T(8,128)} custom-call(f32[512,512]{1,0:T(8,128)S(1)} %get-tuple-element.52.sums_ref, f32[64,512]{1,0:T(8,128)S(1)} %collective-permute-done.4.from_below_ref, f32[64,512]{1,0:T(8,128)S(1)} %collective-permute-done.3.from_above_ref, bf16[512,512]{1,0:T(8,128)(2,1)S(1)} %copy-done.4, bf16[512,512]{1,0:T(8,128)(2,1)S(1)} %copy-done.5), custom_call_target="tpu_custom_call" | custom-call | flops 24159191040 | bytes 4194304 | tf_op jit(solution)/shard_map/rims/pallas_call | solution.py:413
  74.3 2.0 %collective-permute-done.11.refs_3_ = bf16[1,32,640]{2,1,0:T(8,128)(2,1)S(1)} collective-permute-done((bf16[1,32,640]{2,1,0:T(8,128)(2,1)S(1)}, bf16[1,32,640]{2,1,0:T(8,128)(2,1)S(1)}, u32[]{:S(2)}, u32[]{:S(2)}) %collective-permute-start.11) | collective-permute-done | bytes 40992 | tf_op jit(solution)/shard_map/ppermute | solution.py:259
  76.3 0.7 totals.1
  (32 shorter events, 0.2 us)
Async XLA Ops:
  4.5 9.3 %copy-start.11 = (bf16[512,529]{0,1:T(8,128)(2,1)S(1)}, bf16[512,529]{0,1:T(8,128)(2,1)}, u32[]{:S(2)}) copy-start(bf16[512,529]{0,1:T(8,128)(2,1)} %param.11) | copy-start | bytes 1625092
  4.5 11.6 %collective-permute-start = (bf16[64,512]{1,0:T(8,128)(2,1)S(1)}, bf16[64,512]{1,0:T(8,128)(2,1)S(1)}, u32[]{:S(2)}, u32[]{:S(2)}) collective-permute-start(bf16[64,512]{1,0:T(8,128)(2,1)S(1)} %get-tuple-element.47), channel_id=1, source_target_pairs={{0,1},{1,2},{2,3},{3,4},{4,5},{5,6},{6,7},{7,8},{8,9},{9,10},{10,1... | collective-permute-start | bytes 196616 | tf_op jit(solution)/shard_map/ppermute | solution.py:308
  5.0 11.1 %collective-permute-start.1 = (bf16[64,512]{1,0:T(8,128)(2,1)S(1)}, bf16[64,512]{1,0:T(8,128)(2,1)S(1)}, u32[]{:S(2)}, u32[]{:S(2)}) collective-permute-start(bf16[64,512]{1,0:T(8,128)(2,1)S(1)} %get-tuple-element.48), channel_id=1, source_target_pairs={{1,0},{2,1},{3,2},{4,3},{5,4},{6,5},{7,6},{8,7},{9,8},{10,9},{11,1... | collective-permute-start | bytes 196616 | tf_op jit(solution)/shard_map/ppermute | solution.py:309
  10.0 27.7 %all-to-all-start = ((bf16[16,272,128]{2,1,0:T(8,128)(2,1)}), bf16[16,272,128]{2,1,0:T(8,128)(2,1)S(1)}, u32[]{:S(2)}, u32[]{:S(2)}) async-start(bf16[16,272,128]{2,1,0:T(8,128)(2,1)} %get-tuple-element.45), calls=%async_computation | async-start | bytes 2228224 | tf_op jit(solution)/shard_map/all_to_all | solution.py:310
  13.7 2.3 %copy-start.3 = (bf16[256,512]{1,0:T(8,128)(2,1)S(1)}, bf16[256,512]{1,0:T(8,128)(2,1)}, u32[]{:S(2)}) copy-start(bf16[256,512]{1,0:T(8,128)(2,1)} %feats_ref.3) | copy-start | bytes 786436
  13.8 2.3 %copy-start.4 = (bf16[512,512]{1,0:T(8,128)(2,1)S(1)}, bf16[512,512]{1,0:T(8,128)(2,1)}, u32[]{:S(2)}) copy-start(bf16[512,512]{1,0:T(8,128)(2,1)} %w_src_ref.3) | copy-start | bytes 1572868
  13.8 2.3 %copy-start.5 = (bf16[512,512]{1,0:T(8,128)(2,1)S(1)}, bf16[512,512]{1,0:T(8,128)(2,1)}, u32[]{:S(2)}) copy-start(bf16[512,512]{1,0:T(8,128)(2,1)} %w_dst_ref.3) | copy-start | bytes 1572868
  13.8 2.3 %copy-start.6 = (s32[2048]{0:T(1024)S(1)}, s32[2048]{0:T(1024)}, u32[]{:S(2)}) copy-start(s32[2048]{0:T(1024)} %param.13) | copy-start | bytes 24580
  13.8 2.3 %copy-start.7 = (s32[2048]{0:T(1024)S(1)}, s32[2048]{0:T(1024)}, u32[]{:S(2)}) copy-start(s32[2048]{0:T(1024)} %param.14) | copy-start | bytes 24580
  13.8 2.3 %copy-start.8 = (s32[2048]{0:T(1024)S(1)}, s32[2048]{0:T(1024)}, u32[]{:S(2)}) copy-start(s32[2048]{0:T(1024)} %param.15) | copy-start | bytes 24580
  20.2 1.4 %copy-start = (f32[512,1152]{1,0:T(8,128)}, f32[512,1152]{1,0:T(8,128)S(1)}, u32[]{:S(2)}) copy-start(f32[512,1152]{1,0:T(8,128)S(1)} %get-tuple-element.49.slope_hbm) | copy-start | bytes 7077892
  21.6 1.1 %copy-start.1 = (bf16[640,1152]{1,0:T(8,128)(2,1)}, bf16[640,1152]{1,0:T(8,128)(2,1)S(1)}, u32[]{:S(2)}) copy-start(bf16[640,1152]{1,0:T(8,128)(2,1)S(1)} %get-tuple-element.50.onehot_hbm) | copy-start | bytes 4423684
  22.7 0.7 copy-start.2
  23.5 1.0 %copy-start.9 = (bf16[512,1152]{1,0:T(8,128)(2,1)}, bf16[512,1152]{1,0:T(8,128)(2,1)S(1)}, u32[]{:S(2)}) copy-start(bf16[512,1152]{1,0:T(8,128)(2,1)S(1)} %get-tuple-element.67.hidden_ref) | copy-start | bytes 3538948
  37.7 6.2 %copy-start.10 = (bf16[512,1152]{1,0:T(8,128)(2,1)S(1)}, bf16[512,1152]{1,0:T(8,128)(2,1)}, u32[]{:S(2)}) copy-start(bf16[512,1152]{1,0:T(8,128)(2,1)} %copy-done.9) | copy-start | bytes 3538948
  43.1 14.7 %collective-permute-start.2 = (bf16[8,32,1024]{2,1,0:T(8,128)(2,1)S(1)}, bf16[8,32,1024]{2,1,0:T(8,128)(2,1)S(1)}, u32[]{:S(2)}, u32[]{:S(2)}) collective-permute-start(bf16[8,32,1024]{2,1,0:T(8,128)(2,1)S(1)} %get-tuple-element.54), channel_id=1, source_target_pairs={{0,1},{1,0},{2,3},{3,2},{4,5},{5,4},{6,7},{7,6},{8,9},{9,8},{10,11... | collective-permute-start | bytes 1572872 | tf_op jit(solution)/shard_map/ppermute | solution.py:259
  45.1 13.0 %collective-permute-start.8 = (bf16[8,32,640]{2,1,0:T(8,128)(2,1)S(1)}, bf16[8,32,640]{2,1,0:T(8,128)(2,1)S(1)}, u32[]{:S(2)}, u32[]{:S(2)}) collective-permute-start(bf16[8,32,640]{2,1,0:T(8,128)(2,1)S(1)} %get-tuple-element.70), channel_id=1, source_target_pairs={{0,1},{1,0},{2,3},{3,2},{4,5},{5,4},{6,7},{7,6},{8,9},{9,8},{10,11... | collective-permute-start | bytes 983048 | tf_op jit(solution)/shard_map/ppermute | solution.py:259
  45.2 8.0 %collective-permute-start.3 = (f32[64,512]{1,0:T(8,128)S(1)}, f32[64,512]{1,0:T(8,128)S(1)}, u32[]{:S(2)}, u32[]{:S(2)}) collective-permute-start(f32[64,512]{1,0:T(8,128)S(1)} %get-tuple-element.55), channel_id=1, source_target_pairs={{1,0},{2,1},{3,2},{4,3},{5,4},{6,5},{7,6},{8,7},{9,8},{10,9},{11,1... | collective-permute-start | bytes 393224 | tf_op jit(solution)/shard_map/ppermute | solution.py:400
  50.7 7.2 %collective-permute-start.4 = (f32[64,512]{1,0:T(8,128)S(1)}, f32[64,512]{1,0:T(8,128)S(1)}, u32[]{:S(2)}, u32[]{:S(2)}) collective-permute-start(f32[64,512]{1,0:T(8,128)S(1)} %get-tuple-element.56), channel_id=1, source_target_pairs={{0,1},{1,2},{2,3},{3,4},{4,5},{5,6},{6,7},{7,8},{8,9},{9,10},{10,1... | collective-permute-start | bytes 393224 | tf_op jit(solution)/shard_map/ppermute | solution.py:401
  58.0 6.4 %collective-permute-start.5 = (bf16[4,32,1024]{2,1,0:T(8,128)(2,1)S(1)}, bf16[4,32,1024]{2,1,0:T(8,128)(2,1)S(1)}, u32[]{:S(2)}, u32[]{:S(2)}) collective-permute-start(bf16[4,32,1024]{2,1,0:T(8,128)(2,1)S(1)} %get-tuple-element.62), channel_id=1, source_target_pairs={{0,2},{1,3},{2,0},{3,1},{4,6},{5,7},{6,4},{7,5},{8,10},{9,11},{10,... | collective-permute-start | bytes 786440 | tf_op jit(solution)/shard_map/ppermute | solution.py:259
  58.2 6.4 %collective-permute-start.9 = (bf16[4,32,640]{2,1,0:T(8,128)(2,1)S(1)}, bf16[4,32,640]{2,1,0:T(8,128)(2,1)S(1)}, u32[]{:S(2)}, u32[]{:S(2)}) collective-permute-start(bf16[4,32,640]{2,1,0:T(8,128)(2,1)S(1)} %get-tuple-element.74), channel_id=1, source_target_pairs={{0,4},{1,5},{2,6},{3,7},{4,0},{5,1},{6,2},{7,3},{8,12},{9,13},{10,... | collective-permute-start | bytes 491528 | tf_op jit(solution)/shard_map/ppermute | solution.py:259
  64.5 5.0 %collective-permute-start.6 = (bf16[2,32,1024]{2,1,0:T(8,128)(2,1)S(1)}, bf16[2,32,1024]{2,1,0:T(8,128)(2,1)S(1)}, u32[]{:S(2)}, u32[]{:S(2)}) collective-permute-start(bf16[2,32,1024]{2,1,0:T(8,128)(2,1)S(1)} %get-tuple-element.64), channel_id=1, source_target_pairs={{0,4},{1,5},{2,6},{3,7},{4,0},{5,1},{6,2},{7,3},{8,12},{9,13},{10,... | collective-permute-start | bytes 393224 | tf_op jit(solution)/shard_map/ppermute | solution.py:259
  64.7 5.2 %collective-permute-start.10 = (bf16[2,32,640]{2,1,0:T(8,128)(2,1)S(1)}, bf16[2,32,640]{2,1,0:T(8,128)(2,1)S(1)}, u32[]{:S(2)}, u32[]{:S(2)}) collective-permute-start(bf16[2,32,640]{2,1,0:T(8,128)(2,1)S(1)} %get-tuple-element.78), channel_id=1, source_target_pairs={{0,2},{1,3},{2,0},{3,1},{4,6},{5,7},{6,4},{7,5},{8,10},{9,11},{10,... | collective-permute-start | bytes 245768 | tf_op jit(solution)/shard_map/ppermute | solution.py:259
  69.6 6.7 %collective-permute-start.7 = (bf16[1,32,1024]{2,1,0:T(8,128)(2,1)S(1)}, bf16[1,32,1024]{2,1,0:T(8,128)(2,1)S(1)}, u32[]{:S(2)}, u32[]{:S(2)}) collective-permute-start(bf16[1,32,1024]{2,1,0:T(8,128)(2,1)S(1)} %get-tuple-element.66), channel_id=1, source_target_pairs={{0,8},{1,9},{2,10},{3,11},{4,12},{5,13},{6,14},{7,15},{8,0},{9,1},... | collective-permute-start | bytes 196616 | tf_op jit(solution)/shard_map/ppermute | solution.py:259
  69.9 6.4 %collective-permute-start.11 = (bf16[1,32,640]{2,1,0:T(8,128)(2,1)S(1)}, bf16[1,32,640]{2,1,0:T(8,128)(2,1)S(1)}, u32[]{:S(2)}, u32[]{:S(2)}) collective-permute-start(bf16[1,32,640]{2,1,0:T(8,128)(2,1)S(1)} %get-tuple-element.82), channel_id=1, source_target_pairs={{0,8},{1,9},{2,10},{3,11},{4,12},{5,13},{6,14},{7,15},{8,0},{9,1},... | collective-permute-start | bytes 122888 | tf_op jit(solution)/shard_map/ppermute | solution.py:259

commit v4 on v3

--- a/solution.py
+++ b/solution.py
@@ -32,7 +32,7 @@
     return [pl.BlockSpec(memory_space=pltpu.VMEM)] * count
 
 
-def pack_kernel(rows, half, me_ref, feats_ref, g_ref, out_ref, own_ref, low_ref, top_ref, late_ref, here_ref, sems, rim_sems):
+def pack_kernel(rows, half, linked, me_ref, feats_ref, g_ref, even_ref, odd_ref, low_ref, top_ref, here_ref, sems, rim_sems):
     entries, slabs, cap = g_ref.shape
     mols = feats_ref.shape[0]
     reach = low_ref.shape[0]
@@ -62,62 +62,70 @@
     size = PACK * slabs
     to = lax.broadcasted_iota(jnp.int32, (size, size), 0)
     source = lax.broadcasted_iota(jnp.int32, (size, size), 1)
-    perm = jnp.where((to % PACK) * slabs + to // PACK == source, 1.0, 0.0).astype(BF16)
+    slab = to // PACK
+    if linked:
+        slab = slab ^ me_ref[0]
+    perm = jnp.where((to % PACK) * slabs + slab == source, 1.0, 0.0).astype(BF16)
+
+    def lanes_of(block):
+        early = []
+        for group in range(groups):
+            first = group * rows + block * PACK
+            valid = max(0, min(PACK, entries - first))
+            tiles = []
+            if valid:
+                tiles.append(here_ref[first : first + valid])
+            if valid < PACK:
+                tiles.append(jnp.zeros((PACK - valid, slabs, cap), BF16))
+            tile = tiles[0] if len(tiles) == 1 else jnp.concatenate(tiles, axis=0)
+            early.append(tile.reshape(size, cap)[:, :half])
+        return early
+
     for begin, end, copies in stages:
         for copy in copies:
             copy.wait()
-        for block in range(begin, end):
-            early, late = [], []
-            for group in range(groups):
-                first = group * rows + block * PACK
-                valid = max(0, min(PACK, entries - first))
-                tiles = []
-                if valid:
-                    tiles.append(here_ref[first : first + valid])
-                if valid < PACK:
-                    tiles.append(jnp.zeros((PACK - valid, slabs, cap), BF16))
-                tile = tiles[0] if len(tiles) == 1 else jnp.concatenate(tiles, axis=0)
-                tile = tile.reshape(size, cap)
-                early.append(tile[:, :half])
-                late.append(tile[:, half:])
-            both = jnp.concatenate(early + late, axis=1)
-            moved = mm(perm, both).astype(BF16).reshape(slabs, PACK, 2 * LANES)
-            here = pl.ds(block * PACK, PACK)
-            out_ref[:, here, :] = moved[:, :, :LANES]
-            late_ref[:, here, :] = moved[:, :, LANES:]
-    own_ref[...] = late_ref[me_ref[0]]
+        for block in range(begin, end, 2):
+            together = range(block, min(block + 2, end))
+            lanes = [piece for one in together for piece in lanes_of(one)]
+            moved = mm(perm, jnp.concatenate(lanes, axis=1)).astype(BF16)
+            for index, one in enumerate(together):
+                chunk = moved[:, index * LANES : (index + 1) * LANES].reshape(slabs // 2, 2, PACK, LANES)
+                here = pl.ds(one * PACK, PACK)
+                even_ref[:, here, :] = chunk[:, 0]
+                odd_ref[:, here, :] = chunk[:, 1]
     for copy in rims:
         copy.wait()
 
 
-def unpack(half, came_ref, own_ref, g_ref):
-    slabs, rows, _ = came_ref.shape
+def unpack(half, chunks, own_ref, g_ref):
     groups = LANES // half
-    for tile in range(slabs // groups + 1):
-        if tile < slabs // groups:
-            chunks = [came_ref[tile * groups + k] for k in range(groups)]
-        else:
-            chunks = [own_ref[...]] + [jnp.zeros((rows, LANES), BF16)] * (groups - 1)
+    rows = g_ref.shape[0] // groups
+    tiles = len(chunks) // groups
+    for tile in range(tiles):
+        here = [chunk() for chunk in chunks[tile * groups : (tile + 1) * groups]]
         for group in range(groups):
             lanes = slice(group * half, (group + 1) * half)
             g_ref[group * rows : (group + 1) * rows, tile * LANES : (tile + 1) * LANES] = jnp.concatenate(
-                [chunk[:, lanes] for chunk in chunks], axis=1
+                [chunk[:, lanes] for chunk in here], axis=1
             )
-
-
-def slot_rows(ref, me, half):
+    g_ref[:, tiles * LANES :] = own_ref[...]
+
+
+def slot_rows(ref, me, half, linked):
     slabs, cap = ref.shape
     per = LANES // half
     rows = []
     for tile in range(slabs // per):
-        rows.append(jnp.concatenate([ref[tile * per + k : tile * per + k + 1, :half] for k in range(per)], axis=1))
+        ids = [tile * per + k for k in range(per)]
+        pieces = [ref[pl.ds(me ^ i if linked else i, 1), :] for i in ids]
+        rows.append(jnp.concatenate([piece[:, :half] for piece in pieces], axis=1))
     own = ref[pl.ds(me, 1), :][:, half:]
     rows.append(jnp.concatenate([own, jnp.full((1, LANES - half), -1, jnp.int32)], axis=1))
     return rows
 
 
 def edge_kernel(
-    half, me_ref, feats_ref, below_ref, above_ref, w_src_ref, w_dst_ref, src_ref, dst_ref, live_ref,
+    half, linked, me_ref, feats_ref, below_ref, above_ref, w_src_ref, w_dst_ref, src_ref, dst_ref, live_ref,
     onehot_ref, hidden_ref, slope_ref, ext_ref,
 ):
     me = me_ref[0]
@@ -133,7 +141,7 @@
     high, low = halves(proj)
     mol_src = lax.broadcasted_iota(jnp.int32, (mols, LANES), 0)
     mol_dst = lax.broadcasted_iota(jnp.int32, (wide, LANES), 0)
-    lists = [slot_rows(ref, me, half) for ref in (src_ref, dst_ref, live_ref)]
+    lists = [slot_rows(ref, me, half, linked) for ref in (src_ref, dst_ref, live_ref)]
     for tile, (src, dst, live) in enumerate(zip(*lists)):
         src = jnp.where(live > 0, src, -1)
         moved = jnp.where(dst < reach, dst + mols, jnp.where(dst < reach + mols, dst - reach, dst))
@@ -171,9 +179,11 @@
 
 
 def grad_kernel(
-    half, factor, me_ref, came_ref, own_ref, w_out_ref, slope_hbm, onehot_hbm, ext_hbm,
-    keep_ref, send_ref, sums_ref, lower_ref, upper_ref, g_ref, slope_ref, onehot_ref, ext_ref, sems,
+    half, factor, me_ref, own_ref, w_out_ref, slope_hbm, onehot_hbm, ext_hbm, *rest,
 ):
+    (
+        *came_refs, keep_ref, send_ref, sums_ref, lower_ref, upper_ref, g_ref, slope_ref, onehot_ref, ext_ref, sems,
+    ) = rest
     odd = me_ref[0] % 2
     width = w_out_ref.shape[0]
     slots = g_ref.shape[1]
@@ -192,7 +202,8 @@
         tiles.append(copies)
     ext_copy = pltpu.make_async_copy(ext_hbm, ext_ref, sems.at[3, 0])
     ext_copy.start()
-    unpack(half, came_ref, own_ref, g_ref)
+    chunks = [functools.partial(lambda ref, i: ref[i], ref, i) for ref in came_refs for i in range(ref.shape[0])]
+    unpack(half, chunks, own_ref, g_ref)
     sums = None
     for tile, copies in enumerate(tiles):
         lanes = slice(tile * step, (tile + 1) * step)
@@ -286,18 +297,18 @@
 
     rows = round_up(pl.cdiv(entries, groups), PACK)
     stages = 4
-    packed, own, low, top = pl.pallas_call(
-        functools.partial(pack_kernel, rows, half),
+    linked = slabs <= 16
+    even, odd, low, top = pl.pallas_call(
+        functools.partial(pack_kernel, rows, half, linked),
         out_shape=(
-            jax.ShapeDtypeStruct((slabs, rows, LANES), BF16),
-            jax.ShapeDtypeStruct((rows, LANES), BF16),
+            jax.ShapeDtypeStruct((slabs // 2, rows, LANES), BF16),
+            jax.ShapeDtypeStruct((slabs // 2, rows, LANES), BF16),
             jax.ShapeDtypeStruct((reach, width), BF16),
             jax.ShapeDtypeStruct((reach, width), BF16),
         ),
         in_specs=[smem, hbm, hbm],
         out_specs=tuple(vmem(4)),
         scratch_shapes=[
-            pltpu.VMEM((slabs, rows, LANES), BF16),
             pltpu.VMEM((entries, slabs, cap), BF16),
             pltpu.SemaphoreType.DMA((stages, groups)),
             pltpu.SemaphoreType.DMA((2,)),
@@ -307,10 +318,21 @@
     )(me, in_hbm(mol_feats), in_hbm(jnp.transpose(grad_blocks[0], (2, 0, 1))))
     below = lax.ppermute(top, "space", up)
     above = lax.ppermute(low, "space", down)
-    came = lax.all_to_all(packed, "space", split_axis=0, concat_axis=0, tiled=True)
+    if linked:
+        other = swap(odd, 0, slabs)
+        messages = [jnp.stack([even[k], other[k]]) for k in range(slabs // 2)]
+        messages = list(lax.optimization_barrier(tuple(messages)))
+        came = messages[:1] + [None] * (slabs // 2 - 1)
+        for k in sorted(range(1, slabs // 2), key=lambda k: (k < slabs // 4, k)):
+            came[k] = lax.ppermute(messages[k], "space", [(i, i ^ (2 * k)) for i in range(slabs)])
+    else:
+        packed = jnp.stack([even, odd], axis=1).reshape(slabs, rows, LANES)
+        came = [lax.all_to_all(packed, "space", split_axis=0, concat_axis=0, tiled=True)]
+    late = lax.dynamic_index_in_dim(grad_blocks[0], me[0], 0, keepdims=False)[half:]
+    own = jnp.pad(late.T, ((0, groups * rows - entries), (0, LANES - half)))
 
     onehot, hidden, slope, ext = pl.pallas_call(
-        functools.partial(edge_kernel, half),
+        functools.partial(edge_kernel, half, linked),
         out_shape=(
             jax.ShapeDtypeStruct((2 * mols + 2 * reach, slots), BF16),
             jax.ShapeDtypeStruct((width, slots), BF16),
@@ -346,7 +368,7 @@
             jax.ShapeDtypeStruct((reach, width), F32),
             jax.ShapeDtypeStruct((entries_wide, slots), BF16),
         ),
-        in_specs=[smem] + vmem(3) + [hbm] * 3,
+        in_specs=[smem] + vmem(2) + [hbm] * 3 + vmem(len(came)),
         out_specs=tuple(vmem(6)),
         scratch_shapes=[
             pltpu.VMEM((width, slots), F32),
@@ -356,7 +378,7 @@
         ],
         compiler_params=big,
         name="grads",
-    )(me, came, own, w_out_wide, in_hbm(slope), in_hbm(onehot), in_hbm(ext))
+    )(me, own, w_out_wide, in_hbm(slope), in_hbm(onehot), in_hbm(ext), *came)
     lanes = round_up(entries_wide, LANES)
     keep_o, send_o = pl.pallas_call(
         functools.partial(outer_kernel, factor),
@@ -401,7 +423,6 @@
     from_below = lax.ppermute(upper, "space", up)
     crossed = swap(send, 0, slabs)
     crossed_o = swap(send_o, 0, slabs)
-    keep, crossed, from_above, from_below = lax.optimization_barrier((keep, crossed, from_above, from_below))
     for (bit, place), (bit_o, place_o) in zip(paths[0][1:], paths[1][1:]):
         keep, send = fold(bit, place, keep, crossed)
         crossed = swap(send, bit, slabs)

time: 77.3 us -> 77.7 us (level)
  starting transfers between devices: 21.3 us -> 36.4 us
  waiting for transfers between devices: 31.1 us -> 16.1 us
  other arithmetic: 0 us -> 2.83 us
  Pallas kernels: 17.1 us -> 15.8 us
  local copies, waits for them, and re-layouts: 6.6 us -> 5.52 us
    all_to_all x1 -> x0, waiting for transfers between devices: 13.2 us -> none  [on_device(): lax.all_to_all(packed, 'space', split_axis=0, concat_axis=0, tiled=True)]
    ppermute x0 -> x7, starting transfers between devices: none -> 12.2 us  [on_device(): lax.ppermute(messages[k], 'space', [(i, i ^ 2 * k) for i in range(slabs)])]
    ppermute x8 -> x9, starting transfers between devices: 6.57 us -> 15.3 us  [swap(): lax.ppermute(block, 'space', [(i, i ^ 1 << bit) for i in range(slabs)])]
    ppermute x0 -> x7, waiting for transfers between devices: none -> 6.09 us  [on_device(): lax.ppermute(messages[k], 'space', [(i, i ^ 2 * k) for i in range(slabs)])]
    ppermute x1, waiting for transfers between devices: 4.69 us -> 0.01 us  [on_device(): from_below = lax.ppermute(upper, 'space', up)]
    all_to_all x1 -> x0, starting transfers between devices: 3.7 us -> none  [on_device(): lax.all_to_all(packed, 'space', split_axis=0, concat_axis=0, tiled=True)]
    another operation x0 -> x4, other arithmetic: none -> 2.83 us  [on_device(): messages = [jnp.stack([even[k], other[k]]) for k in range(slabs // 2)]]
    ppermute x1, waiting for transfers between devices: 2.52 us -> 0.01 us  [on_device(): from_above = lax.ppermute(lower, 'space', down)]
  transfers between devices with their start and end apart: 13 -> 20, of which waited for: 6 -> 8; matrix products, arithmetic and copies ran while one was open for 3% -> 3% of each run, Pallas kernels for 9% -> 9%
where the time goes in v4:
time: 77.7 us; the launch traced here: 77.5 us
  starting transfers between devices  36.4 us (47%)
  waiting for transfers between devices  16.1 us (21%)
  Pallas kernels  15.8 us (20%)
  local copies, waits for them, and re-layouts  5.52 us (7%)
  other arithmetic  2.83 us (4%)
  between operations  0.87 us (1%)
    ppermute x9, starting transfers between devices, swap(): lax.ppermute(block, 'space', [(i, i ^ 1 << bit) for i in range(slabs)])  15.3 us
    ppermute x7, starting transfers between devices, on_device(): lax.ppermute(messages[k], 'space', [(i, i ^ 2 * k) for i in range(slabs)])  12.2 us
    ppermute x9, waiting for transfers between devices, swap(): lax.ppermute(block, 'space', [(i, i ^ 1 << bit) for i in range(slabs)])  9.96 us
    ppermute x7, waiting for transfers between devices, on_device(): lax.ppermute(messages[k], 'space', [(i, i ^ 2 * k) for i in range(slabs)])  6.09 us
    pallas_call x1, Pallas kernels, on_device(): pl.pallas_call(functools.partial(grad_kernel, half, factor), out_shape=(c...  5.44 us
    ppermute x1, starting transfers between devices, on_device(): above = lax.ppermute(low, 'space', down)  4.44 us
    ppermute x1, starting transfers between devices, on_device(): from_above = lax.ppermute(lower, 'space', down)  4.44 us
    pallas_call x1, Pallas kernels, on_device(): pl.pallas_call(functools.partial(edge_kernel, half, linked), out_shape=(j...  4.01 us
  transfers between devices with their start and end apart: 20, of which 8 were waited for; matrix products, arithmetic and copies ran while one was open for 3% of the time, Pallas kernels for 9%

profile of v4, /device:TPU:0, one launch (start us, length us, event | category | flops | bytes accessed | tf_op | source)
XLA Modules:
  0.0 77.5 jit_solution(4350580179375318075)
XLA Ops:
  0.6 2.5 %pack.1 = (bf16[8,272,128]{2,1,0:T(8,128)(2,1)S(1)}, bf16[8,272,128]{2,1,0:T(8,128)(2,1)S(1)}, bf16[64,512]{1,0:T(8,128)(2,1)S(1)}, bf16[64,512]{1,0:T(8,128)(2,1)S(1)}) custom-call(s32[1]{0:T(128)} %bitcast.me_ref, bf16[256,512]{1,0:T(8,128)(2,1)} %feats_ref.3, bf16[529,16,128]{2,1,0:T(8,128)(2,1)} %bitcast.15), custom_call_target="tpu_custom_call" | custom-call | tf_op jit(solution)/shard_map/pack/pallas_call | solution.py:301
  3.7 1.5 %collective-permute-done.2 = bf16[8,272,128]{2,1,0:T(8,128)(2,1)S(1)} collective-permute-done((bf16[8,272,128]{2,1,0:T(8,128)(2,1)S(1)}, bf16[8,272,128]{2,1,0:T(8,128)(2,1)S(1)}, u32[]{:S(2)}, u32[]{:S(2)}) %collective-permute-start.2) | collective-permute-done | bytes 557088 | tf_op jit(solution)/shard_map/ppermute | solution.py:270
  5.3 0.7 pad_maximum_fusion.6
  6.0 0.7 pad_maximum_fusion.4
  6.7 0.7 pad_maximum_fusion.2
  7.5 0.7 pad_maximum_fusion
  8.1 2.9 %collective-permute-start.3 = (bf16[2,272,128]{2,1,0:T(8,128)(2,1)}, bf16[2,272,128]{2,1,0:T(8,128)(2,1)S(1)}, u32[]{:S(2)}, u32[]{:S(2)}) collective-permute-start(bf16[2,272,128]{2,1,0:T(8,128)(2,1)} %get-tuple-element.57), channel_id=1, source_target_pairs={{0,2},{1,3},{2,0},{3,1},{4,6},{5,7},{6,4},{7,5},{8,10},{9,11},{10,... | collective-permute-start | bytes 417800 | tf_op jit(solution)/shard_map/ppermute | solution.py:327
  11.0 1.6 %collective-permute-start.4 = (bf16[2,272,128]{2,1,0:T(8,128)(2,1)}, bf16[2,272,128]{2,1,0:T(8,128)(2,1)S(1)}, u32[]{:S(2)}, u32[]{:S(2)}) collective-permute-start(bf16[2,272,128]{2,1,0:T(8,128)(2,1)} %get-tuple-element.58), channel_id=1, source_target_pairs={{0,4},{1,5},{2,6},{3,7},{4,0},{5,1},{6,2},{7,3},{8,12},{9,13},{10,... | collective-permute-start | bytes 417800 | tf_op jit(solution)/shard_map/ppermute | solution.py:327
  12.6 4.4 %collective-permute-start.1 = (bf16[64,512]{1,0:T(8,128)(2,1)S(1)}, bf16[64,512]{1,0:T(8,128)(2,1)S(1)}, u32[]{:S(2)}, u32[]{:S(2)}) collective-permute-start(bf16[64,512]{1,0:T(8,128)(2,1)S(1)} %get-tuple-element.50), channel_id=1, source_target_pairs={{1,0},{2,1},{3,2},{4,3},{5,4},{6,5},{7,6},{8,7},{9,8},{10,9},{11,1... | collective-permute-start | bytes 196616 | tf_op jit(solution)/shard_map/ppermute | solution.py:320
  17.1 1.7 %constant_dynamic-slice_fusion = bf16[1,1,64,529]{2,1,3,0:T(2,128)(2,1)S(1)} fusion(bf16[1,16,128,529]{2,1,3,0:T(8,128)(2,1)} %param.12, s32[]{:T(128)S(6)} %select_n.4, s32[]{:T(128)S(6)} %add.9), kind=kLoop, calls=%fused_computation.9 | loop fusion | bytes 135432 | tf_op jit(solution)/shard_map/slice | solution.py:331
  19.3 0.8 %collective-permute-start.6 = (bf16[2,272,128]{2,1,0:T(8,128)(2,1)}, bf16[2,272,128]{2,1,0:T(8,128)(2,1)S(1)}, u32[]{:S(2)}, u32[]{:S(2)}) collective-permute-start(bf16[2,272,128]{2,1,0:T(8,128)(2,1)} %get-tuple-element.60), channel_id=1, source_target_pairs={{0,8},{1,9},{2,10},{3,11},{4,12},{5,13},{6,14},{7,15},{8,0},{9,1},... | collective-permute-start | bytes 417800 | tf_op jit(solution)/shard_map/ppermute | solution.py:327
  20.1 1.6 %collective-permute-start.7 = (bf16[2,272,128]{2,1,0:T(8,128)(2,1)}, bf16[2,272,128]{2,1,0:T(8,128)(2,1)S(1)}, u32[]{:S(2)}, u32[]{:S(2)}) collective-permute-start(bf16[2,272,128]{2,1,0:T(8,128)(2,1)} %get-tuple-element.61), channel_id=1, source_target_pairs={{0,10},{1,11},{2,8},{3,9},{4,14},{5,15},{6,12},{7,13},{8,2},{9,3},... | collective-permute-start | bytes 417800 | tf_op jit(solution)/shard_map/ppermute | solution.py:327
  21.8 3.6 %collective-permute-start.8 = (bf16[2,272,128]{2,1,0:T(8,128)(2,1)}, bf16[2,272,128]{2,1,0:T(8,128)(2,1)S(1)}, u32[]{:S(2)}, u32[]{:S(2)}) collective-permute-start(bf16[2,272,128]{2,1,0:T(8,128)(2,1)} %get-tuple-element.62), channel_id=1, source_target_pairs={{0,12},{1,13},{2,14},{3,15},{4,8},{5,9},{6,10},{7,11},{8,4},{9,5},... | collective-permute-start | bytes 417800 | tf_op jit(solution)/shard_map/ppermute | solution.py:327
  25.4 1.7 %collective-permute-start.9 = (bf16[2,272,128]{2,1,0:T(8,128)(2,1)S(1)}, bf16[2,272,128]{2,1,0:T(8,128)(2,1)S(1)}, u32[]{:S(2)}, u32[]{:S(2)}) collective-permute-start(bf16[2,272,128]{2,1,0:T(8,128)(2,1)S(1)} %get-tuple-element.63), channel_id=1, source_target_pairs={{0,14},{1,15},{2,12},{3,13},{4,10},{5,11},{6,8},{7,9},{8,6},{9,7},... | collective-permute-start | bytes 417800 | tf_op jit(solution)/shard_map/ppermute | solution.py:327
  27.1 4.0 %edges.1 = (bf16[640,1152]{1,0:T(8,128)(2,1)S(1)}, bf16[512,1152]{1,0:T(8,128)(2,1)S(1)}, f32[512,1152]{1,0:T(8,128)S(1)}, bf16[512,384]{1,0:T(8,128)(2,1)S(1)}) custom-call(s32[1]{0:T(128)} %bitcast.me_ref, bf16[256,512]{1,0:T(8,128)(2,1)S(1)} %copy-done.3, bf16[64,512]{1,0:T(8,128)(2,1)S(1)} %collective-permute-done.below_ref, ...), custom_call_target="tpu_custom_call" | custom-call | flops 30198988800 | bytes 8388608 | tf_op jit(solution)/shard_map/edges/pallas_call | solution.py:334
  31.1 1.4 %copy-done = f32[512,1152]{1,0:T(8,128)} copy-done((f32[512,1152]{1,0:T(8,128)}, f32[512,1152]{1,0:T(8,128)S(1)}, u32[]{:S(2)}) %copy-start) | copy-done | bytes 2359320
  32.5 1.1 %copy-done.1 = bf16[640,1152]{1,0:T(8,128)(2,1)} copy-done((bf16[640,1152]{1,0:T(8,128)(2,1)}, bf16[640,1152]{1,0:T(8,128)(2,1)S(1)}, u32[]{:S(2)}) %copy-start.1) | copy-done | bytes 1474584
  33.6 0.7 copy-done.2
  34.4 4.1 %collective-permute-done.6.rest_4_ = bf16[2,272,128]{2,1,0:T(8,128)(2,1)S(1)} collective-permute-done((bf16[2,272,128]{2,1,0:T(8,128)(2,1)}, bf16[2,272,128]{2,1,0:T(8,128)(2,1)S(1)}, u32[]{:S(2)}, u32[]{:S(2)}) %collective-permute-start.6) | collective-permute-done | bytes 139296 | tf_op jit(solution)/shard_map/ppermute | solution.py:327
  38.4 2.0 %collective-permute-done.7.rest_5_ = bf16[2,272,128]{2,1,0:T(8,128)(2,1)S(1)} collective-permute-done((bf16[2,272,128]{2,1,0:T(8,128)(2,1)}, bf16[2,272,128]{2,1,0:T(8,128)(2,1)S(1)}, u32[]{:S(2)}, u32[]{:S(2)}) %collective-permute-start.7) | collective-permute-done | bytes 139296 | tf_op jit(solution)/shard_map/ppermute | solution.py:327
  40.5 5.4 %grads.1 = (f32[8,32,1024]{2,1,0:T(8,128)S(1)}, bf16[8,32,1024]{2,1,0:T(8,128)(2,1)S(1)}, f32[512,512]{1,0:T(8,128)S(1)}, f32[64,512]{1,0:T(8,128)S(1)}, f32[64,...) custom-call(s32[1]{0:T(128)} %bitcast.me_ref, bf16[544,128]{1,0:T(8,128)(2,1)S(1)} %pad.8.own_ref, ...), custom_call_target="tpu_custom_call" | custom-call | tf_op jit(solution)/shard_map/grads/pallas_call | solution.py:361
  46.0 1.2 %outer.1 = (f32[8,32,640]{2,1,0:T(8,128)S(1)}, bf16[8,32,640]{2,1,0:T(8,128)(2,1)S(1)}) custom-call(s32[1]{0:T(128)} %bitcast.me_ref, bf16[512,1152]{1,0:T(8,128)(2,1)S(1)} %get-tuple-element.75.hidden_ref, bf16[544,1152]{1,0:T(8,128)(2,1)S(1)} %get-tuple-element.76.g_ref), custom_call_target="tpu_custom_call" | custom-call | flops 12834570240 | bytes 4194304 | tf_op jit(solution)/shard_map/outer/pallas_call | solution.py:383
  47.2 0.6 collective-permute-start.16
  48.0 2.5 %collective-permute-start.13 = (bf16[4,32,1024]{2,1,0:T(8,128)(2,1)S(1)}, bf16[4,32,1024]{2,1,0:T(8,128)(2,1)S(1)}, u32[]{:S(2)}, u32[]{:S(2)}) collective-permute-start(bf16[4,32,1024]{2,1,0:T(8,128)(2,1)S(1)} %get-tuple-element.70), channel_id=1, source_target_pairs={{0,2},{1,3},{2,0},{3,1},{4,6},{5,7},{6,4},{7,5},{8,10},{9,11},{10,... | collective-permute-start | bytes 786440 | tf_op jit(solution)/shard_map/ppermute | solution.py:270
  50.6 5.5 %collective-permute-start.17 = (bf16[4,32,640]{2,1,0:T(8,128)(2,1)S(1)}, bf16[4,32,640]{2,1,0:T(8,128)(2,1)S(1)}, u32[]{:S(2)}, u32[]{:S(2)}) collective-permute-start(bf16[4,32,640]{2,1,0:T(8,128)(2,1)S(1)} %get-tuple-element.82), channel_id=1, source_target_pairs={{0,4},{1,5},{2,6},{3,7},{4,0},{5,1},{6,2},{7,3},{8,12},{9,13},{10,... | collective-permute-start | bytes 491528 | tf_op jit(solution)/shard_map/ppermute | solution.py:270
  56.1 1.0 %collective-permute-done.13.came_ref = bf16[4,32,1024]{2,1,0:T(8,128)(2,1)S(1)} collective-permute-done((bf16[4,32,1024]{2,1,0:T(8,128)(2,1)S(1)}, bf16[4,32,1024]{2,1,0:T(8,128)(2,1)S(1)}, u32[]{:S(2)}, u32[]{:S(2)}) %collective-permute-start.13) | collective-permute-done | bytes 262176 | tf_op jit(solution)/shard_map/ppermute | solution.py:270
  57.2 5.5 %collective-permute-start.14 = (bf16[2,32,1024]{2,1,0:T(8,128)(2,1)S(1)}, bf16[2,32,1024]{2,1,0:T(8,128)(2,1)S(1)}, u32[]{:S(2)}, u32[]{:S(2)}) collective-permute-start(bf16[2,32,1024]{2,1,0:T(8,128)(2,1)S(1)} %get-tuple-element.72), channel_id=1, source_target_pairs={{0,4},{1,5},{2,6},{3,7},{4,0},{5,1},{6,2},{7,3},{8,12},{9,13},{10,... | collective-permute-start | bytes 393224 | tf_op jit(solution)/shard_map/ppermute | solution.py:270
  62.7 4.4 %collective-permute-start.11 = (f32[64,512]{1,0:T(8,128)S(1)}, f32[64,512]{1,0:T(8,128)S(1)}, u32[]{:S(2)}, u32[]{:S(2)}) collective-permute-start(f32[64,512]{1,0:T(8,128)S(1)} %get-tuple-element.66), channel_id=1, source_target_pairs={{1,0},{2,1},{3,2},{4,3},{5,4},{6,5},{7,6},{8,7},{9,8},{10,9},{11,1... | collective-permute-start | bytes 393224 | tf_op jit(solution)/shard_map/ppermute | solution.py:422
  67.9 4.0 %collective-permute-done.18.came_ref = bf16[2,32,640]{2,1,0:T(8,128)(2,1)S(1)} collective-permute-done((bf16[2,32,640]{2,1,0:T(8,128)(2,1)S(1)}, bf16[2,32,640]{2,1,0:T(8,128)(2,1)S(1)}, u32[]{:S(2)}, u32[]{:S(2)}) %collective-permute-start.18) | collective-permute-done | bytes 81952 | tf_op jit(solution)/shard_map/ppermute | solution.py:270
  72.0 1.5 %rims.1 = f32[256,512]{1,0:T(8,128)} custom-call(f32[512,512]{1,0:T(8,128)S(1)} %get-tuple-element.64.sums_ref, f32[64,512]{1,0:T(8,128)S(1)} %collective-permute-done.10.from_below_ref, f32[64,512]{1,0:T(8,128)S(1)} %collective-permute-done.11.from_above_ref, bf16[512,512]{1,0:T(8,128)(2,1)S(1)} %copy-done.4, bf16[512,512]{1,0:T(8,128)(2,1)S(1)} %copy-done.5), custom_call_target="tpu_custom_call" | custom-call | flops 24159191040 | bytes 4194304 | tf_op jit(solution)/shard_map/rims/pallas_call | solution.py:434
  73.5 3.3 %collective-permute-done.19.refs_3_ = bf16[1,32,640]{2,1,0:T(8,128)(2,1)S(1)} collective-permute-done((bf16[1,32,640]{2,1,0:T(8,128)(2,1)S(1)}, bf16[1,32,640]{2,1,0:T(8,128)(2,1)S(1)}, u32[]{:S(2)}, u32[]{:S(2)}) %collective-permute-start.19) | collective-permute-done | bytes 40992 | tf_op jit(solution)/shard_map/ppermute | solution.py:270
  76.8 0.7 totals.1
  (51 shorter events, 2.5 us)
Async XLA Ops:
  3.1 2.1 %collective-permute-start.2 = (bf16[8,272,128]{2,1,0:T(8,128)(2,1)S(1)}, bf16[8,272,128]{2,1,0:T(8,128)(2,1)S(1)}, u32[]{:S(2)}, u32[]{:S(2)}) collective-permute-start(bf16[8,272,128]{2,1,0:T(8,128)(2,1)S(1)} %get-tuple-element.55), channel_id=1, source_target_pairs={{0,1},{1,0},{2,3},{3,2},{4,5},{5,4},{6,7},{7,6},{8,9},{9,8},{10,11... | collective-permute-start | bytes 1671176 | tf_op jit(solution)/shard_map/ppermute | solution.py:270
  3.7 15.1 %copy-start.9 = (bf16[512,529]{0,1:T(8,128)(2,1)S(1)}, bf16[512,529]{0,1:T(8,128)(2,1)}, u32[]{:S(2)}) copy-start(bf16[512,529]{0,1:T(8,128)(2,1)} %param.11) | copy-start | bytes 1625092
  7.4 19.6 %copy-start.3 = (bf16[256,512]{1,0:T(8,128)(2,1)S(1)}, bf16[256,512]{1,0:T(8,128)(2,1)}, u32[]{:S(2)}) copy-start(bf16[256,512]{1,0:T(8,128)(2,1)} %feats_ref.3) | copy-start | bytes 786436
  7.4 19.6 %copy-start.4 = (bf16[512,512]{1,0:T(8,128)(2,1)S(1)}, bf16[512,512]{1,0:T(8,128)(2,1)}, u32[]{:S(2)}) copy-start(bf16[512,512]{1,0:T(8,128)(2,1)} %w_src_ref.3) | copy-start | bytes 1572868
  7.4 19.6 %copy-start.5 = (bf16[512,512]{1,0:T(8,128)(2,1)S(1)}, bf16[512,512]{1,0:T(8,128)(2,1)}, u32[]{:S(2)}) copy-start(bf16[512,512]{1,0:T(8,128)(2,1)} %w_dst_ref.3) | copy-start | bytes 1572868
  7.4 19.6 %copy-start.6 = (s32[2048]{0:T(1024)S(1)}, s32[2048]{0:T(1024)}, u32[]{:S(2)}) copy-start(s32[2048]{0:T(1024)} %param.13) | copy-start | bytes 24580
  7.4 19.6 %copy-start.7 = (s32[2048]{0:T(1024)S(1)}, s32[2048]{0:T(1024)}, u32[]{:S(2)}) copy-start(s32[2048]{0:T(1024)} %param.14) | copy-start | bytes 24580
  7.4 19.6 %copy-start.8 = (s32[2048]{0:T(1024)S(1)}, s32[2048]{0:T(1024)}, u32[]{:S(2)}) copy-start(s32[2048]{0:T(1024)} %param.15) | copy-start | bytes 24580
  8.1 13.6 %collective-permute-start.3 = (bf16[2,272,128]{2,1,0:T(8,128)(2,1)}, bf16[2,272,128]{2,1,0:T(8,128)(2,1)S(1)}, u32[]{:S(2)}, u32[]{:S(2)}) collective-permute-start(bf16[2,272,128]{2,1,0:T(8,128)(2,1)} %get-tuple-element.57), channel_id=1, source_target_pairs={{0,2},{1,3},{2,0},{3,1},{4,6},{5,7},{6,4},{7,5},{8,10},{9,11},{10,... | collective-permute-start | bytes 417800 | tf_op jit(solution)/shard_map/ppermute | solution.py:327
  11.0 14.3 %collective-permute-start.4 = (bf16[2,272,128]{2,1,0:T(8,128)(2,1)}, bf16[2,272,128]{2,1,0:T(8,128)(2,1)S(1)}, u32[]{:S(2)}, u32[]{:S(2)}) collective-permute-start(bf16[2,272,128]{2,1,0:T(8,128)(2,1)} %get-tuple-element.58), channel_id=1, source_target_pairs={{0,4},{1,5},{2,6},{3,7},{4,0},{5,1},{6,2},{7,3},{8,12},{9,13},{10,... | collective-permute-start | bytes 417800 | tf_op jit(solution)/shard_map/ppermute | solution.py:327
  12.6 6.7 %collective-permute-start = (bf16[64,512]{1,0:T(8,128)(2,1)S(1)}, bf16[64,512]{1,0:T(8,128)(2,1)S(1)}, u32[]{:S(2)}, u32[]{:S(2)}) collective-permute-start(bf16[64,512]{1,0:T(8,128)(2,1)S(1)} %get-tuple-element.49), channel_id=1, source_target_pairs={{0,1},{1,2},{2,3},{3,4},{4,5},{5,6},{6,7},{7,8},{8,9},{9,10},{10,1... | collective-permute-start | bytes 196616 | tf_op jit(solution)/shard_map/ppermute | solution.py:319
  12.6 7.5 %collective-permute-start.1 = (bf16[64,512]{1,0:T(8,128)(2,1)S(1)}, bf16[64,512]{1,0:T(8,128)(2,1)S(1)}, u32[]{:S(2)}, u32[]{:S(2)}) collective-permute-start(bf16[64,512]{1,0:T(8,128)(2,1)S(1)} %get-tuple-element.50), channel_id=1, source_target_pairs={{1,0},{2,1},{3,2},{4,3},{5,4},{6,5},{7,6},{8,7},{9,8},{10,9},{11,1... | collective-permute-start | bytes 196616 | tf_op jit(solution)/shard_map/ppermute | solution.py:320
  19.2 15.2 %collective-permute-start.5 = (bf16[2,272,128]{2,1,0:T(8,128)(2,1)}, bf16[2,272,128]{2,1,0:T(8,128)(2,1)S(1)}, u32[]{:S(2)}, u32[]{:S(2)}) collective-permute-start(bf16[2,272,128]{2,1,0:T(8,128)(2,1)} %get-tuple-element.59), channel_id=1, source_target_pairs={{0,6},{1,7},{2,4},{3,5},{4,2},{5,3},{6,0},{7,1},{8,14},{9,15},{10,... | collective-permute-start | bytes 417800 | tf_op jit(solution)/shard_map/ppermute | solution.py:327
  19.3 19.1 %collective-permute-start.6 = (bf16[2,272,128]{2,1,0:T(8,128)(2,1)}, bf16[2,272,128]{2,1,0:T(8,128)(2,1)S(1)}, u32[]{:S(2)}, u32[]{:S(2)}) collective-permute-start(bf16[2,272,128]{2,1,0:T(8,128)(2,1)} %get-tuple-element.60), channel_id=1, source_target_pairs={{0,8},{1,9},{2,10},{3,11},{4,12},{5,13},{6,14},{7,15},{8,0},{9,1},... | collective-permute-start | bytes 417800 | tf_op jit(solution)/shard_map/ppermute | solution.py:327
  20.1 20.3 %collective-permute-start.7 = (bf16[2,272,128]{2,1,0:T(8,128)(2,1)}, bf16[2,272,128]{2,1,0:T(8,128)(2,1)S(1)}, u32[]{:S(2)}, u32[]{:S(2)}) collective-permute-start(bf16[2,272,128]{2,1,0:T(8,128)(2,1)} %get-tuple-element.61), channel_id=1, source_target_pairs={{0,10},{1,11},{2,8},{3,9},{4,14},{5,15},{6,12},{7,13},{8,2},{9,3},... | collective-permute-start | bytes 417800 | tf_op jit(solution)/shard_map/ppermute | solution.py:327
  21.8 18.7 %collective-permute-start.8 = (bf16[2,272,128]{2,1,0:T(8,128)(2,1)}, bf16[2,272,128]{2,1,0:T(8,128)(2,1)S(1)}, u32[]{:S(2)}, u32[]{:S(2)}) collective-permute-start(bf16[2,272,128]{2,1,0:T(8,128)(2,1)} %get-tuple-element.62), channel_id=1, source_target_pairs={{0,12},{1,13},{2,14},{3,15},{4,8},{5,9},{6,10},{7,11},{8,4},{9,5},... | collective-permute-start | bytes 417800 | tf_op jit(solution)/shard_map/ppermute | solution.py:327
  25.4 15.1 %collective-permute-start.9 = (bf16[2,272,128]{2,1,0:T(8,128)(2,1)S(1)}, bf16[2,272,128]{2,1,0:T(8,128)(2,1)S(1)}, u32[]{:S(2)}, u32[]{:S(2)}) collective-permute-start(bf16[2,272,128]{2,1,0:T(8,128)(2,1)S(1)} %get-tuple-element.63), channel_id=1, source_target_pairs={{0,14},{1,15},{2,12},{3,13},{4,10},{5,11},{6,8},{7,9},{8,6},{9,7},... | collective-permute-start | bytes 417800 | tf_op jit(solution)/shard_map/ppermute | solution.py:327
  31.1 1.4 %copy-start = (f32[512,1152]{1,0:T(8,128)}, f32[512,1152]{1,0:T(8,128)S(1)}, u32[]{:S(2)}) copy-start(f32[512,1152]{1,0:T(8,128)S(1)} %get-tuple-element.51.slope_hbm) | copy-start | bytes 7077892
  32.5 1.1 %copy-start.1 = (bf16[640,1152]{1,0:T(8,128)(2,1)}, bf16[640,1152]{1,0:T(8,128)(2,1)S(1)}, u32[]{:S(2)}) copy-start(bf16[640,1152]{1,0:T(8,128)(2,1)S(1)} %get-tuple-element.52.onehot_hbm) | copy-start | bytes 4423684
  33.6 0.7 copy-start.2
  45.9 2.0 %collective-permute-start.12 = (bf16[8,32,1024]{2,1,0:T(8,128)(2,1)S(1)}, bf16[8,32,1024]{2,1,0:T(8,128)(2,1)S(1)}, u32[]{:S(2)}, u32[]{:S(2)}) collective-permute-start(bf16[8,32,1024]{2,1,0:T(8,128)(2,1)S(1)} %get-tuple-element.68), channel_id=1, source_target_pairs={{0,1},{1,0},{2,3},{3,2},{4,5},{5,4},{6,7},{7,6},{8,9},{9,8},{10,11... | collective-permute-start | bytes 1572872 | tf_op jit(solution)/shard_map/ppermute | solution.py:270
  47.2 3.3 %collective-permute-start.16 = (bf16[8,32,640]{2,1,0:T(8,128)(2,1)S(1)}, bf16[8,32,640]{2,1,0:T(8,128)(2,1)S(1)}, u32[]{:S(2)}, u32[]{:S(2)}) collective-permute-start(bf16[8,32,640]{2,1,0:T(8,128)(2,1)S(1)} %get-tuple-element.78), channel_id=1, source_target_pairs={{0,1},{1,0},{2,3},{3,2},{4,5},{5,4},{6,7},{7,6},{8,9},{9,8},{10,11... | collective-permute-start | bytes 983048 | tf_op jit(solution)/shard_map/ppermute | solution.py:270
  48.0 9.1 %collective-permute-start.13 = (bf16[4,32,1024]{2,1,0:T(8,128)(2,1)S(1)}, bf16[4,32,1024]{2,1,0:T(8,128)(2,1)S(1)}, u32[]{:S(2)}, u32[]{:S(2)}) collective-permute-start(bf16[4,32,1024]{2,1,0:T(8,128)(2,1)S(1)} %get-tuple-element.70), channel_id=1, source_target_pairs={{0,2},{1,3},{2,0},{3,1},{4,6},{5,7},{6,4},{7,5},{8,10},{9,11},{10,... | collective-permute-start | bytes 786440 | tf_op jit(solution)/shard_map/ppermute | solution.py:270
  50.6 16.5 %collective-permute-start.17 = (bf16[4,32,640]{2,1,0:T(8,128)(2,1)S(1)}, bf16[4,32,640]{2,1,0:T(8,128)(2,1)S(1)}, u32[]{:S(2)}, u32[]{:S(2)}) collective-permute-start(bf16[4,32,640]{2,1,0:T(8,128)(2,1)S(1)} %get-tuple-element.82), channel_id=1, source_target_pairs={{0,4},{1,5},{2,6},{3,7},{4,0},{5,1},{6,2},{7,3},{8,12},{9,13},{10,... | collective-permute-start | bytes 491528 | tf_op jit(solution)/shard_map/ppermute | solution.py:270
  57.2 10.1 %collective-permute-start.14 = (bf16[2,32,1024]{2,1,0:T(8,128)(2,1)S(1)}, bf16[2,32,1024]{2,1,0:T(8,128)(2,1)S(1)}, u32[]{:S(2)}, u32[]{:S(2)}) collective-permute-start(bf16[2,32,1024]{2,1,0:T(8,128)(2,1)S(1)} %get-tuple-element.72), channel_id=1, source_target_pairs={{0,4},{1,5},{2,6},{3,7},{4,0},{5,1},{6,2},{7,3},{8,12},{9,13},{10,... | collective-permute-start | bytes 393224 | tf_op jit(solution)/shard_map/ppermute | solution.py:270
  62.7 9.2 %collective-permute-start.10 = (f32[64,512]{1,0:T(8,128)S(1)}, f32[64,512]{1,0:T(8,128)S(1)}, u32[]{:S(2)}, u32[]{:S(2)}) collective-permute-start(f32[64,512]{1,0:T(8,128)S(1)} %get-tuple-element.65), channel_id=1, source_target_pairs={{0,1},{1,2},{2,3},{3,4},{4,5},{5,6},{6,7},{7,8},{8,9},{9,10},{10,1... | collective-permute-start | bytes 393224 | tf_op jit(solution)/shard_map/ppermute | solution.py:423
  62.7 9.2 %collective-permute-start.11 = (f32[64,512]{1,0:T(8,128)S(1)}, f32[64,512]{1,0:T(8,128)S(1)}, u32[]{:S(2)}, u32[]{:S(2)}) collective-permute-start(f32[64,512]{1,0:T(8,128)S(1)} %get-tuple-element.66), channel_id=1, source_target_pairs={{1,0},{2,1},{3,2},{4,3},{5,4},{6,5},{7,6},{8,7},{9,8},{10,9},{11,1... | collective-permute-start | bytes 393224 | tf_op jit(solution)/shard_map/ppermute | solution.py:422
  67.2 4.6 %collective-permute-start.18 = (bf16[2,32,640]{2,1,0:T(8,128)(2,1)S(1)}, bf16[2,32,640]{2,1,0:T(8,128)(2,1)S(1)}, u32[]{:S(2)}, u32[]{:S(2)}) collective-permute-start(bf16[2,32,640]{2,1,0:T(8,128)(2,1)S(1)} %get-tuple-element.86), channel_id=1, source_target_pairs={{0,2},{1,3},{2,0},{3,1},{4,6},{5,7},{6,4},{7,5},{8,10},{9,11},{10,... | collective-permute-start | bytes 245768 | tf_op jit(solution)/shard_map/ppermute | solution.py:270
  67.3 9.5 %collective-permute-start.15 = (bf16[1,32,1024]{2,1,0:T(8,128)(2,1)S(1)}, bf16[1,32,1024]{2,1,0:T(8,128)(2,1)S(1)}, u32[]{:S(2)}, u32[]{:S(2)}) collective-permute-start(bf16[1,32,1024]{2,1,0:T(8,128)(2,1)S(1)} %get-tuple-element.74), channel_id=1, source_target_pairs={{0,8},{1,9},{2,10},{3,11},{4,12},{5,13},{6,14},{7,15},{8,0},{9,1},... | collective-permute-start | bytes 196616 | tf_op jit(solution)/shard_map/ppermute | solution.py:270
  71.9 5.0 %collective-permute-start.19 = (bf16[1,32,640]{2,1,0:T(8,128)(2,1)S(1)}, bf16[1,32,640]{2,1,0:T(8,128)(2,1)S(1)}, u32[]{:S(2)}, u32[]{:S(2)}) collective-permute-start(bf16[1,32,640]{2,1,0:T(8,128)(2,1)S(1)} %get-tuple-element.90), channel_id=1, source_target_pairs={{0,8},{1,9},{2,10},{3,11},{4,12},{5,13},{6,14},{7,15},{8,0},{9,1},... | collective-permute-start | bytes 122888 | tf_op jit(solution)/shard_map/ppermute | solution.py:270

commit v5 on v4

--- a/solution.py
+++ b/solution.py
@@ -97,6 +97,12 @@
         copy.wait()
 
 
+def join_kernel(even_ref, other_ref, *message_refs):
+    for k, message_ref in enumerate(message_refs):
+        message_ref[0] = even_ref[k]
+        message_ref[1] = other_ref[k]
+
+
 def unpack(half, chunks, own_ref, g_ref):
     groups = LANES // half
     rows = g_ref.shape[0] // groups
@@ -111,13 +117,13 @@
     g_ref[:, tiles * LANES :] = own_ref[...]
 
 
-def slot_rows(ref, me, half, linked):
+def slot_rows(ref, me, half, order):
     slabs, cap = ref.shape
     per = LANES // half
     rows = []
     for tile in range(slabs // per):
-        ids = [tile * per + k for k in range(per)]
-        pieces = [ref[pl.ds(me ^ i if linked else i, 1), :] for i in ids]
+        ids = range(tile * per, tile * per + per)
+        pieces = [ref[pl.ds(me ^ order[i] if order else i, 1), :] for i in ids]
         rows.append(jnp.concatenate([piece[:, :half] for piece in pieces], axis=1))
     own = ref[pl.ds(me, 1), :][:, half:]
     rows.append(jnp.concatenate([own, jnp.full((1, LANES - half), -1, jnp.int32)], axis=1))
@@ -125,7 +131,7 @@
 
 
 def edge_kernel(
-    half, linked, me_ref, feats_ref, below_ref, above_ref, w_src_ref, w_dst_ref, src_ref, dst_ref, live_ref,
+    half, order, me_ref, feats_ref, below_ref, above_ref, w_src_ref, w_dst_ref, src_ref, dst_ref, live_ref,
     onehot_ref, hidden_ref, slope_ref, ext_ref,
 ):
     me = me_ref[0]
@@ -141,7 +147,7 @@
     high, low = halves(proj)
     mol_src = lax.broadcasted_iota(jnp.int32, (mols, LANES), 0)
     mol_dst = lax.broadcasted_iota(jnp.int32, (wide, LANES), 0)
-    lists = [slot_rows(ref, me, half, linked) for ref in (src_ref, dst_ref, live_ref)]
+    lists = [slot_rows(ref, me, half, order) for ref in (src_ref, dst_ref, live_ref)]
     for tile, (src, dst, live) in enumerate(zip(*lists)):
         src = jnp.where(live > 0, src, -1)
         moved = jnp.where(dst < reach, dst + mols, jnp.where(dst < reach + mols, dst - reach, dst))
@@ -214,8 +220,8 @@
         term = mm(onehot_ref[:, lanes], dpre, NT)
         sums = term if sums is None else sums + term
     reach = lower_ref.shape[0]
-    lower_ref[...] = sums[inside : inside + reach]
-    upper_ref[...] = sums[inside + reach :]
+    lower_ref[...] = sums[inside : inside + reach].astype(BF16)
+    upper_ref[...] = sums[inside + reach :].astype(BF16)
     sums_ref[...] = sums[:inside]
     high, low = halves(sums)
     ext_copy.wait()
@@ -239,7 +245,12 @@
     src = sums_ref[:mols]
     dst = sums_ref[mols:]
     dst = jnp.concatenate(
-        [dst[:reach] + from_below_ref[...], dst[reach : mols - reach], dst[mols - reach :] + from_above_ref[...]], axis=0
+        [
+            dst[:reach] + from_below_ref[...].astype(F32),
+            dst[reach : mols - reach],
+            dst[mols - reach :] + from_above_ref[...].astype(F32),
+        ],
+        axis=0,
     )
     w_src = w_src_ref[...]
     w_dst = w_dst_ref[...]
@@ -318,21 +329,30 @@
     )(me, in_hbm(mol_feats), in_hbm(jnp.transpose(grad_blocks[0], (2, 0, 1))))
     below = lax.ppermute(top, "space", up)
     above = lax.ppermute(low, "space", down)
+    order = ()
     if linked:
         other = swap(odd, 0, slabs)
-        messages = [jnp.stack([even[k], other[k]]) for k in range(slabs // 2)]
-        messages = list(lax.optimization_barrier(tuple(messages)))
-        came = messages[:1] + [None] * (slabs // 2 - 1)
-        for k in sorted(range(1, slabs // 2), key=lambda k: (k < slabs // 4, k)):
-            came[k] = lax.ppermute(messages[k], "space", [(i, i ^ (2 * k)) for i in range(slabs)])
+        other, below, above = lax.optimization_barrier((other, below, above))
+        messages = pl.pallas_call(
+            join_kernel,
+            out_shape=(jax.ShapeDtypeStruct((2, rows, LANES), BF16),) * (slabs // 2),
+            in_specs=vmem(2),
+            out_specs=tuple(vmem(slabs // 2)),
+            compiler_params=big,
+            name="join",
+        )(even, other)
+        turns = sorted(range(slabs // 2), key=lambda k: (k < slabs // 4, k))
+        order = tuple(2 * k + j for k in turns for j in range(2))
+        came = [
+            lax.ppermute(messages[k], "space", [(i, i ^ (2 * k)) for i in range(slabs)]) if k else messages[0]
+            for k in turns
+        ]
     else:
         packed = jnp.stack([even, odd], axis=1).reshape(slabs, rows, LANES)
         came = [lax.all_to_all(packed, "space", split_axis=0, concat_axis=0, tiled=True)]
-    late = lax.dynamic_index_in_dim(grad_blocks[0], me[0], 0, keepdims=False)[half:]
-    own = jnp.pad(late.T, ((0, groups * rows - entries), (0, LANES - half)))
 
     onehot, hidden, slope, ext = pl.pallas_call(
-        functools.partial(edge_kernel, half, linked),
+        functools.partial(edge_kernel, half, order),
         out_shape=(
             jax.ShapeDtypeStruct((2 * mols + 2 * reach, slots), BF16),
             jax.ShapeDtypeStruct((width, slots), BF16),
@@ -351,6 +371,10 @@
         me, mol_feats, below, above, w_src, w_dst,
         edge_src.reshape(slabs, cap), edge_dst.reshape(slabs, cap), edge_live.reshape(slabs, cap),
     )
+
+    here, w_out, slope = lax.optimization_barrier((me, w_out, slope))
+    late = lax.dynamic_index_in_dim(grad_blocks[0], here[0], 0, keepdims=False)[half:]
+    own = jnp.pad(late.T, ((0, groups * rows - entries), (0, LANES - half)))
 
     def chunks(count, lanes, dtype):
         return jax.ShapeDtypeStruct((count, part, lanes), dtype)
@@ -364,8 +388,8 @@
             chunks(slabs // 2, 2 * width, F32),
             chunks(slabs // 2, 2 * width, BF16),
             jax.ShapeDtypeStruct((2 * mols, width), F32),
-            jax.ShapeDtypeStruct((reach, width), F32),
-            jax.ShapeDtypeStruct((reach, width), F32),
+            jax.ShapeDtypeStruct((reach, width), BF16),
+            jax.ShapeDtypeStruct((reach, width), BF16),
             jax.ShapeDtypeStruct((entries_wide, slots), BF16),
         ),
         in_specs=[smem] + vmem(2) + [hbm] * 3 + vmem(len(came)),
@@ -423,6 +447,7 @@
     from_below = lax.ppermute(upper, "space", up)
     crossed = swap(send, 0, slabs)
     crossed_o = swap(send_o, 0, slabs)
+    crossed_o, from_above, from_below = lax.optimization_barrier((crossed_o, from_above, from_below))
     for (bit, place), (bit_o, place_o) in zip(paths[0][1:], paths[1][1:]):
         keep, send = fold(bit, place, keep, crossed)
         crossed = swap(send, bit, slabs)

time: 77.7 us -> 82.4 us (1.060)
  waiting for transfers between devices: 16.1 us -> 32.3 us
  starting transfers between devices: 36.4 us -> 23.7 us
  local copies, waits for them, and re-layouts: 5.52 us -> 9.42 us
  other arithmetic: 2.83 us -> 0 us
    ppermute x9, starting transfers between devices: 15.3 us -> 6.47 us  [swap(): lax.ppermute(block, 'space', [(i, i ^ 1 << bit) for i in range(slabs)])]
    ppermute x7, waiting for transfers between devices: 6.09 us -> 11.6 us  [on_device(): lax.ppermute(messages[k], 'space', [(i, i ^ 2 * k) for i in range(slabs)])]
    ppermute x1, waiting for transfers between devices: 0.01 us -> 4.48 us  [on_device(): from_below = lax.ppermute(upper, 'space', up)]
    another operation x4 -> x0, other arithmetic: 2.83 us -> none  [on_device(): messages = [jnp.stack([even[k], other[k]]) for k in range(slabs // 2)]]
    ppermute x7, starting transfers between devices: 12.2 us -> 9.47 us  [on_device(): lax.ppermute(messages[k], 'space', [(i, i ^ 2 * k) for i in range(slabs)])]
    ppermute x1, starting transfers between devices: 4.44 us -> 2.04 us  [on_device(): from_above = lax.ppermute(lower, 'space', down)]
    ppermute x9, waiting for transfers between devices: 9.96 us -> 12.3 us  [swap(): lax.ppermute(block, 'space', [(i, i ^ 1 << bit) for i in range(slabs)])]
    optimization_barrier x0 -> x1, local copies, waits for them, and re-layouts: none -> 2.15 us  [on_device(): here, w_out, slope = lax.optimization_barrier((me, w_out, slope))]
  transfers between devices with their start and end apart: 20 -> 20, of which waited for: 8 -> 10; matrix products, arithmetic and copies ran while one was open for 3% -> 6% of each run, Pallas kernels for 9% -> 9%
where the time goes in v5:
time: 82.4 us; the launch traced here: 82.2 us
  waiting for transfers between devices  32.3 us (39%)
  starting transfers between devices  23.7 us (29%)
  Pallas kernels  15.9 us (19%)
  local copies, waits for them, and re-layouts  9.42 us (11%)
  between operations  0.89 us (1%)
    ppermute x9, waiting for transfers between devices, swap(): lax.ppermute(block, 'space', [(i, i ^ 1 << bit) for i in range(slabs)])  12.3 us
    ppermute x7, waiting for transfers between devices, on_device(): lax.ppermute(messages[k], 'space', [(i, i ^ 2 * k) for i in range(slabs)])  11.6 us
    ppermute x7, starting transfers between devices, on_device(): lax.ppermute(messages[k], 'space', [(i, i ^ 2 * k) for i in range(slabs)])  9.47 us
    ppermute x9, starting transfers between devices, swap(): lax.ppermute(block, 'space', [(i, i ^ 1 << bit) for i in range(slabs)])  6.47 us
    ppermute x1, starting transfers between devices, on_device(): above = lax.ppermute(low, 'space', down)  5.61 us
    pallas_call x1, Pallas kernels, on_device(): pl.pallas_call(functools.partial(grad_kernel, half, factor), out_shape=(c...  5.45 us
    ppermute x1, waiting for transfers between devices, on_device(): from_below = lax.ppermute(upper, 'space', up)  4.48 us
    unnamed x23, local copies, waits for them, and re-layouts  4.38 us
  transfers between devices with their start and end apart: 20, of which 10 were waited for; matrix products, arithmetic and copies ran while one was open for 6% of the time, Pallas kernels for 9%

profile of v5, /device:TPU:0, one launch (start us, length us, event | category | flops | bytes accessed | tf_op | source)
XLA Modules:
  0.0 82.2 jit_solution(7155589262950188904)
XLA Ops:
  0.7 2.6 %pack.1 = (bf16[8,272,128]{2,1,0:T(8,128)(2,1)S(1)}, bf16[8,272,128]{2,1,0:T(8,128)(2,1)S(1)}, bf16[64,512]{1,0:T(8,128)(2,1)S(1)}, bf16[64,512]{1,0:T(8,128)(2,1)S(1)}) custom-call(s32[1]{0:T(128)} %bitcast.me_ref, bf16[256,512]{1,0:T(8,128)(2,1)} %feats_ref.3, bf16[529,16,128]{2,1,0:T(8,128)(2,1)} %bitcast.16), custom_call_target="tpu_custom_call" | custom-call | tf_op jit(solution)/shard_map/pack/pallas_call | solution.py:312
  3.3 0.5 collective-permute-start
  3.9 5.6 %collective-permute-start.2 = (bf16[64,512]{1,0:T(8,128)(2,1)S(1)}, bf16[64,512]{1,0:T(8,128)(2,1)S(1)}, u32[]{:S(2)}, u32[]{:S(2)}) collective-permute-start(bf16[64,512]{1,0:T(8,128)(2,1)S(1)} %get-tuple-element.60), channel_id=1, source_target_pairs={{1,0},{2,1},{3,2},{4,3},{5,4},{6,5},{7,6},{8,7},{9,8},{10,9},{11,1... | collective-permute-start | bytes 196616 | tf_op jit(solution)/shard_map/ppermute | solution.py:331
  9.5 1.9 %collective-permute-done.1.below_ref = bf16[64,512]{1,0:T(8,128)(2,1)S(1)} collective-permute-done((bf16[64,512]{1,0:T(8,128)(2,1)S(1)}, bf16[64,512]{1,0:T(8,128)(2,1)S(1)}, u32[]{:S(2)}, u32[]{:S(2)}) %collective-permute-start.1) | collective-permute-done | bytes 65568 | tf_op jit(solution)/shard_map/ppermute | solution.py:330
  11.5 0.7 collective-permute-start.3
  12.6 3.6 %collective-permute-start.5 = (bf16[2,272,128]{2,1,0:T(8,128)(2,1)S(1)}, bf16[2,272,128]{2,1,0:T(8,128)(2,1)S(1)}, u32[]{:S(2)}, u32[]{:S(2)}) collective-permute-start(bf16[2,272,128]{2,1,0:T(8,128)(2,1)S(1)} %get-tuple-element.73), channel_id=1, source_target_pairs={{0,12},{1,13},{2,14},{3,15},{4,8},{5,9},{6,10},{7,11},{8,4},{9,5},... | collective-permute-start | bytes 417800 | tf_op jit(solution)/shard_map/ppermute | solution.py:347
  16.2 3.0 %collective-permute-start.6 = (bf16[2,272,128]{2,1,0:T(8,128)(2,1)S(1)}, bf16[2,272,128]{2,1,0:T(8,128)(2,1)S(1)}, u32[]{:S(2)}, u32[]{:S(2)}) collective-permute-start(bf16[2,272,128]{2,1,0:T(8,128)(2,1)S(1)} %get-tuple-element.74), channel_id=1, source_target_pairs={{0,14},{1,15},{2,12},{3,13},{4,10},{5,11},{6,8},{7,9},{8,6},{9,7},... | collective-permute-start | bytes 417800 | tf_op jit(solution)/shard_map/ppermute | solution.py:347
  19.2 10.8 %collective-permute-done.3.rest_0_ = bf16[2,272,128]{2,1,0:T(8,128)(2,1)S(1)} collective-permute-done((bf16[2,272,128]{2,1,0:T(8,128)(2,1)S(1)}, bf16[2,272,128]{2,1,0:T(8,128)(2,1)S(1)}, u32[]{:S(2)}, u32[]{:S(2)}) %collective-permute-start.3) | collective-permute-done | bytes 139296 | tf_op jit(solution)/shard_map/ppermute | solution.py:347
  30.0 0.9 %collective-permute-done.4.rest_1_ = bf16[2,272,128]{2,1,0:T(8,128)(2,1)S(1)} collective-permute-done((bf16[2,272,128]{2,1,0:T(8,128)(2,1)S(1)}, bf16[2,272,128]{2,1,0:T(8,128)(2,1)S(1)}, u32[]{:S(2)}, u32[]{:S(2)}) %collective-permute-start.4) | collective-permute-done | bytes 139296 | tf_op jit(solution)/shard_map/ppermute | solution.py:347
  30.8 1.8 %collective-permute-start.9 = (bf16[2,272,128]{2,1,0:T(8,128)(2,1)S(1)}, bf16[2,272,128]{2,1,0:T(8,128)(2,1)S(1)}, u32[]{:S(2)}, u32[]{:S(2)}) collective-permute-start(bf16[2,272,128]{2,1,0:T(8,128)(2,1)S(1)} %get-tuple-element.78), channel_id=1, source_target_pairs={{0,6},{1,7},{2,4},{3,5},{4,2},{5,3},{6,0},{7,1},{8,14},{9,15},{10,... | collective-permute-start | bytes 417800 | tf_op jit(solution)/shard_map/ppermute | solution.py:347
  32.6 4.0 %edges.1 = (bf16[640,1152]{1,0:T(8,128)(2,1)S(1)}, bf16[512,1152]{1,0:T(8,128)(2,1)S(1)}, f32[512,1152]{1,0:T(8,128)S(1)}, bf16[512,384]{1,0:T(8,128)(2,1)S(1)}) custom-call(s32[1]{0:T(128)} %bitcast.me_ref, bf16[256,512]{1,0:T(8,128)(2,1)S(1)} %copy-done.3, bf16[64,512]{1,0:T(8,128)(2,1)S(1)} %collective-permute-done.1.below_ref, ...), custom_call_target="tpu_custom_call" | custom-call | flops 30198988800 | bytes 8388608 | tf_op jit(solution)/shard_map/edges/pallas_call | solution.py:354
  36.7 1.4 %copy-done = f32[512,1152]{1,0:T(8,128)} copy-done((f32[512,1152]{1,0:T(8,128)}, f32[512,1152]{1,0:T(8,128)S(1)}, u32[]{:S(2)}) %copy-start) | copy-done | bytes 2359320
  38.1 1.1 %copy-done.1 = bf16[640,1152]{1,0:T(8,128)(2,1)} copy-done((bf16[640,1152]{1,0:T(8,128)(2,1)}, bf16[640,1152]{1,0:T(8,128)(2,1)S(1)}, u32[]{:S(2)}) %copy-start.1) | copy-done | bytes 1474584
  39.2 0.7 copy-done.2
  39.9 1.1 %copy-done.9 = bf16[512,1152]{1,0:T(8,128)(2,1)} copy-done((bf16[512,1152]{1,0:T(8,128)(2,1)}, bf16[512,1152]{1,0:T(8,128)(2,1)S(1)}, u32[]{:S(2)}) %copy-start.9) | copy-done | bytes 1179672
  41.0 1.7 %constant_dynamic-slice_fusion = bf16[1,1,64,529]{2,1,3,0:T(2,128)(2,1)S(1)} fusion(bf16[1,16,128,529]{2,1,3,0:T(8,128)(2,1)} %param.12, s32[]{:T(128)S(6)} %select_n.4, s32[]{:T(128)S(6)} %add.9), kind=kLoop, calls=%fused_computation.1 | loop fusion | bytes 135432 | tf_op jit(solution)/shard_map/slice | solution.py:376
  42.7 2.1 %copy.13 = bf16[512,529]{1,0:T(8,128)(2,1)} copy(bf16[512,529]{0,1:T(8,128)(2,1)} %param.11) | data formatting | bytes 1083392 | tf_op jit(solution)/shard_map/optimization_barrier | solution.py:375
  44.9 1.2 %pad.9.w_out_ref = bf16[512,544]{1,0:T(8,128)(2,1)S(1)} pad(bf16[512,529]{1,0:T(8,128)(2,1)} %copy.13, bf16[]{:T(256)} %constant.13.clone.1), padding=0_0x0_15 | pad | bytes 1098754 | tf_op jit(solution)/shard_map/jit(_pad)/pad | solution.py:383
  46.1 5.5 %grads.1 = (f32[8,32,1024]{2,1,0:T(8,128)S(1)}, bf16[8,32,1024]{2,1,0:T(8,128)(2,1)S(1)}, f32[512,512]{1,0:T(8,128)S(1)}, bf16[64,512]{1,0:T(8,128)(2,1)S(1)}, b...) custom-call(s32[1]{0:T(128)} %bitcast.me_ref, bf16[544,128]{1,0:T(8,128)(2,1)S(1)} %pad.8.own_ref, ...), custom_call_target="tpu_custom_call" | custom-call | tf_op jit(solution)/shard_map/grads/pallas_call | solution.py:385
  52.1 1.2 %outer.1 = (f32[8,32,640]{2,1,0:T(8,128)S(1)}, bf16[8,32,640]{2,1,0:T(8,128)(2,1)S(1)}) custom-call(s32[1]{0:T(128)} %bitcast.me_ref, bf16[512,1152]{1,0:T(8,128)(2,1)S(1)} %copy-done.10, bf16[544,1152]{1,0:T(8,128)(2,1)S(1)} %get-tuple-element.81.g_ref), custom_call_target="tpu_custom_call" | custom-call | flops 12834570240 | bytes 4194304 | tf_op jit(solution)/shard_map/outer/pallas_call | solution.py:407
  53.8 1.8 %collective-permute-start.14 = (bf16[4,32,1024]{2,1,0:T(8,128)(2,1)S(1)}, bf16[4,32,1024]{2,1,0:T(8,128)(2,1)S(1)}, u32[]{:S(2)}, u32[]{:S(2)}) collective-permute-start(bf16[4,32,1024]{2,1,0:T(8,128)(2,1)S(1)} %get-tuple-element.90), channel_id=1, source_target_pairs={{0,2},{1,3},{2,0},{3,1},{4,6},{5,7},{6,4},{7,5},{8,10},{9,11},{10,... | collective-permute-start | bytes 786440 | tf_op jit(solution)/shard_map/ppermute | solution.py:281
  55.6 2.0 %collective-permute-start.11 = (bf16[64,512]{1,0:T(8,128)(2,1)S(1)}, bf16[64,512]{1,0:T(8,128)(2,1)S(1)}, u32[]{:S(2)}, u32[]{:S(2)}) collective-permute-start(bf16[64,512]{1,0:T(8,128)(2,1)S(1)} %get-tuple-element.83), channel_id=1, source_target_pairs={{1,0},{2,1},{3,2},{4,3},{5,4},{6,5},{7,6},{8,7},{9,8},{10,9},{11,1... | collective-permute-start | bytes 196616 | tf_op jit(solution)/shard_map/ppermute | solution.py:446
  57.6 1.9 %collective-permute-done.11.from_above_ref = bf16[64,512]{1,0:T(8,128)(2,1)S(1)} collective-permute-done((bf16[64,512]{1,0:T(8,128)(2,1)S(1)}, bf16[64,512]{1,0:T(8,128)(2,1)S(1)}, u32[]{:S(2)}, u32[]{:S(2)}) %collective-permute-start.11) | collective-permute-done | bytes 65568 | tf_op jit(solution)/shard_map/ppermute | solution.py:446
  59.5 4.5 %collective-permute-done.12.from_below_ref = bf16[64,512]{1,0:T(8,128)(2,1)S(1)} collective-permute-done((bf16[64,512]{1,0:T(8,128)(2,1)S(1)}, bf16[64,512]{1,0:T(8,128)(2,1)S(1)}, u32[]{:S(2)}, u32[]{:S(2)}) %collective-permute-start.12) | collective-permute-done | bytes 65568 | tf_op jit(solution)/shard_map/ppermute | solution.py:447
  64.3 2.1 %collective-permute-start.15 = (bf16[2,32,1024]{2,1,0:T(8,128)(2,1)S(1)}, bf16[2,32,1024]{2,1,0:T(8,128)(2,1)S(1)}, u32[]{:S(2)}, u32[]{:S(2)}) collective-permute-start(bf16[2,32,1024]{2,1,0:T(8,128)(2,1)S(1)} %get-tuple-element.92), channel_id=1, source_target_pairs={{0,4},{1,5},{2,6},{3,7},{4,0},{5,1},{6,2},{7,3},{8,12},{9,13},{10,... | collective-permute-start | bytes 393224 | tf_op jit(solution)/shard_map/ppermute | solution.py:281
  66.3 4.9 %collective-permute-done.17.came_ref = bf16[4,32,640]{2,1,0:T(8,128)(2,1)S(1)} collective-permute-done((bf16[4,32,640]{2,1,0:T(8,128)(2,1)S(1)}, bf16[4,32,640]{2,1,0:T(8,128)(2,1)S(1)}, u32[]{:S(2)}, u32[]{:S(2)}) %collective-permute-start.17) | collective-permute-done | bytes 163872 | tf_op jit(solution)/shard_map/ppermute | solution.py:281
  71.4 2.6 %collective-permute-done.15.came_ref = bf16[2,32,1024]{2,1,0:T(8,128)(2,1)S(1)} collective-permute-done((bf16[2,32,1024]{2,1,0:T(8,128)(2,1)S(1)}, bf16[2,32,1024]{2,1,0:T(8,128)(2,1)S(1)}, u32[]{:S(2)}, u32[]{:S(2)}) %collective-permute-start.15) | collective-permute-done | bytes 131104 | tf_op jit(solution)/shard_map/ppermute | solution.py:281
  74.0 1.7 %collective-permute-done.18.came_ref = bf16[2,32,640]{2,1,0:T(8,128)(2,1)S(1)} collective-permute-done((bf16[2,32,640]{2,1,0:T(8,128)(2,1)S(1)}, bf16[2,32,640]{2,1,0:T(8,128)(2,1)S(1)}, u32[]{:S(2)}, u32[]{:S(2)}) %collective-permute-start.18) | collective-permute-done | bytes 81952 | tf_op jit(solution)/shard_map/ppermute | solution.py:281
  75.8 1.2 %collective-permute-start.19 = (bf16[1,32,640]{2,1,0:T(8,128)(2,1)S(1)}, bf16[1,32,640]{2,1,0:T(8,128)(2,1)S(1)}, u32[]{:S(2)}, u32[]{:S(2)}) collective-permute-start(bf16[1,32,640]{2,1,0:T(8,128)(2,1)S(1)} %get-tuple-element.108), channel_id=1, source_target_pairs={{0,8},{1,9},{2,10},{3,11},{4,12},{5,13},{6,14},{7,15},{8,0},{9,1},... | collective-permute-start | bytes 122888 | tf_op jit(solution)/shard_map/ppermute | solution.py:281
  77.0 1.5 %rims.1 = f32[256,512]{1,0:T(8,128)} custom-call(f32[512,512]{1,0:T(8,128)S(1)} %get-tuple-element.79.sums_ref, bf16[64,512]{1,0:T(8,128)(2,1)S(1)} %collective-permute-done.12.from_below_ref, bf16[64,512]{1,0:T(8,128)(2,1)S(1)} %collective-permute-done.11.from_above_ref, bf16[512,512]{1,0:T(8,128)(2,1)S(1)} %copy-done.4, bf16[512,512]{1,0:T(8,128)(2,1)S(1)} %copy-done.5), custom_call_target="tpu_custom_call" | custom-call | flops 24159191040 | bytes 4194304 | tf_op jit(solution)/shard_map/rims/pallas_call | solution.py:459
  78.6 2.9 %collective-permute-done.19.refs_3_ = bf16[1,32,640]{2,1,0:T(8,128)(2,1)S(1)} collective-permute-done((bf16[1,32,640]{2,1,0:T(8,128)(2,1)S(1)}, bf16[1,32,640]{2,1,0:T(8,128)(2,1)S(1)}, u32[]{:S(2)}, u32[]{:S(2)}) %collective-permute-start.19) | collective-permute-done | bytes 40992 | tf_op jit(solution)/shard_map/ppermute | solution.py:281
  81.5 0.7 totals.1
  (48 shorter events, 2.1 us)
Async XLA Ops:
  0.6 32.0 %copy-start.3 = (bf16[256,512]{1,0:T(8,128)(2,1)S(1)}, bf16[256,512]{1,0:T(8,128)(2,1)}, u32[]{:S(2)}) copy-start(bf16[256,512]{1,0:T(8,128)(2,1)} %feats_ref.3) | copy-start | bytes 786436
  0.6 32.0 %copy-start.5 = (bf16[512,512]{1,0:T(8,128)(2,1)S(1)}, bf16[512,512]{1,0:T(8,128)(2,1)}, u32[]{:S(2)}) copy-start(bf16[512,512]{1,0:T(8,128)(2,1)} %w_dst_ref.3) | copy-start | bytes 1572868
  0.7 32.0 %copy-start.4 = (bf16[512,512]{1,0:T(8,128)(2,1)S(1)}, bf16[512,512]{1,0:T(8,128)(2,1)}, u32[]{:S(2)}) copy-start(bf16[512,512]{1,0:T(8,128)(2,1)} %w_src_ref.3) | copy-start | bytes 1572868
  0.7 32.0 %copy-start.8 = (s32[2048]{0:T(1024)S(1)}, s32[2048]{0:T(1024)}, u32[]{:S(2)}) copy-start(s32[2048]{0:T(1024)} %param.15) | copy-start | bytes 24580
  0.7 31.9 %copy-start.7 = (s32[2048]{0:T(1024)S(1)}, s32[2048]{0:T(1024)}, u32[]{:S(2)}) copy-start(s32[2048]{0:T(1024)} %param.14) | copy-start | bytes 24580
  0.7 31.9 %copy-start.6 = (s32[2048]{0:T(1024)S(1)}, s32[2048]{0:T(1024)}, u32[]{:S(2)}) copy-start(s32[2048]{0:T(1024)} %param.13) | copy-start | bytes 24580
  3.3 8.1 %collective-permute-start = (bf16[8,272,128]{2,1,0:T(8,128)(2,1)S(1)}, bf16[8,272,128]{2,1,0:T(8,128)(2,1)S(1)}, u32[]{:S(2)}, u32[]{:S(2)}) collective-permute-start(bf16[8,272,128]{2,1,0:T(8,128)(2,1)S(1)} %get-tuple-element.58), channel_id=1, source_target_pairs={{0,1},{1,0},{2,3},{3,2},{4,5},{5,4},{6,7},{7,6},{8,9},{9,8},{10,11... | collective-permute-start | bytes 1671176 | tf_op jit(solution)/shard_map/ppermute | solution.py:281
  3.8 7.6 %collective-permute-start.1 = (bf16[64,512]{1,0:T(8,128)(2,1)S(1)}, bf16[64,512]{1,0:T(8,128)(2,1)S(1)}, u32[]{:S(2)}, u32[]{:S(2)}) collective-permute-start(bf16[64,512]{1,0:T(8,128)(2,1)S(1)} %get-tuple-element.59), channel_id=1, source_target_pairs={{0,1},{1,2},{2,3},{3,4},{4,5},{5,6},{6,7},{7,8},{8,9},{9,10},{10,1... | collective-permute-start | bytes 196616 | tf_op jit(solution)/shard_map/ppermute | solution.py:330
  3.9 7.6 %collective-permute-start.2 = (bf16[64,512]{1,0:T(8,128)(2,1)S(1)}, bf16[64,512]{1,0:T(8,128)(2,1)S(1)}, u32[]{:S(2)}, u32[]{:S(2)}) collective-permute-start(bf16[64,512]{1,0:T(8,128)(2,1)S(1)} %get-tuple-element.60), channel_id=1, source_target_pairs={{1,0},{2,1},{3,2},{4,3},{5,4},{6,5},{7,6},{8,7},{9,8},{10,9},{11,1... | collective-permute-start | bytes 196616 | tf_op jit(solution)/shard_map/ppermute | solution.py:331
  11.5 18.5 %collective-permute-start.3 = (bf16[2,272,128]{2,1,0:T(8,128)(2,1)S(1)}, bf16[2,272,128]{2,1,0:T(8,128)(2,1)S(1)}, u32[]{:S(2)}, u32[]{:S(2)}) collective-permute-start(bf16[2,272,128]{2,1,0:T(8,128)(2,1)S(1)} %get-tuple-element.71), channel_id=1, source_target_pairs={{0,8},{1,9},{2,10},{3,11},{4,12},{5,13},{6,14},{7,15},{8,0},{9,1},... | collective-permute-start | bytes 417800 | tf_op jit(solution)/shard_map/ppermute | solution.py:347
  12.2 18.7 %collective-permute-start.4 = (bf16[2,272,128]{2,1,0:T(8,128)(2,1)S(1)}, bf16[2,272,128]{2,1,0:T(8,128)(2,1)S(1)}, u32[]{:S(2)}, u32[]{:S(2)}) collective-permute-start(bf16[2,272,128]{2,1,0:T(8,128)(2,1)S(1)} %get-tuple-element.72), channel_id=1, source_target_pairs={{0,10},{1,11},{2,8},{3,9},{4,14},{5,15},{6,12},{7,13},{8,2},{9,3},... | collective-permute-start | bytes 417800 | tf_op jit(solution)/shard_map/ppermute | solution.py:347
  12.6 33.5 %collective-permute-start.5 = (bf16[2,272,128]{2,1,0:T(8,128)(2,1)S(1)}, bf16[2,272,128]{2,1,0:T(8,128)(2,1)S(1)}, u32[]{:S(2)}, u32[]{:S(2)}) collective-permute-start(bf16[2,272,128]{2,1,0:T(8,128)(2,1)S(1)} %get-tuple-element.73), channel_id=1, source_target_pairs={{0,12},{1,13},{2,14},{3,15},{4,8},{5,9},{6,10},{7,11},{8,4},{9,5},... | collective-permute-start | bytes 417800 | tf_op jit(solution)/shard_map/ppermute | solution.py:347
  16.2 29.9 %collective-permute-start.6 = (bf16[2,272,128]{2,1,0:T(8,128)(2,1)S(1)}, bf16[2,272,128]{2,1,0:T(8,128)(2,1)S(1)}, u32[]{:S(2)}, u32[]{:S(2)}) collective-permute-start(bf16[2,272,128]{2,1,0:T(8,128)(2,1)S(1)} %get-tuple-element.74), channel_id=1, source_target_pairs={{0,14},{1,15},{2,12},{3,13},{4,10},{5,11},{6,8},{7,9},{8,6},{9,7},... | collective-permute-start | bytes 417800 | tf_op jit(solution)/shard_map/ppermute | solution.py:347
  19.2 26.9 %collective-permute-start.7 = (bf16[2,272,128]{2,1,0:T(8,128)(2,1)S(1)}, bf16[2,272,128]{2,1,0:T(8,128)(2,1)S(1)}, u32[]{:S(2)}, u32[]{:S(2)}) collective-permute-start(bf16[2,272,128]{2,1,0:T(8,128)(2,1)S(1)} %get-tuple-element.76), channel_id=1, source_target_pairs={{0,2},{1,3},{2,0},{3,1},{4,6},{5,7},{6,4},{7,5},{8,10},{9,11},{10,... | collective-permute-start | bytes 417800 | tf_op jit(solution)/shard_map/ppermute | solution.py:347
  30.0 16.1 %collective-permute-start.8 = (bf16[2,272,128]{2,1,0:T(8,128)(2,1)S(1)}, bf16[2,272,128]{2,1,0:T(8,128)(2,1)S(1)}, u32[]{:S(2)}, u32[]{:S(2)}) collective-permute-start(bf16[2,272,128]{2,1,0:T(8,128)(2,1)S(1)} %get-tuple-element.77), channel_id=1, source_target_pairs={{0,4},{1,5},{2,6},{3,7},{4,0},{5,1},{6,2},{7,3},{8,12},{9,13},{10,... | collective-permute-start | bytes 417800 | tf_op jit(solution)/shard_map/ppermute | solution.py:347
  30.8 15.3 %collective-permute-start.9 = (bf16[2,272,128]{2,1,0:T(8,128)(2,1)S(1)}, bf16[2,272,128]{2,1,0:T(8,128)(2,1)S(1)}, u32[]{:S(2)}, u32[]{:S(2)}) collective-permute-start(bf16[2,272,128]{2,1,0:T(8,128)(2,1)S(1)} %get-tuple-element.78), channel_id=1, source_target_pairs={{0,6},{1,7},{2,4},{3,5},{4,2},{5,3},{6,0},{7,1},{8,14},{9,15},{10,... | collective-permute-start | bytes 417800 | tf_op jit(solution)/shard_map/ppermute | solution.py:347
  36.7 1.4 %copy-start = (f32[512,1152]{1,0:T(8,128)}, f32[512,1152]{1,0:T(8,128)S(1)}, u32[]{:S(2)}) copy-start(f32[512,1152]{1,0:T(8,128)S(1)} %get-tuple-element.66.slope_hbm) | copy-start | bytes 7077892
  38.1 1.1 %copy-start.1 = (bf16[640,1152]{1,0:T(8,128)(2,1)}, bf16[640,1152]{1,0:T(8,128)(2,1)S(1)}, u32[]{:S(2)}) copy-start(bf16[640,1152]{1,0:T(8,128)(2,1)S(1)} %get-tuple-element.67.onehot_hbm) | copy-start | bytes 4423684
  39.2 0.7 copy-start.2
  39.9 1.1 %copy-start.9 = (bf16[512,1152]{1,0:T(8,128)(2,1)}, bf16[512,1152]{1,0:T(8,128)(2,1)S(1)}, u32[]{:S(2)}) copy-start(bf16[512,1152]{1,0:T(8,128)(2,1)S(1)} %get-tuple-element.80.hidden_ref) | copy-start | bytes 3538948
  46.1 6.0 %copy-start.10 = (bf16[512,1152]{1,0:T(8,128)(2,1)S(1)}, bf16[512,1152]{1,0:T(8,128)(2,1)}, u32[]{:S(2)}) copy-start(bf16[512,1152]{1,0:T(8,128)(2,1)} %copy-done.9) | copy-start | bytes 3538948
  51.6 2.0 %collective-permute-start.13 = (bf16[8,32,1024]{2,1,0:T(8,128)(2,1)S(1)}, bf16[8,32,1024]{2,1,0:T(8,128)(2,1)S(1)}, u32[]{:S(2)}, u32[]{:S(2)}) collective-permute-start(bf16[8,32,1024]{2,1,0:T(8,128)(2,1)S(1)} %get-tuple-element.88), channel_id=1, source_target_pairs={{0,1},{1,0},{2,3},{3,2},{4,5},{5,4},{6,7},{7,6},{8,9},{9,8},{10,11... | collective-permute-start | bytes 1572872 | tf_op jit(solution)/shard_map/ppermute | solution.py:281
  53.3 10.7 %collective-permute-start.10 = (bf16[8,32,640]{2,1,0:T(8,128)(2,1)S(1)}, bf16[8,32,640]{2,1,0:T(8,128)(2,1)S(1)}, u32[]{:S(2)}, u32[]{:S(2)}) collective-permute-start(bf16[8,32,640]{2,1,0:T(8,128)(2,1)S(1)} %get-tuple-element.82), channel_id=1, source_target_pairs={{0,1},{1,0},{2,3},{3,2},{4,5},{5,4},{6,7},{7,6},{8,9},{9,8},{10,11... | collective-permute-start | bytes 983048 | tf_op jit(solution)/shard_map/ppermute | solution.py:281
  53.8 10.4 %collective-permute-start.14 = (bf16[4,32,1024]{2,1,0:T(8,128)(2,1)S(1)}, bf16[4,32,1024]{2,1,0:T(8,128)(2,1)S(1)}, u32[]{:S(2)}, u32[]{:S(2)}) collective-permute-start(bf16[4,32,1024]{2,1,0:T(8,128)(2,1)S(1)} %get-tuple-element.90), channel_id=1, source_target_pairs={{0,2},{1,3},{2,0},{3,1},{4,6},{5,7},{6,4},{7,5},{8,10},{9,11},{10,... | collective-permute-start | bytes 786440 | tf_op jit(solution)/shard_map/ppermute | solution.py:281
  55.6 3.9 %collective-permute-start.11 = (bf16[64,512]{1,0:T(8,128)(2,1)S(1)}, bf16[64,512]{1,0:T(8,128)(2,1)S(1)}, u32[]{:S(2)}, u32[]{:S(2)}) collective-permute-start(bf16[64,512]{1,0:T(8,128)(2,1)S(1)} %get-tuple-element.83), channel_id=1, source_target_pairs={{1,0},{2,1},{3,2},{4,3},{5,4},{6,5},{7,6},{8,7},{9,8},{10,9},{11,1... | collective-permute-start | bytes 196616 | tf_op jit(solution)/shard_map/ppermute | solution.py:446
  57.6 6.4 %collective-permute-start.12 = (bf16[64,512]{1,0:T(8,128)(2,1)S(1)}, bf16[64,512]{1,0:T(8,128)(2,1)S(1)}, u32[]{:S(2)}, u32[]{:S(2)}) collective-permute-start(bf16[64,512]{1,0:T(8,128)(2,1)S(1)} %get-tuple-element.84), channel_id=1, source_target_pairs={{0,1},{1,2},{2,3},{3,4},{4,5},{5,6},{6,7},{7,8},{8,9},{9,10},{10,1... | collective-permute-start | bytes 196616 | tf_op jit(solution)/shard_map/ppermute | solution.py:447
  64.1 7.1 %collective-permute-start.17 = (bf16[4,32,640]{2,1,0:T(8,128)(2,1)S(1)}, bf16[4,32,640]{2,1,0:T(8,128)(2,1)S(1)}, u32[]{:S(2)}, u32[]{:S(2)}) collective-permute-start(bf16[4,32,640]{2,1,0:T(8,128)(2,1)S(1)} %get-tuple-element.100), channel_id=1, source_target_pairs={{0,4},{1,5},{2,6},{3,7},{4,0},{5,1},{6,2},{7,3},{8,12},{9,13},{10,... | collective-permute-start | bytes 491528 | tf_op jit(solution)/shard_map/ppermute | solution.py:281
  64.3 9.7 %collective-permute-start.15 = (bf16[2,32,1024]{2,1,0:T(8,128)(2,1)S(1)}, bf16[2,32,1024]{2,1,0:T(8,128)(2,1)S(1)}, u32[]{:S(2)}, u32[]{:S(2)}) collective-permute-start(bf16[2,32,1024]{2,1,0:T(8,128)(2,1)S(1)} %get-tuple-element.92), channel_id=1, source_target_pairs={{0,4},{1,5},{2,6},{3,7},{4,0},{5,1},{6,2},{7,3},{8,12},{9,13},{10,... | collective-permute-start | bytes 393224 | tf_op jit(solution)/shard_map/ppermute | solution.py:281
  71.3 4.5 %collective-permute-start.18 = (bf16[2,32,640]{2,1,0:T(8,128)(2,1)S(1)}, bf16[2,32,640]{2,1,0:T(8,128)(2,1)S(1)}, u32[]{:S(2)}, u32[]{:S(2)}) collective-permute-start(bf16[2,32,640]{2,1,0:T(8,128)(2,1)S(1)} %get-tuple-element.104), channel_id=1, source_target_pairs={{0,2},{1,3},{2,0},{3,1},{4,6},{5,7},{6,4},{7,5},{8,10},{9,11},{10,... | collective-permute-start | bytes 245768 | tf_op jit(solution)/shard_map/ppermute | solution.py:281
  74.0 7.5 %collective-permute-start.16 = (bf16[1,32,1024]{2,1,0:T(8,128)(2,1)S(1)}, bf16[1,32,1024]{2,1,0:T(8,128)(2,1)S(1)}, u32[]{:S(2)}, u32[]{:S(2)}) collective-permute-start(bf16[1,32,1024]{2,1,0:T(8,128)(2,1)S(1)} %get-tuple-element.94), channel_id=1, source_target_pairs={{0,8},{1,9},{2,10},{3,11},{4,12},{5,13},{6,14},{7,15},{8,0},{9,1},... | collective-permute-start | bytes 196616 | tf_op jit(solution)/shard_map/ppermute | solution.py:281
  75.8 5.7 %collective-permute-start.19 = (bf16[1,32,640]{2,1,0:T(8,128)(2,1)S(1)}, bf16[1,32,640]{2,1,0:T(8,128)(2,1)S(1)}, u32[]{:S(2)}, u32[]{:S(2)}) collective-permute-start(bf16[1,32,640]{2,1,0:T(8,128)(2,1)S(1)} %get-tuple-element.108), channel_id=1, source_target_pairs={{0,8},{1,9},{2,10},{3,11},{4,12},{5,13},{6,14},{7,15},{8,0},{9,1},... | collective-permute-start | bytes 122888 | tf_op jit(solution)/shard_map/ppermute | solution.py:281

commit v6 on v5

--- a/solution.py
+++ b/solution.py
@@ -341,7 +341,8 @@
             compiler_params=big,
             name="join",
         )(even, other)
-        turns = sorted(range(slabs // 2), key=lambda k: (k < slabs // 4, k))
+        far = slabs // 4
+        turns = [0, *range(1, far - 1), *range(far, slabs // 2), *range(max(far - 1, 1), far)]
         order = tuple(2 * k + j for k in turns for j in range(2))
         came = [
             lax.ppermute(messages[k], "space", [(i, i ^ (2 * k)) for i in range(slabs)]) if k else messages[0]
@@ -447,8 +448,9 @@
     from_below = lax.ppermute(upper, "space", up)
     crossed = swap(send, 0, slabs)
     crossed_o = swap(send_o, 0, slabs)
-    crossed_o, from_above, from_below = lax.optimization_barrier((crossed_o, from_above, from_below))
     for (bit, place), (bit_o, place_o) in zip(paths[0][1:], paths[1][1:]):
+        if bit == 2:
+            keep, crossed, from_above, from_below = lax.optimization_barrier((keep, crossed, from_above, from_below))
         keep, send = fold(bit, place, keep, crossed)
         crossed = swap(send, bit, slabs)
         keep_o, crossed_o, _ = lax.optimization_barrier((keep_o, crossed_o, send))

time: 82.4 us -> 72.3 us (0.88)
  waiting for transfers between devices: 32.3 us -> 20.3 us
  starting transfers between devices: 23.7 us -> 25.5 us
    ppermute x7, waiting for transfers between devices: 11.6 us -> 4.12 us  [on_device(): lax.ppermute(messages[k], 'space', [(i, i ^ 2 * k) for i in range(slabs)])]
    ppermute x9, waiting for transfers between devices: 12.3 us -> 7.89 us  [swap(): lax.ppermute(block, 'space', [(i, i ^ 1 << bit) for i in range(slabs)])]
    ppermute x9, starting transfers between devices: 6.47 us -> 10.2 us  [swap(): lax.ppermute(block, 'space', [(i, i ^ 1 << bit) for i in range(slabs)])]
    ppermute x7, starting transfers between devices: 9.47 us -> 7.97 us  [on_device(): lax.ppermute(messages[k], 'space', [(i, i ^ 2 * k) for i in range(slabs)])]
    ppermute x1, waiting for transfers between devices: 1.9 us -> 3.09 us  [on_device(): from_above = lax.ppermute(lower, 'space', down)]
    ppermute x1, waiting for transfers between devices: 4.48 us -> 3.3 us  [on_device(): from_below = lax.ppermute(upper, 'space', up)]
  transfers between devices with their start and end apart: 20 -> 20, of which waited for: 10 -> 10; matrix products, arithmetic and copies ran while one was open for 6% -> 7% of each run, Pallas kernels for 9% -> 10%
where the time goes in v6:
time: 72.3 us; the launch traced here: 72 us
  starting transfers between devices  25.5 us (35%)
  waiting for transfers between devices  20.3 us (28%)
  Pallas kernels  15.9 us (22%)
  local copies, waits for them, and re-layouts  9.42 us (13%)
  between operations  0.87 us (1%)
    ppermute x9, starting transfers between devices, swap(): lax.ppermute(block, 'space', [(i, i ^ 1 << bit) for i in range(slabs)])  10.2 us
    ppermute x7, starting transfers between devices, on_device(): lax.ppermute(messages[k], 'space', [(i, i ^ 2 * k) for i in range(slabs)])  7.97 us
    ppermute x9, waiting for transfers between devices, swap(): lax.ppermute(block, 'space', [(i, i ^ 1 << bit) for i in range(slabs)])  7.89 us
    ppermute x1, starting transfers between devices, on_device(): above = lax.ppermute(low, 'space', down)  5.61 us
    pallas_call x1, Pallas kernels, on_device(): pl.pallas_call(functools.partial(grad_kernel, half, factor), out_shape=(c...  5.44 us
    unnamed x23, local copies, waits for them, and re-layouts  4.38 us
    ppermute x7, waiting for transfers between devices, on_device(): lax.ppermute(messages[k], 'space', [(i, i ^ 2 * k) for i in range(slabs)])  4.12 us
    pallas_call x1, Pallas kernels, on_device(): pl.pallas_call(functools.partial(edge_kernel, half, order), out_shape=(ja...  4.01 us
  transfers between devices with their start and end apart: 20, of which 10 were waited for; matrix products, arithmetic and copies ran while one was open for 7% of the time, Pallas kernels for 10%

profile of v6, /device:TPU:0, one launch (start us, length us, event | category | flops | bytes accessed | tf_op | source)
XLA Modules:
  0.0 72.0 jit_solution(14664673083698326082)
XLA Ops:
  0.7 2.6 %pack.1 = (bf16[8,272,128]{2,1,0:T(8,128)(2,1)S(1)}, bf16[8,272,128]{2,1,0:T(8,128)(2,1)S(1)}, bf16[64,512]{1,0:T(8,128)(2,1)S(1)}, bf16[64,512]{1,0:T(8,128)(2,1)S(1)}) custom-call(s32[1]{0:T(128)} %bitcast.me_ref, bf16[256,512]{1,0:T(8,128)(2,1)} %feats_ref.3, bf16[529,16,128]{2,1,0:T(8,128)(2,1)} %bitcast.16), custom_call_target="tpu_custom_call" | custom-call | tf_op jit(solution)/shard_map/pack/pallas_call | solution.py:312
  3.9 5.6 %collective-permute-start.2 = (bf16[64,512]{1,0:T(8,128)(2,1)S(1)}, bf16[64,512]{1,0:T(8,128)(2,1)S(1)}, u32[]{:S(2)}, u32[]{:S(2)}) collective-permute-start(bf16[64,512]{1,0:T(8,128)(2,1)S(1)} %get-tuple-element.61), channel_id=1, source_target_pairs={{1,0},{2,1},{3,2},{4,3},{5,4},{6,5},{7,6},{8,7},{9,8},{10,9},{11,1... | collective-permute-start | bytes 196616 | tf_op jit(solution)/shard_map/ppermute | solution.py:331
  9.5 1.9 %collective-permute-done.1.below_ref = bf16[64,512]{1,0:T(8,128)(2,1)S(1)} collective-permute-done((bf16[64,512]{1,0:T(8,128)(2,1)S(1)}, bf16[64,512]{1,0:T(8,128)(2,1)S(1)}, u32[]{:S(2)}, u32[]{:S(2)}) %collective-permute-start.1) | collective-permute-done | bytes 65568 | tf_op jit(solution)/shard_map/ppermute | solution.py:330
  11.8 2.6 %collective-permute-start.5 = (bf16[2,272,128]{2,1,0:T(8,128)(2,1)S(1)}, bf16[2,272,128]{2,1,0:T(8,128)(2,1)S(1)}, u32[]{:S(2)}, u32[]{:S(2)}) collective-permute-start(bf16[2,272,128]{2,1,0:T(8,128)(2,1)S(1)} %get-tuple-element.75), channel_id=1, source_target_pairs={{0,8},{1,9},{2,10},{3,11},{4,12},{5,13},{6,14},{7,15},{8,0},{9,1},... | collective-permute-start | bytes 417800 | tf_op jit(solution)/shard_map/ppermute | solution.py:348
  14.4 1.6 %collective-permute-start.6 = (bf16[2,272,128]{2,1,0:T(8,128)(2,1)S(1)}, bf16[2,272,128]{2,1,0:T(8,128)(2,1)S(1)}, u32[]{:S(2)}, u32[]{:S(2)}) collective-permute-start(bf16[2,272,128]{2,1,0:T(8,128)(2,1)S(1)} %get-tuple-element.76), channel_id=1, source_target_pairs={{0,10},{1,11},{2,8},{3,9},{4,14},{5,15},{6,12},{7,13},{8,2},{9,3},... | collective-permute-start | bytes 417800 | tf_op jit(solution)/shard_map/ppermute | solution.py:348
  16.0 2.1 %collective-permute-start.7 = (bf16[2,272,128]{2,1,0:T(8,128)(2,1)S(1)}, bf16[2,272,128]{2,1,0:T(8,128)(2,1)S(1)}, u32[]{:S(2)}, u32[]{:S(2)}) collective-permute-start(bf16[2,272,128]{2,1,0:T(8,128)(2,1)S(1)} %get-tuple-element.77), channel_id=1, source_target_pairs={{0,12},{1,13},{2,14},{3,15},{4,8},{5,9},{6,10},{7,11},{8,4},{9,5},... | collective-permute-start | bytes 417800 | tf_op jit(solution)/shard_map/ppermute | solution.py:348
  18.0 1.4 %collective-permute-start.8 = (bf16[2,272,128]{2,1,0:T(8,128)(2,1)S(1)}, bf16[2,272,128]{2,1,0:T(8,128)(2,1)S(1)}, u32[]{:S(2)}, u32[]{:S(2)}) collective-permute-start(bf16[2,272,128]{2,1,0:T(8,128)(2,1)S(1)} %get-tuple-element.78), channel_id=1, source_target_pairs={{0,14},{1,15},{2,12},{3,13},{4,10},{5,11},{6,8},{7,9},{8,6},{9,7},... | collective-permute-start | bytes 417800 | tf_op jit(solution)/shard_map/ppermute | solution.py:348
  19.5 1.4 %collective-permute-done.4.rest_2_ = bf16[2,272,128]{2,1,0:T(8,128)(2,1)S(1)} collective-permute-done((bf16[2,272,128]{2,1,0:T(8,128)(2,1)S(1)}, bf16[2,272,128]{2,1,0:T(8,128)(2,1)S(1)}, u32[]{:S(2)}, u32[]{:S(2)}) %collective-permute-start.4) | collective-permute-done | bytes 139296 | tf_op jit(solution)/shard_map/ppermute | solution.py:348
  20.9 4.0 %edges.1 = (bf16[640,1152]{1,0:T(8,128)(2,1)S(1)}, bf16[512,1152]{1,0:T(8,128)(2,1)S(1)}, f32[512,1152]{1,0:T(8,128)S(1)}, bf16[512,384]{1,0:T(8,128)(2,1)S(1)}) custom-call(s32[1]{0:T(128)} %bitcast.me_ref, bf16[256,512]{1,0:T(8,128)(2,1)S(1)} %copy-done.3, bf16[64,512]{1,0:T(8,128)(2,1)S(1)} %collective-permute-done.1.below_ref, ...), custom_call_target="tpu_custom_call" | custom-call | flops 30198988800 | bytes 8388608 | tf_op jit(solution)/shard_map/edges/pallas_call | solution.py:355
  25.0 1.4 %copy-done = f32[512,1152]{1,0:T(8,128)} copy-done((f32[512,1152]{1,0:T(8,128)}, f32[512,1152]{1,0:T(8,128)S(1)}, u32[]{:S(2)}) %copy-start) | copy-done | bytes 2359320
  26.4 1.1 %copy-done.1 = bf16[640,1152]{1,0:T(8,128)(2,1)} copy-done((bf16[640,1152]{1,0:T(8,128)(2,1)}, bf16[640,1152]{1,0:T(8,128)(2,1)S(1)}, u32[]{:S(2)}) %copy-start.1) | copy-done | bytes 1474584
  27.5 0.7 %copy-done.2 = bf16[512,384]{1,0:T(8,128)(2,1)} copy-done((bf16[512,384]{1,0:T(8,128)(2,1)}, bf16[512,384]{1,0:T(8,128)(2,1)S(1)}, u32[]{:S(2)}) %copy-start.2) | copy-done | bytes 393240
  28.3 1.1 %copy-done.9 = bf16[512,1152]{1,0:T(8,128)(2,1)} copy-done((bf16[512,1152]{1,0:T(8,128)(2,1)}, bf16[512,1152]{1,0:T(8,128)(2,1)S(1)}, u32[]{:S(2)}) %copy-start.9) | copy-done | bytes 1179672
  29.3 1.7 %constant_dynamic-slice_fusion = bf16[1,1,64,529]{2,1,3,0:T(2,128)(2,1)S(1)} fusion(bf16[1,16,128,529]{2,1,3,0:T(8,128)(2,1)} %param.12, s32[]{:T(128)S(6)} %select_n.4, s32[]{:T(128)S(6)} %add.9), kind=kLoop, calls=%fused_computation.1 | loop fusion | bytes 135432 | tf_op jit(solution)/shard_map/slice | solution.py:377
  31.0 2.1 %copy.13 = bf16[512,529]{1,0:T(8,128)(2,1)} copy(bf16[512,529]{0,1:T(8,128)(2,1)} %param.11) | data formatting | bytes 1083392 | tf_op jit(solution)/shard_map/optimization_barrier | solution.py:376
  33.2 1.2 %pad.9.w_out_ref = bf16[512,544]{1,0:T(8,128)(2,1)S(1)} pad(bf16[512,529]{1,0:T(8,128)(2,1)} %copy.13, bf16[]{:T(256)} %constant.13.clone.1), padding=0_0x0_15 | pad | bytes 1098754 | tf_op jit(solution)/shard_map/jit(_pad)/pad | solution.py:384
  34.4 1.0 %collective-permute-done.6.rest_4_ = bf16[2,272,128]{2,1,0:T(8,128)(2,1)S(1)} collective-permute-done((bf16[2,272,128]{2,1,0:T(8,128)(2,1)S(1)}, bf16[2,272,128]{2,1,0:T(8,128)(2,1)S(1)}, u32[]{:S(2)}, u32[]{:S(2)}) %collective-permute-start.6) | collective-permute-done | bytes 139296 | tf_op jit(solution)/shard_map/ppermute | solution.py:348
  35.4 1.6 %collective-permute-done.9.rest_7_ = bf16[2,272,128]{2,1,0:T(8,128)(2,1)S(1)} collective-permute-done((bf16[2,272,128]{2,1,0:T(8,128)(2,1)S(1)}, bf16[2,272,128]{2,1,0:T(8,128)(2,1)S(1)}, u32[]{:S(2)}, u32[]{:S(2)}) %collective-permute-start.9) | collective-permute-done | bytes 139296 | tf_op jit(solution)/shard_map/ppermute | solution.py:348
  37.1 5.4 %grads.1 = (f32[8,32,1024]{2,1,0:T(8,128)S(1)}, bf16[8,32,1024]{2,1,0:T(8,128)(2,1)S(1)}, f32[512,512]{1,0:T(8,128)S(1)}, bf16[64,512]{1,0:T(8,128)(2,1)S(1)}, b...) custom-call(s32[1]{0:T(128)} %bitcast.me_ref, bf16[544,128]{1,0:T(8,128)(2,1)S(1)} %pad.8.own_ref, ...), custom_call_target="tpu_custom_call" | custom-call | tf_op jit(solution)/shard_map/grads/pallas_call | solution.py:386
  42.6 1.2 %outer.1 = (f32[8,32,640]{2,1,0:T(8,128)S(1)}, bf16[8,32,640]{2,1,0:T(8,128)(2,1)S(1)}) custom-call(s32[1]{0:T(128)} %bitcast.me_ref, bf16[512,1152]{1,0:T(8,128)(2,1)S(1)} %copy-done.10, bf16[544,1152]{1,0:T(8,128)(2,1)S(1)} %get-tuple-element.96.g_ref), custom_call_target="tpu_custom_call" | custom-call | flops 12834570240 | bytes 4194304 | tf_op jit(solution)/shard_map/outer/pallas_call | solution.py:408
  44.7 0.9 %collective-permute-done.16.came_ref = bf16[8,32,640]{2,1,0:T(8,128)(2,1)S(1)} collective-permute-done((bf16[8,32,640]{2,1,0:T(8,128)(2,1)S(1)}, bf16[8,32,640]{2,1,0:T(8,128)(2,1)S(1)}, u32[]{:S(2)}, u32[]{:S(2)}) %collective-permute-start.16) | collective-permute-done | bytes 327712 | tf_op jit(solution)/shard_map/ppermute | solution.py:281
  45.7 4.9 %collective-permute-start.17 = (bf16[4,32,640]{2,1,0:T(8,128)(2,1)S(1)}, bf16[4,32,640]{2,1,0:T(8,128)(2,1)S(1)}, u32[]{:S(2)}, u32[]{:S(2)}) collective-permute-start(bf16[4,32,640]{2,1,0:T(8,128)(2,1)S(1)} %get-tuple-element.102), channel_id=1, source_target_pairs={{0,4},{1,5},{2,6},{3,7},{4,0},{5,1},{6,2},{7,3},{8,12},{9,13},{10,... | collective-permute-start | bytes 491528 | tf_op jit(solution)/shard_map/ppermute | solution.py:281
  50.6 1.6 %collective-permute-start.12 = (bf16[64,512]{1,0:T(8,128)(2,1)S(1)}, bf16[64,512]{1,0:T(8,128)(2,1)S(1)}, u32[]{:S(2)}, u32[]{:S(2)}) collective-permute-start(bf16[64,512]{1,0:T(8,128)(2,1)S(1)} %get-tuple-element.85), channel_id=1, source_target_pairs={{1,0},{2,1},{3,2},{4,3},{5,4},{6,5},{7,6},{8,7},{9,8},{10,9},{11,1... | collective-permute-start | bytes 196616 | tf_op jit(solution)/shard_map/ppermute | solution.py:447
  52.2 3.1 %collective-permute-done.12.from_above_ref = bf16[64,512]{1,0:T(8,128)(2,1)S(1)} collective-permute-done((bf16[64,512]{1,0:T(8,128)(2,1)S(1)}, bf16[64,512]{1,0:T(8,128)(2,1)S(1)}, u32[]{:S(2)}, u32[]{:S(2)}) %collective-permute-start.12) | collective-permute-done | bytes 65568 | tf_op jit(solution)/shard_map/ppermute | solution.py:447
  55.3 3.3 %collective-permute-done.13.from_below_ref = bf16[64,512]{1,0:T(8,128)(2,1)S(1)} collective-permute-done((bf16[64,512]{1,0:T(8,128)(2,1)S(1)}, bf16[64,512]{1,0:T(8,128)(2,1)S(1)}, u32[]{:S(2)}, u32[]{:S(2)}) %collective-permute-start.13) | collective-permute-done | bytes 65568 | tf_op jit(solution)/shard_map/ppermute | solution.py:448
  58.8 1.0 %collective-permute-start.18 = (bf16[2,32,640]{2,1,0:T(8,128)(2,1)S(1)}, bf16[2,32,640]{2,1,0:T(8,128)(2,1)S(1)}, u32[]{:S(2)}, u32[]{:S(2)}) collective-permute-start(bf16[2,32,640]{2,1,0:T(8,128)(2,1)S(1)} %get-tuple-element.106), channel_id=1, source_target_pairs={{0,2},{1,3},{2,0},{3,1},{4,6},{5,7},{6,4},{7,5},{8,10},{9,11},{10,... | collective-permute-start | bytes 245768 | tf_op jit(solution)/shard_map/ppermute | solution.py:281
  59.8 3.9 %collective-permute-done.14.came_ref = bf16[2,32,1024]{2,1,0:T(8,128)(2,1)S(1)} collective-permute-done((bf16[2,32,1024]{2,1,0:T(8,128)(2,1)S(1)}, bf16[2,32,1024]{2,1,0:T(8,128)(2,1)S(1)}, u32[]{:S(2)}, u32[]{:S(2)}) %collective-permute-start.14) | collective-permute-done | bytes 131104 | tf_op jit(solution)/shard_map/ppermute | solution.py:281
  63.8 1.4 %collective-permute-start.15 = (bf16[1,32,1024]{2,1,0:T(8,128)(2,1)S(1)}, bf16[1,32,1024]{2,1,0:T(8,128)(2,1)S(1)}, u32[]{:S(2)}, u32[]{:S(2)}) collective-permute-start(bf16[1,32,1024]{2,1,0:T(8,128)(2,1)S(1)} %get-tuple-element.94), channel_id=1, source_target_pairs={{0,8},{1,9},{2,10},{3,11},{4,12},{5,13},{6,14},{7,15},{8,0},{9,1},... | collective-permute-start | bytes 196616 | tf_op jit(solution)/shard_map/ppermute | solution.py:281
  65.2 1.6 %collective-permute-start.19 = (bf16[1,32,640]{2,1,0:T(8,128)(2,1)S(1)}, bf16[1,32,640]{2,1,0:T(8,128)(2,1)S(1)}, u32[]{:S(2)}, u32[]{:S(2)}) collective-permute-start(bf16[1,32,640]{2,1,0:T(8,128)(2,1)S(1)} %get-tuple-element.110), channel_id=1, source_target_pairs={{0,8},{1,9},{2,10},{3,11},{4,12},{5,13},{6,14},{7,15},{8,0},{9,1},... | collective-permute-start | bytes 122888 | tf_op jit(solution)/shard_map/ppermute | solution.py:281
  66.9 1.5 %rims.1 = f32[256,512]{1,0:T(8,128)} custom-call(f32[512,512]{1,0:T(8,128)S(1)} %get-tuple-element.80.sums_ref, bf16[64,512]{1,0:T(8,128)(2,1)S(1)} %collective-permute-done.13.from_below_ref, bf16[64,512]{1,0:T(8,128)(2,1)S(1)} %collective-permute-done.12.from_above_ref, bf16[512,512]{1,0:T(8,128)(2,1)S(1)} %copy-done.4, bf16[512,512]{1,0:T(8,128)(2,1)S(1)} %copy-done.5), custom_call_target="tpu_custom_call" | custom-call | flops 24159191040 | bytes 4194304 | tf_op jit(solution)/shard_map/rims/pallas_call | solution.py:461
  68.4 2.9 %collective-permute-done.19.refs_3_ = bf16[1,32,640]{2,1,0:T(8,128)(2,1)S(1)} collective-permute-done((bf16[1,32,640]{2,1,0:T(8,128)(2,1)S(1)}, bf16[1,32,640]{2,1,0:T(8,128)(2,1)S(1)}, u32[]{:S(2)}, u32[]{:S(2)}) %collective-permute-start.19) | collective-permute-done | bytes 40992 | tf_op jit(solution)/shard_map/ppermute | solution.py:281
  71.3 0.7 totals.1
  (48 shorter events, 2.4 us)
Async XLA Ops:
  0.6 20.3 %copy-start.3 = (bf16[256,512]{1,0:T(8,128)(2,1)S(1)}, bf16[256,512]{1,0:T(8,128)(2,1)}, u32[]{:S(2)}) copy-start(bf16[256,512]{1,0:T(8,128)(2,1)} %feats_ref.3) | copy-start | bytes 786436
  0.6 20.3 %copy-start.5 = (bf16[512,512]{1,0:T(8,128)(2,1)S(1)}, bf16[512,512]{1,0:T(8,128)(2,1)}, u32[]{:S(2)}) copy-start(bf16[512,512]{1,0:T(8,128)(2,1)} %w_dst_ref.3) | copy-start | bytes 1572868
  0.7 20.3 %copy-start.4 = (bf16[512,512]{1,0:T(8,128)(2,1)S(1)}, bf16[512,512]{1,0:T(8,128)(2,1)}, u32[]{:S(2)}) copy-start(bf16[512,512]{1,0:T(8,128)(2,1)} %w_src_ref.3) | copy-start | bytes 1572868
  0.7 20.3 %copy-start.8 = (s32[2048]{0:T(1024)S(1)}, s32[2048]{0:T(1024)}, u32[]{:S(2)}) copy-start(s32[2048]{0:T(1024)} %param.15) | copy-start | bytes 24580
  0.7 20.3 %copy-start.7 = (s32[2048]{0:T(1024)S(1)}, s32[2048]{0:T(1024)}, u32[]{:S(2)}) copy-start(s32[2048]{0:T(1024)} %param.14) | copy-start | bytes 24580
  0.7 20.3 %copy-start.6 = (s32[2048]{0:T(1024)S(1)}, s32[2048]{0:T(1024)}, u32[]{:S(2)}) copy-start(s32[2048]{0:T(1024)} %param.13) | copy-start | bytes 24580
  3.3 8.1 %collective-permute-start = (bf16[8,272,128]{2,1,0:T(8,128)(2,1)S(1)}, bf16[8,272,128]{2,1,0:T(8,128)(2,1)S(1)}, u32[]{:S(2)}, u32[]{:S(2)}) collective-permute-start(bf16[8,272,128]{2,1,0:T(8,128)(2,1)S(1)} %get-tuple-element.59), channel_id=1, source_target_pairs={{0,1},{1,0},{2,3},{3,2},{4,5},{5,4},{6,7},{7,6},{8,9},{9,8},{10,11... | collective-permute-start | bytes 1671176 | tf_op jit(solution)/shard_map/ppermute | solution.py:281
  3.8 7.6 %collective-permute-start.1 = (bf16[64,512]{1,0:T(8,128)(2,1)S(1)}, bf16[64,512]{1,0:T(8,128)(2,1)S(1)}, u32[]{:S(2)}, u32[]{:S(2)}) collective-permute-start(bf16[64,512]{1,0:T(8,128)(2,1)S(1)} %get-tuple-element.60), channel_id=1, source_target_pairs={{0,1},{1,2},{2,3},{3,4},{4,5},{5,6},{6,7},{7,8},{8,9},{9,10},{10,1... | collective-permute-start | bytes 196616 | tf_op jit(solution)/shard_map/ppermute | solution.py:330
  3.9 7.6 %collective-permute-start.2 = (bf16[64,512]{1,0:T(8,128)(2,1)S(1)}, bf16[64,512]{1,0:T(8,128)(2,1)S(1)}, u32[]{:S(2)}, u32[]{:S(2)}) collective-permute-start(bf16[64,512]{1,0:T(8,128)(2,1)S(1)} %get-tuple-element.61), channel_id=1, source_target_pairs={{1,0},{2,1},{3,2},{4,3},{5,4},{6,5},{7,6},{8,7},{9,8},{10,9},{11,1... | collective-permute-start | bytes 196616 | tf_op jit(solution)/shard_map/ppermute | solution.py:331
  11.5 6.5 %collective-permute-start.3 = (bf16[2,272,128]{2,1,0:T(8,128)(2,1)S(1)}, bf16[2,272,128]{2,1,0:T(8,128)(2,1)S(1)}, u32[]{:S(2)}, u32[]{:S(2)}) collective-permute-start(bf16[2,272,128]{2,1,0:T(8,128)(2,1)S(1)} %get-tuple-element.73), channel_id=1, source_target_pairs={{0,2},{1,3},{2,0},{3,1},{4,6},{5,7},{6,4},{7,5},{8,10},{9,11},{10,... | collective-permute-start | bytes 417800 | tf_op jit(solution)/shard_map/ppermute | solution.py:348
  11.6 9.3 %collective-permute-start.4 = (bf16[2,272,128]{2,1,0:T(8,128)(2,1)S(1)}, bf16[2,272,128]{2,1,0:T(8,128)(2,1)S(1)}, u32[]{:S(2)}, u32[]{:S(2)}) collective-permute-start(bf16[2,272,128]{2,1,0:T(8,128)(2,1)S(1)} %get-tuple-element.74), channel_id=1, source_target_pairs={{0,4},{1,5},{2,6},{3,7},{4,0},{5,1},{6,2},{7,3},{8,12},{9,13},{10,... | collective-permute-start | bytes 417800 | tf_op jit(solution)/shard_map/ppermute | solution.py:348
  11.8 22.6 %collective-permute-start.5 = (bf16[2,272,128]{2,1,0:T(8,128)(2,1)S(1)}, bf16[2,272,128]{2,1,0:T(8,128)(2,1)S(1)}, u32[]{:S(2)}, u32[]{:S(2)}) collective-permute-start(bf16[2,272,128]{2,1,0:T(8,128)(2,1)S(1)} %get-tuple-element.75), channel_id=1, source_target_pairs={{0,8},{1,9},{2,10},{3,11},{4,12},{5,13},{6,14},{7,15},{8,0},{9,1},... | collective-permute-start | bytes 417800 | tf_op jit(solution)/shard_map/ppermute | solution.py:348
  14.4 21.0 %collective-permute-start.6 = (bf16[2,272,128]{2,1,0:T(8,128)(2,1)S(1)}, bf16[2,272,128]{2,1,0:T(8,128)(2,1)S(1)}, u32[]{:S(2)}, u32[]{:S(2)}) collective-permute-start(bf16[2,272,128]{2,1,0:T(8,128)(2,1)S(1)} %get-tuple-element.76), channel_id=1, source_target_pairs={{0,10},{1,11},{2,8},{3,9},{4,14},{5,15},{6,12},{7,13},{8,2},{9,3},... | collective-permute-start | bytes 417800 | tf_op jit(solution)/shard_map/ppermute | solution.py:348
  16.0 19.5 %collective-permute-start.7 = (bf16[2,272,128]{2,1,0:T(8,128)(2,1)S(1)}, bf16[2,272,128]{2,1,0:T(8,128)(2,1)S(1)}, u32[]{:S(2)}, u32[]{:S(2)}) collective-permute-start(bf16[2,272,128]{2,1,0:T(8,128)(2,1)S(1)} %get-tuple-element.77), channel_id=1, source_target_pairs={{0,12},{1,13},{2,14},{3,15},{4,8},{5,9},{6,10},{7,11},{8,4},{9,5},... | collective-permute-start | bytes 417800 | tf_op jit(solution)/shard_map/ppermute | solution.py:348
  18.0 17.4 %collective-permute-start.8 = (bf16[2,272,128]{2,1,0:T(8,128)(2,1)S(1)}, bf16[2,272,128]{2,1,0:T(8,128)(2,1)S(1)}, u32[]{:S(2)}, u32[]{:S(2)}) collective-permute-start(bf16[2,272,128]{2,1,0:T(8,128)(2,1)S(1)} %get-tuple-element.78), channel_id=1, source_target_pairs={{0,14},{1,15},{2,12},{3,13},{4,10},{5,11},{6,8},{7,9},{8,6},{9,7},... | collective-permute-start | bytes 417800 | tf_op jit(solution)/shard_map/ppermute | solution.py:348
  20.9 16.2 %collective-permute-start.9 = (bf16[2,272,128]{2,1,0:T(8,128)(2,1)S(1)}, bf16[2,272,128]{2,1,0:T(8,128)(2,1)S(1)}, u32[]{:S(2)}, u32[]{:S(2)}) collective-permute-start(bf16[2,272,128]{2,1,0:T(8,128)(2,1)S(1)} %get-tuple-element.79), channel_id=1, source_target_pairs={{0,6},{1,7},{2,4},{3,5},{4,2},{5,3},{6,0},{7,1},{8,14},{9,15},{10,... | collective-permute-start | bytes 417800 | tf_op jit(solution)/shard_map/ppermute | solution.py:348
  25.0 1.4 %copy-start = (f32[512,1152]{1,0:T(8,128)}, f32[512,1152]{1,0:T(8,128)S(1)}, u32[]{:S(2)}) copy-start(f32[512,1152]{1,0:T(8,128)S(1)} %get-tuple-element.67.slope_hbm) | copy-start | bytes 7077892
  26.4 1.1 %copy-start.1 = (bf16[640,1152]{1,0:T(8,128)(2,1)}, bf16[640,1152]{1,0:T(8,128)(2,1)S(1)}, u32[]{:S(2)}) copy-start(bf16[640,1152]{1,0:T(8,128)(2,1)S(1)} %get-tuple-element.68.onehot_hbm) | copy-start | bytes 4423684
  27.5 0.7 %copy-start.2 = (bf16[512,384]{1,0:T(8,128)(2,1)}, bf16[512,384]{1,0:T(8,128)(2,1)S(1)}, u32[]{:S(2)}) copy-start(bf16[512,384]{1,0:T(8,128)(2,1)S(1)} %get-tuple-element.69.ext_hbm) | copy-start | bytes 1179652
  28.3 1.1 %copy-start.9 = (bf16[512,1152]{1,0:T(8,128)(2,1)}, bf16[512,1152]{1,0:T(8,128)(2,1)S(1)}, u32[]{:S(2)}) copy-start(bf16[512,1152]{1,0:T(8,128)(2,1)S(1)} %get-tuple-element.95.hidden_ref) | copy-start | bytes 3538948
  37.1 5.5 %copy-start.10 = (bf16[512,1152]{1,0:T(8,128)(2,1)S(1)}, bf16[512,1152]{1,0:T(8,128)(2,1)}, u32[]{:S(2)}) copy-start(bf16[512,1152]{1,0:T(8,128)(2,1)} %copy-done.9) | copy-start | bytes 3538948
  42.5 2.0 %collective-permute-start.10 = (bf16[8,32,1024]{2,1,0:T(8,128)(2,1)S(1)}, bf16[8,32,1024]{2,1,0:T(8,128)(2,1)S(1)}, u32[]{:S(2)}, u32[]{:S(2)}) collective-permute-start(bf16[8,32,1024]{2,1,0:T(8,128)(2,1)S(1)} %get-tuple-element.82), channel_id=1, source_target_pairs={{0,1},{1,0},{2,3},{3,2},{4,5},{5,4},{6,7},{7,6},{8,9},{9,8},{10,11... | collective-permute-start | bytes 1572872 | tf_op jit(solution)/shard_map/ppermute | solution.py:281
  43.8 1.8 %collective-permute-start.16 = (bf16[8,32,640]{2,1,0:T(8,128)(2,1)S(1)}, bf16[8,32,640]{2,1,0:T(8,128)(2,1)S(1)}, u32[]{:S(2)}, u32[]{:S(2)}) collective-permute-start(bf16[8,32,640]{2,1,0:T(8,128)(2,1)S(1)} %get-tuple-element.98), channel_id=1, source_target_pairs={{0,1},{1,0},{2,3},{3,2},{4,5},{5,4},{6,7},{7,6},{8,9},{9,8},{10,11... | collective-permute-start | bytes 983048 | tf_op jit(solution)/shard_map/ppermute | solution.py:281
  44.6 14.0 %collective-permute-start.11 = (bf16[4,32,1024]{2,1,0:T(8,128)(2,1)S(1)}, bf16[4,32,1024]{2,1,0:T(8,128)(2,1)S(1)}, u32[]{:S(2)}, u32[]{:S(2)}) collective-permute-start(bf16[4,32,1024]{2,1,0:T(8,128)(2,1)S(1)} %get-tuple-element.84), channel_id=1, source_target_pairs={{0,2},{1,3},{2,0},{3,1},{4,6},{5,7},{6,4},{7,5},{8,10},{9,11},{10,... | collective-permute-start | bytes 786440 | tf_op jit(solution)/shard_map/ppermute | solution.py:281
  45.7 13.0 %collective-permute-start.17 = (bf16[4,32,640]{2,1,0:T(8,128)(2,1)S(1)}, bf16[4,32,640]{2,1,0:T(8,128)(2,1)S(1)}, u32[]{:S(2)}, u32[]{:S(2)}) collective-permute-start(bf16[4,32,640]{2,1,0:T(8,128)(2,1)S(1)} %get-tuple-element.102), channel_id=1, source_target_pairs={{0,4},{1,5},{2,6},{3,7},{4,0},{5,1},{6,2},{7,3},{8,12},{9,13},{10,... | collective-permute-start | bytes 491528 | tf_op jit(solution)/shard_map/ppermute | solution.py:281
  50.6 4.7 %collective-permute-start.12 = (bf16[64,512]{1,0:T(8,128)(2,1)S(1)}, bf16[64,512]{1,0:T(8,128)(2,1)S(1)}, u32[]{:S(2)}, u32[]{:S(2)}) collective-permute-start(bf16[64,512]{1,0:T(8,128)(2,1)S(1)} %get-tuple-element.85), channel_id=1, source_target_pairs={{1,0},{2,1},{3,2},{4,3},{5,4},{6,5},{7,6},{8,7},{9,8},{10,9},{11,1... | collective-permute-start | bytes 196616 | tf_op jit(solution)/shard_map/ppermute | solution.py:447
  52.2 6.4 %collective-permute-start.13 = (bf16[64,512]{1,0:T(8,128)(2,1)S(1)}, bf16[64,512]{1,0:T(8,128)(2,1)S(1)}, u32[]{:S(2)}, u32[]{:S(2)}) collective-permute-start(bf16[64,512]{1,0:T(8,128)(2,1)S(1)} %get-tuple-element.86), channel_id=1, source_target_pairs={{0,1},{1,2},{2,3},{3,4},{4,5},{5,6},{6,7},{7,8},{8,9},{9,10},{10,1... | collective-permute-start | bytes 196616 | tf_op jit(solution)/shard_map/ppermute | solution.py:448
  58.7 5.0 %collective-permute-start.14 = (bf16[2,32,1024]{2,1,0:T(8,128)(2,1)S(1)}, bf16[2,32,1024]{2,1,0:T(8,128)(2,1)S(1)}, u32[]{:S(2)}, u32[]{:S(2)}) collective-permute-start(bf16[2,32,1024]{2,1,0:T(8,128)(2,1)S(1)} %get-tuple-element.92), channel_id=1, source_target_pairs={{0,4},{1,5},{2,6},{3,7},{4,0},{5,1},{6,2},{7,3},{8,12},{9,13},{10,... | collective-permute-start | bytes 393224 | tf_op jit(solution)/shard_map/ppermute | solution.py:281
  58.8 6.4 %collective-permute-start.18 = (bf16[2,32,640]{2,1,0:T(8,128)(2,1)S(1)}, bf16[2,32,640]{2,1,0:T(8,128)(2,1)S(1)}, u32[]{:S(2)}, u32[]{:S(2)}) collective-permute-start(bf16[2,32,640]{2,1,0:T(8,128)(2,1)S(1)} %get-tuple-element.106), channel_id=1, source_target_pairs={{0,2},{1,3},{2,0},{3,1},{4,6},{5,7},{6,4},{7,5},{8,10},{9,11},{10,... | collective-permute-start | bytes 245768 | tf_op jit(solution)/shard_map/ppermute | solution.py:281
  63.8 7.6 %collective-permute-start.15 = (bf16[1,32,1024]{2,1,0:T(8,128)(2,1)S(1)}, bf16[1,32,1024]{2,1,0:T(8,128)(2,1)S(1)}, u32[]{:S(2)}, u32[]{:S(2)}) collective-permute-start(bf16[1,32,1024]{2,1,0:T(8,128)(2,1)S(1)} %get-tuple-element.94), channel_id=1, source_target_pairs={{0,8},{1,9},{2,10},{3,11},{4,12},{5,13},{6,14},{7,15},{8,0},{9,1},... | collective-permute-start | bytes 196616 | tf_op jit(solution)/shard_map/ppermute | solution.py:281
  65.2 6.1 %collective-permute-start.19 = (bf16[1,32,640]{2,1,0:T(8,128)(2,1)S(1)}, bf16[1,32,640]{2,1,0:T(8,128)(2,1)S(1)}, u32[]{:S(2)}, u32[]{:S(2)}) collective-permute-start(bf16[1,32,640]{2,1,0:T(8,128)(2,1)S(1)} %get-tuple-element.110), channel_id=1, source_target_pairs={{0,8},{1,9},{2,10},{3,11},{4,12},{5,13},{6,14},{7,15},{8,0},{9,1},... | collective-permute-start | bytes 122888 | tf_op jit(solution)/shard_map/ppermute | solution.py:281

commit v7 on v6

--- a/solution.py
+++ b/solution.py
@@ -103,35 +103,38 @@
         message_ref[1] = other_ref[k]
 
 
-def unpack(half, chunks, own_ref, g_ref):
+def unpack(half, refs, g_ref):
     groups = LANES // half
     rows = g_ref.shape[0] // groups
+    chunks = [(ref, index) for ref in refs for index in range(ref.shape[0])]
     tiles = len(chunks) // groups
     for tile in range(tiles):
-        here = [chunk() for chunk in chunks[tile * groups : (tile + 1) * groups]]
+        here = [ref[index] for ref, index in chunks[tile * groups : (tile + 1) * groups]]
         for group in range(groups):
             lanes = slice(group * half, (group + 1) * half)
             g_ref[group * rows : (group + 1) * rows, tile * LANES : (tile + 1) * LANES] = jnp.concatenate(
                 [chunk[:, lanes] for chunk in here], axis=1
             )
-    g_ref[:, tiles * LANES :] = own_ref[...]
-
-
-def slot_rows(ref, me, half, order):
-    slabs, cap = ref.shape
+    return tiles * LANES
+
+
+def slot_rows(ref, me, half, linked, near, far):
     per = LANES // half
-    rows = []
-    for tile in range(slabs // per):
-        ids = range(tile * per, tile * per + per)
-        pieces = [ref[pl.ds(me ^ order[i] if order else i, 1), :] for i in ids]
-        rows.append(jnp.concatenate([piece[:, :half] for piece in pieces], axis=1))
+
+    def rows_of(ids):
+        rows = []
+        for tile in range(len(ids) // per):
+            pieces = [ref[pl.ds(me ^ i if linked else i, 1), :] for i in ids[tile * per : (tile + 1) * per]]
+            rows.append(jnp.concatenate([piece[:, :half] for piece in pieces], axis=1))
+        return rows
+
     own = ref[pl.ds(me, 1), :][:, half:]
-    rows.append(jnp.concatenate([own, jnp.full((1, LANES - half), -1, jnp.int32)], axis=1))
-    return rows
+    own = jnp.concatenate([own, jnp.full((1, LANES - half), -1, jnp.int32)], axis=1)
+    return rows_of(near) + [own] + rows_of(far)
 
 
 def edge_kernel(
-    half, order, me_ref, feats_ref, below_ref, above_ref, w_src_ref, w_dst_ref, src_ref, dst_ref, live_ref,
+    half, linked, near, far, me_ref, feats_ref, below_ref, above_ref, w_src_ref, w_dst_ref, src_ref, dst_ref, live_ref,
     onehot_ref, hidden_ref, slope_ref, ext_ref,
 ):
     me = me_ref[0]
@@ -147,7 +150,7 @@
     high, low = halves(proj)
     mol_src = lax.broadcasted_iota(jnp.int32, (mols, LANES), 0)
     mol_dst = lax.broadcasted_iota(jnp.int32, (wide, LANES), 0)
-    lists = [slot_rows(ref, me, half, order) for ref in (src_ref, dst_ref, live_ref)]
+    lists = [slot_rows(ref, me, half, linked, near, far) for ref in (src_ref, dst_ref, live_ref)]
     for tile, (src, dst, live) in enumerate(zip(*lists)):
         src = jnp.where(live > 0, src, -1)
         moved = jnp.where(dst < reach, dst + mols, jnp.where(dst < reach + mols, dst - reach, dst))
@@ -184,55 +187,89 @@
     send_ref[...] = (keep_ref[...] + came_ref[...].astype(F32)).astype(BF16)
 
 
-def grad_kernel(
-    half, factor, me_ref, own_ref, w_out_ref, slope_hbm, onehot_hbm, ext_hbm, *rest,
-):
+def slot_tiles(slots):
+    step = 2 * LANES
+    return [(first, min(first + step, slots)) for first in range(0, slots, step)]
+
+
+def start_tiles(slots, offset, slope_hbm, onehot_hbm, slope_ref, onehot_ref, sems):
+    tiles = []
+    for tile, (first, last) in enumerate(slot_tiles(slots)):
+        there, here = pl.ds(offset + first, last - first), pl.ds(first, last - first)
+        copies = [
+            pltpu.make_async_copy(slope_hbm.at[:, there], slope_ref.at[:, here], sems.at[tile, 0]),
+            pltpu.make_async_copy(onehot_hbm.at[:, there], onehot_ref.at[:, here], sems.at[tile, 1]),
+        ]
+        for copy in copies:
+            copy.start()
+        tiles.append((slice(first, last), copies))
+    return tiles
+
+
+def sum_edges(tiles, w_out_ref, g_ref, slope_ref, onehot_ref):
+    sums = None
+    for lanes, copies in tiles:
+        dh = mm(w_out_ref[...], g_ref[:, lanes])
+        for copy in copies:
+            copy.wait()
+        dpre = (dh * slope_ref[:, lanes]).astype(BF16)
+        term = mm(onehot_ref[:, lanes], dpre, NT)
+        sums = term if sums is None else sums + term
+    return sums
+
+
+def near_kernel(half, own_ref, w_out_ref, hidden_ref, slope_hbm, onehot_hbm, *rest):
+    *came_refs, sums_ref, outer_ref, g_ref, slope_ref, onehot_ref, sems = rest
+    slots = g_ref.shape[1]
+    tiles = start_tiles(slots, 0, slope_hbm, onehot_hbm, slope_ref, onehot_ref, sems)
+    filled = unpack(half, came_refs, g_ref)
+    g_ref[:, filled:] = own_ref[...]
+    sums_ref[...] = sum_edges(tiles, w_out_ref, g_ref, slope_ref, onehot_ref)
+    outer_ref[...] = mm(hidden_ref[:, :slots], g_ref[...], NT)
+
+
+def grad_kernel(half, factor, me_ref, w_out_ref, slope_hbm, onehot_hbm, ext_hbm, near_hbm, *rest):
     (
-        *came_refs, keep_ref, send_ref, sums_ref, lower_ref, upper_ref, g_ref, slope_ref, onehot_ref, ext_ref, sems,
+        *came_refs, keep_ref, send_ref, sums_ref, lower_ref, upper_ref, g_ref,
+        slope_ref, onehot_ref, ext_ref, near_ref, tile_sems, sems,
     ) = rest
     odd = me_ref[0] % 2
     width = w_out_ref.shape[0]
     slots = g_ref.shape[1]
     inside = sums_ref.shape[0]
     mols = inside // 2
-    step = slots // 3
-    tiles = []
-    for tile in range(3):
-        lanes = pl.ds(tile * step, step)
-        copies = [
-            pltpu.make_async_copy(slope_hbm.at[:, lanes], slope_ref.at[:, lanes], sems.at[tile, 0]),
-            pltpu.make_async_copy(onehot_hbm.at[:, lanes], onehot_ref.at[:, lanes], sems.at[tile, 1]),
-        ]
-        for copy in copies:
-            copy.start()
-        tiles.append(copies)
-    ext_copy = pltpu.make_async_copy(ext_hbm, ext_ref, sems.at[3, 0])
-    ext_copy.start()
-    chunks = [functools.partial(lambda ref, i: ref[i], ref, i) for ref in came_refs for i in range(ref.shape[0])]
-    unpack(half, chunks, own_ref, g_ref)
-    sums = None
-    for tile, copies in enumerate(tiles):
-        lanes = slice(tile * step, (tile + 1) * step)
-        dh = mm(w_out_ref[...], g_ref[:, lanes])
-        for copy in copies:
-            copy.wait()
-        dpre = (dh * slope_ref[:, lanes]).astype(BF16)
-        term = mm(onehot_ref[:, lanes], dpre, NT)
-        sums = term if sums is None else sums + term
     reach = lower_ref.shape[0]
+    tiles = start_tiles(slots, slope_hbm.shape[1] - slots, slope_hbm, onehot_hbm, slope_ref, onehot_ref, tile_sems)
+    whole = [
+        pltpu.make_async_copy(near_hbm, near_ref, sems.at[0]),
+        pltpu.make_async_copy(ext_hbm, ext_ref, sems.at[1]),
+    ]
+    for copy in whole:
+        copy.start()
+    unpack(half, came_refs, g_ref)
+    sums = sum_edges(tiles, w_out_ref, g_ref, slope_ref, onehot_ref)
+    for copy in whole:
+        copy.wait()
+    sums = sums + near_ref[...]
     lower_ref[...] = sums[inside : inside + reach].astype(BF16)
     upper_ref[...] = sums[inside + reach :].astype(BF16)
     sums_ref[...] = sums[:inside]
     high, low = halves(sums)
-    ext_copy.wait()
     feats = ext_ref[:, :mols]
-    ext = ext_ref[...]
+    rim = ext_ref[:, mols:]
     halve(factor * (mm(feats, high[:mols]) + mm(feats, low[:mols])), odd, 0, keep_ref, send_ref, 0)
-    halve(factor * (mm(ext, high[mols:]) + mm(ext, low[mols:])), odd, 0, keep_ref, send_ref, width)
-
-
-def outer_kernel(factor, me_ref, hidden_ref, g_ref, keep_ref, send_ref):
-    term = factor * mm(hidden_ref[...], g_ref[...], NT)
+    rim_term = mm(jnp.concatenate([rim, rim], axis=1), jnp.concatenate([high[inside:], low[inside:]], axis=0))
+    dst_term = mm(feats, high[mols:inside]) + mm(feats, low[mols:inside]) + rim_term
+    halve(factor * dst_term, odd, 0, keep_ref, send_ref, width)
+
+
+def outer_kernel(factor, me_ref, hidden_ref, g_ref, near_hbm, keep_ref, send_ref, near_ref, sem):
+    copy = pltpu.make_async_copy(near_hbm, near_ref, sem)
+    copy.start()
+    slots = g_ref.shape[1]
+    term = mm(hidden_ref[:, hidden_ref.shape[1] - slots :], g_ref[...], NT)
+    copy.wait()
+    term = factor * (term + near_ref[...])
     padding = keep_ref.shape[2] - term.shape[1]
     if padding > 0:
         term = jnp.concatenate([term, jnp.zeros((term.shape[0], padding), F32)], axis=1)
@@ -329,7 +366,6 @@
     )(me, in_hbm(mol_feats), in_hbm(jnp.transpose(grad_blocks[0], (2, 0, 1))))
     below = lax.ppermute(top, "space", up)
     above = lax.ppermute(low, "space", down)
-    order = ()
     if linked:
         other = swap(odd, 0, slabs)
         other, below, above = lax.optimization_barrier((other, below, above))
@@ -341,19 +377,26 @@
             compiler_params=big,
             name="join",
         )(even, other)
-        far = slabs // 4
-        turns = [0, *range(1, far - 1), *range(far, slabs // 2), *range(max(far - 1, 1), far)]
-        order = tuple(2 * k + j for k in turns for j in range(2))
-        came = [
-            lax.ppermute(messages[k], "space", [(i, i ^ (2 * k)) for i in range(slabs)]) if k else messages[0]
-            for k in turns
-        ]
+        quarter = slabs // 4
+        came = {0: messages[0]}
+        for k in (*range(1, quarter - 1), *range(quarter, 2 * quarter), *range(max(quarter - 1, 1), quarter)):
+            came[k] = lax.ppermute(messages[k], "space", [(i, i ^ (2 * k)) for i in range(slabs)])
+        for k in range(1, quarter - 1):
+            came[k], below, above, me = lax.optimization_barrier((came[k], below, above, me))
+        near = tuple(range(2 * quarter))
+        far = tuple(range(2 * quarter, slabs))
+        came_near = [came[k] for k in range(quarter)]
+        came_far = [came[k] for k in range(quarter, 2 * quarter)]
     else:
         packed = jnp.stack([even, odd], axis=1).reshape(slabs, rows, LANES)
-        came = [lax.all_to_all(packed, "space", split_axis=0, concat_axis=0, tiled=True)]
+        near, far = (), tuple(range(slabs))
+        came_near = []
+        came_far = [lax.all_to_all(packed, "space", split_axis=0, concat_axis=0, tiled=True)]
+    far_slots = len(far) * half
+    near_slots = slots - far_slots
 
     onehot, hidden, slope, ext = pl.pallas_call(
-        functools.partial(edge_kernel, half, order),
+        functools.partial(edge_kernel, half, linked, near, far),
         out_shape=(
             jax.ShapeDtypeStruct((2 * mols + 2 * reach, slots), BF16),
             jax.ShapeDtypeStruct((width, slots), BF16),
@@ -373,8 +416,8 @@
         edge_src.reshape(slabs, cap), edge_dst.reshape(slabs, cap), edge_live.reshape(slabs, cap),
     )
 
-    here, w_out, slope = lax.optimization_barrier((me, w_out, slope))
-    late = lax.dynamic_index_in_dim(grad_blocks[0], here[0], 0, keepdims=False)[half:]
+    w_out = lax.optimization_barrier((w_out, me))[0]
+    late = lax.dynamic_index_in_dim(grad_blocks[0], me[0], 0, keepdims=False)[half:]
     own = jnp.pad(late.T, ((0, groups * rows - entries), (0, LANES - half)))
 
     def chunks(count, lanes, dtype):
@@ -383,6 +426,26 @@
     entries_wide = groups * rows
     w_out_wide = jnp.pad(w_out, ((0, 0), (0, entries_wide - entries)))
     wide = mols + 2 * reach
+    near_sums, near_outer = pl.pallas_call(
+        functools.partial(near_kernel, half),
+        out_shape=(
+            jax.ShapeDtypeStruct((mols + wide, width), F32),
+            jax.ShapeDtypeStruct((width, entries_wide), F32),
+        ),
+        in_specs=vmem(3) + [hbm] * 2 + vmem(len(came_near)),
+        out_specs=tuple(vmem(2)),
+        scratch_shapes=[
+            pltpu.VMEM((entries_wide, near_slots), BF16),
+            pltpu.VMEM((width, near_slots), F32),
+            pltpu.VMEM((mols + wide, near_slots), BF16),
+            pltpu.SemaphoreType.DMA((len(slot_tiles(near_slots)), 2)),
+        ],
+        compiler_params=big,
+        name="near",
+        cost_estimate=pl.CostEstimate(
+            flops=40 * width * near_slots * entries_wide, bytes_accessed=6 * 1024 * 1024, transcendentals=0
+        ),
+    )(own, w_out_wide, hidden, in_hbm(slope), in_hbm(onehot), *came_near)
     keep, send, sums, lower, upper, g = pl.pallas_call(
         functools.partial(grad_kernel, half, factor),
         out_shape=(
@@ -391,31 +454,34 @@
             jax.ShapeDtypeStruct((2 * mols, width), F32),
             jax.ShapeDtypeStruct((reach, width), BF16),
             jax.ShapeDtypeStruct((reach, width), BF16),
-            jax.ShapeDtypeStruct((entries_wide, slots), BF16),
-        ),
-        in_specs=[smem] + vmem(2) + [hbm] * 3 + vmem(len(came)),
+            jax.ShapeDtypeStruct((entries_wide, far_slots), BF16),
+        ),
+        in_specs=[smem] + vmem(1) + [hbm] * 4 + vmem(len(came_far)),
         out_specs=tuple(vmem(6)),
         scratch_shapes=[
-            pltpu.VMEM((width, slots), F32),
-            pltpu.VMEM((mols + wide, slots), BF16),
+            pltpu.VMEM((width, far_slots), F32),
+            pltpu.VMEM((mols + wide, far_slots), BF16),
             pltpu.VMEM((width, wide), BF16),
-            pltpu.SemaphoreType.DMA((4, 2)),
+            pltpu.VMEM((mols + wide, width), F32),
+            pltpu.SemaphoreType.DMA((len(slot_tiles(far_slots)), 2)),
+            pltpu.SemaphoreType.DMA((2,)),
         ],
         compiler_params=big,
         name="grads",
-    )(me, own, w_out_wide, in_hbm(slope), in_hbm(onehot), in_hbm(ext), *came)
+    )(me, w_out_wide, in_hbm(slope), in_hbm(onehot), in_hbm(ext), in_hbm(near_sums), *came_far)
     lanes = round_up(entries_wide, LANES)
     keep_o, send_o = pl.pallas_call(
         functools.partial(outer_kernel, factor),
         out_shape=(chunks(slabs // 2, lanes, F32), chunks(slabs // 2, lanes, BF16)),
-        in_specs=[smem] + vmem(2),
+        in_specs=[smem] + vmem(2) + [hbm],
         out_specs=tuple(vmem(2)),
+        scratch_shapes=[pltpu.VMEM((width, entries_wide), F32), pltpu.SemaphoreType.DMA(())],
         compiler_params=big,
         name="outer",
         cost_estimate=pl.CostEstimate(
             flops=40 * width * slots * entries_wide, bytes_accessed=4 * 1024 * 1024, transcendentals=0
         ),
-    )(me, hidden, g)
+    )(me, hidden, g, in_hbm(near_outer))
 
     def fold(bit, place, keep, crossed):
         shape = (keep.shape[0] // 2, keep.shape[2])

time: 72.3 us -> 74.5 us (1.030)
  Pallas kernels: 15.9 us -> 18.9 us
  local copies, waits for them, and re-layouts: 9.42 us -> 11.8 us
  waiting for transfers between devices: 20.3 us -> 18.4 us
  starting transfers between devices: 25.5 us -> 24.1 us
    pallas_call x1 -> x2, Pallas kernels: 4.01 us -> 7.9 us  [the longest x1 4.01 us: on_device(): pl.pallas_call(functools.partial(edge_kernel, half, linked, near, far), o...]
    ppermute x9, starting transfers between devices: 10.2 us -> 7.32 us  [swap(): lax.ppermute(block, 'space', [(i, i ^ 1 << bit) for i in range(slabs)])]
    unnamed x23 -> x27, local copies, waits for them, and re-layouts: 4.38 us -> 6.73 us
    ppermute x7, waiting for transfers between devices: 4.12 us -> 1.84 us  [on_device(): lax.ppermute(messages[k], 'space', [(i, i ^ 2 * k) for i in range(slabs)])]
    pallas_call x1, Pallas kernels: 5.44 us -> 3.75 us  [on_device(): pl.pallas_call(functools.partial(grad_kernel, half, factor), out_shape=(c...]
    ppermute x7, starting transfers between devices: 7.97 us -> 9.38 us  [on_device(): lax.ppermute(messages[k], 'space', [(i, i ^ 2 * k) for i in range(slabs)])]
  transfers between devices with their start and end apart: 20 -> 20, of which waited for: 10 -> 7; matrix products, arithmetic and copies ran while one was open for 7% -> 7% of each run, Pallas kernels for 10% -> 16%
where the time goes in v7:
time: 74.5 us; the launch traced here: 74.1 us
  starting transfers between devices  24.1 us (32%)
  Pallas kernels  18.9 us (25%)
  waiting for transfers between devices  18.4 us (25%)
  local copies, waits for them, and re-layouts  11.8 us (16%)
  between operations  0.89 us (1%)
    ppermute x7, starting transfers between devices, on_device(): lax.ppermute(messages[k], 'space', [(i, i ^ 2 * k) for i in range(slabs)])  9.38 us
    ppermute x9, waiting for transfers between devices, swap(): lax.ppermute(block, 'space', [(i, i ^ 1 << bit) for i in range(slabs)])  8.11 us
    ppermute x9, starting transfers between devices, swap(): lax.ppermute(block, 'space', [(i, i ^ 1 << bit) for i in range(slabs)])  7.32 us
    unnamed x27, local copies, waits for them, and re-layouts  6.73 us
    ppermute x1, starting transfers between devices, on_device(): above = lax.ppermute(low, 'space', down)  5.61 us
    pallas_call x1, Pallas kernels, on_device(): pl.pallas_call(functools.partial(edge_kernel, half, linked, near, far), o...  4.01 us
    pallas_call x1, Pallas kernels, on_device(): pl.pallas_call(functools.partial(near_kernel, half), out_shape=(jax.Shape...  3.9 us
    pallas_call x1, Pallas kernels, on_device(): pl.pallas_call(functools.partial(grad_kernel, half, factor), out_shape=(c...  3.75 us
  transfers between devices with their start and end apart: 20, of which 7 were waited for; matrix products, arithmetic and copies ran while one was open for 7% of the time, Pallas kernels for 16%

profile of v7, /device:TPU:0, one launch (start us, length us, event | category | flops | bytes accessed | tf_op | source)
XLA Modules:
  0.0 74.1 jit_solution(7856909945108452415)
XLA Ops:
  0.7 2.6 %pack.1 = (bf16[8,272,128]{2,1,0:T(8,128)(2,1)S(1)}, bf16[8,272,128]{2,1,0:T(8,128)(2,1)S(1)}, bf16[64,512]{1,0:T(8,128)(2,1)S(1)}, bf16[64,512]{1,0:T(8,128)(2,1)S(1)}) custom-call(s32[1]{0:T(128)} %bitcast.me_ref, bf16[256,512]{1,0:T(8,128)(2,1)} %feats_ref.3, bf16[529,16,128]{2,1,0:T(8,128)(2,1)} %bitcast.16), custom_call_target="tpu_custom_call" | custom-call | tf_op jit(solution)/shard_map/pack/pallas_call | solution.py:349
  3.9 5.6 %collective-permute-start.2 = (bf16[64,512]{1,0:T(8,128)(2,1)S(1)}, bf16[64,512]{1,0:T(8,128)(2,1)S(1)}, u32[]{:S(2)}, u32[]{:S(2)}) collective-permute-start(bf16[64,512]{1,0:T(8,128)(2,1)S(1)} %get-tuple-element.70), channel_id=1, source_target_pairs={{1,0},{2,1},{3,2},{4,3},{5,4},{6,5},{7,6},{8,7},{9,8},{10,9},{11,1... | collective-permute-start | bytes 196616 | tf_op jit(solution)/shard_map/ppermute | solution.py:368
  9.5 1.9 %collective-permute-done.1.below_ref = bf16[64,512]{1,0:T(8,128)(2,1)S(1)} collective-permute-done((bf16[64,512]{1,0:T(8,128)(2,1)S(1)}, bf16[64,512]{1,0:T(8,128)(2,1)S(1)}, u32[]{:S(2)}, u32[]{:S(2)}) %collective-permute-start.1) | collective-permute-done | bytes 65568 | tf_op jit(solution)/shard_map/ppermute | solution.py:367
  11.8 3.3 %collective-permute-start.5 = (bf16[2,272,128]{2,1,0:T(8,128)(2,1)S(1)}, bf16[2,272,128]{2,1,0:T(8,128)(2,1)S(1)}, u32[]{:S(2)}, u32[]{:S(2)}) collective-permute-start(bf16[2,272,128]{2,1,0:T(8,128)(2,1)S(1)} %get-tuple-element.90), channel_id=1, source_target_pairs={{0,6},{1,7},{2,4},{3,5},{4,2},{5,3},{6,0},{7,1},{8,14},{9,15},{10,... | collective-permute-start | bytes 417800 | tf_op jit(solution)/shard_map/ppermute | solution.py:383
  15.7 1.8 %collective-permute-start.7 = (bf16[2,272,128]{2,1,0:T(8,128)(2,1)S(1)}, bf16[2,272,128]{2,1,0:T(8,128)(2,1)S(1)}, u32[]{:S(2)}, u32[]{:S(2)}) collective-permute-start(bf16[2,272,128]{2,1,0:T(8,128)(2,1)S(1)} %get-tuple-element.93), channel_id=1, source_target_pairs={{0,10},{1,11},{2,8},{3,9},{4,14},{5,15},{6,12},{7,13},{8,2},{9,3},... | collective-permute-start | bytes 417800 | tf_op jit(solution)/shard_map/ppermute | solution.py:383
  17.5 2.2 %collective-permute-start.8 = (bf16[2,272,128]{2,1,0:T(8,128)(2,1)S(1)}, bf16[2,272,128]{2,1,0:T(8,128)(2,1)S(1)}, u32[]{:S(2)}, u32[]{:S(2)}) collective-permute-start(bf16[2,272,128]{2,1,0:T(8,128)(2,1)S(1)} %get-tuple-element.94), channel_id=1, source_target_pairs={{0,12},{1,13},{2,14},{3,15},{4,8},{5,9},{6,10},{7,11},{8,4},{9,5},... | collective-permute-start | bytes 417800 | tf_op jit(solution)/shard_map/ppermute | solution.py:383
  19.7 1.8 %collective-permute-done.3.rest_2_ = bf16[2,272,128]{2,1,0:T(8,128)(2,1)S(1)} collective-permute-done((bf16[2,272,128]{2,1,0:T(8,128)(2,1)S(1)}, bf16[2,272,128]{2,1,0:T(8,128)(2,1)S(1)}, u32[]{:S(2)}, u32[]{:S(2)}) %collective-permute-start.3) | collective-permute-done | bytes 139296 | tf_op jit(solution)/shard_map/ppermute | solution.py:383
  21.5 1.2 %collective-permute-start.9 = (bf16[2,272,128]{2,1,0:T(8,128)(2,1)S(1)}, bf16[2,272,128]{2,1,0:T(8,128)(2,1)S(1)}, u32[]{:S(2)}, u32[]{:S(2)}) collective-permute-start(bf16[2,272,128]{2,1,0:T(8,128)(2,1)S(1)} %get-tuple-element.95), channel_id=1, source_target_pairs={{0,14},{1,15},{2,12},{3,13},{4,10},{5,11},{6,8},{7,9},{8,6},{9,7},... | collective-permute-start | bytes 417800 | tf_op jit(solution)/shard_map/ppermute | solution.py:383
  22.7 4.0 %edges.1 = (bf16[640,1152]{1,0:T(8,128)(2,1)S(1)}, bf16[512,1152]{1,0:T(8,128)(2,1)S(1)}, f32[512,1152]{1,0:T(8,128)S(1)}, bf16[512,384]{1,0:T(8,128)(2,1)S(1)}) custom-call(s32[1]{0:T(128)} %bitcast.me_ref, bf16[256,512]{1,0:T(8,128)(2,1)S(1)} %copy-done.4, bf16[64,512]{1,0:T(8,128)(2,1)S(1)} %collective-permute-done.1.below_ref, ...), custom_call_target="tpu_custom_call" | custom-call | flops 30198988800 | bytes 8388608 | tf_op jit(solution)/shard_map/edges/pallas_call | solution.py:398
  26.8 1.4 %copy-done = f32[512,1152]{1,0:T(8,128)} copy-done((f32[512,1152]{1,0:T(8,128)}, f32[512,1152]{1,0:T(8,128)S(1)}, u32[]{:S(2)}) %copy-start) | copy-done | bytes 2359320
  28.2 1.1 %copy-done.1 = bf16[640,1152]{1,0:T(8,128)(2,1)} copy-done((bf16[640,1152]{1,0:T(8,128)(2,1)}, bf16[640,1152]{1,0:T(8,128)(2,1)S(1)}, u32[]{:S(2)}) %copy-start.1) | copy-done | bytes 1474584
  29.3 0.7 %copy-done.3 = bf16[512,384]{1,0:T(8,128)(2,1)} copy-done((bf16[512,384]{1,0:T(8,128)(2,1)}, bf16[512,384]{1,0:T(8,128)(2,1)S(1)}, u32[]{:S(2)}) %copy-start.3) | copy-done | bytes 393240
  30.1 1.1 %copy-done.11 = bf16[512,1152]{1,0:T(8,128)(2,1)} copy-done((bf16[512,1152]{1,0:T(8,128)(2,1)}, bf16[512,1152]{1,0:T(8,128)(2,1)S(1)}, u32[]{:S(2)}) %copy-start.11) | copy-done | bytes 1179672
  31.1 1.7 %constant_dynamic-slice_fusion = bf16[1,1,64,529]{2,1,3,0:T(2,128)(2,1)S(1)} fusion(bf16[1,16,128,529]{2,1,3,0:T(8,128)(2,1)} %param.12, s32[]{:T(128)S(6)} %select_n.4, s32[]{:T(128)S(6)} %add.9), kind=kLoop, calls=%fused_computation.1 | loop fusion | bytes 135432 | tf_op jit(solution)/shard_map/slice | solution.py:420
  32.8 2.1 %copy.12 = bf16[512,529]{1,0:T(8,128)(2,1)} copy(bf16[512,529]{0,1:T(8,128)(2,1)} %param.11) | data formatting | bytes 1083392 | tf_op jit(solution)/shard_map/optimization_barrier | solution.py:419
  35.0 1.2 %pad.8.w_out_ref = bf16[512,544]{1,0:T(8,128)(2,1)S(1)} pad(bf16[512,529]{1,0:T(8,128)(2,1)} %copy.12, bf16[]{:T(256)} %constant.11.clone.1), padding=0_0x0_15 | pad | bytes 1098754 | tf_op jit(solution)/shard_map/jit(_pad)/pad | solution.py:427
  36.4 3.9 %near.1 = (f32[640,512]{1,0:T(8,128)S(1)}, f32[512,544]{1,0:T(8,128)S(1)}) custom-call(bf16[544,128]{1,0:T(8,128)(2,1)S(1)} %pad.9.own_ref, bf16[512,544]{1,0:T(8,128)(2,1)S(1)} %pad.8.w_out_ref, bf16[512,1152]{1,0:T(8,128)(2,1)S(1)} %copy-done.12, f32[512,1152]{1,0:T(8,128)} %copy-done, bf16[640,1152]{1,0:T(8,128)(2,1)} %copy-done.1, ...), custom_call_target="tpu_custom_call" | custom-call | flops 7130316800 | bytes 6291456 | tf_op jit(solution)/shard_map/near/pallas_call | solution.py:429
  40.4 1.1 %copy-done.2 = f32[640,512]{1,0:T(8,128)} copy-done((f32[640,512]{1,0:T(8,128)}, f32[640,512]{1,0:T(8,128)S(1)}, u32[]{:S(2)}) %copy-start.2) | copy-done | bytes 1310744
  41.4 1.1 %copy-done.10 = f32[512,544]{1,0:T(8,128)} copy-done((f32[512,544]{1,0:T(8,128)}, f32[512,544]{1,0:T(8,128)S(1)}, u32[]{:S(2)}) %copy-start.10) | copy-done | bytes 1114136
  42.6 3.8 %grads.1 = (f32[8,32,1024]{2,1,0:T(8,128)S(1)}, bf16[8,32,1024]{2,1,0:T(8,128)(2,1)S(1)}, f32[512,512]{1,0:T(8,128)S(1)}, bf16[64,512]{1,0:T(8,128)(2,1)S(1)}, b...) custom-call(s32[1]{0:T(128)} %bitcast.me_ref, bf16[512,544]{1,0:T(8,128)(2,1)S(1)} %pad.8.w_out_ref, ...), custom_call_target="tpu_custom_call" | custom-call | tf_op jit(solution)/shard_map/grads/pallas_call | solution.py:449
  46.3 2.0 %collective-permute-start.10 = (bf16[8,32,1024]{2,1,0:T(8,128)(2,1)S(1)}, bf16[8,32,1024]{2,1,0:T(8,128)(2,1)S(1)}, u32[]{:S(2)}, u32[]{:S(2)}) collective-permute-start(bf16[8,32,1024]{2,1,0:T(8,128)(2,1)S(1)} %get-tuple-element.98), channel_id=1, source_target_pairs={{0,1},{1,0},{2,3},{3,2},{4,5},{5,4},{6,7},{7,6},{8,9},{9,8},{10,11... | collective-permute-start | bytes 1572872 | tf_op jit(solution)/shard_map/ppermute | solution.py:318
  48.3 1.9 %outer.1 = (f32[8,32,640]{2,1,0:T(8,128)S(1)}, bf16[8,32,640]{2,1,0:T(8,128)(2,1)S(1)}) custom-call(s32[1]{0:T(128)} %bitcast.me_ref, bf16[512,1152]{1,0:T(8,128)(2,1)S(1)} %copy-done.12, bf16[544,512]{1,0:T(8,128)(2,1)S(1)} %get-tuple-element.111.g_ref, f32[512,544]{1,0:T(8,128)} %copy-done.10), custom_call_target="tpu_custom_call" | custom-call | flops 12834570240 | bytes 4194304 | tf_op jit(solution)/shard_map/outer/pallas_call | solution.py:473
  51.1 0.8 %collective-permute-done.16.came_ref = bf16[8,32,640]{2,1,0:T(8,128)(2,1)S(1)} collective-permute-done((bf16[8,32,640]{2,1,0:T(8,128)(2,1)S(1)}, bf16[8,32,640]{2,1,0:T(8,128)(2,1)S(1)}, u32[]{:S(2)}, u32[]{:S(2)}) %collective-permute-start.16) | collective-permute-done | bytes 327712 | tf_op jit(solution)/shard_map/ppermute | solution.py:318
  52.1 1.8 %collective-permute-start.12 = (bf16[64,512]{1,0:T(8,128)(2,1)S(1)}, bf16[64,512]{1,0:T(8,128)(2,1)S(1)}, u32[]{:S(2)}, u32[]{:S(2)}) collective-permute-start(bf16[64,512]{1,0:T(8,128)(2,1)S(1)} %get-tuple-element.101), channel_id=1, source_target_pairs={{1,0},{2,1},{3,2},{4,3},{5,4},{6,5},{7,6},{8,7},{9,8},{10,9},{11,1... | collective-permute-start | bytes 196616 | tf_op jit(solution)/shard_map/ppermute | solution.py:513
  53.9 3.0 %collective-permute-done.12.from_above_ref = bf16[64,512]{1,0:T(8,128)(2,1)S(1)} collective-permute-done((bf16[64,512]{1,0:T(8,128)(2,1)S(1)}, bf16[64,512]{1,0:T(8,128)(2,1)S(1)}, u32[]{:S(2)}, u32[]{:S(2)}) %collective-permute-start.12) | collective-permute-done | bytes 65568 | tf_op jit(solution)/shard_map/ppermute | solution.py:513
  56.8 3.5 %collective-permute-done.13.from_below_ref = bf16[64,512]{1,0:T(8,128)(2,1)S(1)} collective-permute-done((bf16[64,512]{1,0:T(8,128)(2,1)S(1)}, bf16[64,512]{1,0:T(8,128)(2,1)S(1)}, u32[]{:S(2)}, u32[]{:S(2)}) %collective-permute-start.13) | collective-permute-done | bytes 65568 | tf_op jit(solution)/shard_map/ppermute | solution.py:514
  60.6 0.9 %collective-permute-start.18 = (bf16[2,32,640]{2,1,0:T(8,128)(2,1)S(1)}, bf16[2,32,640]{2,1,0:T(8,128)(2,1)S(1)}, u32[]{:S(2)}, u32[]{:S(2)}) collective-permute-start(bf16[2,32,640]{2,1,0:T(8,128)(2,1)S(1)} %get-tuple-element.122), channel_id=1, source_target_pairs={{0,2},{1,3},{2,0},{3,1},{4,6},{5,7},{6,4},{7,5},{8,10},{9,11},{10,... | collective-permute-start | bytes 245768 | tf_op jit(solution)/shard_map/ppermute | solution.py:318
  61.5 4.5 %collective-permute-done.14.came_ref = bf16[2,32,1024]{2,1,0:T(8,128)(2,1)S(1)} collective-permute-done((bf16[2,32,1024]{2,1,0:T(8,128)(2,1)S(1)}, bf16[2,32,1024]{2,1,0:T(8,128)(2,1)S(1)}, u32[]{:S(2)}, u32[]{:S(2)}) %collective-permute-start.14) | collective-permute-done | bytes 131104 | tf_op jit(solution)/shard_map/ppermute | solution.py:318
  66.6 2.6 %collective-permute-start.19 = (bf16[1,32,640]{2,1,0:T(8,128)(2,1)S(1)}, bf16[1,32,640]{2,1,0:T(8,128)(2,1)S(1)}, u32[]{:S(2)}, u32[]{:S(2)}) collective-permute-start(bf16[1,32,640]{2,1,0:T(8,128)(2,1)S(1)} %get-tuple-element.126), channel_id=1, source_target_pairs={{0,8},{1,9},{2,10},{3,11},{4,12},{5,13},{6,14},{7,15},{8,0},{9,1},... | collective-permute-start | bytes 122888 | tf_op jit(solution)/shard_map/ppermute | solution.py:318
  69.1 1.5 %rims.1 = f32[256,512]{1,0:T(8,128)} custom-call(f32[512,512]{1,0:T(8,128)S(1)} %get-tuple-element.96.sums_ref, bf16[64,512]{1,0:T(8,128)(2,1)S(1)} %collective-permute-done.13.from_below_ref, bf16[64,512]{1,0:T(8,128)(2,1)S(1)} %collective-permute-done.12.from_above_ref, bf16[512,512]{1,0:T(8,128)(2,1)S(1)} %copy-done.5, bf16[512,512]{1,0:T(8,128)(2,1)S(1)} %copy-done.6), custom_call_target="tpu_custom_call" | custom-call | flops 24159191040 | bytes 4194304 | tf_op jit(solution)/shard_map/rims/pallas_call | solution.py:527
  70.7 2.8 %collective-permute-done.19.refs_3_ = bf16[1,32,640]{2,1,0:T(8,128)(2,1)S(1)} collective-permute-done((bf16[1,32,640]{2,1,0:T(8,128)(2,1)S(1)}, bf16[1,32,640]{2,1,0:T(8,128)(2,1)S(1)}, u32[]{:S(2)}, u32[]{:S(2)}) %collective-permute-start.19) | collective-permute-done | bytes 40992 | tf_op jit(solution)/shard_map/ppermute | solution.py:318
  73.4 0.7 totals.1
  (53 shorter events, 3.6 us)
Async XLA Ops:
  0.6 22.1 %copy-start.4 = (bf16[256,512]{1,0:T(8,128)(2,1)S(1)}, bf16[256,512]{1,0:T(8,128)(2,1)}, u32[]{:S(2)}) copy-start(bf16[256,512]{1,0:T(8,128)(2,1)} %feats_ref.3) | copy-start | bytes 786436
  0.6 22.1 %copy-start.5 = (bf16[512,512]{1,0:T(8,128)(2,1)S(1)}, bf16[512,512]{1,0:T(8,128)(2,1)}, u32[]{:S(2)}) copy-start(bf16[512,512]{1,0:T(8,128)(2,1)} %w_src_ref.3) | copy-start | bytes 1572868
  0.7 22.1 %copy-start.6 = (bf16[512,512]{1,0:T(8,128)(2,1)S(1)}, bf16[512,512]{1,0:T(8,128)(2,1)}, u32[]{:S(2)}) copy-start(bf16[512,512]{1,0:T(8,128)(2,1)} %w_dst_ref.3) | copy-start | bytes 1572868
  0.7 22.1 %copy-start.7 = (s32[2048]{0:T(1024)S(1)}, s32[2048]{0:T(1024)}, u32[]{:S(2)}) copy-start(s32[2048]{0:T(1024)} %param.13) | copy-start | bytes 24580
  0.7 22.1 %copy-start.8 = (s32[2048]{0:T(1024)S(1)}, s32[2048]{0:T(1024)}, u32[]{:S(2)}) copy-start(s32[2048]{0:T(1024)} %param.14) | copy-start | bytes 24580
  0.7 22.1 %copy-start.9 = (s32[2048]{0:T(1024)S(1)}, s32[2048]{0:T(1024)}, u32[]{:S(2)}) copy-start(s32[2048]{0:T(1024)} %param.15) | copy-start | bytes 24580
  3.3 8.1 %collective-permute-start = (bf16[8,272,128]{2,1,0:T(8,128)(2,1)S(1)}, bf16[8,272,128]{2,1,0:T(8,128)(2,1)S(1)}, u32[]{:S(2)}, u32[]{:S(2)}) collective-permute-start(bf16[8,272,128]{2,1,0:T(8,128)(2,1)S(1)} %get-tuple-element.68), channel_id=1, source_target_pairs={{0,1},{1,0},{2,3},{3,2},{4,5},{5,4},{6,7},{7,6},{8,9},{9,8},{10,11... | collective-permute-start | bytes 1671176 | tf_op jit(solution)/shard_map/ppermute | solution.py:318
  3.8 7.6 %collective-permute-start.1 = (bf16[64,512]{1,0:T(8,128)(2,1)S(1)}, bf16[64,512]{1,0:T(8,128)(2,1)S(1)}, u32[]{:S(2)}, u32[]{:S(2)}) collective-permute-start(bf16[64,512]{1,0:T(8,128)(2,1)S(1)} %get-tuple-element.69), channel_id=1, source_target_pairs={{0,1},{1,2},{2,3},{3,4},{4,5},{5,6},{6,7},{7,8},{8,9},{9,10},{10,1... | collective-permute-start | bytes 196616 | tf_op jit(solution)/shard_map/ppermute | solution.py:367
  3.9 7.6 %collective-permute-start.2 = (bf16[64,512]{1,0:T(8,128)(2,1)S(1)}, bf16[64,512]{1,0:T(8,128)(2,1)S(1)}, u32[]{:S(2)}, u32[]{:S(2)}) collective-permute-start(bf16[64,512]{1,0:T(8,128)(2,1)S(1)} %get-tuple-element.70), channel_id=1, source_target_pairs={{1,0},{2,1},{3,2},{4,3},{5,4},{6,5},{7,6},{8,7},{9,8},{10,9},{11,1... | collective-permute-start | bytes 196616 | tf_op jit(solution)/shard_map/ppermute | solution.py:368
  11.5 6.0 %collective-permute-start.4 = (bf16[2,272,128]{2,1,0:T(8,128)(2,1)S(1)}, bf16[2,272,128]{2,1,0:T(8,128)(2,1)S(1)}, u32[]{:S(2)}, u32[]{:S(2)}) collective-permute-start(bf16[2,272,128]{2,1,0:T(8,128)(2,1)S(1)} %get-tuple-element.73), channel_id=1, source_target_pairs={{0,2},{1,3},{2,0},{3,1},{4,6},{5,7},{6,4},{7,5},{8,10},{9,11},{10,... | collective-permute-start | bytes 417800 | tf_op jit(solution)/shard_map/ppermute | solution.py:383
  11.6 9.9 %collective-permute-start.3 = (bf16[2,272,128]{2,1,0:T(8,128)(2,1)S(1)}, bf16[2,272,128]{2,1,0:T(8,128)(2,1)S(1)}, u32[]{:S(2)}, u32[]{:S(2)}) collective-permute-start(bf16[2,272,128]{2,1,0:T(8,128)(2,1)S(1)} %get-tuple-element.72), channel_id=1, source_target_pairs={{0,4},{1,5},{2,6},{3,7},{4,0},{5,1},{6,2},{7,3},{8,12},{9,13},{10,... | collective-permute-start | bytes 417800 | tf_op jit(solution)/shard_map/ppermute | solution.py:383
  11.8 24.5 %collective-permute-start.5 = (bf16[2,272,128]{2,1,0:T(8,128)(2,1)S(1)}, bf16[2,272,128]{2,1,0:T(8,128)(2,1)S(1)}, u32[]{:S(2)}, u32[]{:S(2)}) collective-permute-start(bf16[2,272,128]{2,1,0:T(8,128)(2,1)S(1)} %get-tuple-element.90), channel_id=1, source_target_pairs={{0,6},{1,7},{2,4},{3,5},{4,2},{5,3},{6,0},{7,1},{8,14},{9,15},{10,... | collective-permute-start | bytes 417800 | tf_op jit(solution)/shard_map/ppermute | solution.py:383
  15.1 27.5 %collective-permute-start.6 = (bf16[2,272,128]{2,1,0:T(8,128)(2,1)S(1)}, bf16[2,272,128]{2,1,0:T(8,128)(2,1)S(1)}, u32[]{:S(2)}, u32[]{:S(2)}) collective-permute-start(bf16[2,272,128]{2,1,0:T(8,128)(2,1)S(1)} %get-tuple-element.92), channel_id=1, source_target_pairs={{0,8},{1,9},{2,10},{3,11},{4,12},{5,13},{6,14},{7,15},{8,0},{9,1},... | collective-permute-start | bytes 417800 | tf_op jit(solution)/shard_map/ppermute | solution.py:383
  15.7 26.8 %collective-permute-start.7 = (bf16[2,272,128]{2,1,0:T(8,128)(2,1)S(1)}, bf16[2,272,128]{2,1,0:T(8,128)(2,1)S(1)}, u32[]{:S(2)}, u32[]{:S(2)}) collective-permute-start(bf16[2,272,128]{2,1,0:T(8,128)(2,1)S(1)} %get-tuple-element.93), channel_id=1, source_target_pairs={{0,10},{1,11},{2,8},{3,9},{4,14},{5,15},{6,12},{7,13},{8,2},{9,3},... | collective-permute-start | bytes 417800 | tf_op jit(solution)/shard_map/ppermute | solution.py:383
  17.5 25.0 %collective-permute-start.8 = (bf16[2,272,128]{2,1,0:T(8,128)(2,1)S(1)}, bf16[2,272,128]{2,1,0:T(8,128)(2,1)S(1)}, u32[]{:S(2)}, u32[]{:S(2)}) collective-permute-start(bf16[2,272,128]{2,1,0:T(8,128)(2,1)S(1)} %get-tuple-element.94), channel_id=1, source_target_pairs={{0,12},{1,13},{2,14},{3,15},{4,8},{5,9},{6,10},{7,11},{8,4},{9,5},... | collective-permute-start | bytes 417800 | tf_op jit(solution)/shard_map/ppermute | solution.py:383
  21.5 21.0 %collective-permute-start.9 = (bf16[2,272,128]{2,1,0:T(8,128)(2,1)S(1)}, bf16[2,272,128]{2,1,0:T(8,128)(2,1)S(1)}, u32[]{:S(2)}, u32[]{:S(2)}) collective-permute-start(bf16[2,272,128]{2,1,0:T(8,128)(2,1)S(1)} %get-tuple-element.95), channel_id=1, source_target_pairs={{0,14},{1,15},{2,12},{3,13},{4,10},{5,11},{6,8},{7,9},{8,6},{9,7},... | collective-permute-start | bytes 417800 | tf_op jit(solution)/shard_map/ppermute | solution.py:383
  26.8 1.4 %copy-start = (f32[512,1152]{1,0:T(8,128)}, f32[512,1152]{1,0:T(8,128)S(1)}, u32[]{:S(2)}) copy-start(f32[512,1152]{1,0:T(8,128)S(1)} %get-tuple-element.83.slope_hbm) | copy-start | bytes 7077892
  28.2 1.1 %copy-start.1 = (bf16[640,1152]{1,0:T(8,128)(2,1)}, bf16[640,1152]{1,0:T(8,128)(2,1)S(1)}, u32[]{:S(2)}) copy-start(bf16[640,1152]{1,0:T(8,128)(2,1)S(1)} %get-tuple-element.84.onehot_hbm) | copy-start | bytes 4423684
  30.1 1.1 %copy-start.11 = (bf16[512,1152]{1,0:T(8,128)(2,1)}, bf16[512,1152]{1,0:T(8,128)(2,1)S(1)}, u32[]{:S(2)}) copy-start(bf16[512,1152]{1,0:T(8,128)(2,1)S(1)} %get-tuple-element.86.hidden_ref) | copy-start | bytes 3538948
  35.0 1.5 %copy-start.12 = (bf16[512,1152]{1,0:T(8,128)(2,1)S(1)}, bf16[512,1152]{1,0:T(8,128)(2,1)}, u32[]{:S(2)}) copy-start(bf16[512,1152]{1,0:T(8,128)(2,1)} %copy-done.11) | copy-start | bytes 3538948
  40.4 1.1 %copy-start.2 = (f32[640,512]{1,0:T(8,128)}, f32[640,512]{1,0:T(8,128)S(1)}, u32[]{:S(2)}) copy-start(f32[640,512]{1,0:T(8,128)S(1)} %get-tuple-element.91.near_hbm) | copy-start | bytes 3932164
  41.4 1.1 %copy-start.10 = (f32[512,544]{1,0:T(8,128)}, f32[512,544]{1,0:T(8,128)S(1)}, u32[]{:S(2)}) copy-start(f32[512,544]{1,0:T(8,128)S(1)} %get-tuple-element.112.near_hbm) | copy-start | bytes 3342340
  46.3 4.0 %collective-permute-start.10 = (bf16[8,32,1024]{2,1,0:T(8,128)(2,1)S(1)}, bf16[8,32,1024]{2,1,0:T(8,128)(2,1)S(1)}, u32[]{:S(2)}, u32[]{:S(2)}) collective-permute-start(bf16[8,32,1024]{2,1,0:T(8,128)(2,1)S(1)} %get-tuple-element.98), channel_id=1, source_target_pairs={{0,1},{1,0},{2,3},{3,2},{4,5},{5,4},{6,7},{7,6},{8,9},{9,8},{10,11... | collective-permute-start | bytes 1572872 | tf_op jit(solution)/shard_map/ppermute | solution.py:318
  50.2 1.7 %collective-permute-start.16 = (bf16[8,32,640]{2,1,0:T(8,128)(2,1)S(1)}, bf16[8,32,640]{2,1,0:T(8,128)(2,1)S(1)}, u32[]{:S(2)}, u32[]{:S(2)}) collective-permute-start(bf16[8,32,640]{2,1,0:T(8,128)(2,1)S(1)} %get-tuple-element.114), channel_id=1, source_target_pairs={{0,1},{1,0},{2,3},{3,2},{4,5},{5,4},{6,7},{7,6},{8,9},{9,8},{10,11... | collective-permute-start | bytes 983048 | tf_op jit(solution)/shard_map/ppermute | solution.py:318
  50.5 9.9 %collective-permute-start.11 = (bf16[4,32,1024]{2,1,0:T(8,128)(2,1)S(1)}, bf16[4,32,1024]{2,1,0:T(8,128)(2,1)S(1)}, u32[]{:S(2)}, u32[]{:S(2)}) collective-permute-start(bf16[4,32,1024]{2,1,0:T(8,128)(2,1)S(1)} %get-tuple-element.100), channel_id=1, source_target_pairs={{0,2},{1,3},{2,0},{3,1},{4,6},{5,7},{6,4},{7,5},{8,10},{9,11},{10,... | collective-permute-start | bytes 786440 | tf_op jit(solution)/shard_map/ppermute | solution.py:318
  52.0 8.5 %collective-permute-start.17 = (bf16[4,32,640]{2,1,0:T(8,128)(2,1)S(1)}, bf16[4,32,640]{2,1,0:T(8,128)(2,1)S(1)}, u32[]{:S(2)}, u32[]{:S(2)}) collective-permute-start(bf16[4,32,640]{2,1,0:T(8,128)(2,1)S(1)} %get-tuple-element.118), channel_id=1, source_target_pairs={{0,4},{1,5},{2,6},{3,7},{4,0},{5,1},{6,2},{7,3},{8,12},{9,13},{10,... | collective-permute-start | bytes 491528 | tf_op jit(solution)/shard_map/ppermute | solution.py:318
  52.1 4.7 %collective-permute-start.12 = (bf16[64,512]{1,0:T(8,128)(2,1)S(1)}, bf16[64,512]{1,0:T(8,128)(2,1)S(1)}, u32[]{:S(2)}, u32[]{:S(2)}) collective-permute-start(bf16[64,512]{1,0:T(8,128)(2,1)S(1)} %get-tuple-element.101), channel_id=1, source_target_pairs={{1,0},{2,1},{3,2},{4,3},{5,4},{6,5},{7,6},{8,7},{9,8},{10,9},{11,1... | collective-permute-start | bytes 196616 | tf_op jit(solution)/shard_map/ppermute | solution.py:513
  53.9 6.5 %collective-permute-start.13 = (bf16[64,512]{1,0:T(8,128)(2,1)S(1)}, bf16[64,512]{1,0:T(8,128)(2,1)S(1)}, u32[]{:S(2)}, u32[]{:S(2)}) collective-permute-start(bf16[64,512]{1,0:T(8,128)(2,1)S(1)} %get-tuple-element.102), channel_id=1, source_target_pairs={{0,1},{1,2},{2,3},{3,4},{4,5},{5,6},{6,7},{7,8},{8,9},{9,10},{10,1... | collective-permute-start | bytes 196616 | tf_op jit(solution)/shard_map/ppermute | solution.py:514
  60.4 5.6 %collective-permute-start.14 = (bf16[2,32,1024]{2,1,0:T(8,128)(2,1)S(1)}, bf16[2,32,1024]{2,1,0:T(8,128)(2,1)S(1)}, u32[]{:S(2)}, u32[]{:S(2)}) collective-permute-start(bf16[2,32,1024]{2,1,0:T(8,128)(2,1)S(1)} %get-tuple-element.108), channel_id=1, source_target_pairs={{0,4},{1,5},{2,6},{3,7},{4,0},{5,1},{6,2},{7,3},{8,12},{9,13},{10,... | collective-permute-start | bytes 393224 | tf_op jit(solution)/shard_map/ppermute | solution.py:318
  60.6 6.0 %collective-permute-start.18 = (bf16[2,32,640]{2,1,0:T(8,128)(2,1)S(1)}, bf16[2,32,640]{2,1,0:T(8,128)(2,1)S(1)}, u32[]{:S(2)}, u32[]{:S(2)}) collective-permute-start(bf16[2,32,640]{2,1,0:T(8,128)(2,1)S(1)} %get-tuple-element.122), channel_id=1, source_target_pairs={{0,2},{1,3},{2,0},{3,1},{4,6},{5,7},{6,4},{7,5},{8,10},{9,11},{10,... | collective-permute-start | bytes 245768 | tf_op jit(solution)/shard_map/ppermute | solution.py:318
  66.1 7.4 %collective-permute-start.15 = (bf16[1,32,1024]{2,1,0:T(8,128)(2,1)S(1)}, bf16[1,32,1024]{2,1,0:T(8,128)(2,1)S(1)}, u32[]{:S(2)}, u32[]{:S(2)}) collective-permute-start(bf16[1,32,1024]{2,1,0:T(8,128)(2,1)S(1)} %get-tuple-element.110), channel_id=1, source_target_pairs={{0,8},{1,9},{2,10},{3,11},{4,12},{5,13},{6,14},{7,15},{8,0},{9,1},... | collective-permute-start | bytes 196616 | tf_op jit(solution)/shard_map/ppermute | solution.py:318
  66.6 6.9 %collective-permute-start.19 = (bf16[1,32,640]{2,1,0:T(8,128)(2,1)S(1)}, bf16[1,32,640]{2,1,0:T(8,128)(2,1)S(1)}, u32[]{:S(2)}, u32[]{:S(2)}) collective-permute-start(bf16[1,32,640]{2,1,0:T(8,128)(2,1)S(1)} %get-tuple-element.126), channel_id=1, source_target_pairs={{0,8},{1,9},{2,10},{3,11},{4,12},{5,13},{6,14},{7,15},{8,0},{9,1},... | collective-permute-start | bytes 122888 | tf_op jit(solution)/shard_map/ppermute | solution.py:318
  (1 other events, 0.7 us)

commit v8 on v7

--- a/solution.py
+++ b/solution.py
@@ -134,16 +134,28 @@
 
 
 def edge_kernel(
-    half, linked, near, far, me_ref, feats_ref, below_ref, above_ref, w_src_ref, w_dst_ref, src_ref, dst_ref, live_ref,
-    onehot_ref, hidden_ref, slope_ref, ext_ref,
+    half, linked, near, far, me_ref, feats_ref, below_ref, above_ref, w_src_ref, w_dst_ref, w_out_ref, src_ref, dst_ref,
+    live_ref, onehot_hbm, slope_hbm, ext_hbm, near_hidden_ref, far_hidden_ref, w_wide_ref,
+    onehot_ref, slope_ref, ext_ref, w_rows_ref, sems,
 ):
     me = me_ref[0]
     mols = feats_ref.shape[0]
     reach = below_ref.shape[0]
     wide = mols + 2 * reach
+    slots = slope_ref.shape[1]
+    entries = w_out_ref.shape[0]
+    near_slots = near_hidden_ref.shape[1]
+    copies = []
+
+    def send(source, target):
+        copy = pltpu.make_async_copy(source, target, sems.at[len(copies)])
+        copy.start()
+        copies.append(copy)
+
     feats = feats_ref[...]
     ext = jnp.concatenate([feats, below_ref[...], above_ref[...]], axis=0)
     ext_ref[...] = ext.T
+    send(ext_ref, ext_hbm)
     proj_src = mm(feats, w_src_ref[...])
     proj_dst = mm(ext, w_dst_ref[...])
     proj = jnp.concatenate([proj_src, proj_dst], axis=0).T
@@ -157,13 +169,28 @@
         dst = jnp.where(live > 0, moved, -1)
         one_src = jnp.where(mol_src == src, 1.0, 0.0).astype(BF16)
         one_dst = jnp.where(mol_dst == dst, 1.0, 0.0).astype(BF16)
-        onehot = jnp.concatenate([one_src, one_dst], axis=0)
         here = pl.ds(tile * LANES, LANES)
-        onehot_ref[:, here] = onehot
+        onehot_ref[:, here] = jnp.concatenate([one_src, one_dst], axis=0)
+    for first, last in slot_tiles(near_slots) + [(near_slots + f, near_slots + l) for f, l in slot_tiles(slots - near_slots)]:
+        here = pl.ds(first, last - first)
+        send(onehot_ref.at[:, here], onehot_hbm.at[:, here])
+        onehot = onehot_ref[:, here]
         pre = mm(high, onehot) + mm(low, onehot)
         sigma = 1.0 / (1.0 + jnp.exp(-pre))
-        hidden_ref[:, here] = (pre * sigma).astype(BF16)
+        hidden = (pre * sigma).astype(BF16)
+        if first < near_slots:
+            near_hidden_ref[:, here] = hidden
+        else:
+            far_hidden_ref[:, pl.ds(first - near_slots, last - first)] = hidden
         slope_ref[:, here] = sigma * (1.0 + pre * (1.0 - sigma))
+        send(slope_ref.at[:, here], slope_hbm.at[:, here])
+    whole = entries // LANES * LANES
+    w_rows_ref[whole:] = jnp.zeros((w_rows_ref.shape[0] - whole, w_rows_ref.shape[1]), BF16)
+    w_rows_ref[:whole] = w_out_ref[:whole]
+    w_rows_ref[whole:entries] = w_out_ref[whole:]
+    w_wide_ref[...] = w_rows_ref[...].T
+    for copy in copies:
+        copy.wait()
 
 
 def halve(terms, odd, place, keep_ref, send_ref, first):
@@ -219,13 +246,19 @@
 
 
 def near_kernel(half, own_ref, w_out_ref, hidden_ref, slope_hbm, onehot_hbm, *rest):
-    *came_refs, sums_ref, outer_ref, g_ref, slope_ref, onehot_ref, sems = rest
+    *came_refs, sums_hbm, outer_hbm, g_ref, slope_ref, onehot_ref, sums_ref, outer_ref, sems, out_sems = rest
     slots = g_ref.shape[1]
     tiles = start_tiles(slots, 0, slope_hbm, onehot_hbm, slope_ref, onehot_ref, sems)
     filled = unpack(half, came_refs, g_ref)
     g_ref[:, filled:] = own_ref[...]
+    outer_ref[...] = mm(hidden_ref[...], g_ref[...], NT)
+    outer_copy = pltpu.make_async_copy(outer_ref, outer_hbm, out_sems.at[0])
+    outer_copy.start()
     sums_ref[...] = sum_edges(tiles, w_out_ref, g_ref, slope_ref, onehot_ref)
-    outer_ref[...] = mm(hidden_ref[:, :slots], g_ref[...], NT)
+    sums_copy = pltpu.make_async_copy(sums_ref, sums_hbm, out_sems.at[1])
+    sums_copy.start()
+    outer_copy.wait()
+    sums_copy.wait()
 
 
 def grad_kernel(half, factor, me_ref, w_out_ref, slope_hbm, onehot_hbm, ext_hbm, near_hbm, *rest):
@@ -266,8 +299,7 @@
 def outer_kernel(factor, me_ref, hidden_ref, g_ref, near_hbm, keep_ref, send_ref, near_ref, sem):
     copy = pltpu.make_async_copy(near_hbm, near_ref, sem)
     copy.start()
-    slots = g_ref.shape[1]
-    term = mm(hidden_ref[:, hidden_ref.shape[1] - slots :], g_ref[...], NT)
+    term = mm(hidden_ref[...], g_ref[...], NT)
     copy.wait()
     term = factor * (term + near_ref[...])
     padding = keep_ref.shape[2] - term.shape[1]
@@ -366,9 +398,11 @@
     )(me, in_hbm(mol_feats), in_hbm(jnp.transpose(grad_blocks[0], (2, 0, 1))))
     below = lax.ppermute(top, "space", up)
     above = lax.ppermute(low, "space", down)
+    late = lax.dynamic_index_in_dim(grad_blocks[0], me[0], 0, keepdims=False)[half:]
+    own = jnp.pad(late.T, ((0, groups * rows - entries), (0, LANES - half)))
     if linked:
         other = swap(odd, 0, slabs)
-        other, below, above = lax.optimization_barrier((other, below, above))
+        other, below, above, own = lax.optimization_barrier((other, below, above, own))
         messages = pl.pallas_call(
             join_kernel,
             out_shape=(jax.ShapeDtypeStruct((2, rows, LANES), BF16),) * (slabs // 2),
@@ -395,16 +429,28 @@
     far_slots = len(far) * half
     near_slots = slots - far_slots
 
-    onehot, hidden, slope, ext = pl.pallas_call(
+    wide = mols + 2 * reach
+    entries_wide = groups * rows
+    pieces = len(slot_tiles(near_slots)) + len(slot_tiles(far_slots))
+    onehot, slope, ext, near_hidden, far_hidden, w_out_wide = pl.pallas_call(
         functools.partial(edge_kernel, half, linked, near, far),
         out_shape=(
-            jax.ShapeDtypeStruct((2 * mols + 2 * reach, slots), BF16),
-            jax.ShapeDtypeStruct((width, slots), BF16),
-            jax.ShapeDtypeStruct((width, slots), F32),
-            jax.ShapeDtypeStruct((width, mols + 2 * reach), BF16),
-        ),
-        in_specs=[smem] + vmem(8),
-        out_specs=tuple(vmem(4)),
+            pltpu.HBM((mols + wide, slots), BF16),
+            pltpu.HBM((width, slots), F32),
+            pltpu.HBM((width, wide), BF16),
+            jax.ShapeDtypeStruct((width, near_slots), BF16),
+            jax.ShapeDtypeStruct((width, far_slots), BF16),
+            jax.ShapeDtypeStruct((width, entries_wide), BF16),
+        ),
+        in_specs=[smem] + vmem(9),
+        out_specs=(hbm,) * 3 + tuple(vmem(3)),
+        scratch_shapes=[
+            pltpu.VMEM((mols + wide, slots), BF16),
+            pltpu.VMEM((width, slots), F32),
+            pltpu.VMEM((width, wide), BF16),
+            pltpu.VMEM((entries_wide, width), BF16),
+            pltpu.SemaphoreType.DMA((2 * pieces + 1,)),
+        ],
         compiler_params=big,
         name="edges",
         cost_estimate=pl.CostEstimate(
@@ -412,40 +458,38 @@
             transcendentals=width * slots,
         ),
     )(
-        me, mol_feats, below, above, w_src, w_dst,
+        me, mol_feats, below, above, w_src, w_dst, w_out.T,
         edge_src.reshape(slabs, cap), edge_dst.reshape(slabs, cap), edge_live.reshape(slabs, cap),
     )
-
-    w_out = lax.optimization_barrier((w_out, me))[0]
-    late = lax.dynamic_index_in_dim(grad_blocks[0], me[0], 0, keepdims=False)[half:]
-    own = jnp.pad(late.T, ((0, groups * rows - entries), (0, LANES - half)))
+    onehot, slope, ext = in_hbm(onehot), in_hbm(slope), in_hbm(ext)
 
     def chunks(count, lanes, dtype):
         return jax.ShapeDtypeStruct((count, part, lanes), dtype)
 
-    entries_wide = groups * rows
-    w_out_wide = jnp.pad(w_out, ((0, 0), (0, entries_wide - entries)))
-    wide = mols + 2 * reach
     near_sums, near_outer = pl.pallas_call(
         functools.partial(near_kernel, half),
         out_shape=(
-            jax.ShapeDtypeStruct((mols + wide, width), F32),
-            jax.ShapeDtypeStruct((width, entries_wide), F32),
+            pltpu.HBM((mols + wide, width), F32),
+            pltpu.HBM((width, entries_wide), F32),
         ),
         in_specs=vmem(3) + [hbm] * 2 + vmem(len(came_near)),
-        out_specs=tuple(vmem(2)),
+        out_specs=(hbm, hbm),
         scratch_shapes=[
             pltpu.VMEM((entries_wide, near_slots), BF16),
             pltpu.VMEM((width, near_slots), F32),
             pltpu.VMEM((mols + wide, near_slots), BF16),
+            pltpu.VMEM((mols + wide, width), F32),
+            pltpu.VMEM((width, entries_wide), F32),
             pltpu.SemaphoreType.DMA((len(slot_tiles(near_slots)), 2)),
+            pltpu.SemaphoreType.DMA((2,)),
         ],
         compiler_params=big,
         name="near",
         cost_estimate=pl.CostEstimate(
             flops=40 * width * near_slots * entries_wide, bytes_accessed=6 * 1024 * 1024, transcendentals=0
         ),
-    )(own, w_out_wide, hidden, in_hbm(slope), in_hbm(onehot), *came_near)
+    )(own, w_out_wide, near_hidden, slope, onehot, *came_near)
+    near_sums, near_outer = in_hbm(near_sums), in_hbm(near_outer)
     keep, send, sums, lower, upper, g = pl.pallas_call(
         functools.partial(grad_kernel, half, factor),
         out_shape=(
@@ -468,7 +512,7 @@
         ],
         compiler_params=big,
         name="grads",
-    )(me, w_out_wide, in_hbm(slope), in_hbm(onehot), in_hbm(ext), in_hbm(near_sums), *came_far)
+    )(me, w_out_wide, slope, onehot, ext, near_sums, *came_far)
     lanes = round_up(entries_wide, LANES)
     keep_o, send_o = pl.pallas_call(
         functools.partial(outer_kernel, factor),
@@ -481,7 +525,7 @@
         cost_estimate=pl.CostEstimate(
             flops=40 * width * slots * entries_wide, bytes_accessed=4 * 1024 * 1024, transcendentals=0
         ),
-    )(me, hidden, g, in_hbm(near_outer))
+    )(me, far_hidden, g, near_outer)
 
     def fold(bit, place, keep, crossed):
         shape = (keep.shape[0] // 2, keep.shape[2])

time: 74.5 us -> 73.5 us (0.987)
  local copies, waits for them, and re-layouts: 11.8 us -> 1.79 us
  starting transfers between devices: 24.1 us -> 28.7 us
  Pallas kernels: 18.9 us -> 21.8 us
  waiting for transfers between devices: 18.4 us -> 20 us
    unnamed x27 -> x15, local copies, waits for them, and re-layouts: 6.73 us -> 0.05 us
    ppermute x7, waiting for transfers between devices: 1.84 us -> 5.89 us  [on_device(): lax.ppermute(messages[k], 'space', [(i, i ^ 2 * k) for i in range(slabs)])]
    ppermute x9, starting transfers between devices: 7.32 us -> 11 us  [swap(): lax.ppermute(block, 'space', [(i, i ^ 1 << bit) for i in range(slabs)])]
    optimization_barrier x1 -> x0, local copies, waits for them, and re-layouts: 2.13 us -> none  [on_device(): w_out = lax.optimization_barrier((w_out, me))[0]]
    ppermute x1, waiting for transfers between devices: 1.94 us -> 0.49 us  [on_device(): below = lax.ppermute(top, 'space', up)]
    pallas_call x1, Pallas kernels: 4.01 us -> 5.32 us  [on_device(): pl.pallas_call(functools.partial(edge_kernel, half, linked, near, far), o...]
    pad x1 -> x0, local copies, waits for them, and re-layouts: 1.24 us -> none  [on_device(): w_out_wide = jnp.pad(w_out, ((0, 0), (0, entries_wide - entries)))]
    ppermute x1, waiting for transfers between devices: 2.97 us -> 1.98 us  [on_device(): from_above = lax.ppermute(lower, 'space', down)]
  transfers between devices with their start and end apart: 20 -> 20, of which waited for: 7 -> 8; matrix products, arithmetic and copies ran while one was open for 7% -> 2% of each run, Pallas kernels for 16% -> 19%
where the time goes in v8:
time: 73.5 us; the launch traced here: 73.2 us
  starting transfers between devices  28.7 us (39%)
  Pallas kernels  21.8 us (30%)
  waiting for transfers between devices  20 us (27%)
  local copies, waits for them, and re-layouts  1.79 us (2%)
  between operations  0.88 us (1%)
    ppermute x9, starting transfers between devices, swap(): lax.ppermute(block, 'space', [(i, i ^ 1 << bit) for i in range(slabs)])  11 us
    ppermute x7, starting transfers between devices, on_device(): lax.ppermute(messages[k], 'space', [(i, i ^ 2 * k) for i in range(slabs)])  9.38 us
    ppermute x9, waiting for transfers between devices, swap(): lax.ppermute(block, 'space', [(i, i ^ 1 << bit) for i in range(slabs)])  7.23 us
    ppermute x7, waiting for transfers between devices, on_device(): lax.ppermute(messages[k], 'space', [(i, i ^ 2 * k) for i in range(slabs)])  5.89 us
    ppermute x1, starting transfers between devices, on_device(): above = lax.ppermute(low, 'space', down)  5.61 us
    pallas_call x1, Pallas kernels, on_device(): pl.pallas_call(functools.partial(edge_kernel, half, linked, near, far), o...  5.32 us
    pallas_call x1, Pallas kernels, on_device(): pl.pallas_call(functools.partial(near_kernel, half), out_shape=(pltpu.HBM...  4.81 us
    ppermute x1, waiting for transfers between devices, on_device(): from_below = lax.ppermute(upper, 'space', up)  4.42 us
  transfers between devices with their start and end apart: 20, of which 8 were waited for; matrix products, arithmetic and copies ran while one was open for 2% of the time, Pallas kernels for 19%

profile of v8, /device:TPU:0, one launch (start us, length us, event | category | flops | bytes accessed | tf_op | source)
XLA Modules:
  0.0 73.2 jit_solution(3863676512306155490)
XLA Ops:
  0.7 3.3 %pack.1 = (bf16[8,272,128]{2,1,0:T(8,128)(2,1)S(1)}, bf16[8,272,128]{2,1,0:T(8,128)(2,1)S(1)}, bf16[64,512]{1,0:T(8,128)(2,1)}, bf16[64,512]{1,0:T(8,128)(2,1)}) custom-call(s32[1]{0:T(128)} %bitcast.me_ref, bf16[256,512]{1,0:T(8,128)(2,1)} %feats_ref.3, bf16[529,16,128]{2,1,0:T(8,128)(2,1)} %bitcast.17), custom_call_target="tpu_custom_call" | custom-call | tf_op jit(solution)/shard_map/pack/pallas_call | solution.py:381
  4.0 0.5 collective-permute-start
  4.6 5.6 %collective-permute-start.2 = (bf16[64,512]{1,0:T(8,128)(2,1)}, bf16[64,512]{1,0:T(8,128)(2,1)}, u32[]{:S(2)}, u32[]{:S(2)}) collective-permute-start(bf16[64,512]{1,0:T(8,128)(2,1)} %get-tuple-element.72), channel_id=1, source_target_pairs={{1,0},{2,1},{3,2},{4,3},{5,4},{6,5},{7,6},{8,7},{9,8},{10,9},{11,1... | collective-permute-start | bytes 196616 | tf_op jit(solution)/shard_map/ppermute | solution.py:400
  10.2 1.7 %constant_dynamic-slice_fusion = bf16[1,1,64,529]{2,1,3,0:T(2,128)(2,1)S(1)} fusion(bf16[1,16,128,529]{2,1,3,0:T(8,128)(2,1)} %param.12, s32[]{:T(128)S(6)} %select_n.4, s32[]{:T(128)S(6)} %add.7), kind=kLoop, calls=%fused_computation.1 | loop fusion | bytes 135432 | tf_op jit(solution)/shard_map/slice | solution.py:401
  11.9 0.5 collective-permute-done.1.below_ref
  12.6 0.2 collective-permute-start.3
  12.8 3.3 %collective-permute-start.5 = (bf16[2,272,128]{2,1,0:T(8,128)(2,1)S(1)}, bf16[2,272,128]{2,1,0:T(8,128)(2,1)S(1)}, u32[]{:S(2)}, u32[]{:S(2)}) collective-permute-start(bf16[2,272,128]{2,1,0:T(8,128)(2,1)S(1)} %get-tuple-element.93), channel_id=1, source_target_pairs={{0,6},{1,7},{2,4},{3,5},{4,2},{5,3},{6,0},{7,1},{8,14},{9,15},{10,... | collective-permute-start | bytes 417800 | tf_op jit(solution)/shard_map/ppermute | solution.py:417
  16.1 0.6 collective-permute-start.6
  16.7 1.8 %collective-permute-start.7 = (bf16[2,272,128]{2,1,0:T(8,128)(2,1)S(1)}, bf16[2,272,128]{2,1,0:T(8,128)(2,1)S(1)}, u32[]{:S(2)}, u32[]{:S(2)}) collective-permute-start(bf16[2,272,128]{2,1,0:T(8,128)(2,1)S(1)} %get-tuple-element.96), channel_id=1, source_target_pairs={{0,10},{1,11},{2,8},{3,9},{4,14},{5,15},{6,12},{7,13},{8,2},{9,3},... | collective-permute-start | bytes 417800 | tf_op jit(solution)/shard_map/ppermute | solution.py:417
  18.5 2.2 %collective-permute-start.8 = (bf16[2,272,128]{2,1,0:T(8,128)(2,1)S(1)}, bf16[2,272,128]{2,1,0:T(8,128)(2,1)S(1)}, u32[]{:S(2)}, u32[]{:S(2)}) collective-permute-start(bf16[2,272,128]{2,1,0:T(8,128)(2,1)S(1)} %get-tuple-element.97), channel_id=1, source_target_pairs={{0,12},{1,13},{2,14},{3,15},{4,8},{5,9},{6,10},{7,11},{8,4},{9,5},... | collective-permute-start | bytes 417800 | tf_op jit(solution)/shard_map/ppermute | solution.py:417
  20.7 1.8 %collective-permute-done.3.rest_2_ = bf16[2,272,128]{2,1,0:T(8,128)(2,1)S(1)} collective-permute-done((bf16[2,272,128]{2,1,0:T(8,128)(2,1)S(1)}, bf16[2,272,128]{2,1,0:T(8,128)(2,1)S(1)}, u32[]{:S(2)}, u32[]{:S(2)}) %collective-permute-start.3) | collective-permute-done | bytes 139296 | tf_op jit(solution)/shard_map/ppermute | solution.py:417
  22.5 1.2 %collective-permute-start.9 = (bf16[2,272,128]{2,1,0:T(8,128)(2,1)S(1)}, bf16[2,272,128]{2,1,0:T(8,128)(2,1)S(1)}, u32[]{:S(2)}, u32[]{:S(2)}) collective-permute-start(bf16[2,272,128]{2,1,0:T(8,128)(2,1)S(1)} %get-tuple-element.98), channel_id=1, source_target_pairs={{0,14},{1,15},{2,12},{3,13},{4,10},{5,11},{6,8},{7,9},{8,6},{9,7},... | collective-permute-start | bytes 417800 | tf_op jit(solution)/shard_map/ppermute | solution.py:417
  23.8 5.3 %edges.1 = (bf16[640,1152]{1,0:T(8,128)(2,1)}, f32[512,1152]{1,0:T(8,128)}, bf16[512,384]{1,0:T(8,128)(2,1)}, bf16[512,640]{1,0:T(8,128)(2,1)S(1)}, bf16[512,512...) custom-call(s32[1]{0:T(128)} %bitcast.me_ref, bf16[256,512]{1,0:T(8,128)(2,1)S(1)} %copy-done, ...), custom_call_target="tpu_custom_call" | custom-call | flops 30198988800 | bytes 8388608 | tf_op jit(solution)/shard_map/edges/pallas_call | solution.py:435
  29.1 4.8 %near.1 = (f32[640,512]{1,0:T(8,128)}, f32[512,544]{1,0:T(8,128)}) custom-call(bf16[544,128]{1,0:T(8,128)(2,1)S(1)} %pad.4.own_ref, bf16[512,544]{1,0:T(8,128)(2,1)S(1)} %get-tuple-element.84.w_out_ref, bf16[512,640]{1,0:T(8,128)(2,1)S(1)} %get-tuple-element.89.hidden_ref, f32[512,1152]{1,0:T(8,128)} %get-tuple-element.85.slope_hbm, ...), custom_call_target="tpu_custom_call" | custom-call | flops 7130316800 | bytes 6291456 | tf_op jit(solution)/shard_map/near/pallas_call | solution.py:469
  33.9 4.1 %collective-permute-done.7.rest_1_ = bf16[2,272,128]{2,1,0:T(8,128)(2,1)S(1)} collective-permute-done((bf16[2,272,128]{2,1,0:T(8,128)(2,1)S(1)}, bf16[2,272,128]{2,1,0:T(8,128)(2,1)S(1)}, u32[]{:S(2)}, u32[]{:S(2)}) %collective-permute-start.7) | collective-permute-done | bytes 139296 | tf_op jit(solution)/shard_map/ppermute | solution.py:417
  38.0 3.7 %grads.1 = (f32[8,32,1024]{2,1,0:T(8,128)S(1)}, bf16[8,32,1024]{2,1,0:T(8,128)(2,1)S(1)}, f32[512,512]{1,0:T(8,128)S(1)}, bf16[64,512]{1,0:T(8,128)(2,1)S(1)}, b...) custom-call(s32[1]{0:T(128)} %bitcast.me_ref, bf16[512,544]{1,0:T(8,128)(2,1)S(1)} %get-tuple-element.84.w_out_ref, ...), custom_call_target="tpu_custom_call" | custom-call | tf_op jit(solution)/shard_map/grads/pallas_call | solution.py:493
  41.8 2.0 %outer.1 = (f32[8,32,640]{2,1,0:T(8,128)S(1)}, bf16[8,32,640]{2,1,0:T(8,128)(2,1)S(1)}) custom-call(s32[1]{0:T(128)} %bitcast.me_ref, bf16[512,512]{1,0:T(8,128)(2,1)S(1)} %get-tuple-element.114.hidden_ref, bf16[544,512]{1,0:T(8,128)(2,1)S(1)} %get-tuple-element.115.g_ref, f32[512,544]{1,0:T(8,128)} %get-tuple-element.116.near_hbm), custom_call_target="tpu_custom_call" | custom-call | flops 12834570240 | bytes 4194304 | tf_op jit(solution)/shard_map/outer/pallas_call | solution.py:517
  43.8 0.5 collective-permute-start.16
  44.3 0.1 fold.6
  44.5 0.3 collective-permute-start.11
  44.8 0.8 %collective-permute-done.16.came_ref = bf16[8,32,640]{2,1,0:T(8,128)(2,1)S(1)} collective-permute-done((bf16[8,32,640]{2,1,0:T(8,128)(2,1)S(1)}, bf16[8,32,640]{2,1,0:T(8,128)(2,1)S(1)}, u32[]{:S(2)}, u32[]{:S(2)}) %collective-permute-start.16) | collective-permute-done | bytes 327712 | tf_op jit(solution)/shard_map/ppermute | solution.py:350
  45.6 0.1 fold.9
  45.7 6.3 %collective-permute-start.17 = (bf16[4,32,640]{2,1,0:T(8,128)(2,1)S(1)}, bf16[4,32,640]{2,1,0:T(8,128)(2,1)S(1)}, u32[]{:S(2)}, u32[]{:S(2)}) collective-permute-start(bf16[4,32,640]{2,1,0:T(8,128)(2,1)S(1)} %get-tuple-element.122), channel_id=1, source_target_pairs={{0,4},{1,5},{2,6},{3,7},{4,0},{5,1},{6,2},{7,3},{8,12},{9,13},{10,... | collective-permute-start | bytes 491528 | tf_op jit(solution)/shard_map/ppermute | solution.py:350
  52.0 2.7 %collective-permute-start.12 = (bf16[64,512]{1,0:T(8,128)(2,1)S(1)}, bf16[64,512]{1,0:T(8,128)(2,1)S(1)}, u32[]{:S(2)}, u32[]{:S(2)}) collective-permute-start(bf16[64,512]{1,0:T(8,128)(2,1)S(1)} %get-tuple-element.104), channel_id=1, source_target_pairs={{1,0},{2,1},{3,2},{4,3},{5,4},{6,5},{7,6},{8,7},{9,8},{10,9},{11,1... | collective-permute-start | bytes 196616 | tf_op jit(solution)/shard_map/ppermute | solution.py:557
  54.7 2.0 %collective-permute-done.12.from_above_ref = bf16[64,512]{1,0:T(8,128)(2,1)S(1)} collective-permute-done((bf16[64,512]{1,0:T(8,128)(2,1)S(1)}, bf16[64,512]{1,0:T(8,128)(2,1)S(1)}, u32[]{:S(2)}, u32[]{:S(2)}) %collective-permute-start.12) | collective-permute-done | bytes 65568 | tf_op jit(solution)/shard_map/ppermute | solution.py:557
  56.7 4.4 %collective-permute-done.13.from_below_ref = bf16[64,512]{1,0:T(8,128)(2,1)S(1)} collective-permute-done((bf16[64,512]{1,0:T(8,128)(2,1)S(1)}, bf16[64,512]{1,0:T(8,128)(2,1)S(1)}, u32[]{:S(2)}, u32[]{:S(2)}) %collective-permute-start.13) | collective-permute-done | bytes 65568 | tf_op jit(solution)/shard_map/ppermute | solution.py:558
  61.4 4.8 %collective-permute-done.14.came_ref = bf16[2,32,1024]{2,1,0:T(8,128)(2,1)S(1)} collective-permute-done((bf16[2,32,1024]{2,1,0:T(8,128)(2,1)S(1)}, bf16[2,32,1024]{2,1,0:T(8,128)(2,1)S(1)}, u32[]{:S(2)}, u32[]{:S(2)}) %collective-permute-start.14) | collective-permute-done | bytes 131104 | tf_op jit(solution)/shard_map/ppermute | solution.py:350
  66.2 0.5 collective-permute-start.15
  66.7 2.6 %collective-permute-start.19 = (bf16[1,32,640]{2,1,0:T(8,128)(2,1)S(1)}, bf16[1,32,640]{2,1,0:T(8,128)(2,1)S(1)}, u32[]{:S(2)}, u32[]{:S(2)}) collective-permute-start(bf16[1,32,640]{2,1,0:T(8,128)(2,1)S(1)} %get-tuple-element.130), channel_id=1, source_target_pairs={{0,8},{1,9},{2,10},{3,11},{4,12},{5,13},{6,14},{7,15},{8,0},{9,1},... | collective-permute-start | bytes 122888 | tf_op jit(solution)/shard_map/ppermute | solution.py:350
  69.3 1.5 %rims.1 = f32[256,512]{1,0:T(8,128)} custom-call(f32[512,512]{1,0:T(8,128)S(1)} %get-tuple-element.99.sums_ref, bf16[64,512]{1,0:T(8,128)(2,1)S(1)} %collective-permute-done.13.from_below_ref, bf16[64,512]{1,0:T(8,128)(2,1)S(1)} %collective-permute-done.12.from_above_ref, bf16[512,512]{1,0:T(8,128)(2,1)S(1)} %copy-done.2, bf16[512,512]{1,0:T(8,128)(2,1)S(1)} %copy-done.3), custom_call_target="tpu_custom_call" | custom-call | flops 24159191040 | bytes 4194304 | tf_op jit(solution)/shard_map/rims/pallas_call | solution.py:571
  70.9 1.6 %collective-permute-done.19.refs_3_ = bf16[1,32,640]{2,1,0:T(8,128)(2,1)S(1)} collective-permute-done((bf16[1,32,640]{2,1,0:T(8,128)(2,1)S(1)}, bf16[1,32,640]{2,1,0:T(8,128)(2,1)S(1)}, u32[]{:S(2)}, u32[]{:S(2)}) %collective-permute-start.19) | collective-permute-done | bytes 40992 | tf_op jit(solution)/shard_map/ppermute | solution.py:350
  72.5 0.7 totals.1
  (39 shorter events, 0.7 us)
Async XLA Ops:
  0.6 23.1 %copy-start = (bf16[256,512]{1,0:T(8,128)(2,1)S(1)}, bf16[256,512]{1,0:T(8,128)(2,1)}, u32[]{:S(2)}) copy-start(bf16[256,512]{1,0:T(8,128)(2,1)} %feats_ref.3) | copy-start | bytes 786436
  0.6 23.1 %copy-start.1 = (bf16[512,529]{0,1:T(8,128)(2,1)S(1)}, bf16[512,529]{0,1:T(8,128)(2,1)}, u32[]{:S(2)}) copy-start(bf16[512,529]{0,1:T(8,128)(2,1)} %param.11) | copy-start | bytes 1625092
  0.7 23.1 %copy-start.2 = (bf16[512,512]{1,0:T(8,128)(2,1)S(1)}, bf16[512,512]{1,0:T(8,128)(2,1)}, u32[]{:S(2)}) copy-start(bf16[512,512]{1,0:T(8,128)(2,1)} %w_src_ref.3) | copy-start | bytes 1572868
  0.7 23.1 %copy-start.3 = (bf16[512,512]{1,0:T(8,128)(2,1)S(1)}, bf16[512,512]{1,0:T(8,128)(2,1)}, u32[]{:S(2)}) copy-start(bf16[512,512]{1,0:T(8,128)(2,1)} %w_dst_ref.3) | copy-start | bytes 1572868
  0.7 23.1 %copy-start.4 = (s32[2048]{0:T(1024)S(1)}, s32[2048]{0:T(1024)}, u32[]{:S(2)}) copy-start(s32[2048]{0:T(1024)} %param.13) | copy-start | bytes 24580
  0.7 23.1 %copy-start.5 = (s32[2048]{0:T(1024)S(1)}, s32[2048]{0:T(1024)}, u32[]{:S(2)}) copy-start(s32[2048]{0:T(1024)} %param.14) | copy-start | bytes 24580
  0.7 23.1 %copy-start.6 = (s32[2048]{0:T(1024)S(1)}, s32[2048]{0:T(1024)}, u32[]{:S(2)}) copy-start(s32[2048]{0:T(1024)} %param.15) | copy-start | bytes 24580
  4.0 8.5 %collective-permute-start = (bf16[8,272,128]{2,1,0:T(8,128)(2,1)S(1)}, bf16[8,272,128]{2,1,0:T(8,128)(2,1)S(1)}, u32[]{:S(2)}, u32[]{:S(2)}) collective-permute-start(bf16[8,272,128]{2,1,0:T(8,128)(2,1)S(1)} %get-tuple-element.70), channel_id=1, source_target_pairs={{0,1},{1,0},{2,3},{3,2},{4,5},{5,4},{6,7},{7,6},{8,9},{9,8},{10,11... | collective-permute-start | bytes 1671176 | tf_op jit(solution)/shard_map/ppermute | solution.py:350
  4.5 7.9 %collective-permute-start.1 = (bf16[64,512]{1,0:T(8,128)(2,1)}, bf16[64,512]{1,0:T(8,128)(2,1)}, u32[]{:S(2)}, u32[]{:S(2)}) collective-permute-start(bf16[64,512]{1,0:T(8,128)(2,1)} %get-tuple-element.71), channel_id=1, source_target_pairs={{0,1},{1,2},{2,3},{3,4},{4,5},{5,6},{6,7},{7,8},{8,9},{9,10},{10,1... | collective-permute-start | bytes 196616 | tf_op jit(solution)/shard_map/ppermute | solution.py:399
  4.6 7.9 %collective-permute-start.2 = (bf16[64,512]{1,0:T(8,128)(2,1)}, bf16[64,512]{1,0:T(8,128)(2,1)}, u32[]{:S(2)}, u32[]{:S(2)}) collective-permute-start(bf16[64,512]{1,0:T(8,128)(2,1)} %get-tuple-element.72), channel_id=1, source_target_pairs={{1,0},{2,1},{3,2},{4,3},{5,4},{6,5},{7,6},{8,7},{9,8},{10,9},{11,1... | collective-permute-start | bytes 196616 | tf_op jit(solution)/shard_map/ppermute | solution.py:400
  12.5 6.0 %collective-permute-start.4 = (bf16[2,272,128]{2,1,0:T(8,128)(2,1)S(1)}, bf16[2,272,128]{2,1,0:T(8,128)(2,1)S(1)}, u32[]{:S(2)}, u32[]{:S(2)}) collective-permute-start(bf16[2,272,128]{2,1,0:T(8,128)(2,1)S(1)} %get-tuple-element.75), channel_id=1, source_target_pairs={{0,2},{1,3},{2,0},{3,1},{4,6},{5,7},{6,4},{7,5},{8,10},{9,11},{10,... | collective-permute-start | bytes 417800 | tf_op jit(solution)/shard_map/ppermute | solution.py:417
  12.6 9.9 %collective-permute-start.3 = (bf16[2,272,128]{2,1,0:T(8,128)(2,1)S(1)}, bf16[2,272,128]{2,1,0:T(8,128)(2,1)S(1)}, u32[]{:S(2)}, u32[]{:S(2)}) collective-permute-start(bf16[2,272,128]{2,1,0:T(8,128)(2,1)S(1)} %get-tuple-element.74), channel_id=1, source_target_pairs={{0,4},{1,5},{2,6},{3,7},{4,0},{5,1},{6,2},{7,3},{8,12},{9,13},{10,... | collective-permute-start | bytes 417800 | tf_op jit(solution)/shard_map/ppermute | solution.py:417
  12.8 16.3 %collective-permute-start.5 = (bf16[2,272,128]{2,1,0:T(8,128)(2,1)S(1)}, bf16[2,272,128]{2,1,0:T(8,128)(2,1)S(1)}, u32[]{:S(2)}, u32[]{:S(2)}) collective-permute-start(bf16[2,272,128]{2,1,0:T(8,128)(2,1)S(1)} %get-tuple-element.93), channel_id=1, source_target_pairs={{0,6},{1,7},{2,4},{3,5},{4,2},{5,3},{6,0},{7,1},{8,14},{9,15},{10,... | collective-permute-start | bytes 417800 | tf_op jit(solution)/shard_map/ppermute | solution.py:417
  16.1 17.9 %collective-permute-start.6 = (bf16[2,272,128]{2,1,0:T(8,128)(2,1)S(1)}, bf16[2,272,128]{2,1,0:T(8,128)(2,1)S(1)}, u32[]{:S(2)}, u32[]{:S(2)}) collective-permute-start(bf16[2,272,128]{2,1,0:T(8,128)(2,1)S(1)} %get-tuple-element.95), channel_id=1, source_target_pairs={{0,8},{1,9},{2,10},{3,11},{4,12},{5,13},{6,14},{7,15},{8,0},{9,1},... | collective-permute-start | bytes 417800 | tf_op jit(solution)/shard_map/ppermute | solution.py:417
  16.7 21.3 %collective-permute-start.7 = (bf16[2,272,128]{2,1,0:T(8,128)(2,1)S(1)}, bf16[2,272,128]{2,1,0:T(8,128)(2,1)S(1)}, u32[]{:S(2)}, u32[]{:S(2)}) collective-permute-start(bf16[2,272,128]{2,1,0:T(8,128)(2,1)S(1)} %get-tuple-element.96), channel_id=1, source_target_pairs={{0,10},{1,11},{2,8},{3,9},{4,14},{5,15},{6,12},{7,13},{8,2},{9,3},... | collective-permute-start | bytes 417800 | tf_op jit(solution)/shard_map/ppermute | solution.py:417
  18.5 19.5 %collective-permute-start.8 = (bf16[2,272,128]{2,1,0:T(8,128)(2,1)S(1)}, bf16[2,272,128]{2,1,0:T(8,128)(2,1)S(1)}, u32[]{:S(2)}, u32[]{:S(2)}) collective-permute-start(bf16[2,272,128]{2,1,0:T(8,128)(2,1)S(1)} %get-tuple-element.97), channel_id=1, source_target_pairs={{0,12},{1,13},{2,14},{3,15},{4,8},{5,9},{6,10},{7,11},{8,4},{9,5},... | collective-permute-start | bytes 417800 | tf_op jit(solution)/shard_map/ppermute | solution.py:417
  22.5 15.5 %collective-permute-start.9 = (bf16[2,272,128]{2,1,0:T(8,128)(2,1)S(1)}, bf16[2,272,128]{2,1,0:T(8,128)(2,1)S(1)}, u32[]{:S(2)}, u32[]{:S(2)}) collective-permute-start(bf16[2,272,128]{2,1,0:T(8,128)(2,1)S(1)} %get-tuple-element.98), channel_id=1, source_target_pairs={{0,14},{1,15},{2,12},{3,13},{4,10},{5,11},{6,8},{7,9},{8,6},{9,7},... | collective-permute-start | bytes 417800 | tf_op jit(solution)/shard_map/ppermute | solution.py:417
  41.8 2.6 %collective-permute-start.10 = (bf16[8,32,1024]{2,1,0:T(8,128)(2,1)S(1)}, bf16[8,32,1024]{2,1,0:T(8,128)(2,1)S(1)}, u32[]{:S(2)}, u32[]{:S(2)}) collective-permute-start(bf16[8,32,1024]{2,1,0:T(8,128)(2,1)S(1)} %get-tuple-element.101), channel_id=1, source_target_pairs={{0,1},{1,0},{2,3},{3,2},{4,5},{5,4},{6,7},{7,6},{8,9},{9,8},{10,11... | collective-permute-start | bytes 1572872 | tf_op jit(solution)/shard_map/ppermute | solution.py:350
  43.8 1.8 %collective-permute-start.16 = (bf16[8,32,640]{2,1,0:T(8,128)(2,1)S(1)}, bf16[8,32,640]{2,1,0:T(8,128)(2,1)S(1)}, u32[]{:S(2)}, u32[]{:S(2)}) collective-permute-start(bf16[8,32,640]{2,1,0:T(8,128)(2,1)S(1)} %get-tuple-element.118), channel_id=1, source_target_pairs={{0,1},{1,0},{2,3},{3,2},{4,5},{5,4},{6,7},{7,6},{8,9},{9,8},{10,11... | collective-permute-start | bytes 983048 | tf_op jit(solution)/shard_map/ppermute | solution.py:350
  44.5 16.6 %collective-permute-start.11 = (bf16[4,32,1024]{2,1,0:T(8,128)(2,1)S(1)}, bf16[4,32,1024]{2,1,0:T(8,128)(2,1)S(1)}, u32[]{:S(2)}, u32[]{:S(2)}) collective-permute-start(bf16[4,32,1024]{2,1,0:T(8,128)(2,1)S(1)} %get-tuple-element.103), channel_id=1, source_target_pairs={{0,2},{1,3},{2,0},{3,1},{4,6},{5,7},{6,4},{7,5},{8,10},{9,11},{10,... | collective-permute-start | bytes 786440 | tf_op jit(solution)/shard_map/ppermute | solution.py:350
  45.7 15.6 %collective-permute-start.17 = (bf16[4,32,640]{2,1,0:T(8,128)(2,1)S(1)}, bf16[4,32,640]{2,1,0:T(8,128)(2,1)S(1)}, u32[]{:S(2)}, u32[]{:S(2)}) collective-permute-start(bf16[4,32,640]{2,1,0:T(8,128)(2,1)S(1)} %get-tuple-element.122), channel_id=1, source_target_pairs={{0,4},{1,5},{2,6},{3,7},{4,0},{5,1},{6,2},{7,3},{8,12},{9,13},{10,... | collective-permute-start | bytes 491528 | tf_op jit(solution)/shard_map/ppermute | solution.py:350
  52.0 4.7 %collective-permute-start.12 = (bf16[64,512]{1,0:T(8,128)(2,1)S(1)}, bf16[64,512]{1,0:T(8,128)(2,1)S(1)}, u32[]{:S(2)}, u32[]{:S(2)}) collective-permute-start(bf16[64,512]{1,0:T(8,128)(2,1)S(1)} %get-tuple-element.104), channel_id=1, source_target_pairs={{1,0},{2,1},{3,2},{4,3},{5,4},{6,5},{7,6},{8,7},{9,8},{10,9},{11,1... | collective-permute-start | bytes 196616 | tf_op jit(solution)/shard_map/ppermute | solution.py:557
  54.7 6.4 %collective-permute-start.13 = (bf16[64,512]{1,0:T(8,128)(2,1)S(1)}, bf16[64,512]{1,0:T(8,128)(2,1)S(1)}, u32[]{:S(2)}, u32[]{:S(2)}) collective-permute-start(bf16[64,512]{1,0:T(8,128)(2,1)S(1)} %get-tuple-element.105), channel_id=1, source_target_pairs={{0,1},{1,2},{2,3},{3,4},{4,5},{5,6},{6,7},{7,8},{8,9},{9,10},{10,1... | collective-permute-start | bytes 196616 | tf_op jit(solution)/shard_map/ppermute | solution.py:558
  61.2 5.0 %collective-permute-start.14 = (bf16[2,32,1024]{2,1,0:T(8,128)(2,1)S(1)}, bf16[2,32,1024]{2,1,0:T(8,128)(2,1)S(1)}, u32[]{:S(2)}, u32[]{:S(2)}) collective-permute-start(bf16[2,32,1024]{2,1,0:T(8,128)(2,1)S(1)} %get-tuple-element.111), channel_id=1, source_target_pairs={{0,4},{1,5},{2,6},{3,7},{4,0},{5,1},{6,2},{7,3},{8,12},{9,13},{10,... | collective-permute-start | bytes 393224 | tf_op jit(solution)/shard_map/ppermute | solution.py:350
  61.3 5.4 %collective-permute-start.18 = (bf16[2,32,640]{2,1,0:T(8,128)(2,1)S(1)}, bf16[2,32,640]{2,1,0:T(8,128)(2,1)S(1)}, u32[]{:S(2)}, u32[]{:S(2)}) collective-permute-start(bf16[2,32,640]{2,1,0:T(8,128)(2,1)S(1)} %get-tuple-element.126), channel_id=1, source_target_pairs={{0,2},{1,3},{2,0},{3,1},{4,6},{5,7},{6,4},{7,5},{8,10},{9,11},{10,... | collective-permute-start | bytes 245768 | tf_op jit(solution)/shard_map/ppermute | solution.py:350
  66.2 6.3 %collective-permute-start.15 = (bf16[1,32,1024]{2,1,0:T(8,128)(2,1)S(1)}, bf16[1,32,1024]{2,1,0:T(8,128)(2,1)S(1)}, u32[]{:S(2)}, u32[]{:S(2)}) collective-permute-start(bf16[1,32,1024]{2,1,0:T(8,128)(2,1)S(1)} %get-tuple-element.113), channel_id=1, source_target_pairs={{0,8},{1,9},{2,10},{3,11},{4,12},{5,13},{6,14},{7,15},{8,0},{9,1},... | collective-permute-start | bytes 196616 | tf_op jit(solution)/shard_map/ppermute | solution.py:350
  66.7 5.8 %collective-permute-start.19 = (bf16[1,32,640]{2,1,0:T(8,128)(2,1)S(1)}, bf16[1,32,640]{2,1,0:T(8,128)(2,1)S(1)}, u32[]{:S(2)}, u32[]{:S(2)}) collective-permute-start(bf16[1,32,640]{2,1,0:T(8,128)(2,1)S(1)} %get-tuple-element.130), channel_id=1, source_target_pairs={{0,8},{1,9},{2,10},{3,11},{4,12},{5,13},{6,14},{7,15},{8,0},{9,1},... | collective-permute-start | bytes 122888 | tf_op jit(solution)/shard_map/ppermute | solution.py:350

commit v9 on v8

--- a/solution.py
+++ b/solution.py
@@ -134,10 +134,18 @@
 
 
 def edge_kernel(
-    half, linked, near, far, me_ref, feats_ref, below_ref, above_ref, w_src_ref, w_dst_ref, w_out_ref, src_ref, dst_ref,
+    half, linked, near, far, me_ref, feats_hbm, w_src_hbm, w_dst_hbm, w_out_hbm, below_ref, above_ref, src_ref, dst_ref,
     live_ref, onehot_hbm, slope_hbm, ext_hbm, near_hidden_ref, far_hidden_ref, w_wide_ref,
-    onehot_ref, slope_ref, ext_ref, w_rows_ref, sems,
+    onehot_ref, slope_ref, ext_ref, w_rows_ref, feats_ref, w_src_ref, w_dst_ref, w_out_ref, sems, in_sems,
 ):
+    inputs = [
+        pltpu.make_async_copy(hbm, ref, in_sems.at[index])
+        for index, (hbm, ref) in enumerate(
+            ((feats_hbm, feats_ref), (w_src_hbm, w_src_ref), (w_dst_hbm, w_dst_ref), (w_out_hbm, w_out_ref))
+        )
+    ]
+    for copy in inputs:
+        copy.start()
     me = me_ref[0]
     mols = feats_ref.shape[0]
     reach = below_ref.shape[0]
@@ -152,14 +160,6 @@
         copy.start()
         copies.append(copy)
 
-    feats = feats_ref[...]
-    ext = jnp.concatenate([feats, below_ref[...], above_ref[...]], axis=0)
-    ext_ref[...] = ext.T
-    send(ext_ref, ext_hbm)
-    proj_src = mm(feats, w_src_ref[...])
-    proj_dst = mm(ext, w_dst_ref[...])
-    proj = jnp.concatenate([proj_src, proj_dst], axis=0).T
-    high, low = halves(proj)
     mol_src = lax.broadcasted_iota(jnp.int32, (mols, LANES), 0)
     mol_dst = lax.broadcasted_iota(jnp.int32, (wide, LANES), 0)
     lists = [slot_rows(ref, me, half, linked, near, far) for ref in (src_ref, dst_ref, live_ref)]
@@ -171,6 +171,16 @@
         one_dst = jnp.where(mol_dst == dst, 1.0, 0.0).astype(BF16)
         here = pl.ds(tile * LANES, LANES)
         onehot_ref[:, here] = jnp.concatenate([one_src, one_dst], axis=0)
+    for copy in inputs[:3]:
+        copy.wait()
+    feats = feats_ref[...]
+    ext = jnp.concatenate([feats, below_ref[...], above_ref[...]], axis=0)
+    ext_ref[...] = ext.T
+    send(ext_ref, ext_hbm)
+    proj_src = mm(feats, w_src_ref[...])
+    proj_dst = mm(ext, w_dst_ref[...])
+    proj = jnp.concatenate([proj_src, proj_dst], axis=0).T
+    high, low = halves(proj)
     for first, last in slot_tiles(near_slots) + [(near_slots + f, near_slots + l) for f, l in slot_tiles(slots - near_slots)]:
         here = pl.ds(first, last - first)
         send(onehot_ref.at[:, here], onehot_hbm.at[:, here])
@@ -184,6 +194,7 @@
             far_hidden_ref[:, pl.ds(first - near_slots, last - first)] = hidden
         slope_ref[:, here] = sigma * (1.0 + pre * (1.0 - sigma))
         send(slope_ref.at[:, here], slope_hbm.at[:, here])
+    inputs[3].wait()
     whole = entries // LANES * LANES
     w_rows_ref[whole:] = jnp.zeros((w_rows_ref.shape[0] - whole, w_rows_ref.shape[1]), BF16)
     w_rows_ref[:whole] = w_out_ref[:whole]
@@ -413,10 +424,11 @@
         )(even, other)
         quarter = slabs // 4
         came = {0: messages[0]}
-        for k in (*range(1, quarter - 1), *range(quarter, 2 * quarter), *range(max(quarter - 1, 1), quarter)):
-            came[k] = lax.ppermute(messages[k], "space", [(i, i ^ (2 * k)) for i in range(slabs)])
-        for k in range(1, quarter - 1):
-            came[k], below, above, me = lax.optimization_barrier((came[k], below, above, me))
+        for k in range(1, 2 * quarter):
+            message = messages[k]
+            if k == quarter - 1:
+                message = lax.optimization_barrier((message, came[1], came[2]))[0]
+            came[k] = lax.ppermute(message, "space", [(i, i ^ (2 * k)) for i in range(slabs)])
         near = tuple(range(2 * quarter))
         far = tuple(range(2 * quarter, slabs))
         came_near = [came[k] for k in range(quarter)]
@@ -442,14 +454,19 @@
             jax.ShapeDtypeStruct((width, far_slots), BF16),
             jax.ShapeDtypeStruct((width, entries_wide), BF16),
         ),
-        in_specs=[smem] + vmem(9),
+        in_specs=[smem] + [hbm] * 4 + vmem(5),
         out_specs=(hbm,) * 3 + tuple(vmem(3)),
         scratch_shapes=[
             pltpu.VMEM((mols + wide, slots), BF16),
             pltpu.VMEM((width, slots), F32),
             pltpu.VMEM((width, wide), BF16),
             pltpu.VMEM((entries_wide, width), BF16),
+            pltpu.VMEM((mols, width), BF16),
+            pltpu.VMEM((width, width), BF16),
+            pltpu.VMEM((width, width), BF16),
+            pltpu.VMEM((entries, width), BF16),
             pltpu.SemaphoreType.DMA((2 * pieces + 1,)),
+            pltpu.SemaphoreType.DMA((4,)),
         ],
         compiler_params=big,
         name="edges",
@@ -458,7 +475,7 @@
             transcendentals=width * slots,
         ),
     )(
-        me, mol_feats, below, above, w_src, w_dst, w_out.T,
+        me, in_hbm(mol_feats), in_hbm(w_src), in_hbm(w_dst), in_hbm(w_out.T), below, above,
         edge_src.reshape(slabs, cap), edge_dst.reshape(slabs, cap), edge_live.reshape(slabs, cap),
     )
     onehot, slope, ext = in_hbm(onehot), in_hbm(slope), in_hbm(ext)

time: 73.5 us -> 71.4 us (0.971)
  starting transfers between devices: 28.7 us -> 20.8 us
  waiting for transfers between devices: 20 us -> 26.2 us
    ppermute x9, starting transfers between devices: 11 us -> 4.49 us  [swap(): lax.ppermute(block, 'space', [(i, i ^ 1 << bit) for i in range(slabs)])]
    ppermute x7, waiting for transfers between devices: 5.89 us -> 11.7 us  [on_device(): lax.ppermute(message, 'space', [(i, i ^ 2 * k) for i in range(slabs)])]
    ppermute x7, starting transfers between devices: 9.38 us -> 7.97 us  [on_device(): lax.ppermute(message, 'space', [(i, i ^ 2 * k) for i in range(slabs)])]
    pallas_call x1, Pallas kernels: 3.26 us -> 2.5 us  [on_device(): pl.pallas_call(functools.partial(pack_kernel, rows, half, linked), out_sh...]
  transfers between devices with their start and end apart: 20 -> 20, of which waited for: 8 -> 8; matrix products, arithmetic and copies ran while one was open for 2% -> 2% of each run, Pallas kernels for 19% -> 20%
where the time goes in v9:
time: 71.4 us; the launch traced here: 71.1 us
  waiting for transfers between devices  26.2 us (37%)
  Pallas kernels  21.6 us (30%)
  starting transfers between devices  20.8 us (29%)
  local copies, waits for them, and re-layouts  1.78 us (2%)
  between operations  0.85 us (1%)
    ppermute x7, waiting for transfers between devices, on_device(): lax.ppermute(message, 'space', [(i, i ^ 2 * k) for i in range(slabs)])  11.7 us
    ppermute x7, starting transfers between devices, on_device(): lax.ppermute(message, 'space', [(i, i ^ 2 * k) for i in range(slabs)])  7.97 us
    ppermute x9, waiting for transfers between devices, swap(): lax.ppermute(block, 'space', [(i, i ^ 1 << bit) for i in range(slabs)])  7.93 us
    pallas_call x1, Pallas kernels, on_device(): pl.pallas_call(functools.partial(edge_kernel, half, linked, near, far), o...  5.91 us
    ppermute x1, starting transfers between devices, on_device(): above = lax.ppermute(low, 'space', down)  5.61 us
    pallas_call x1, Pallas kernels, on_device(): pl.pallas_call(functools.partial(near_kernel, half), out_shape=(pltpu.HBM...  4.78 us
    ppermute x9, starting transfers between devices, swap(): lax.ppermute(block, 'space', [(i, i ^ 1 << bit) for i in range(slabs)])  4.49 us
    ppermute x1, waiting for transfers between devices, on_device(): from_below = lax.ppermute(upper, 'space', up)  4.04 us
  transfers between devices with their start and end apart: 20, of which 8 were waited for; matrix products, arithmetic and copies ran while one was open for 2% of the time, Pallas kernels for 20%

profile of v9, /device:TPU:0, one launch (start us, length us, event | category | flops | bytes accessed | tf_op | source)
XLA Modules:
  0.0 71.1 jit_solution(13396082773218486736)
XLA Ops:
  0.7 2.5 %pack.1 = (bf16[8,272,128]{2,1,0:T(8,128)(2,1)S(1)}, bf16[8,272,128]{2,1,0:T(8,128)(2,1)S(1)}, bf16[64,512]{1,0:T(8,128)(2,1)S(1)}, bf16[64,512]{1,0:T(8,128)(2,1)S(1)}) custom-call(s32[1]{0:T(128)} %bitcast.me_ref, bf16[256,512]{1,0:T(8,128)(2,1)} %feats_hbm.1, bf16[529,16,128]{2,1,0:T(8,128)(2,1)} %bitcast.16), custom_call_target="tpu_custom_call" | custom-call | tf_op jit(solution)/shard_map/pack/pallas_call | solution.py:392
  3.2 0.5 collective-permute-start
  3.8 5.6 %collective-permute-start.2 = (bf16[64,512]{1,0:T(8,128)(2,1)S(1)}, bf16[64,512]{1,0:T(8,128)(2,1)S(1)}, u32[]{:S(2)}, u32[]{:S(2)}) collective-permute-start(bf16[64,512]{1,0:T(8,128)(2,1)S(1)} %get-tuple-element.64), channel_id=1, source_target_pairs={{1,0},{2,1},{3,2},{4,3},{5,4},{6,5},{7,6},{8,7},{9,8},{10,9},{11,1... | collective-permute-start | bytes 196616 | tf_op jit(solution)/shard_map/ppermute | solution.py:411
  9.4 1.7 %constant_dynamic-slice_fusion = bf16[1,1,64,529]{2,1,3,0:T(2,128)(2,1)S(1)} fusion(bf16[1,16,128,529]{2,1,3,0:T(8,128)(2,1)} %param.12, s32[]{:T(128)S(6)} %select_n.4, s32[]{:T(128)S(6)} %add.7), kind=kLoop, calls=%fused_computation.1 | loop fusion | bytes 135432 | tf_op jit(solution)/shard_map/slice | solution.py:412
  11.1 0.2 collective-permute-done.1.below_ref
  11.3 0.1 join.1
  11.4 0.1 collective-permute-start.3
  11.5 0.2 collective-permute-start.4
  11.7 2.6 %collective-permute-start.6 = (bf16[2,272,128]{2,1,0:T(8,128)(2,1)S(1)}, bf16[2,272,128]{2,1,0:T(8,128)(2,1)S(1)}, u32[]{:S(2)}, u32[]{:S(2)}) collective-permute-start(bf16[2,272,128]{2,1,0:T(8,128)(2,1)S(1)} %get-tuple-element.81), channel_id=1, source_target_pairs={{0,8},{1,9},{2,10},{3,11},{4,12},{5,13},{6,14},{7,15},{8,0},{9,1},... | collective-permute-start | bytes 417800 | tf_op jit(solution)/shard_map/ppermute | solution.py:431
  14.3 1.6 %collective-permute-start.7 = (bf16[2,272,128]{2,1,0:T(8,128)(2,1)S(1)}, bf16[2,272,128]{2,1,0:T(8,128)(2,1)S(1)}, u32[]{:S(2)}, u32[]{:S(2)}) collective-permute-start(bf16[2,272,128]{2,1,0:T(8,128)(2,1)S(1)} %get-tuple-element.82), channel_id=1, source_target_pairs={{0,10},{1,11},{2,8},{3,9},{4,14},{5,15},{6,12},{7,13},{8,2},{9,3},... | collective-permute-start | bytes 417800 | tf_op jit(solution)/shard_map/ppermute | solution.py:431
  15.9 2.1 %collective-permute-start.8 = (bf16[2,272,128]{2,1,0:T(8,128)(2,1)S(1)}, bf16[2,272,128]{2,1,0:T(8,128)(2,1)S(1)}, u32[]{:S(2)}, u32[]{:S(2)}) collective-permute-start(bf16[2,272,128]{2,1,0:T(8,128)(2,1)S(1)} %get-tuple-element.83), channel_id=1, source_target_pairs={{0,12},{1,13},{2,14},{3,15},{4,8},{5,9},{6,10},{7,11},{8,4},{9,5},... | collective-permute-start | bytes 417800 | tf_op jit(solution)/shard_map/ppermute | solution.py:431
  17.9 1.4 %collective-permute-start.9 = (bf16[2,272,128]{2,1,0:T(8,128)(2,1)S(1)}, bf16[2,272,128]{2,1,0:T(8,128)(2,1)S(1)}, u32[]{:S(2)}, u32[]{:S(2)}) collective-permute-start(bf16[2,272,128]{2,1,0:T(8,128)(2,1)S(1)} %get-tuple-element.84), channel_id=1, source_target_pairs={{0,14},{1,15},{2,12},{3,13},{4,10},{5,11},{6,8},{7,9},{8,6},{9,7},... | collective-permute-start | bytes 417800 | tf_op jit(solution)/shard_map/ppermute | solution.py:431
  19.3 1.4 %collective-permute-done.4.rest_2_ = bf16[2,272,128]{2,1,0:T(8,128)(2,1)S(1)} collective-permute-done((bf16[2,272,128]{2,1,0:T(8,128)(2,1)S(1)}, bf16[2,272,128]{2,1,0:T(8,128)(2,1)S(1)}, u32[]{:S(2)}, u32[]{:S(2)}) %collective-permute-start.4) | collective-permute-done | bytes 139296 | tf_op jit(solution)/shard_map/ppermute | solution.py:431
  20.8 5.9 %edges.1 = (bf16[640,1152]{1,0:T(8,128)(2,1)}, f32[512,1152]{1,0:T(8,128)}, bf16[512,384]{1,0:T(8,128)(2,1)}, bf16[512,640]{1,0:T(8,128)(2,1)S(1)}, bf16[512,512...) custom-call(s32[1]{0:T(128)} %bitcast.me_ref, bf16[256,512]{1,0:T(8,128)(2,1)} %feats_hbm.1, bf16[512,512]{1,0:T(8,128)(2,1)} %w_src_ref.1, ...), custom_call_target="tpu_custom_call" | custom-call | flops 30198988800 | bytes 8388608 | tf_op jit(solution)/shard_map/edges/pallas_call | solution.py:447
  26.7 10.2 %collective-permute-done.5.rest_3_ = bf16[2,272,128]{2,1,0:T(8,128)(2,1)S(1)} collective-permute-done((bf16[2,272,128]{2,1,0:T(8,128)(2,1)S(1)}, bf16[2,272,128]{2,1,0:T(8,128)(2,1)S(1)}, u32[]{:S(2)}, u32[]{:S(2)}) %collective-permute-start.5) | collective-permute-done | bytes 139296 | tf_op jit(solution)/shard_map/ppermute | solution.py:431
  37.0 4.8 %near.1 = (f32[640,512]{1,0:T(8,128)}, f32[512,544]{1,0:T(8,128)}) custom-call(bf16[544,128]{1,0:T(8,128)(2,1)S(1)} %pad.4.own_ref, bf16[512,544]{1,0:T(8,128)(2,1)S(1)} %get-tuple-element.67.w_out_ref, bf16[512,640]{1,0:T(8,128)(2,1)S(1)} %get-tuple-element.72.hidden_ref, f32[512,1152]{1,0:T(8,128)} %get-tuple-element.68.slope_hbm, ...), custom_call_target="tpu_custom_call" | custom-call | flops 7130316800 | bytes 6291456 | tf_op jit(solution)/shard_map/near/pallas_call | solution.py:486
  41.8 3.8 %grads.1 = (f32[8,32,1024]{2,1,0:T(8,128)S(1)}, bf16[8,32,1024]{2,1,0:T(8,128)(2,1)S(1)}, f32[512,512]{1,0:T(8,128)S(1)}, bf16[64,512]{1,0:T(8,128)(2,1)S(1)}, b...) custom-call(s32[1]{0:T(128)} %bitcast.me_ref, bf16[512,544]{1,0:T(8,128)(2,1)S(1)} %get-tuple-element.67.w_out_ref, ...), custom_call_target="tpu_custom_call" | custom-call | tf_op jit(solution)/shard_map/grads/pallas_call | solution.py:510
  45.6 1.9 %outer.1 = (f32[8,32,640]{2,1,0:T(8,128)S(1)}, bf16[8,32,640]{2,1,0:T(8,128)(2,1)S(1)}) custom-call(s32[1]{0:T(128)} %bitcast.me_ref, bf16[512,512]{1,0:T(8,128)(2,1)S(1)} %get-tuple-element.100.hidden_ref, bf16[544,512]{1,0:T(8,128)(2,1)S(1)} %get-tuple-element.101.g_ref, f32[512,544]{1,0:T(8,128)} %get-tuple-element.102.near_hbm), custom_call_target="tpu_custom_call" | custom-call | flops 12834570240 | bytes 4194304 | tf_op jit(solution)/shard_map/outer/pallas_call | solution.py:534
  47.6 0.6 collective-permute-start.16
  48.2 0.1 fold.6
  48.3 0.1 collective-permute-start.11
  48.4 1.0 %collective-permute-done.16.came_ref = bf16[8,32,640]{2,1,0:T(8,128)(2,1)S(1)} collective-permute-done((bf16[8,32,640]{2,1,0:T(8,128)(2,1)S(1)}, bf16[8,32,640]{2,1,0:T(8,128)(2,1)S(1)}, u32[]{:S(2)}, u32[]{:S(2)}) %collective-permute-start.16) | collective-permute-done | bytes 327712 | tf_op jit(solution)/shard_map/ppermute | solution.py:361
  49.4 0.1 fold.9
  49.6 2.6 %collective-permute-start.12 = (bf16[64,512]{1,0:T(8,128)(2,1)S(1)}, bf16[64,512]{1,0:T(8,128)(2,1)S(1)}, u32[]{:S(2)}, u32[]{:S(2)}) collective-permute-start(bf16[64,512]{1,0:T(8,128)(2,1)S(1)} %get-tuple-element.90), channel_id=1, source_target_pairs={{1,0},{2,1},{3,2},{4,3},{5,4},{6,5},{7,6},{8,7},{9,8},{10,9},{11,1... | collective-permute-start | bytes 196616 | tf_op jit(solution)/shard_map/ppermute | solution.py:574
  52.2 2.3 %collective-permute-done.12.from_above_ref = bf16[64,512]{1,0:T(8,128)(2,1)S(1)} collective-permute-done((bf16[64,512]{1,0:T(8,128)(2,1)S(1)}, bf16[64,512]{1,0:T(8,128)(2,1)S(1)}, u32[]{:S(2)}, u32[]{:S(2)}) %collective-permute-start.12) | collective-permute-done | bytes 65568 | tf_op jit(solution)/shard_map/ppermute | solution.py:574
  54.5 4.0 %collective-permute-done.13.from_below_ref = bf16[64,512]{1,0:T(8,128)(2,1)S(1)} collective-permute-done((bf16[64,512]{1,0:T(8,128)(2,1)S(1)}, bf16[64,512]{1,0:T(8,128)(2,1)S(1)}, u32[]{:S(2)}, u32[]{:S(2)}) %collective-permute-start.13) | collective-permute-done | bytes 65568 | tf_op jit(solution)/shard_map/ppermute | solution.py:575
  58.9 4.8 %collective-permute-done.14.came_ref = bf16[2,32,1024]{2,1,0:T(8,128)(2,1)S(1)} collective-permute-done((bf16[2,32,1024]{2,1,0:T(8,128)(2,1)S(1)}, bf16[2,32,1024]{2,1,0:T(8,128)(2,1)S(1)}, u32[]{:S(2)}, u32[]{:S(2)}) %collective-permute-start.14) | collective-permute-done | bytes 131104 | tf_op jit(solution)/shard_map/ppermute | solution.py:361
  63.7 0.9 %collective-permute-start.15 = (bf16[1,32,1024]{2,1,0:T(8,128)(2,1)S(1)}, bf16[1,32,1024]{2,1,0:T(8,128)(2,1)S(1)}, u32[]{:S(2)}, u32[]{:S(2)}) collective-permute-start(bf16[1,32,1024]{2,1,0:T(8,128)(2,1)S(1)} %get-tuple-element.99), channel_id=1, source_target_pairs={{0,8},{1,9},{2,10},{3,11},{4,12},{5,13},{6,14},{7,15},{8,0},{9,1},... | collective-permute-start | bytes 196616 | tf_op jit(solution)/shard_map/ppermute | solution.py:361
  64.7 2.1 %collective-permute-start.19 = (bf16[1,32,640]{2,1,0:T(8,128)(2,1)S(1)}, bf16[1,32,640]{2,1,0:T(8,128)(2,1)S(1)}, u32[]{:S(2)}, u32[]{:S(2)}) collective-permute-start(bf16[1,32,640]{2,1,0:T(8,128)(2,1)S(1)} %get-tuple-element.116), channel_id=1, source_target_pairs={{0,8},{1,9},{2,10},{3,11},{4,12},{5,13},{6,14},{7,15},{8,0},{9,1},... | collective-permute-start | bytes 122888 | tf_op jit(solution)/shard_map/ppermute | solution.py:361
  66.8 1.5 %rims.1 = f32[256,512]{1,0:T(8,128)} custom-call(f32[512,512]{1,0:T(8,128)S(1)} %get-tuple-element.85.sums_ref, bf16[64,512]{1,0:T(8,128)(2,1)S(1)} %collective-permute-done.13.from_below_ref, bf16[64,512]{1,0:T(8,128)(2,1)S(1)} %collective-permute-done.12.from_above_ref, bf16[512,512]{1,0:T(8,128)(2,1)S(1)} %copy-done, bf16[512,512]{1,0:T(8,128)(2,1)S(1)} %copy-done.1), custom_call_target="tpu_custom_call" | custom-call | flops 24159191040 | bytes 4194304 | tf_op jit(solution)/shard_map/rims/pallas_call | solution.py:588
  68.4 2.1 %collective-permute-done.19.refs_3_ = bf16[1,32,640]{2,1,0:T(8,128)(2,1)S(1)} collective-permute-done((bf16[1,32,640]{2,1,0:T(8,128)(2,1)S(1)}, bf16[1,32,640]{2,1,0:T(8,128)(2,1)S(1)}, u32[]{:S(2)}, u32[]{:S(2)}) %collective-permute-start.19) | collective-permute-done | bytes 40992 | tf_op jit(solution)/shard_map/ppermute | solution.py:361
  70.4 0.7 totals.1
  (35 shorter events, 0.7 us)
Async XLA Ops:
  0.6 20.2 %copy-start.2 = (s32[2048]{0:T(1024)S(1)}, s32[2048]{0:T(1024)}, u32[]{:S(2)}) copy-start(s32[2048]{0:T(1024)} %param.13) | copy-start | bytes 24580
  0.6 20.2 %copy-start.3 = (s32[2048]{0:T(1024)S(1)}, s32[2048]{0:T(1024)}, u32[]{:S(2)}) copy-start(s32[2048]{0:T(1024)} %param.14) | copy-start | bytes 24580
  0.7 20.2 %copy-start.4 = (s32[2048]{0:T(1024)S(1)}, s32[2048]{0:T(1024)}, u32[]{:S(2)}) copy-start(s32[2048]{0:T(1024)} %param.15) | copy-start | bytes 24580
  3.2 8.1 %collective-permute-start = (bf16[8,272,128]{2,1,0:T(8,128)(2,1)S(1)}, bf16[8,272,128]{2,1,0:T(8,128)(2,1)S(1)}, u32[]{:S(2)}, u32[]{:S(2)}) collective-permute-start(bf16[8,272,128]{2,1,0:T(8,128)(2,1)S(1)} %get-tuple-element.62), channel_id=1, source_target_pairs={{0,1},{1,0},{2,3},{3,2},{4,5},{5,4},{6,7},{7,6},{8,9},{9,8},{10,11... | collective-permute-start | bytes 1671176 | tf_op jit(solution)/shard_map/ppermute | solution.py:361
  3.7 7.6 %collective-permute-start.1 = (bf16[64,512]{1,0:T(8,128)(2,1)S(1)}, bf16[64,512]{1,0:T(8,128)(2,1)S(1)}, u32[]{:S(2)}, u32[]{:S(2)}) collective-permute-start(bf16[64,512]{1,0:T(8,128)(2,1)S(1)} %get-tuple-element.63), channel_id=1, source_target_pairs={{0,1},{1,2},{2,3},{3,4},{4,5},{5,6},{6,7},{7,8},{8,9},{9,10},{10,1... | collective-permute-start | bytes 196616 | tf_op jit(solution)/shard_map/ppermute | solution.py:410
  3.8 7.6 %collective-permute-start.2 = (bf16[64,512]{1,0:T(8,128)(2,1)S(1)}, bf16[64,512]{1,0:T(8,128)(2,1)S(1)}, u32[]{:S(2)}, u32[]{:S(2)}) collective-permute-start(bf16[64,512]{1,0:T(8,128)(2,1)S(1)} %get-tuple-element.64), channel_id=1, source_target_pairs={{1,0},{2,1},{3,2},{4,3},{5,4},{6,5},{7,6},{8,7},{9,8},{10,9},{11,1... | collective-permute-start | bytes 196616 | tf_op jit(solution)/shard_map/ppermute | solution.py:411
  11.4 6.5 %collective-permute-start.3 = (bf16[2,272,128]{2,1,0:T(8,128)(2,1)S(1)}, bf16[2,272,128]{2,1,0:T(8,128)(2,1)S(1)}, u32[]{:S(2)}, u32[]{:S(2)}) collective-permute-start(bf16[2,272,128]{2,1,0:T(8,128)(2,1)S(1)} %get-tuple-element.76), channel_id=1, source_target_pairs={{0,2},{1,3},{2,0},{3,1},{4,6},{5,7},{6,4},{7,5},{8,10},{9,11},{10,... | collective-permute-start | bytes 417800 | tf_op jit(solution)/shard_map/ppermute | solution.py:431
  11.5 9.3 %collective-permute-start.4 = (bf16[2,272,128]{2,1,0:T(8,128)(2,1)S(1)}, bf16[2,272,128]{2,1,0:T(8,128)(2,1)S(1)}, u32[]{:S(2)}, u32[]{:S(2)}) collective-permute-start(bf16[2,272,128]{2,1,0:T(8,128)(2,1)S(1)} %get-tuple-element.77), channel_id=1, source_target_pairs={{0,4},{1,5},{2,6},{3,7},{4,0},{5,1},{6,2},{7,3},{8,12},{9,13},{10,... | collective-permute-start | bytes 417800 | tf_op jit(solution)/shard_map/ppermute | solution.py:431
  11.7 30.1 %collective-permute-start.6 = (bf16[2,272,128]{2,1,0:T(8,128)(2,1)S(1)}, bf16[2,272,128]{2,1,0:T(8,128)(2,1)S(1)}, u32[]{:S(2)}, u32[]{:S(2)}) collective-permute-start(bf16[2,272,128]{2,1,0:T(8,128)(2,1)S(1)} %get-tuple-element.81), channel_id=1, source_target_pairs={{0,8},{1,9},{2,10},{3,11},{4,12},{5,13},{6,14},{7,15},{8,0},{9,1},... | collective-permute-start | bytes 417800 | tf_op jit(solution)/shard_map/ppermute | solution.py:431
  14.3 27.5 %collective-permute-start.7 = (bf16[2,272,128]{2,1,0:T(8,128)(2,1)S(1)}, bf16[2,272,128]{2,1,0:T(8,128)(2,1)S(1)}, u32[]{:S(2)}, u32[]{:S(2)}) collective-permute-start(bf16[2,272,128]{2,1,0:T(8,128)(2,1)S(1)} %get-tuple-element.82), channel_id=1, source_target_pairs={{0,10},{1,11},{2,8},{3,9},{4,14},{5,15},{6,12},{7,13},{8,2},{9,3},... | collective-permute-start | bytes 417800 | tf_op jit(solution)/shard_map/ppermute | solution.py:431
  15.9 25.9 %collective-permute-start.8 = (bf16[2,272,128]{2,1,0:T(8,128)(2,1)S(1)}, bf16[2,272,128]{2,1,0:T(8,128)(2,1)S(1)}, u32[]{:S(2)}, u32[]{:S(2)}) collective-permute-start(bf16[2,272,128]{2,1,0:T(8,128)(2,1)S(1)} %get-tuple-element.83), channel_id=1, source_target_pairs={{0,12},{1,13},{2,14},{3,15},{4,8},{5,9},{6,10},{7,11},{8,4},{9,5},... | collective-permute-start | bytes 417800 | tf_op jit(solution)/shard_map/ppermute | solution.py:431
  17.9 23.9 %collective-permute-start.9 = (bf16[2,272,128]{2,1,0:T(8,128)(2,1)S(1)}, bf16[2,272,128]{2,1,0:T(8,128)(2,1)S(1)}, u32[]{:S(2)}, u32[]{:S(2)}) collective-permute-start(bf16[2,272,128]{2,1,0:T(8,128)(2,1)S(1)} %get-tuple-element.84), channel_id=1, source_target_pairs={{0,14},{1,15},{2,12},{3,13},{4,10},{5,11},{6,8},{7,9},{8,6},{9,7},... | collective-permute-start | bytes 417800 | tf_op jit(solution)/shard_map/ppermute | solution.py:431
  20.8 16.2 %collective-permute-start.5 = (bf16[2,272,128]{2,1,0:T(8,128)(2,1)S(1)}, bf16[2,272,128]{2,1,0:T(8,128)(2,1)S(1)}, u32[]{:S(2)}, u32[]{:S(2)}) collective-permute-start(bf16[2,272,128]{2,1,0:T(8,128)(2,1)S(1)} %get-tuple-element.79), channel_id=1, source_target_pairs={{0,6},{1,7},{2,4},{3,5},{4,2},{5,3},{6,0},{7,1},{8,14},{9,15},{10,... | collective-permute-start | bytes 417800 | tf_op jit(solution)/shard_map/ppermute | solution.py:431
  45.6 2.6 %collective-permute-start.10 = (bf16[8,32,1024]{2,1,0:T(8,128)(2,1)S(1)}, bf16[8,32,1024]{2,1,0:T(8,128)(2,1)S(1)}, u32[]{:S(2)}, u32[]{:S(2)}) collective-permute-start(bf16[8,32,1024]{2,1,0:T(8,128)(2,1)S(1)} %get-tuple-element.87), channel_id=1, source_target_pairs={{0,1},{1,0},{2,3},{3,2},{4,5},{5,4},{6,7},{7,6},{8,9},{9,8},{10,11... | collective-permute-start | bytes 1572872 | tf_op jit(solution)/shard_map/ppermute | solution.py:361
  47.6 1.8 %collective-permute-start.16 = (bf16[8,32,640]{2,1,0:T(8,128)(2,1)S(1)}, bf16[8,32,640]{2,1,0:T(8,128)(2,1)S(1)}, u32[]{:S(2)}, u32[]{:S(2)}) collective-permute-start(bf16[8,32,640]{2,1,0:T(8,128)(2,1)S(1)} %get-tuple-element.104), channel_id=1, source_target_pairs={{0,1},{1,0},{2,3},{3,2},{4,5},{5,4},{6,7},{7,6},{8,9},{9,8},{10,11... | collective-permute-start | bytes 983048 | tf_op jit(solution)/shard_map/ppermute | solution.py:361
  48.2 18.7 %copy-start = (bf16[512,512]{1,0:T(8,128)(2,1)S(1)}, bf16[512,512]{1,0:T(8,128)(2,1)}, u32[]{:S(2)}) copy-start(bf16[512,512]{1,0:T(8,128)(2,1)} %w_src_ref.1) | copy-start | bytes 1572868
  48.2 18.7 %copy-start.1 = (bf16[512,512]{1,0:T(8,128)(2,1)S(1)}, bf16[512,512]{1,0:T(8,128)(2,1)}, u32[]{:S(2)}) copy-start(bf16[512,512]{1,0:T(8,128)(2,1)} %w_dst_ref.1) | copy-start | bytes 1572868
  48.3 10.3 %collective-permute-start.11 = (bf16[4,32,1024]{2,1,0:T(8,128)(2,1)S(1)}, bf16[4,32,1024]{2,1,0:T(8,128)(2,1)S(1)}, u32[]{:S(2)}, u32[]{:S(2)}) collective-permute-start(bf16[4,32,1024]{2,1,0:T(8,128)(2,1)S(1)} %get-tuple-element.89), channel_id=1, source_target_pairs={{0,2},{1,3},{2,0},{3,1},{4,6},{5,7},{6,4},{7,5},{8,10},{9,11},{10,... | collective-permute-start | bytes 786440 | tf_op jit(solution)/shard_map/ppermute | solution.py:361
  49.5 9.2 %collective-permute-start.17 = (bf16[4,32,640]{2,1,0:T(8,128)(2,1)S(1)}, bf16[4,32,640]{2,1,0:T(8,128)(2,1)S(1)}, u32[]{:S(2)}, u32[]{:S(2)}) collective-permute-start(bf16[4,32,640]{2,1,0:T(8,128)(2,1)S(1)} %get-tuple-element.108), channel_id=1, source_target_pairs={{0,4},{1,5},{2,6},{3,7},{4,0},{5,1},{6,2},{7,3},{8,12},{9,13},{10,... | collective-permute-start | bytes 491528 | tf_op jit(solution)/shard_map/ppermute | solution.py:361
  49.6 5.0 %collective-permute-start.12 = (bf16[64,512]{1,0:T(8,128)(2,1)S(1)}, bf16[64,512]{1,0:T(8,128)(2,1)S(1)}, u32[]{:S(2)}, u32[]{:S(2)}) collective-permute-start(bf16[64,512]{1,0:T(8,128)(2,1)S(1)} %get-tuple-element.90), channel_id=1, source_target_pairs={{1,0},{2,1},{3,2},{4,3},{5,4},{6,5},{7,6},{8,7},{9,8},{10,9},{11,1... | collective-permute-start | bytes 196616 | tf_op jit(solution)/shard_map/ppermute | solution.py:574
  52.2 6.4 %collective-permute-start.13 = (bf16[64,512]{1,0:T(8,128)(2,1)S(1)}, bf16[64,512]{1,0:T(8,128)(2,1)S(1)}, u32[]{:S(2)}, u32[]{:S(2)}) collective-permute-start(bf16[64,512]{1,0:T(8,128)(2,1)S(1)} %get-tuple-element.91), channel_id=1, source_target_pairs={{0,1},{1,2},{2,3},{3,4},{4,5},{5,6},{6,7},{7,8},{8,9},{9,10},{10,1... | collective-permute-start | bytes 196616 | tf_op jit(solution)/shard_map/ppermute | solution.py:575
  58.7 5.0 %collective-permute-start.14 = (bf16[2,32,1024]{2,1,0:T(8,128)(2,1)S(1)}, bf16[2,32,1024]{2,1,0:T(8,128)(2,1)S(1)}, u32[]{:S(2)}, u32[]{:S(2)}) collective-permute-start(bf16[2,32,1024]{2,1,0:T(8,128)(2,1)S(1)} %get-tuple-element.97), channel_id=1, source_target_pairs={{0,4},{1,5},{2,6},{3,7},{4,0},{5,1},{6,2},{7,3},{8,12},{9,13},{10,... | collective-permute-start | bytes 393224 | tf_op jit(solution)/shard_map/ppermute | solution.py:361
  58.8 5.8 %collective-permute-start.18 = (bf16[2,32,640]{2,1,0:T(8,128)(2,1)S(1)}, bf16[2,32,640]{2,1,0:T(8,128)(2,1)S(1)}, u32[]{:S(2)}, u32[]{:S(2)}) collective-permute-start(bf16[2,32,640]{2,1,0:T(8,128)(2,1)S(1)} %get-tuple-element.112), channel_id=1, source_target_pairs={{0,2},{1,3},{2,0},{3,1},{4,6},{5,7},{6,4},{7,5},{8,10},{9,11},{10,... | collective-permute-start | bytes 245768 | tf_op jit(solution)/shard_map/ppermute | solution.py:361
  63.7 6.7 %collective-permute-start.15 = (bf16[1,32,1024]{2,1,0:T(8,128)(2,1)S(1)}, bf16[1,32,1024]{2,1,0:T(8,128)(2,1)S(1)}, u32[]{:S(2)}, u32[]{:S(2)}) collective-permute-start(bf16[1,32,1024]{2,1,0:T(8,128)(2,1)S(1)} %get-tuple-element.99), channel_id=1, source_target_pairs={{0,8},{1,9},{2,10},{3,11},{4,12},{5,13},{6,14},{7,15},{8,0},{9,1},... | collective-permute-start | bytes 196616 | tf_op jit(solution)/shard_map/ppermute | solution.py:361
  64.7 5.8 %collective-permute-start.19 = (bf16[1,32,640]{2,1,0:T(8,128)(2,1)S(1)}, bf16[1,32,640]{2,1,0:T(8,128)(2,1)S(1)}, u32[]{:S(2)}, u32[]{:S(2)}) collective-permute-start(bf16[1,32,640]{2,1,0:T(8,128)(2,1)S(1)} %get-tuple-element.116), channel_id=1, source_target_pairs={{0,8},{1,9},{2,10},{3,11},{4,12},{5,13},{6,14},{7,15},{8,0},{9,1},... | collective-permute-start | bytes 122888 | tf_op jit(solution)/shard_map/ppermute | solution.py:361

commit v10 on v9

--- a/solution.py
+++ b/solution.py
@@ -425,14 +425,14 @@
         quarter = slabs // 4
         came = {0: messages[0]}
         for k in range(1, 2 * quarter):
-            message = messages[k]
-            if k == quarter - 1:
-                message = lax.optimization_barrier((message, came[1], came[2]))[0]
-            came[k] = lax.ppermute(message, "space", [(i, i ^ (2 * k)) for i in range(slabs)])
-        near = tuple(range(2 * quarter))
-        far = tuple(range(2 * quarter, slabs))
-        came_near = [came[k] for k in range(quarter)]
-        came_far = [came[k] for k in range(quarter, 2 * quarter)]
+            came[k] = lax.ppermute(messages[k], "space", [(i, i ^ (2 * k)) for i in range(slabs)])
+        for k in range(1, quarter - 1):
+            came[k], below, above, me = lax.optimization_barrier((came[k], below, above, me))
+        turns = [*range(quarter - 1), *range(quarter, 2 * quarter), quarter - 1]
+        near = tuple(2 * k + j for k in turns[: quarter - 1] for j in range(2))
+        far = tuple(2 * k + j for k in turns[quarter - 1 :] for j in range(2))
+        came_near = [came[k] for k in turns[: quarter - 1]]
+        came_far = [came[k] for k in turns[quarter - 1 :]]
     else:
         packed = jnp.stack([even, odd], axis=1).reshape(slabs, rows, LANES)
         near, far = (), tuple(range(slabs))

time: 71.4 us -> 72 us (level)
  starting transfers between devices: 20.8 us -> 25.4 us
  waiting for transfers between devices: 26.2 us -> 22.2 us
    ppermute x9, starting transfers between devices: 4.49 us -> 10.2 us  [swap(): lax.ppermute(block, 'space', [(i, i ^ 1 << bit) for i in range(slabs)])]
    ppermute x7, waiting for transfers between devices: 11.7 us -> 7.76 us  [on_device(): lax.ppermute(messages[k], 'space', [(i, i ^ 2 * k) for i in range(slabs)])]
    ppermute x1, starting transfers between devices: 2.62 us -> 1.48 us  [on_device(): from_above = lax.ppermute(lower, 'space', down)]
    ppermute x1, waiting for transfers between devices: 2.35 us -> 3.2 us  [on_device(): from_above = lax.ppermute(lower, 'space', down)]
    ppermute x1, waiting for transfers between devices: 4.04 us -> 3.18 us  [on_device(): from_below = lax.ppermute(upper, 'space', up)]
    pallas_call x1, Pallas kernels: 4.78 us -> 4.05 us  [on_device(): pl.pallas_call(functools.partial(near_kernel, half), out_shape=(pltpu.HBM...]
  transfers between devices with their start and end apart: 20 -> 20, of which waited for: 8 -> 9; matrix products, arithmetic and copies ran while one was open for 2% -> 2% of each run, Pallas kernels for 20% -> 19%
where the time goes in v10:
time: 72 us; the launch traced here: 71.7 us
  starting transfers between devices  25.4 us (35%)
  waiting for transfers between devices  22.2 us (31%)
  Pallas kernels  21.5 us (30%)
  local copies, waits for them, and re-layouts  1.78 us (2%)
  between operations  0.82 us (1%)
    ppermute x9, starting transfers between devices, swap(): lax.ppermute(block, 'space', [(i, i ^ 1 << bit) for i in range(slabs)])  10.2 us
    ppermute x7, starting transfers between devices, on_device(): lax.ppermute(messages[k], 'space', [(i, i ^ 2 * k) for i in range(slabs)])  7.97 us
    ppermute x9, waiting for transfers between devices, swap(): lax.ppermute(block, 'space', [(i, i ^ 1 << bit) for i in range(slabs)])  7.91 us
    ppermute x7, waiting for transfers between devices, on_device(): lax.ppermute(messages[k], 'space', [(i, i ^ 2 * k) for i in range(slabs)])  7.76 us
    pallas_call x1, Pallas kernels, on_device(): pl.pallas_call(functools.partial(edge_kernel, half, linked, near, far), o...  5.74 us
    ppermute x1, starting transfers between devices, on_device(): above = lax.ppermute(low, 'space', down)  5.61 us
    pallas_call x1, Pallas kernels, on_device(): pl.pallas_call(functools.partial(grad_kernel, half, factor), out_shape=(c...  4.46 us
    pallas_call x1, Pallas kernels, on_device(): pl.pallas_call(functools.partial(near_kernel, half), out_shape=(pltpu.HBM...  4.05 us
  transfers between devices with their start and end apart: 20, of which 9 were waited for; matrix products, arithmetic and copies ran while one was open for 2% of the time, Pallas kernels for 19%

profile of v10, /device:TPU:0, one launch (start us, length us, event | category | flops | bytes accessed | tf_op | source)
XLA Modules:
  0.0 71.7 jit_solution(10830071675909502025)
XLA Ops:
  0.7 2.5 %pack.1 = (bf16[8,272,128]{2,1,0:T(8,128)(2,1)S(1)}, bf16[8,272,128]{2,1,0:T(8,128)(2,1)S(1)}, bf16[64,512]{1,0:T(8,128)(2,1)S(1)}, bf16[64,512]{1,0:T(8,128)(2,1)S(1)}) custom-call(s32[1]{0:T(128)} %bitcast.me_ref, bf16[256,512]{1,0:T(8,128)(2,1)} %feats_hbm.1, bf16[529,16,128]{2,1,0:T(8,128)(2,1)} %bitcast.16), custom_call_target="tpu_custom_call" | custom-call | tf_op jit(solution)/shard_map/pack/pallas_call | solution.py:392
  3.2 0.5 collective-permute-start
  3.8 5.6 %collective-permute-start.2 = (bf16[64,512]{1,0:T(8,128)(2,1)S(1)}, bf16[64,512]{1,0:T(8,128)(2,1)S(1)}, u32[]{:S(2)}, u32[]{:S(2)}) collective-permute-start(bf16[64,512]{1,0:T(8,128)(2,1)S(1)} %get-tuple-element.72), channel_id=1, source_target_pairs={{1,0},{2,1},{3,2},{4,3},{5,4},{6,5},{7,6},{8,7},{9,8},{10,9},{11,1... | collective-permute-start | bytes 196616 | tf_op jit(solution)/shard_map/ppermute | solution.py:411
  9.4 1.7 %constant_dynamic-slice_fusion = bf16[1,1,64,529]{2,1,3,0:T(2,128)(2,1)S(1)} fusion(bf16[1,16,128,529]{2,1,3,0:T(8,128)(2,1)} %param.12, s32[]{:T(128)S(6)} %select_n.4, s32[]{:T(128)S(6)} %add.7), kind=kLoop, calls=%fused_computation.1 | loop fusion | bytes 135432 | tf_op jit(solution)/shard_map/slice | solution.py:412
  11.1 0.2 collective-permute-done.1.below_ref
  11.5 0.2 collective-permute-start.3
  11.7 2.6 %collective-permute-start.5 = (bf16[2,272,128]{2,1,0:T(8,128)(2,1)S(1)}, bf16[2,272,128]{2,1,0:T(8,128)(2,1)S(1)}, u32[]{:S(2)}, u32[]{:S(2)}) collective-permute-start(bf16[2,272,128]{2,1,0:T(8,128)(2,1)S(1)} %get-tuple-element.94), channel_id=1, source_target_pairs={{0,8},{1,9},{2,10},{3,11},{4,12},{5,13},{6,14},{7,15},{8,0},{9,1},... | collective-permute-start | bytes 417800 | tf_op jit(solution)/shard_map/ppermute | solution.py:428
  14.3 1.6 %collective-permute-start.6 = (bf16[2,272,128]{2,1,0:T(8,128)(2,1)S(1)}, bf16[2,272,128]{2,1,0:T(8,128)(2,1)S(1)}, u32[]{:S(2)}, u32[]{:S(2)}) collective-permute-start(bf16[2,272,128]{2,1,0:T(8,128)(2,1)S(1)} %get-tuple-element.95), channel_id=1, source_target_pairs={{0,10},{1,11},{2,8},{3,9},{4,14},{5,15},{6,12},{7,13},{8,2},{9,3},... | collective-permute-start | bytes 417800 | tf_op jit(solution)/shard_map/ppermute | solution.py:428
  15.9 2.1 %collective-permute-start.7 = (bf16[2,272,128]{2,1,0:T(8,128)(2,1)S(1)}, bf16[2,272,128]{2,1,0:T(8,128)(2,1)S(1)}, u32[]{:S(2)}, u32[]{:S(2)}) collective-permute-start(bf16[2,272,128]{2,1,0:T(8,128)(2,1)S(1)} %get-tuple-element.96), channel_id=1, source_target_pairs={{0,12},{1,13},{2,14},{3,15},{4,8},{5,9},{6,10},{7,11},{8,4},{9,5},... | collective-permute-start | bytes 417800 | tf_op jit(solution)/shard_map/ppermute | solution.py:428
  17.9 1.4 %collective-permute-start.8 = (bf16[2,272,128]{2,1,0:T(8,128)(2,1)S(1)}, bf16[2,272,128]{2,1,0:T(8,128)(2,1)S(1)}, u32[]{:S(2)}, u32[]{:S(2)}) collective-permute-start(bf16[2,272,128]{2,1,0:T(8,128)(2,1)S(1)} %get-tuple-element.97), channel_id=1, source_target_pairs={{0,14},{1,15},{2,12},{3,13},{4,10},{5,11},{6,8},{7,9},{8,6},{9,7},... | collective-permute-start | bytes 417800 | tf_op jit(solution)/shard_map/ppermute | solution.py:428
  19.3 1.4 %collective-permute-done.3.rest_2_ = bf16[2,272,128]{2,1,0:T(8,128)(2,1)S(1)} collective-permute-done((bf16[2,272,128]{2,1,0:T(8,128)(2,1)S(1)}, bf16[2,272,128]{2,1,0:T(8,128)(2,1)S(1)}, u32[]{:S(2)}, u32[]{:S(2)}) %collective-permute-start.3) | collective-permute-done | bytes 139296 | tf_op jit(solution)/shard_map/ppermute | solution.py:428
  20.8 5.7 %edges.1 = (bf16[640,1152]{1,0:T(8,128)(2,1)}, f32[512,1152]{1,0:T(8,128)}, bf16[512,384]{1,0:T(8,128)(2,1)}, bf16[512,512]{1,0:T(8,128)(2,1)S(1)}, bf16[512,640...) custom-call(s32[1]{0:T(128)} %bitcast.me_ref, bf16[256,512]{1,0:T(8,128)(2,1)} %feats_hbm.1, bf16[512,512]{1,0:T(8,128)(2,1)} %w_src_ref.1, ...), custom_call_target="tpu_custom_call" | custom-call | flops 30198988800 | bytes 8388608 | tf_op jit(solution)/shard_map/edges/pallas_call | solution.py:447
  26.6 4.1 %near.1 = (f32[640,512]{1,0:T(8,128)}, f32[512,544]{1,0:T(8,128)}) custom-call(bf16[544,128]{1,0:T(8,128)(2,1)S(1)} %pad.4.own_ref, bf16[512,544]{1,0:T(8,128)(2,1)S(1)} %get-tuple-element.84.w_out_ref, bf16[512,512]{1,0:T(8,128)(2,1)S(1)} %get-tuple-element.89.hidden_ref, f32[512,1152]{1,0:T(8,128)} %get-tuple-element.85.slope_hbm, ...), custom_call_target="tpu_custom_call" | custom-call | flops 5704253440 | bytes 6291456 | tf_op jit(solution)/shard_map/near/pallas_call | solution.py:486
  30.6 4.7 %collective-permute-done.6.rest_1_ = bf16[2,272,128]{2,1,0:T(8,128)(2,1)S(1)} collective-permute-done((bf16[2,272,128]{2,1,0:T(8,128)(2,1)S(1)}, bf16[2,272,128]{2,1,0:T(8,128)(2,1)S(1)}, u32[]{:S(2)}, u32[]{:S(2)}) %collective-permute-start.6) | collective-permute-done | bytes 139296 | tf_op jit(solution)/shard_map/ppermute | solution.py:428
  35.3 1.6 %collective-permute-done.9.rest_4_ = bf16[2,272,128]{2,1,0:T(8,128)(2,1)S(1)} collective-permute-done((bf16[2,272,128]{2,1,0:T(8,128)(2,1)S(1)}, bf16[2,272,128]{2,1,0:T(8,128)(2,1)S(1)}, u32[]{:S(2)}, u32[]{:S(2)}) %collective-permute-start.9) | collective-permute-done | bytes 139296 | tf_op jit(solution)/shard_map/ppermute | solution.py:428
  37.0 4.5 %grads.1 = (f32[8,32,1024]{2,1,0:T(8,128)S(1)}, bf16[8,32,1024]{2,1,0:T(8,128)(2,1)S(1)}, f32[512,512]{1,0:T(8,128)S(1)}, bf16[64,512]{1,0:T(8,128)(2,1)S(1)}, b...) custom-call(s32[1]{0:T(128)} %bitcast.me_ref, bf16[512,544]{1,0:T(8,128)(2,1)S(1)} %get-tuple-element.84.w_out_ref, ...), custom_call_target="tpu_custom_call" | custom-call | tf_op jit(solution)/shard_map/grads/pallas_call | solution.py:510
  41.5 2.1 %outer.1 = (f32[8,32,640]{2,1,0:T(8,128)S(1)}, bf16[8,32,640]{2,1,0:T(8,128)(2,1)S(1)}) custom-call(s32[1]{0:T(128)} %bitcast.me_ref, bf16[512,640]{1,0:T(8,128)(2,1)S(1)} %get-tuple-element.114.hidden_ref, bf16[544,640]{1,0:T(8,128)(2,1)S(1)} %get-tuple-element.115.g_ref, f32[512,544]{1,0:T(8,128)} %get-tuple-element.116.near_hbm), custom_call_target="tpu_custom_call" | custom-call | flops 12834570240 | bytes 4194304 | tf_op jit(solution)/shard_map/outer/pallas_call | solution.py:534
  43.6 0.6 collective-permute-start.16
  44.2 0.1 fold.6
  44.4 1.0 %collective-permute-done.16.came_ref = bf16[8,32,640]{2,1,0:T(8,128)(2,1)S(1)} collective-permute-done((bf16[8,32,640]{2,1,0:T(8,128)(2,1)S(1)}, bf16[8,32,640]{2,1,0:T(8,128)(2,1)S(1)}, u32[]{:S(2)}, u32[]{:S(2)}) %collective-permute-start.16) | collective-permute-done | bytes 327712 | tf_op jit(solution)/shard_map/ppermute | solution.py:361
  45.4 0.1 fold.9
  45.5 4.9 %collective-permute-start.17 = (bf16[4,32,640]{2,1,0:T(8,128)(2,1)S(1)}, bf16[4,32,640]{2,1,0:T(8,128)(2,1)S(1)}, u32[]{:S(2)}, u32[]{:S(2)}) collective-permute-start(bf16[4,32,640]{2,1,0:T(8,128)(2,1)S(1)} %get-tuple-element.122), channel_id=1, source_target_pairs={{0,4},{1,5},{2,6},{3,7},{4,0},{5,1},{6,2},{7,3},{8,12},{9,13},{10,... | collective-permute-start | bytes 491528 | tf_op jit(solution)/shard_map/ppermute | solution.py:361
  50.4 1.5 %collective-permute-start.12 = (bf16[64,512]{1,0:T(8,128)(2,1)S(1)}, bf16[64,512]{1,0:T(8,128)(2,1)S(1)}, u32[]{:S(2)}, u32[]{:S(2)}) collective-permute-start(bf16[64,512]{1,0:T(8,128)(2,1)S(1)} %get-tuple-element.104), channel_id=1, source_target_pairs={{1,0},{2,1},{3,2},{4,3},{5,4},{6,5},{7,6},{8,7},{9,8},{10,9},{11,1... | collective-permute-start | bytes 196616 | tf_op jit(solution)/shard_map/ppermute | solution.py:574
  51.9 3.2 %collective-permute-done.12.from_above_ref = bf16[64,512]{1,0:T(8,128)(2,1)S(1)} collective-permute-done((bf16[64,512]{1,0:T(8,128)(2,1)S(1)}, bf16[64,512]{1,0:T(8,128)(2,1)S(1)}, u32[]{:S(2)}, u32[]{:S(2)}) %collective-permute-start.12) | collective-permute-done | bytes 65568 | tf_op jit(solution)/shard_map/ppermute | solution.py:574
  55.1 3.2 %collective-permute-done.13.from_below_ref = bf16[64,512]{1,0:T(8,128)(2,1)S(1)} collective-permute-done((bf16[64,512]{1,0:T(8,128)(2,1)S(1)}, bf16[64,512]{1,0:T(8,128)(2,1)S(1)}, u32[]{:S(2)}, u32[]{:S(2)}) %collective-permute-start.13) | collective-permute-done | bytes 65568 | tf_op jit(solution)/shard_map/ppermute | solution.py:575
  58.5 1.0 %collective-permute-start.18 = (bf16[2,32,640]{2,1,0:T(8,128)(2,1)S(1)}, bf16[2,32,640]{2,1,0:T(8,128)(2,1)S(1)}, u32[]{:S(2)}, u32[]{:S(2)}) collective-permute-start(bf16[2,32,640]{2,1,0:T(8,128)(2,1)S(1)} %get-tuple-element.126), channel_id=1, source_target_pairs={{0,2},{1,3},{2,0},{3,1},{4,6},{5,7},{6,4},{7,5},{8,10},{9,11},{10,... | collective-permute-start | bytes 245768 | tf_op jit(solution)/shard_map/ppermute | solution.py:361
  59.5 3.9 %collective-permute-done.14.came_ref = bf16[2,32,1024]{2,1,0:T(8,128)(2,1)S(1)} collective-permute-done((bf16[2,32,1024]{2,1,0:T(8,128)(2,1)S(1)}, bf16[2,32,1024]{2,1,0:T(8,128)(2,1)S(1)}, u32[]{:S(2)}, u32[]{:S(2)}) %collective-permute-start.14) | collective-permute-done | bytes 131104 | tf_op jit(solution)/shard_map/ppermute | solution.py:361
  63.4 1.4 %collective-permute-start.15 = (bf16[1,32,1024]{2,1,0:T(8,128)(2,1)S(1)}, bf16[1,32,1024]{2,1,0:T(8,128)(2,1)S(1)}, u32[]{:S(2)}, u32[]{:S(2)}) collective-permute-start(bf16[1,32,1024]{2,1,0:T(8,128)(2,1)S(1)} %get-tuple-element.113), channel_id=1, source_target_pairs={{0,8},{1,9},{2,10},{3,11},{4,12},{5,13},{6,14},{7,15},{8,0},{9,1},... | collective-permute-start | bytes 196616 | tf_op jit(solution)/shard_map/ppermute | solution.py:361
  64.9 1.6 %collective-permute-start.19 = (bf16[1,32,640]{2,1,0:T(8,128)(2,1)S(1)}, bf16[1,32,640]{2,1,0:T(8,128)(2,1)S(1)}, u32[]{:S(2)}, u32[]{:S(2)}) collective-permute-start(bf16[1,32,640]{2,1,0:T(8,128)(2,1)S(1)} %get-tuple-element.130), channel_id=1, source_target_pairs={{0,8},{1,9},{2,10},{3,11},{4,12},{5,13},{6,14},{7,15},{8,0},{9,1},... | collective-permute-start | bytes 122888 | tf_op jit(solution)/shard_map/ppermute | solution.py:361
  66.5 1.5 %rims.1 = f32[256,512]{1,0:T(8,128)} custom-call(f32[512,512]{1,0:T(8,128)S(1)} %get-tuple-element.99.sums_ref, bf16[64,512]{1,0:T(8,128)(2,1)S(1)} %collective-permute-done.13.from_below_ref, bf16[64,512]{1,0:T(8,128)(2,1)S(1)} %collective-permute-done.12.from_above_ref, bf16[512,512]{1,0:T(8,128)(2,1)S(1)} %copy-done, bf16[512,512]{1,0:T(8,128)(2,1)S(1)} %copy-done.1), custom_call_target="tpu_custom_call" | custom-call | flops 24159191040 | bytes 4194304 | tf_op jit(solution)/shard_map/rims/pallas_call | solution.py:588
  68.1 2.9 %collective-permute-done.19.refs_3_ = bf16[1,32,640]{2,1,0:T(8,128)(2,1)S(1)} collective-permute-done((bf16[1,32,640]{2,1,0:T(8,128)(2,1)S(1)}, bf16[1,32,640]{2,1,0:T(8,128)(2,1)S(1)}, u32[]{:S(2)}, u32[]{:S(2)}) %collective-permute-start.19) | collective-permute-done | bytes 40992 | tf_op jit(solution)/shard_map/ppermute | solution.py:361
  71.0 0.7 totals.1
  (35 shorter events, 0.7 us)
Async XLA Ops:
  0.6 20.2 %copy-start.2 = (s32[2048]{0:T(1024)S(1)}, s32[2048]{0:T(1024)}, u32[]{:S(2)}) copy-start(s32[2048]{0:T(1024)} %param.13) | copy-start | bytes 24580
  0.6 20.2 %copy-start.3 = (s32[2048]{0:T(1024)S(1)}, s32[2048]{0:T(1024)}, u32[]{:S(2)}) copy-start(s32[2048]{0:T(1024)} %param.14) | copy-start | bytes 24580
  0.7 20.2 %copy-start.4 = (s32[2048]{0:T(1024)S(1)}, s32[2048]{0:T(1024)}, u32[]{:S(2)}) copy-start(s32[2048]{0:T(1024)} %param.15) | copy-start | bytes 24580
  3.2 8.1 %collective-permute-start = (bf16[8,272,128]{2,1,0:T(8,128)(2,1)S(1)}, bf16[8,272,128]{2,1,0:T(8,128)(2,1)S(1)}, u32[]{:S(2)}, u32[]{:S(2)}) collective-permute-start(bf16[8,272,128]{2,1,0:T(8,128)(2,1)S(1)} %get-tuple-element.70), channel_id=1, source_target_pairs={{0,1},{1,0},{2,3},{3,2},{4,5},{5,4},{6,7},{7,6},{8,9},{9,8},{10,11... | collective-permute-start | bytes 1671176 | tf_op jit(solution)/shard_map/ppermute | solution.py:361
  3.7 7.6 %collective-permute-start.1 = (bf16[64,512]{1,0:T(8,128)(2,1)S(1)}, bf16[64,512]{1,0:T(8,128)(2,1)S(1)}, u32[]{:S(2)}, u32[]{:S(2)}) collective-permute-start(bf16[64,512]{1,0:T(8,128)(2,1)S(1)} %get-tuple-element.71), channel_id=1, source_target_pairs={{0,1},{1,2},{2,3},{3,4},{4,5},{5,6},{6,7},{7,8},{8,9},{9,10},{10,1... | collective-permute-start | bytes 196616 | tf_op jit(solution)/shard_map/ppermute | solution.py:410
  3.8 7.6 %collective-permute-start.2 = (bf16[64,512]{1,0:T(8,128)(2,1)S(1)}, bf16[64,512]{1,0:T(8,128)(2,1)S(1)}, u32[]{:S(2)}, u32[]{:S(2)}) collective-permute-start(bf16[64,512]{1,0:T(8,128)(2,1)S(1)} %get-tuple-element.72), channel_id=1, source_target_pairs={{1,0},{2,1},{3,2},{4,3},{5,4},{6,5},{7,6},{8,7},{9,8},{10,9},{11,1... | collective-permute-start | bytes 196616 | tf_op jit(solution)/shard_map/ppermute | solution.py:411
  11.4 6.5 %collective-permute-start.4 = (bf16[2,272,128]{2,1,0:T(8,128)(2,1)S(1)}, bf16[2,272,128]{2,1,0:T(8,128)(2,1)S(1)}, u32[]{:S(2)}, u32[]{:S(2)}) collective-permute-start(bf16[2,272,128]{2,1,0:T(8,128)(2,1)S(1)} %get-tuple-element.75), channel_id=1, source_target_pairs={{0,2},{1,3},{2,0},{3,1},{4,6},{5,7},{6,4},{7,5},{8,10},{9,11},{10,... | collective-permute-start | bytes 417800 | tf_op jit(solution)/shard_map/ppermute | solution.py:428
  11.5 9.3 %collective-permute-start.3 = (bf16[2,272,128]{2,1,0:T(8,128)(2,1)S(1)}, bf16[2,272,128]{2,1,0:T(8,128)(2,1)S(1)}, u32[]{:S(2)}, u32[]{:S(2)}) collective-permute-start(bf16[2,272,128]{2,1,0:T(8,128)(2,1)S(1)} %get-tuple-element.74), channel_id=1, source_target_pairs={{0,4},{1,5},{2,6},{3,7},{4,0},{5,1},{6,2},{7,3},{8,12},{9,13},{10,... | collective-permute-start | bytes 417800 | tf_op jit(solution)/shard_map/ppermute | solution.py:428
  11.7 18.9 %collective-permute-start.5 = (bf16[2,272,128]{2,1,0:T(8,128)(2,1)S(1)}, bf16[2,272,128]{2,1,0:T(8,128)(2,1)S(1)}, u32[]{:S(2)}, u32[]{:S(2)}) collective-permute-start(bf16[2,272,128]{2,1,0:T(8,128)(2,1)S(1)} %get-tuple-element.94), channel_id=1, source_target_pairs={{0,8},{1,9},{2,10},{3,11},{4,12},{5,13},{6,14},{7,15},{8,0},{9,1},... | collective-permute-start | bytes 417800 | tf_op jit(solution)/shard_map/ppermute | solution.py:428
  14.3 21.0 %collective-permute-start.6 = (bf16[2,272,128]{2,1,0:T(8,128)(2,1)S(1)}, bf16[2,272,128]{2,1,0:T(8,128)(2,1)S(1)}, u32[]{:S(2)}, u32[]{:S(2)}) collective-permute-start(bf16[2,272,128]{2,1,0:T(8,128)(2,1)S(1)} %get-tuple-element.95), channel_id=1, source_target_pairs={{0,10},{1,11},{2,8},{3,9},{4,14},{5,15},{6,12},{7,13},{8,2},{9,3},... | collective-permute-start | bytes 417800 | tf_op jit(solution)/shard_map/ppermute | solution.py:428
  15.9 19.5 %collective-permute-start.7 = (bf16[2,272,128]{2,1,0:T(8,128)(2,1)S(1)}, bf16[2,272,128]{2,1,0:T(8,128)(2,1)S(1)}, u32[]{:S(2)}, u32[]{:S(2)}) collective-permute-start(bf16[2,272,128]{2,1,0:T(8,128)(2,1)S(1)} %get-tuple-element.96), channel_id=1, source_target_pairs={{0,12},{1,13},{2,14},{3,15},{4,8},{5,9},{6,10},{7,11},{8,4},{9,5},... | collective-permute-start | bytes 417800 | tf_op jit(solution)/shard_map/ppermute | solution.py:428
  17.9 17.4 %collective-permute-start.8 = (bf16[2,272,128]{2,1,0:T(8,128)(2,1)S(1)}, bf16[2,272,128]{2,1,0:T(8,128)(2,1)S(1)}, u32[]{:S(2)}, u32[]{:S(2)}) collective-permute-start(bf16[2,272,128]{2,1,0:T(8,128)(2,1)S(1)} %get-tuple-element.97), channel_id=1, source_target_pairs={{0,14},{1,15},{2,12},{3,13},{4,10},{5,11},{6,8},{7,9},{8,6},{9,7},... | collective-permute-start | bytes 417800 | tf_op jit(solution)/shard_map/ppermute | solution.py:428
  20.8 16.2 %collective-permute-start.9 = (bf16[2,272,128]{2,1,0:T(8,128)(2,1)S(1)}, bf16[2,272,128]{2,1,0:T(8,128)(2,1)S(1)}, u32[]{:S(2)}, u32[]{:S(2)}) collective-permute-start(bf16[2,272,128]{2,1,0:T(8,128)(2,1)S(1)} %get-tuple-element.98), channel_id=1, source_target_pairs={{0,6},{1,7},{2,4},{3,5},{4,2},{5,3},{6,0},{7,1},{8,14},{9,15},{10,... | collective-permute-start | bytes 417800 | tf_op jit(solution)/shard_map/ppermute | solution.py:428
  41.4 2.7 %collective-permute-start.10 = (bf16[8,32,1024]{2,1,0:T(8,128)(2,1)S(1)}, bf16[8,32,1024]{2,1,0:T(8,128)(2,1)S(1)}, u32[]{:S(2)}, u32[]{:S(2)}) collective-permute-start(bf16[8,32,1024]{2,1,0:T(8,128)(2,1)S(1)} %get-tuple-element.101), channel_id=1, source_target_pairs={{0,1},{1,0},{2,3},{3,2},{4,5},{5,4},{6,7},{7,6},{8,9},{9,8},{10,11... | collective-permute-start | bytes 1572872 | tf_op jit(solution)/shard_map/ppermute | solution.py:361
  43.6 1.8 %collective-permute-start.16 = (bf16[8,32,640]{2,1,0:T(8,128)(2,1)S(1)}, bf16[8,32,640]{2,1,0:T(8,128)(2,1)S(1)}, u32[]{:S(2)}, u32[]{:S(2)}) collective-permute-start(bf16[8,32,640]{2,1,0:T(8,128)(2,1)S(1)} %get-tuple-element.118), channel_id=1, source_target_pairs={{0,1},{1,0},{2,3},{3,2},{4,5},{5,4},{6,7},{7,6},{8,9},{9,8},{10,11... | collective-permute-start | bytes 983048 | tf_op jit(solution)/shard_map/ppermute | solution.py:361
  44.2 22.4 %copy-start = (bf16[512,512]{1,0:T(8,128)(2,1)S(1)}, bf16[512,512]{1,0:T(8,128)(2,1)}, u32[]{:S(2)}) copy-start(bf16[512,512]{1,0:T(8,128)(2,1)} %w_src_ref.1) | copy-start | bytes 1572868
  44.2 22.4 %copy-start.1 = (bf16[512,512]{1,0:T(8,128)(2,1)S(1)}, bf16[512,512]{1,0:T(8,128)(2,1)}, u32[]{:S(2)}) copy-start(bf16[512,512]{1,0:T(8,128)(2,1)} %w_dst_ref.1) | copy-start | bytes 1572868
  44.3 14.0 %collective-permute-start.11 = (bf16[4,32,1024]{2,1,0:T(8,128)(2,1)S(1)}, bf16[4,32,1024]{2,1,0:T(8,128)(2,1)S(1)}, u32[]{:S(2)}, u32[]{:S(2)}) collective-permute-start(bf16[4,32,1024]{2,1,0:T(8,128)(2,1)S(1)} %get-tuple-element.103), channel_id=1, source_target_pairs={{0,2},{1,3},{2,0},{3,1},{4,6},{5,7},{6,4},{7,5},{8,10},{9,11},{10,... | collective-permute-start | bytes 786440 | tf_op jit(solution)/shard_map/ppermute | solution.py:361
  45.5 12.9 %collective-permute-start.17 = (bf16[4,32,640]{2,1,0:T(8,128)(2,1)S(1)}, bf16[4,32,640]{2,1,0:T(8,128)(2,1)S(1)}, u32[]{:S(2)}, u32[]{:S(2)}) collective-permute-start(bf16[4,32,640]{2,1,0:T(8,128)(2,1)S(1)} %get-tuple-element.122), channel_id=1, source_target_pairs={{0,4},{1,5},{2,6},{3,7},{4,0},{5,1},{6,2},{7,3},{8,12},{9,13},{10,... | collective-permute-start | bytes 491528 | tf_op jit(solution)/shard_map/ppermute | solution.py:361
  50.4 4.7 %collective-permute-start.12 = (bf16[64,512]{1,0:T(8,128)(2,1)S(1)}, bf16[64,512]{1,0:T(8,128)(2,1)S(1)}, u32[]{:S(2)}, u32[]{:S(2)}) collective-permute-start(bf16[64,512]{1,0:T(8,128)(2,1)S(1)} %get-tuple-element.104), channel_id=1, source_target_pairs={{1,0},{2,1},{3,2},{4,3},{5,4},{6,5},{7,6},{8,7},{9,8},{10,9},{11,1... | collective-permute-start | bytes 196616 | tf_op jit(solution)/shard_map/ppermute | solution.py:574
  51.9 6.4 %collective-permute-start.13 = (bf16[64,512]{1,0:T(8,128)(2,1)S(1)}, bf16[64,512]{1,0:T(8,128)(2,1)S(1)}, u32[]{:S(2)}, u32[]{:S(2)}) collective-permute-start(bf16[64,512]{1,0:T(8,128)(2,1)S(1)} %get-tuple-element.105), channel_id=1, source_target_pairs={{0,1},{1,2},{2,3},{3,4},{4,5},{5,6},{6,7},{7,8},{8,9},{9,10},{10,1... | collective-permute-start | bytes 196616 | tf_op jit(solution)/shard_map/ppermute | solution.py:575
  58.4 5.0 %collective-permute-start.14 = (bf16[2,32,1024]{2,1,0:T(8,128)(2,1)S(1)}, bf16[2,32,1024]{2,1,0:T(8,128)(2,1)S(1)}, u32[]{:S(2)}, u32[]{:S(2)}) collective-permute-start(bf16[2,32,1024]{2,1,0:T(8,128)(2,1)S(1)} %get-tuple-element.111), channel_id=1, source_target_pairs={{0,4},{1,5},{2,6},{3,7},{4,0},{5,1},{6,2},{7,3},{8,12},{9,13},{10,... | collective-permute-start | bytes 393224 | tf_op jit(solution)/shard_map/ppermute | solution.py:361
  58.5 6.4 %collective-permute-start.18 = (bf16[2,32,640]{2,1,0:T(8,128)(2,1)S(1)}, bf16[2,32,640]{2,1,0:T(8,128)(2,1)S(1)}, u32[]{:S(2)}, u32[]{:S(2)}) collective-permute-start(bf16[2,32,640]{2,1,0:T(8,128)(2,1)S(1)} %get-tuple-element.126), channel_id=1, source_target_pairs={{0,2},{1,3},{2,0},{3,1},{4,6},{5,7},{6,4},{7,5},{8,10},{9,11},{10,... | collective-permute-start | bytes 245768 | tf_op jit(solution)/shard_map/ppermute | solution.py:361
  63.4 7.6 %collective-permute-start.15 = (bf16[1,32,1024]{2,1,0:T(8,128)(2,1)S(1)}, bf16[1,32,1024]{2,1,0:T(8,128)(2,1)S(1)}, u32[]{:S(2)}, u32[]{:S(2)}) collective-permute-start(bf16[1,32,1024]{2,1,0:T(8,128)(2,1)S(1)} %get-tuple-element.113), channel_id=1, source_target_pairs={{0,8},{1,9},{2,10},{3,11},{4,12},{5,13},{6,14},{7,15},{8,0},{9,1},... | collective-permute-start | bytes 196616 | tf_op jit(solution)/shard_map/ppermute | solution.py:361
  64.9 6.1 %collective-permute-start.19 = (bf16[1,32,640]{2,1,0:T(8,128)(2,1)S(1)}, bf16[1,32,640]{2,1,0:T(8,128)(2,1)S(1)}, u32[]{:S(2)}, u32[]{:S(2)}) collective-permute-start(bf16[1,32,640]{2,1,0:T(8,128)(2,1)S(1)} %get-tuple-element.130), channel_id=1, source_target_pairs={{0,8},{1,9},{2,10},{3,11},{4,12},{5,13},{6,14},{7,15},{8,0},{9,1},... | collective-permute-start | bytes 122888 | tf_op jit(solution)/shard_map/ppermute | solution.py:361

commit v11 on v10

--- a/solution.py
+++ b/solution.py
@@ -97,8 +97,13 @@
         copy.wait()
 
 
-def join_kernel(even_ref, other_ref, *message_refs):
-    for k, message_ref in enumerate(message_refs):
+def by_core(pair, me):
+    return pair[0] + (me % 2) * (pair[1] - pair[0])
+
+
+def join_kernel(turns, me_ref, even_ref, other_ref, *message_refs):
+    for pair, message_ref in zip(turns, message_refs):
+        k = by_core(pair, me_ref[0])
         message_ref[0] = even_ref[k]
         message_ref[1] = other_ref[k]
 
@@ -124,7 +129,8 @@
     def rows_of(ids):
         rows = []
         for tile in range(len(ids) // per):
-            pieces = [ref[pl.ds(me ^ i if linked else i, 1), :] for i in ids[tile * per : (tile + 1) * per]]
+            here = ids[tile * per : (tile + 1) * per]
+            pieces = [ref[pl.ds(me ^ by_core(i, me) if linked else i, 1), :] for i in here]
             rows.append(jnp.concatenate([piece[:, :half] for piece in pieces], axis=1))
         return rows
 
@@ -414,25 +420,26 @@
     if linked:
         other = swap(odd, 0, slabs)
         other, below, above, own = lax.optimization_barrier((other, below, above, own))
+        quarter = slabs // 4
+        mixed = [pair for k in range(1, quarter) for pair in ((quarter + k - 1, k), (k, quarter + k - 1))]
+        turns = [(0, 0), *mixed, (2 * quarter - 1, 2 * quarter - 1)]
         messages = pl.pallas_call(
-            join_kernel,
+            functools.partial(join_kernel, turns),
             out_shape=(jax.ShapeDtypeStruct((2, rows, LANES), BF16),) * (slabs // 2),
-            in_specs=vmem(2),
+            in_specs=[smem] + vmem(2),
             out_specs=tuple(vmem(slabs // 2)),
             compiler_params=big,
             name="join",
-        )(even, other)
-        quarter = slabs // 4
-        came = {0: messages[0]}
-        for k in range(1, 2 * quarter):
-            came[k] = lax.ppermute(messages[k], "space", [(i, i ^ (2 * k)) for i in range(slabs)])
-        for k in range(1, quarter - 1):
-            came[k], below, above, me = lax.optimization_barrier((came[k], below, above, me))
-        turns = [*range(quarter - 1), *range(quarter, 2 * quarter), quarter - 1]
-        near = tuple(2 * k + j for k in turns[: quarter - 1] for j in range(2))
-        far = tuple(2 * k + j for k in turns[quarter - 1 :] for j in range(2))
-        came_near = [came[k] for k in turns[: quarter - 1]]
-        came_far = [came[k] for k in turns[quarter - 1 :]]
+        )(me, even, other)
+        came = [messages[0]]
+        for turn in range(1, 2 * quarter):
+            route = [(i, i ^ (2 * turns[turn][i % 2])) for i in range(slabs)]
+            came.append(lax.ppermute(messages[turn], "space", route))
+        for turn in range(1, quarter - 1):
+            came[turn], below, above, me = lax.optimization_barrier((came[turn], below, above, me))
+        ids = [(2 * first + j, 2 * second + j) for first, second in turns for j in range(2)]
+        near, far = tuple(ids[: 2 * quarter - 2]), tuple(ids[2 * quarter - 2 :])
+        came_near, came_far = came[: quarter - 1], came[quarter - 1 :]
     else:
         packed = jnp.stack([even, odd], axis=1).reshape(slabs, rows, LANES)
         near, far = (), tuple(range(slabs))

time: 72 us -> 69.9 us (0.971)
  waiting for transfers between devices: 22.2 us -> 17.7 us
  starting transfers between devices: 25.4 us -> 27.9 us
    ppermute x7, waiting for transfers between devices: 7.76 us -> 5.11 us  [on_device(): came.append(lax.ppermute(messages[turn], 'space', route))]
    ppermute x9, waiting for transfers between devices: 7.91 us -> 6.02 us  [swap(): lax.ppermute(block, 'space', [(i, i ^ 1 << bit) for i in range(slabs)])]
    ppermute x1, waiting for transfers between devices: 3.2 us -> 1.98 us  [on_device(): from_above = lax.ppermute(lower, 'space', down)]
    ppermute x1, waiting for transfers between devices: 3.18 us -> 4.4 us  [on_device(): from_below = lax.ppermute(upper, 'space', up)]
    ppermute x7, starting transfers between devices: 7.97 us -> 9.18 us  [on_device(): came.append(lax.ppermute(messages[turn], 'space', route))]
  transfers between devices with their start and end apart: 20 -> 20, of which waited for: 9 -> 6; matrix products, arithmetic and copies ran while one was open for 2% -> 3% of each run, Pallas kernels for 19% -> 20%
where the time goes in v11:
time: 69.9 us; the launch traced here: 69.6 us
  starting transfers between devices  27.9 us (40%)
  Pallas kernels  21.4 us (31%)
  waiting for transfers between devices  17.7 us (25%)
  local copies, waits for them, and re-layouts  1.78 us (3%)
  between operations  0.83 us (1%)
    ppermute x9, starting transfers between devices, swap(): lax.ppermute(block, 'space', [(i, i ^ 1 << bit) for i in range(slabs)])  10.9 us
    ppermute x7, starting transfers between devices, on_device(): came.append(lax.ppermute(messages[turn], 'space', route))  9.18 us
    ppermute x9, waiting for transfers between devices, swap(): lax.ppermute(block, 'space', [(i, i ^ 1 << bit) for i in range(slabs)])  6.02 us
    pallas_call x1, Pallas kernels, on_device(): pl.pallas_call(functools.partial(edge_kernel, half, linked, near, far), o...  5.66 us
    ppermute x1, starting transfers between devices, on_device(): above = lax.ppermute(low, 'space', down)  5.61 us
    ppermute x7, waiting for transfers between devices, on_device(): came.append(lax.ppermute(messages[turn], 'space', route))  5.11 us
    pallas_call x1, Pallas kernels, on_device(): pl.pallas_call(functools.partial(grad_kernel, half, factor), out_shape=(c...  4.46 us
    ppermute x1, waiting for transfers between devices, on_device(): from_below = lax.ppermute(upper, 'space', up)  4.4 us
  transfers between devices with their start and end apart: 20, of which 6 were waited for; matrix products, arithmetic and copies ran while one was open for 3% of the time, Pallas kernels for 20%

profile of v11, /device:TPU:0, one launch (start us, length us, event | category | flops | bytes accessed | tf_op | source)
XLA Modules:
  0.0 69.6 jit_solution(6157694090059480498)
XLA Ops:
  0.7 2.5 %pack.1 = (bf16[8,272,128]{2,1,0:T(8,128)(2,1)S(1)}, bf16[8,272,128]{2,1,0:T(8,128)(2,1)S(1)}, bf16[64,512]{1,0:T(8,128)(2,1)S(1)}, bf16[64,512]{1,0:T(8,128)(2,1)S(1)}) custom-call(s32[1]{0:T(128)} %bitcast.me_ref, bf16[256,512]{1,0:T(8,128)(2,1)} %feats_hbm.1, bf16[529,16,128]{2,1,0:T(8,128)(2,1)} %bitcast.16), custom_call_target="tpu_custom_call" | custom-call | tf_op jit(solution)/shard_map/pack/pallas_call | solution.py:398
  3.2 0.5 collective-permute-start
  3.8 5.6 %collective-permute-start.2 = (bf16[64,512]{1,0:T(8,128)(2,1)S(1)}, bf16[64,512]{1,0:T(8,128)(2,1)S(1)}, u32[]{:S(2)}, u32[]{:S(2)}) collective-permute-start(bf16[64,512]{1,0:T(8,128)(2,1)S(1)} %get-tuple-element.72), channel_id=1, source_target_pairs={{1,0},{2,1},{3,2},{4,3},{5,4},{6,5},{7,6},{8,7},{9,8},{10,9},{11,1... | collective-permute-start | bytes 196616 | tf_op jit(solution)/shard_map/ppermute | solution.py:417
  9.4 1.7 %constant_dynamic-slice_fusion = bf16[1,1,64,529]{2,1,3,0:T(2,128)(2,1)S(1)} fusion(bf16[1,16,128,529]{2,1,3,0:T(8,128)(2,1)} %param.12, s32[]{:T(128)S(6)} %select_n.4, s32[]{:T(128)S(6)} %add.7), kind=kLoop, calls=%fused_computation.1 | loop fusion | bytes 135432 | tf_op jit(solution)/shard_map/slice | solution.py:418
  11.1 0.2 collective-permute-done.1.below_ref
  11.3 0.1 join.1
  11.4 0.7 collective-permute-start.4
  12.1 0.6 collective-permute-start.3
  12.7 3.1 %collective-permute-start.5 = (bf16[2,272,128]{2,1,0:T(8,128)(2,1)S(1)}, bf16[2,272,128]{2,1,0:T(8,128)(2,1)S(1)}, u32[]{:S(2)}, u32[]{:S(2)}) collective-permute-start(bf16[2,272,128]{2,1,0:T(8,128)(2,1)S(1)} %get-tuple-element.94), channel_id=1, source_target_pairs={{0,10},{1,5},{2,8},{3,7},{4,14},{5,1},{6,12},{7,3},{8,2},{9,13},{1... | collective-permute-start | bytes 417800 | tf_op jit(solution)/shard_map/ppermute | solution.py:437
  15.9 2.1 %collective-permute-start.7 = (bf16[2,272,128]{2,1,0:T(8,128)(2,1)S(1)}, bf16[2,272,128]{2,1,0:T(8,128)(2,1)S(1)}, u32[]{:S(2)}, u32[]{:S(2)}) collective-permute-start(bf16[2,272,128]{2,1,0:T(8,128)(2,1)S(1)} %get-tuple-element.96), channel_id=1, source_target_pairs={{0,12},{1,7},{2,14},{3,5},{4,8},{5,3},{6,10},{7,1},{8,4},{9,15},{1... | collective-permute-start | bytes 417800 | tf_op jit(solution)/shard_map/ppermute | solution.py:437
  17.9 5.1 %collective-permute-done.4.rest_1_ = bf16[2,272,128]{2,1,0:T(8,128)(2,1)S(1)} collective-permute-done((bf16[2,272,128]{2,1,0:T(8,128)(2,1)S(1)}, bf16[2,272,128]{2,1,0:T(8,128)(2,1)S(1)}, u32[]{:S(2)}, u32[]{:S(2)}) %collective-permute-start.4) | collective-permute-done | bytes 139296 | tf_op jit(solution)/shard_map/ppermute | solution.py:437
  23.0 2.6 %collective-permute-start.9 = (bf16[2,272,128]{2,1,0:T(8,128)(2,1)S(1)}, bf16[2,272,128]{2,1,0:T(8,128)(2,1)S(1)}, u32[]{:S(2)}, u32[]{:S(2)}) collective-permute-start(bf16[2,272,128]{2,1,0:T(8,128)(2,1)S(1)} %get-tuple-element.98), channel_id=1, source_target_pairs={{0,14},{1,15},{2,12},{3,13},{4,10},{5,11},{6,8},{7,9},{8,6},{9,7},... | collective-permute-start | bytes 417800 | tf_op jit(solution)/shard_map/ppermute | solution.py:437
  25.7 5.7 %edges.1 = (bf16[640,1152]{1,0:T(8,128)(2,1)}, f32[512,1152]{1,0:T(8,128)}, bf16[512,384]{1,0:T(8,128)(2,1)}, bf16[512,512]{1,0:T(8,128)(2,1)S(1)}, bf16[512,640...) custom-call(s32[1]{0:T(128)} %bitcast.me_ref, bf16[256,512]{1,0:T(8,128)(2,1)} %feats_hbm.1, bf16[512,512]{1,0:T(8,128)(2,1)} %w_src_ref.1, ...), custom_call_target="tpu_custom_call" | custom-call | flops 30198988800 | bytes 8388608 | tf_op jit(solution)/shard_map/edges/pallas_call | solution.py:454
  31.4 4.1 %near.1 = (f32[640,512]{1,0:T(8,128)}, f32[512,544]{1,0:T(8,128)}) custom-call(bf16[544,128]{1,0:T(8,128)(2,1)S(1)} %pad.4.own_ref, bf16[512,544]{1,0:T(8,128)(2,1)S(1)} %get-tuple-element.84.w_out_ref, bf16[512,512]{1,0:T(8,128)(2,1)S(1)} %get-tuple-element.89.hidden_ref, f32[512,1152]{1,0:T(8,128)} %get-tuple-element.85.slope_hbm, ...), custom_call_target="tpu_custom_call" | custom-call | flops 5704253440 | bytes 6291456 | tf_op jit(solution)/shard_map/near/pallas_call | solution.py:493
  35.5 4.5 %grads.1 = (f32[8,32,1024]{2,1,0:T(8,128)S(1)}, bf16[8,32,1024]{2,1,0:T(8,128)(2,1)S(1)}, f32[512,512]{1,0:T(8,128)S(1)}, bf16[64,512]{1,0:T(8,128)(2,1)S(1)}, b...) custom-call(s32[1]{0:T(128)} %bitcast.me_ref, bf16[512,544]{1,0:T(8,128)(2,1)S(1)} %get-tuple-element.84.w_out_ref, ...), custom_call_target="tpu_custom_call" | custom-call | tf_op jit(solution)/shard_map/grads/pallas_call | solution.py:517
  39.9 0.5 collective-permute-start.10
  40.4 2.1 %outer.1 = (f32[8,32,640]{2,1,0:T(8,128)S(1)}, bf16[8,32,640]{2,1,0:T(8,128)(2,1)S(1)}) custom-call(s32[1]{0:T(128)} %bitcast.me_ref, bf16[512,640]{1,0:T(8,128)(2,1)S(1)} %get-tuple-element.114.hidden_ref, bf16[544,640]{1,0:T(8,128)(2,1)S(1)} %get-tuple-element.115.g_ref, f32[512,544]{1,0:T(8,128)} %get-tuple-element.116.near_hbm), custom_call_target="tpu_custom_call" | custom-call | flops 12834570240 | bytes 4194304 | tf_op jit(solution)/shard_map/outer/pallas_call | solution.py:541
  42.5 0.1 collective-permute-start.16
  42.7 0.1 fold.6
  42.8 1.7 %collective-permute-start.11 = (bf16[4,32,1024]{2,1,0:T(8,128)(2,1)S(1)}, bf16[4,32,1024]{2,1,0:T(8,128)(2,1)S(1)}, u32[]{:S(2)}, u32[]{:S(2)}) collective-permute-start(bf16[4,32,1024]{2,1,0:T(8,128)(2,1)S(1)} %get-tuple-element.103), channel_id=1, source_target_pairs={{0,2},{1,3},{2,0},{3,1},{4,6},{5,7},{6,4},{7,5},{8,10},{9,11},{10,... | collective-permute-start | bytes 786440 | tf_op jit(solution)/shard_map/ppermute | solution.py:367
  44.6 0.1 fold.9
  44.7 3.8 %collective-permute-start.17 = (bf16[4,32,640]{2,1,0:T(8,128)(2,1)S(1)}, bf16[4,32,640]{2,1,0:T(8,128)(2,1)S(1)}, u32[]{:S(2)}, u32[]{:S(2)}) collective-permute-start(bf16[4,32,640]{2,1,0:T(8,128)(2,1)S(1)} %get-tuple-element.122), channel_id=1, source_target_pairs={{0,4},{1,5},{2,6},{3,7},{4,0},{5,1},{6,2},{7,3},{8,12},{9,13},{10,... | collective-permute-start | bytes 491528 | tf_op jit(solution)/shard_map/ppermute | solution.py:367
  48.4 2.2 %collective-permute-start.12 = (bf16[64,512]{1,0:T(8,128)(2,1)S(1)}, bf16[64,512]{1,0:T(8,128)(2,1)S(1)}, u32[]{:S(2)}, u32[]{:S(2)}) collective-permute-start(bf16[64,512]{1,0:T(8,128)(2,1)S(1)} %get-tuple-element.104), channel_id=1, source_target_pairs={{1,0},{2,1},{3,2},{4,3},{5,4},{6,5},{7,6},{8,7},{9,8},{10,9},{11,1... | collective-permute-start | bytes 196616 | tf_op jit(solution)/shard_map/ppermute | solution.py:581
  50.6 2.0 %collective-permute-done.12.from_above_ref = bf16[64,512]{1,0:T(8,128)(2,1)S(1)} collective-permute-done((bf16[64,512]{1,0:T(8,128)(2,1)S(1)}, bf16[64,512]{1,0:T(8,128)(2,1)S(1)}, u32[]{:S(2)}, u32[]{:S(2)}) %collective-permute-start.12) | collective-permute-done | bytes 65568 | tf_op jit(solution)/shard_map/ppermute | solution.py:581
  52.6 4.4 %collective-permute-done.13.from_below_ref = bf16[64,512]{1,0:T(8,128)(2,1)S(1)} collective-permute-done((bf16[64,512]{1,0:T(8,128)(2,1)S(1)}, bf16[64,512]{1,0:T(8,128)(2,1)S(1)}, u32[]{:S(2)}, u32[]{:S(2)}) %collective-permute-start.13) | collective-permute-done | bytes 65568 | tf_op jit(solution)/shard_map/ppermute | solution.py:582
  57.2 1.0 %collective-permute-start.18 = (bf16[2,32,640]{2,1,0:T(8,128)(2,1)S(1)}, bf16[2,32,640]{2,1,0:T(8,128)(2,1)S(1)}, u32[]{:S(2)}, u32[]{:S(2)}) collective-permute-start(bf16[2,32,640]{2,1,0:T(8,128)(2,1)S(1)} %get-tuple-element.126), channel_id=1, source_target_pairs={{0,2},{1,3},{2,0},{3,1},{4,6},{5,7},{6,4},{7,5},{8,10},{9,11},{10,... | collective-permute-start | bytes 245768 | tf_op jit(solution)/shard_map/ppermute | solution.py:367
  58.3 3.9 %collective-permute-done.14.came_ref = bf16[2,32,1024]{2,1,0:T(8,128)(2,1)S(1)} collective-permute-done((bf16[2,32,1024]{2,1,0:T(8,128)(2,1)S(1)}, bf16[2,32,1024]{2,1,0:T(8,128)(2,1)S(1)}, u32[]{:S(2)}, u32[]{:S(2)}) %collective-permute-start.14) | collective-permute-done | bytes 131104 | tf_op jit(solution)/shard_map/ppermute | solution.py:367
  62.1 0.8 %collective-permute-start.15 = (bf16[1,32,1024]{2,1,0:T(8,128)(2,1)S(1)}, bf16[1,32,1024]{2,1,0:T(8,128)(2,1)S(1)}, u32[]{:S(2)}, u32[]{:S(2)}) collective-permute-start(bf16[1,32,1024]{2,1,0:T(8,128)(2,1)S(1)} %get-tuple-element.113), channel_id=1, source_target_pairs={{0,8},{1,9},{2,10},{3,11},{4,12},{5,13},{6,14},{7,15},{8,0},{9,1},... | collective-permute-start | bytes 196616 | tf_op jit(solution)/shard_map/ppermute | solution.py:367
  63.0 2.3 %collective-permute-start.19 = (bf16[1,32,640]{2,1,0:T(8,128)(2,1)S(1)}, bf16[1,32,640]{2,1,0:T(8,128)(2,1)S(1)}, u32[]{:S(2)}, u32[]{:S(2)}) collective-permute-start(bf16[1,32,640]{2,1,0:T(8,128)(2,1)S(1)} %get-tuple-element.130), channel_id=1, source_target_pairs={{0,8},{1,9},{2,10},{3,11},{4,12},{5,13},{6,14},{7,15},{8,0},{9,1},... | collective-permute-start | bytes 122888 | tf_op jit(solution)/shard_map/ppermute | solution.py:367
  65.2 1.5 %rims.1 = f32[256,512]{1,0:T(8,128)} custom-call(f32[512,512]{1,0:T(8,128)S(1)} %get-tuple-element.99.sums_ref, bf16[64,512]{1,0:T(8,128)(2,1)S(1)} %collective-permute-done.13.from_below_ref, bf16[64,512]{1,0:T(8,128)(2,1)S(1)} %collective-permute-done.12.from_above_ref, bf16[512,512]{1,0:T(8,128)(2,1)S(1)} %copy-done, bf16[512,512]{1,0:T(8,128)(2,1)S(1)} %copy-done.1), custom_call_target="tpu_custom_call" | custom-call | flops 24159191040 | bytes 4194304 | tf_op jit(solution)/shard_map/rims/pallas_call | solution.py:595
  66.8 2.1 %collective-permute-done.19.refs_3_ = bf16[1,32,640]{2,1,0:T(8,128)(2,1)S(1)} collective-permute-done((bf16[1,32,640]{2,1,0:T(8,128)(2,1)S(1)}, bf16[1,32,640]{2,1,0:T(8,128)(2,1)S(1)}, u32[]{:S(2)}, u32[]{:S(2)}) %collective-permute-start.19) | collective-permute-done | bytes 40992 | tf_op jit(solution)/shard_map/ppermute | solution.py:367
  68.9 0.7 %totals.1 = (f32[32,512]{1,0:T(8,128)}, f32[32,512]{1,0:T(8,128)}, f32[32,529]{1,0:T(8,128)}) custom-call(f32[1,32,1024]{2,1,0:T(8,128)S(1)} %get-tuple-element.112.refs_0_, bf16[1,32,1024]{2,1,0:T(8,128)(2,1)S(1)} %collective-permute-done.15.refs_1_, f32[1,32,640]{2,1,0:T(8,128)S(1)} %get-tuple-element.129.refs_2_, ...), custom_call_target="tpu_custom_call" | custom-call | tf_op jit(solution)/shard_map/totals/pallas_call | solution.py:604
  (35 shorter events, 0.4 us)
Async XLA Ops:
  0.6 25.0 %copy-start.2 = (s32[2048]{0:T(1024)S(1)}, s32[2048]{0:T(1024)}, u32[]{:S(2)}) copy-start(s32[2048]{0:T(1024)} %param.13) | copy-start | bytes 24580
  0.6 25.0 %copy-start.3 = (s32[2048]{0:T(1024)S(1)}, s32[2048]{0:T(1024)}, u32[]{:S(2)}) copy-start(s32[2048]{0:T(1024)} %param.14) | copy-start | bytes 24580
  0.7 25.0 %copy-start.4 = (s32[2048]{0:T(1024)S(1)}, s32[2048]{0:T(1024)}, u32[]{:S(2)}) copy-start(s32[2048]{0:T(1024)} %param.15) | copy-start | bytes 24580
  3.2 8.1 %collective-permute-start = (bf16[8,272,128]{2,1,0:T(8,128)(2,1)S(1)}, bf16[8,272,128]{2,1,0:T(8,128)(2,1)S(1)}, u32[]{:S(2)}, u32[]{:S(2)}) collective-permute-start(bf16[8,272,128]{2,1,0:T(8,128)(2,1)S(1)} %get-tuple-element.70), channel_id=1, source_target_pairs={{0,1},{1,0},{2,3},{3,2},{4,5},{5,4},{6,7},{7,6},{8,9},{9,8},{10,11... | collective-permute-start | bytes 1671176 | tf_op jit(solution)/shard_map/ppermute | solution.py:367
  3.7 7.6 %collective-permute-start.1 = (bf16[64,512]{1,0:T(8,128)(2,1)S(1)}, bf16[64,512]{1,0:T(8,128)(2,1)S(1)}, u32[]{:S(2)}, u32[]{:S(2)}) collective-permute-start(bf16[64,512]{1,0:T(8,128)(2,1)S(1)} %get-tuple-element.71), channel_id=1, source_target_pairs={{0,1},{1,2},{2,3},{3,4},{4,5},{5,6},{6,7},{7,8},{8,9},{9,10},{10,1... | collective-permute-start | bytes 196616 | tf_op jit(solution)/shard_map/ppermute | solution.py:416
  3.8 7.6 %collective-permute-start.2 = (bf16[64,512]{1,0:T(8,128)(2,1)S(1)}, bf16[64,512]{1,0:T(8,128)(2,1)S(1)}, u32[]{:S(2)}, u32[]{:S(2)}) collective-permute-start(bf16[64,512]{1,0:T(8,128)(2,1)S(1)} %get-tuple-element.72), channel_id=1, source_target_pairs={{1,0},{2,1},{3,2},{4,3},{5,4},{6,5},{7,6},{8,7},{9,8},{10,9},{11,1... | collective-permute-start | bytes 196616 | tf_op jit(solution)/shard_map/ppermute | solution.py:417
  11.4 11.6 %collective-permute-start.4 = (bf16[2,272,128]{2,1,0:T(8,128)(2,1)S(1)}, bf16[2,272,128]{2,1,0:T(8,128)(2,1)S(1)}, u32[]{:S(2)}, u32[]{:S(2)}) collective-permute-start(bf16[2,272,128]{2,1,0:T(8,128)(2,1)S(1)} %get-tuple-element.75), channel_id=1, source_target_pairs={{0,8},{1,3},{2,10},{3,1},{4,12},{5,7},{6,14},{7,5},{8,0},{9,11},{1... | collective-permute-start | bytes 417800 | tf_op jit(solution)/shard_map/ppermute | solution.py:437
  12.1 10.9 %collective-permute-start.3 = (bf16[2,272,128]{2,1,0:T(8,128)(2,1)S(1)}, bf16[2,272,128]{2,1,0:T(8,128)(2,1)S(1)}, u32[]{:S(2)}, u32[]{:S(2)}) collective-permute-start(bf16[2,272,128]{2,1,0:T(8,128)(2,1)S(1)} %get-tuple-element.74), channel_id=1, source_target_pairs={{0,2},{1,9},{2,0},{3,11},{4,6},{5,13},{6,4},{7,15},{8,10},{9,1},{1... | collective-permute-start | bytes 417800 | tf_op jit(solution)/shard_map/ppermute | solution.py:437
  12.7 22.7 %collective-permute-start.5 = (bf16[2,272,128]{2,1,0:T(8,128)(2,1)S(1)}, bf16[2,272,128]{2,1,0:T(8,128)(2,1)S(1)}, u32[]{:S(2)}, u32[]{:S(2)}) collective-permute-start(bf16[2,272,128]{2,1,0:T(8,128)(2,1)S(1)} %get-tuple-element.94), channel_id=1, source_target_pairs={{0,10},{1,5},{2,8},{3,7},{4,14},{5,1},{6,12},{7,3},{8,2},{9,13},{1... | collective-permute-start | bytes 417800 | tf_op jit(solution)/shard_map/ppermute | solution.py:437
  15.8 19.6 %collective-permute-start.6 = (bf16[2,272,128]{2,1,0:T(8,128)(2,1)S(1)}, bf16[2,272,128]{2,1,0:T(8,128)(2,1)S(1)}, u32[]{:S(2)}, u32[]{:S(2)}) collective-permute-start(bf16[2,272,128]{2,1,0:T(8,128)(2,1)S(1)} %get-tuple-element.95), channel_id=1, source_target_pairs={{0,4},{1,11},{2,6},{3,9},{4,0},{5,15},{6,2},{7,13},{8,12},{9,3},{1... | collective-permute-start | bytes 417800 | tf_op jit(solution)/shard_map/ppermute | solution.py:437
  15.9 19.6 %collective-permute-start.7 = (bf16[2,272,128]{2,1,0:T(8,128)(2,1)S(1)}, bf16[2,272,128]{2,1,0:T(8,128)(2,1)S(1)}, u32[]{:S(2)}, u32[]{:S(2)}) collective-permute-start(bf16[2,272,128]{2,1,0:T(8,128)(2,1)S(1)} %get-tuple-element.96), channel_id=1, source_target_pairs={{0,12},{1,7},{2,14},{3,5},{4,8},{5,3},{6,10},{7,1},{8,4},{9,15},{1... | collective-permute-start | bytes 417800 | tf_op jit(solution)/shard_map/ppermute | solution.py:437
  23.0 12.4 %collective-permute-start.8 = (bf16[2,272,128]{2,1,0:T(8,128)(2,1)S(1)}, bf16[2,272,128]{2,1,0:T(8,128)(2,1)S(1)}, u32[]{:S(2)}, u32[]{:S(2)}) collective-permute-start(bf16[2,272,128]{2,1,0:T(8,128)(2,1)S(1)} %get-tuple-element.97), channel_id=1, source_target_pairs={{0,6},{1,13},{2,4},{3,15},{4,2},{5,9},{6,0},{7,11},{8,14},{9,5},{1... | collective-permute-start | bytes 417800 | tf_op jit(solution)/shard_map/ppermute | solution.py:437
  23.0 12.4 %collective-permute-start.9 = (bf16[2,272,128]{2,1,0:T(8,128)(2,1)S(1)}, bf16[2,272,128]{2,1,0:T(8,128)(2,1)S(1)}, u32[]{:S(2)}, u32[]{:S(2)}) collective-permute-start(bf16[2,272,128]{2,1,0:T(8,128)(2,1)S(1)} %get-tuple-element.98), channel_id=1, source_target_pairs={{0,14},{1,15},{2,12},{3,13},{4,10},{5,11},{6,8},{7,9},{8,6},{9,7},... | collective-permute-start | bytes 417800 | tf_op jit(solution)/shard_map/ppermute | solution.py:437
  39.9 2.7 %collective-permute-start.10 = (bf16[8,32,1024]{2,1,0:T(8,128)(2,1)S(1)}, bf16[8,32,1024]{2,1,0:T(8,128)(2,1)S(1)}, u32[]{:S(2)}, u32[]{:S(2)}) collective-permute-start(bf16[8,32,1024]{2,1,0:T(8,128)(2,1)S(1)} %get-tuple-element.101), channel_id=1, source_target_pairs={{0,1},{1,0},{2,3},{3,2},{4,5},{5,4},{6,7},{7,6},{8,9},{9,8},{10,11... | collective-permute-start | bytes 1572872 | tf_op jit(solution)/shard_map/ppermute | solution.py:367
  42.5 2.0 %collective-permute-start.16 = (bf16[8,32,640]{2,1,0:T(8,128)(2,1)S(1)}, bf16[8,32,640]{2,1,0:T(8,128)(2,1)S(1)}, u32[]{:S(2)}, u32[]{:S(2)}) collective-permute-start(bf16[8,32,640]{2,1,0:T(8,128)(2,1)S(1)} %get-tuple-element.118), channel_id=1, source_target_pairs={{0,1},{1,0},{2,3},{3,2},{4,5},{5,4},{6,7},{7,6},{8,9},{9,8},{10,11... | collective-permute-start | bytes 983048 | tf_op jit(solution)/shard_map/ppermute | solution.py:367
  42.7 22.6 %copy-start = (bf16[512,512]{1,0:T(8,128)(2,1)S(1)}, bf16[512,512]{1,0:T(8,128)(2,1)}, u32[]{:S(2)}) copy-start(bf16[512,512]{1,0:T(8,128)(2,1)} %w_src_ref.1) | copy-start | bytes 1572868
  42.7 22.6 %copy-start.1 = (bf16[512,512]{1,0:T(8,128)(2,1)S(1)}, bf16[512,512]{1,0:T(8,128)(2,1)}, u32[]{:S(2)}) copy-start(bf16[512,512]{1,0:T(8,128)(2,1)} %w_dst_ref.1) | copy-start | bytes 1572868
  42.8 14.2 %collective-permute-start.11 = (bf16[4,32,1024]{2,1,0:T(8,128)(2,1)S(1)}, bf16[4,32,1024]{2,1,0:T(8,128)(2,1)S(1)}, u32[]{:S(2)}, u32[]{:S(2)}) collective-permute-start(bf16[4,32,1024]{2,1,0:T(8,128)(2,1)S(1)} %get-tuple-element.103), channel_id=1, source_target_pairs={{0,2},{1,3},{2,0},{3,1},{4,6},{5,7},{6,4},{7,5},{8,10},{9,11},{10,... | collective-permute-start | bytes 786440 | tf_op jit(solution)/shard_map/ppermute | solution.py:367
  44.7 12.5 %collective-permute-start.17 = (bf16[4,32,640]{2,1,0:T(8,128)(2,1)S(1)}, bf16[4,32,640]{2,1,0:T(8,128)(2,1)S(1)}, u32[]{:S(2)}, u32[]{:S(2)}) collective-permute-start(bf16[4,32,640]{2,1,0:T(8,128)(2,1)S(1)} %get-tuple-element.122), channel_id=1, source_target_pairs={{0,4},{1,5},{2,6},{3,7},{4,0},{5,1},{6,2},{7,3},{8,12},{9,13},{10,... | collective-permute-start | bytes 491528 | tf_op jit(solution)/shard_map/ppermute | solution.py:367
  48.4 4.2 %collective-permute-start.12 = (bf16[64,512]{1,0:T(8,128)(2,1)S(1)}, bf16[64,512]{1,0:T(8,128)(2,1)S(1)}, u32[]{:S(2)}, u32[]{:S(2)}) collective-permute-start(bf16[64,512]{1,0:T(8,128)(2,1)S(1)} %get-tuple-element.104), channel_id=1, source_target_pairs={{1,0},{2,1},{3,2},{4,3},{5,4},{6,5},{7,6},{8,7},{9,8},{10,9},{11,1... | collective-permute-start | bytes 196616 | tf_op jit(solution)/shard_map/ppermute | solution.py:581
  50.6 6.4 %collective-permute-start.13 = (bf16[64,512]{1,0:T(8,128)(2,1)S(1)}, bf16[64,512]{1,0:T(8,128)(2,1)S(1)}, u32[]{:S(2)}, u32[]{:S(2)}) collective-permute-start(bf16[64,512]{1,0:T(8,128)(2,1)S(1)} %get-tuple-element.105), channel_id=1, source_target_pairs={{0,1},{1,2},{2,3},{3,4},{4,5},{5,6},{6,7},{7,8},{8,9},{9,10},{10,1... | collective-permute-start | bytes 196616 | tf_op jit(solution)/shard_map/ppermute | solution.py:582
  57.1 5.0 %collective-permute-start.14 = (bf16[2,32,1024]{2,1,0:T(8,128)(2,1)S(1)}, bf16[2,32,1024]{2,1,0:T(8,128)(2,1)S(1)}, u32[]{:S(2)}, u32[]{:S(2)}) collective-permute-start(bf16[2,32,1024]{2,1,0:T(8,128)(2,1)S(1)} %get-tuple-element.111), channel_id=1, source_target_pairs={{0,4},{1,5},{2,6},{3,7},{4,0},{5,1},{6,2},{7,3},{8,12},{9,13},{10,... | collective-permute-start | bytes 393224 | tf_op jit(solution)/shard_map/ppermute | solution.py:367
  57.2 5.7 %collective-permute-start.18 = (bf16[2,32,640]{2,1,0:T(8,128)(2,1)S(1)}, bf16[2,32,640]{2,1,0:T(8,128)(2,1)S(1)}, u32[]{:S(2)}, u32[]{:S(2)}) collective-permute-start(bf16[2,32,640]{2,1,0:T(8,128)(2,1)S(1)} %get-tuple-element.126), channel_id=1, source_target_pairs={{0,2},{1,3},{2,0},{3,1},{4,6},{5,7},{6,4},{7,5},{8,10},{9,11},{10,... | collective-permute-start | bytes 245768 | tf_op jit(solution)/shard_map/ppermute | solution.py:367
  62.1 6.8 %collective-permute-start.15 = (bf16[1,32,1024]{2,1,0:T(8,128)(2,1)S(1)}, bf16[1,32,1024]{2,1,0:T(8,128)(2,1)S(1)}, u32[]{:S(2)}, u32[]{:S(2)}) collective-permute-start(bf16[1,32,1024]{2,1,0:T(8,128)(2,1)S(1)} %get-tuple-element.113), channel_id=1, source_target_pairs={{0,8},{1,9},{2,10},{3,11},{4,12},{5,13},{6,14},{7,15},{8,0},{9,1},... | collective-permute-start | bytes 196616 | tf_op jit(solution)/shard_map/ppermute | solution.py:367
  63.0 6.0 %collective-permute-start.19 = (bf16[1,32,640]{2,1,0:T(8,128)(2,1)S(1)}, bf16[1,32,640]{2,1,0:T(8,128)(2,1)S(1)}, u32[]{:S(2)}, u32[]{:S(2)}) collective-permute-start(bf16[1,32,640]{2,1,0:T(8,128)(2,1)S(1)} %get-tuple-element.130), channel_id=1, source_target_pairs={{0,8},{1,9},{2,10},{3,11},{4,12},{5,13},{6,14},{7,15},{8,0},{9,1},... | collective-permute-start | bytes 122888 | tf_op jit(solution)/shard_map/ppermute | solution.py:367

commit v12 on v11

--- a/solution.py
+++ b/solution.py
@@ -438,8 +438,8 @@
         for turn in range(1, quarter - 1):
             came[turn], below, above, me = lax.optimization_barrier((came[turn], below, above, me))
         ids = [(2 * first + j, 2 * second + j) for first, second in turns for j in range(2)]
-        near, far = tuple(ids[: 2 * quarter - 2]), tuple(ids[2 * quarter - 2 :])
-        came_near, came_far = came[: quarter - 1], came[quarter - 1 :]
+        near, far = tuple(ids[: 2 * quarter]), tuple(ids[2 * quarter :])
+        came_near, came_far = came[:quarter], came[quarter:]
     else:
         packed = jnp.stack([even, odd], axis=1).reshape(slabs, rows, LANES)
         near, far = (), tuple(range(slabs))

time: 69.9 us -> 69.1 us (0.989)
  starting transfers between devices: 27.9 us -> 27 us
    ppermute x9, starting transfers between devices: 10.9 us -> 9.96 us  [swap(): lax.ppermute(block, 'space', [(i, i ^ 1 << bit) for i in range(slabs)])]
    pallas_call x1, Pallas kernels: 4.05 us -> 4.78 us  [on_device(): pl.pallas_call(functools.partial(near_kernel, half), out_shape=(pltpu.HBM...]
    pallas_call x1, Pallas kernels: 4.46 us -> 3.75 us  [on_device(): pl.pallas_call(functools.partial(grad_kernel, half, factor), out_shape=(c...]
  transfers between devices with their start and end apart: 20 -> 20, of which waited for: 6 -> 6; matrix products, arithmetic and copies ran while one was open for 3% -> 3% of each run, Pallas kernels for 20% -> 21%
where the time goes in v12:
time: 69.1 us; the launch traced here: 68.8 us
  starting transfers between devices  27 us (39%)
  Pallas kernels  21.5 us (31%)
  waiting for transfers between devices  17.7 us (26%)
  local copies, waits for them, and re-layouts  1.78 us (3%)
  between operations  0.83 us (1%)
    ppermute x9, starting transfers between devices, swap(): lax.ppermute(block, 'space', [(i, i ^ 1 << bit) for i in range(slabs)])  9.96 us
    ppermute x7, starting transfers between devices, on_device(): came.append(lax.ppermute(messages[turn], 'space', route))  9.18 us
    ppermute x9, waiting for transfers between devices, swap(): lax.ppermute(block, 'space', [(i, i ^ 1 << bit) for i in range(slabs)])  6.03 us
    pallas_call x1, Pallas kernels, on_device(): pl.pallas_call(functools.partial(edge_kernel, half, linked, near, far), o...  5.82 us
    ppermute x1, starting transfers between devices, on_device(): above = lax.ppermute(low, 'space', down)  5.61 us
    ppermute x7, waiting for transfers between devices, on_device(): came.append(lax.ppermute(messages[turn], 'space', route))  5.11 us
    pallas_call x1, Pallas kernels, on_device(): pl.pallas_call(functools.partial(near_kernel, half), out_shape=(pltpu.HBM...  4.78 us
    ppermute x1, waiting for transfers between devices, on_device(): from_below = lax.ppermute(upper, 'space', up)  4.4 us
  transfers between devices with their start and end apart: 20, of which 6 were waited for; matrix products, arithmetic and copies ran while one was open for 3% of the time, Pallas kernels for 21%

profile of v12, /device:TPU:0, one launch (start us, length us, event | category | flops | bytes accessed | tf_op | source)
XLA Modules:
  0.0 68.8 jit_solution(3684357364172364496)
XLA Ops:
  0.7 2.5 %pack.1 = (bf16[8,272,128]{2,1,0:T(8,128)(2,1)S(1)}, bf16[8,272,128]{2,1,0:T(8,128)(2,1)S(1)}, bf16[64,512]{1,0:T(8,128)(2,1)S(1)}, bf16[64,512]{1,0:T(8,128)(2,1)S(1)}) custom-call(s32[1]{0:T(128)} %bitcast.me_ref, bf16[256,512]{1,0:T(8,128)(2,1)} %feats_hbm.1, bf16[529,16,128]{2,1,0:T(8,128)(2,1)} %bitcast.16), custom_call_target="tpu_custom_call" | custom-call | tf_op jit(solution)/shard_map/pack/pallas_call | solution.py:398
  3.2 0.5 collective-permute-start
  3.8 5.6 %collective-permute-start.2 = (bf16[64,512]{1,0:T(8,128)(2,1)S(1)}, bf16[64,512]{1,0:T(8,128)(2,1)S(1)}, u32[]{:S(2)}, u32[]{:S(2)}) collective-permute-start(bf16[64,512]{1,0:T(8,128)(2,1)S(1)} %get-tuple-element.72), channel_id=1, source_target_pairs={{1,0},{2,1},{3,2},{4,3},{5,4},{6,5},{7,6},{8,7},{9,8},{10,9},{11,1... | collective-permute-start | bytes 196616 | tf_op jit(solution)/shard_map/ppermute | solution.py:417
  9.4 1.7 %constant_dynamic-slice_fusion = bf16[1,1,64,529]{2,1,3,0:T(2,128)(2,1)S(1)} fusion(bf16[1,16,128,529]{2,1,3,0:T(8,128)(2,1)} %param.12, s32[]{:T(128)S(6)} %select_n.4, s32[]{:T(128)S(6)} %add.7), kind=kLoop, calls=%fused_computation.1 | loop fusion | bytes 135432 | tf_op jit(solution)/shard_map/slice | solution.py:418
  11.1 0.2 collective-permute-done.1.below_ref
  11.3 0.1 join.1
  11.4 0.7 %collective-permute-start.4 = (bf16[2,272,128]{2,1,0:T(8,128)(2,1)S(1)}, bf16[2,272,128]{2,1,0:T(8,128)(2,1)S(1)}, u32[]{:S(2)}, u32[]{:S(2)}) collective-permute-start(bf16[2,272,128]{2,1,0:T(8,128)(2,1)S(1)} %get-tuple-element.75), channel_id=1, source_target_pairs={{0,8},{1,3},{2,10},{3,1},{4,12},{5,7},{6,14},{7,5},{8,0},{9,11},{1... | collective-permute-start | bytes 417800 | tf_op jit(solution)/shard_map/ppermute | solution.py:437
  12.1 0.6 collective-permute-start.3
  12.7 3.1 %collective-permute-start.5 = (bf16[2,272,128]{2,1,0:T(8,128)(2,1)S(1)}, bf16[2,272,128]{2,1,0:T(8,128)(2,1)S(1)}, u32[]{:S(2)}, u32[]{:S(2)}) collective-permute-start(bf16[2,272,128]{2,1,0:T(8,128)(2,1)S(1)} %get-tuple-element.93), channel_id=1, source_target_pairs={{0,10},{1,5},{2,8},{3,7},{4,14},{5,1},{6,12},{7,3},{8,2},{9,13},{1... | collective-permute-start | bytes 417800 | tf_op jit(solution)/shard_map/ppermute | solution.py:437
  15.9 2.1 %collective-permute-start.7 = (bf16[2,272,128]{2,1,0:T(8,128)(2,1)S(1)}, bf16[2,272,128]{2,1,0:T(8,128)(2,1)S(1)}, u32[]{:S(2)}, u32[]{:S(2)}) collective-permute-start(bf16[2,272,128]{2,1,0:T(8,128)(2,1)S(1)} %get-tuple-element.96), channel_id=1, source_target_pairs={{0,12},{1,7},{2,14},{3,5},{4,8},{5,3},{6,10},{7,1},{8,4},{9,15},{1... | collective-permute-start | bytes 417800 | tf_op jit(solution)/shard_map/ppermute | solution.py:437
  17.9 5.1 %collective-permute-done.4.rest_1_ = bf16[2,272,128]{2,1,0:T(8,128)(2,1)S(1)} collective-permute-done((bf16[2,272,128]{2,1,0:T(8,128)(2,1)S(1)}, bf16[2,272,128]{2,1,0:T(8,128)(2,1)S(1)}, u32[]{:S(2)}, u32[]{:S(2)}) %collective-permute-start.4) | collective-permute-done | bytes 139296 | tf_op jit(solution)/shard_map/ppermute | solution.py:437
  23.0 2.6 %collective-permute-start.9 = (bf16[2,272,128]{2,1,0:T(8,128)(2,1)S(1)}, bf16[2,272,128]{2,1,0:T(8,128)(2,1)S(1)}, u32[]{:S(2)}, u32[]{:S(2)}) collective-permute-start(bf16[2,272,128]{2,1,0:T(8,128)(2,1)S(1)} %get-tuple-element.98), channel_id=1, source_target_pairs={{0,14},{1,15},{2,12},{3,13},{4,10},{5,11},{6,8},{7,9},{8,6},{9,7},... | collective-permute-start | bytes 417800 | tf_op jit(solution)/shard_map/ppermute | solution.py:437
  25.7 5.8 %edges.1 = (bf16[640,1152]{1,0:T(8,128)(2,1)}, f32[512,1152]{1,0:T(8,128)}, bf16[512,384]{1,0:T(8,128)(2,1)}, bf16[512,640]{1,0:T(8,128)(2,1)S(1)}, bf16[512,512...) custom-call(s32[1]{0:T(128)} %bitcast.me_ref, bf16[256,512]{1,0:T(8,128)(2,1)} %feats_hbm.1, bf16[512,512]{1,0:T(8,128)(2,1)} %w_src_ref.1, ...), custom_call_target="tpu_custom_call" | custom-call | flops 30198988800 | bytes 8388608 | tf_op jit(solution)/shard_map/edges/pallas_call | solution.py:454
  31.5 4.8 %near.1 = (f32[640,512]{1,0:T(8,128)}, f32[512,544]{1,0:T(8,128)}) custom-call(bf16[544,128]{1,0:T(8,128)(2,1)S(1)} %pad.4.own_ref, bf16[512,544]{1,0:T(8,128)(2,1)S(1)} %get-tuple-element.84.w_out_ref, bf16[512,640]{1,0:T(8,128)(2,1)S(1)} %get-tuple-element.89.hidden_ref, f32[512,1152]{1,0:T(8,128)} %get-tuple-element.85.slope_hbm, ...), custom_call_target="tpu_custom_call" | custom-call | flops 7130316800 | bytes 6291456 | tf_op jit(solution)/shard_map/near/pallas_call | solution.py:493
  36.4 3.8 %grads.1 = (f32[8,32,1024]{2,1,0:T(8,128)S(1)}, bf16[8,32,1024]{2,1,0:T(8,128)(2,1)S(1)}, f32[512,512]{1,0:T(8,128)S(1)}, bf16[64,512]{1,0:T(8,128)(2,1)S(1)}, b...) custom-call(s32[1]{0:T(128)} %bitcast.me_ref, bf16[512,544]{1,0:T(8,128)(2,1)S(1)} %get-tuple-element.84.w_out_ref, ...), custom_call_target="tpu_custom_call" | custom-call | tf_op jit(solution)/shard_map/grads/pallas_call | solution.py:517
  40.1 0.5 collective-permute-start.10
  40.6 1.9 %outer.1 = (f32[8,32,640]{2,1,0:T(8,128)S(1)}, bf16[8,32,640]{2,1,0:T(8,128)(2,1)S(1)}) custom-call(s32[1]{0:T(128)} %bitcast.me_ref, bf16[512,512]{1,0:T(8,128)(2,1)S(1)} %get-tuple-element.114.hidden_ref, bf16[544,512]{1,0:T(8,128)(2,1)S(1)} %get-tuple-element.115.g_ref, f32[512,544]{1,0:T(8,128)} %get-tuple-element.116.near_hbm), custom_call_target="tpu_custom_call" | custom-call | flops 12834570240 | bytes 4194304 | tf_op jit(solution)/shard_map/outer/pallas_call | solution.py:541
  42.6 0.1 collective-permute-start.16
  42.7 0.1 fold.6
  42.9 1.7 %collective-permute-start.11 = (bf16[4,32,1024]{2,1,0:T(8,128)(2,1)S(1)}, bf16[4,32,1024]{2,1,0:T(8,128)(2,1)S(1)}, u32[]{:S(2)}, u32[]{:S(2)}) collective-permute-start(bf16[4,32,1024]{2,1,0:T(8,128)(2,1)S(1)} %get-tuple-element.103), channel_id=1, source_target_pairs={{0,2},{1,3},{2,0},{3,1},{4,6},{5,7},{6,4},{7,5},{8,10},{9,11},{10,... | collective-permute-start | bytes 786440 | tf_op jit(solution)/shard_map/ppermute | solution.py:367
  44.6 0.1 fold.9
  44.7 2.9 %collective-permute-start.17 = (bf16[4,32,640]{2,1,0:T(8,128)(2,1)S(1)}, bf16[4,32,640]{2,1,0:T(8,128)(2,1)S(1)}, u32[]{:S(2)}, u32[]{:S(2)}) collective-permute-start(bf16[4,32,640]{2,1,0:T(8,128)(2,1)S(1)} %get-tuple-element.122), channel_id=1, source_target_pairs={{0,4},{1,5},{2,6},{3,7},{4,0},{5,1},{6,2},{7,3},{8,12},{9,13},{10,... | collective-permute-start | bytes 491528 | tf_op jit(solution)/shard_map/ppermute | solution.py:367
  47.6 2.2 %collective-permute-start.12 = (bf16[64,512]{1,0:T(8,128)(2,1)S(1)}, bf16[64,512]{1,0:T(8,128)(2,1)S(1)}, u32[]{:S(2)}, u32[]{:S(2)}) collective-permute-start(bf16[64,512]{1,0:T(8,128)(2,1)S(1)} %get-tuple-element.104), channel_id=1, source_target_pairs={{1,0},{2,1},{3,2},{4,3},{5,4},{6,5},{7,6},{8,7},{9,8},{10,9},{11,1... | collective-permute-start | bytes 196616 | tf_op jit(solution)/shard_map/ppermute | solution.py:581
  49.8 2.0 %collective-permute-done.12.from_above_ref = bf16[64,512]{1,0:T(8,128)(2,1)S(1)} collective-permute-done((bf16[64,512]{1,0:T(8,128)(2,1)S(1)}, bf16[64,512]{1,0:T(8,128)(2,1)S(1)}, u32[]{:S(2)}, u32[]{:S(2)}) %collective-permute-start.12) | collective-permute-done | bytes 65568 | tf_op jit(solution)/shard_map/ppermute | solution.py:581
  51.7 4.4 %collective-permute-done.13.from_below_ref = bf16[64,512]{1,0:T(8,128)(2,1)S(1)} collective-permute-done((bf16[64,512]{1,0:T(8,128)(2,1)S(1)}, bf16[64,512]{1,0:T(8,128)(2,1)S(1)}, u32[]{:S(2)}, u32[]{:S(2)}) %collective-permute-start.13) | collective-permute-done | bytes 65568 | tf_op jit(solution)/shard_map/ppermute | solution.py:582
  56.4 1.0 %collective-permute-start.18 = (bf16[2,32,640]{2,1,0:T(8,128)(2,1)S(1)}, bf16[2,32,640]{2,1,0:T(8,128)(2,1)S(1)}, u32[]{:S(2)}, u32[]{:S(2)}) collective-permute-start(bf16[2,32,640]{2,1,0:T(8,128)(2,1)S(1)} %get-tuple-element.126), channel_id=1, source_target_pairs={{0,2},{1,3},{2,0},{3,1},{4,6},{5,7},{6,4},{7,5},{8,10},{9,11},{10,... | collective-permute-start | bytes 245768 | tf_op jit(solution)/shard_map/ppermute | solution.py:367
  57.4 3.8 %collective-permute-done.14.came_ref = bf16[2,32,1024]{2,1,0:T(8,128)(2,1)S(1)} collective-permute-done((bf16[2,32,1024]{2,1,0:T(8,128)(2,1)S(1)}, bf16[2,32,1024]{2,1,0:T(8,128)(2,1)S(1)}, u32[]{:S(2)}, u32[]{:S(2)}) %collective-permute-start.14) | collective-permute-done | bytes 131104 | tf_op jit(solution)/shard_map/ppermute | solution.py:367
  61.3 0.8 %collective-permute-start.15 = (bf16[1,32,1024]{2,1,0:T(8,128)(2,1)S(1)}, bf16[1,32,1024]{2,1,0:T(8,128)(2,1)S(1)}, u32[]{:S(2)}, u32[]{:S(2)}) collective-permute-start(bf16[1,32,1024]{2,1,0:T(8,128)(2,1)S(1)} %get-tuple-element.113), channel_id=1, source_target_pairs={{0,8},{1,9},{2,10},{3,11},{4,12},{5,13},{6,14},{7,15},{8,0},{9,1},... | collective-permute-start | bytes 196616 | tf_op jit(solution)/shard_map/ppermute | solution.py:367
  62.1 2.3 %collective-permute-start.19 = (bf16[1,32,640]{2,1,0:T(8,128)(2,1)S(1)}, bf16[1,32,640]{2,1,0:T(8,128)(2,1)S(1)}, u32[]{:S(2)}, u32[]{:S(2)}) collective-permute-start(bf16[1,32,640]{2,1,0:T(8,128)(2,1)S(1)} %get-tuple-element.130), channel_id=1, source_target_pairs={{0,8},{1,9},{2,10},{3,11},{4,12},{5,13},{6,14},{7,15},{8,0},{9,1},... | collective-permute-start | bytes 122888 | tf_op jit(solution)/shard_map/ppermute | solution.py:367
  64.4 1.5 %rims.1 = f32[256,512]{1,0:T(8,128)} custom-call(f32[512,512]{1,0:T(8,128)S(1)} %get-tuple-element.99.sums_ref, bf16[64,512]{1,0:T(8,128)(2,1)S(1)} %collective-permute-done.13.from_below_ref, bf16[64,512]{1,0:T(8,128)(2,1)S(1)} %collective-permute-done.12.from_above_ref, bf16[512,512]{1,0:T(8,128)(2,1)S(1)} %copy-done, bf16[512,512]{1,0:T(8,128)(2,1)S(1)} %copy-done.1), custom_call_target="tpu_custom_call" | custom-call | flops 24159191040 | bytes 4194304 | tf_op jit(solution)/shard_map/rims/pallas_call | solution.py:595
  65.9 2.2 %collective-permute-done.19.refs_3_ = bf16[1,32,640]{2,1,0:T(8,128)(2,1)S(1)} collective-permute-done((bf16[1,32,640]{2,1,0:T(8,128)(2,1)S(1)}, bf16[1,32,640]{2,1,0:T(8,128)(2,1)S(1)}, u32[]{:S(2)}, u32[]{:S(2)}) %collective-permute-start.19) | collective-permute-done | bytes 40992 | tf_op jit(solution)/shard_map/ppermute | solution.py:367
  68.1 0.7 %totals.1 = (f32[32,512]{1,0:T(8,128)}, f32[32,512]{1,0:T(8,128)}, f32[32,529]{1,0:T(8,128)}) custom-call(f32[1,32,1024]{2,1,0:T(8,128)S(1)} %get-tuple-element.112.refs_0_, bf16[1,32,1024]{2,1,0:T(8,128)(2,1)S(1)} %collective-permute-done.15.refs_1_, f32[1,32,640]{2,1,0:T(8,128)S(1)} %get-tuple-element.129.refs_2_, ...), custom_call_target="tpu_custom_call" | custom-call | tf_op jit(solution)/shard_map/totals/pallas_call | solution.py:604
  (35 shorter events, 0.4 us)
Async XLA Ops:
  0.6 25.0 %copy-start.2 = (s32[2048]{0:T(1024)S(1)}, s32[2048]{0:T(1024)}, u32[]{:S(2)}) copy-start(s32[2048]{0:T(1024)} %param.13) | copy-start | bytes 24580
  0.6 25.0 %copy-start.3 = (s32[2048]{0:T(1024)S(1)}, s32[2048]{0:T(1024)}, u32[]{:S(2)}) copy-start(s32[2048]{0:T(1024)} %param.14) | copy-start | bytes 24580
  0.7 25.0 %copy-start.4 = (s32[2048]{0:T(1024)S(1)}, s32[2048]{0:T(1024)}, u32[]{:S(2)}) copy-start(s32[2048]{0:T(1024)} %param.15) | copy-start | bytes 24580
  3.2 8.1 %collective-permute-start = (bf16[8,272,128]{2,1,0:T(8,128)(2,1)S(1)}, bf16[8,272,128]{2,1,0:T(8,128)(2,1)S(1)}, u32[]{:S(2)}, u32[]{:S(2)}) collective-permute-start(bf16[8,272,128]{2,1,0:T(8,128)(2,1)S(1)} %get-tuple-element.70), channel_id=1, source_target_pairs={{0,1},{1,0},{2,3},{3,2},{4,5},{5,4},{6,7},{7,6},{8,9},{9,8},{10,11... | collective-permute-start | bytes 1671176 | tf_op jit(solution)/shard_map/ppermute | solution.py:367
  3.7 7.6 %collective-permute-start.1 = (bf16[64,512]{1,0:T(8,128)(2,1)S(1)}, bf16[64,512]{1,0:T(8,128)(2,1)S(1)}, u32[]{:S(2)}, u32[]{:S(2)}) collective-permute-start(bf16[64,512]{1,0:T(8,128)(2,1)S(1)} %get-tuple-element.71), channel_id=1, source_target_pairs={{0,1},{1,2},{2,3},{3,4},{4,5},{5,6},{6,7},{7,8},{8,9},{9,10},{10,1... | collective-permute-start | bytes 196616 | tf_op jit(solution)/shard_map/ppermute | solution.py:416
  3.8 7.6 %collective-permute-start.2 = (bf16[64,512]{1,0:T(8,128)(2,1)S(1)}, bf16[64,512]{1,0:T(8,128)(2,1)S(1)}, u32[]{:S(2)}, u32[]{:S(2)}) collective-permute-start(bf16[64,512]{1,0:T(8,128)(2,1)S(1)} %get-tuple-element.72), channel_id=1, source_target_pairs={{1,0},{2,1},{3,2},{4,3},{5,4},{6,5},{7,6},{8,7},{9,8},{10,9},{11,1... | collective-permute-start | bytes 196616 | tf_op jit(solution)/shard_map/ppermute | solution.py:417
  11.4 11.6 %collective-permute-start.4 = (bf16[2,272,128]{2,1,0:T(8,128)(2,1)S(1)}, bf16[2,272,128]{2,1,0:T(8,128)(2,1)S(1)}, u32[]{:S(2)}, u32[]{:S(2)}) collective-permute-start(bf16[2,272,128]{2,1,0:T(8,128)(2,1)S(1)} %get-tuple-element.75), channel_id=1, source_target_pairs={{0,8},{1,3},{2,10},{3,1},{4,12},{5,7},{6,14},{7,5},{8,0},{9,11},{1... | collective-permute-start | bytes 417800 | tf_op jit(solution)/shard_map/ppermute | solution.py:437
  12.1 10.9 %collective-permute-start.3 = (bf16[2,272,128]{2,1,0:T(8,128)(2,1)S(1)}, bf16[2,272,128]{2,1,0:T(8,128)(2,1)S(1)}, u32[]{:S(2)}, u32[]{:S(2)}) collective-permute-start(bf16[2,272,128]{2,1,0:T(8,128)(2,1)S(1)} %get-tuple-element.74), channel_id=1, source_target_pairs={{0,2},{1,9},{2,0},{3,11},{4,6},{5,13},{6,4},{7,15},{8,10},{9,1},{1... | collective-permute-start | bytes 417800 | tf_op jit(solution)/shard_map/ppermute | solution.py:437
  12.7 18.8 %collective-permute-start.5 = (bf16[2,272,128]{2,1,0:T(8,128)(2,1)S(1)}, bf16[2,272,128]{2,1,0:T(8,128)(2,1)S(1)}, u32[]{:S(2)}, u32[]{:S(2)}) collective-permute-start(bf16[2,272,128]{2,1,0:T(8,128)(2,1)S(1)} %get-tuple-element.93), channel_id=1, source_target_pairs={{0,10},{1,5},{2,8},{3,7},{4,14},{5,1},{6,12},{7,3},{8,2},{9,13},{1... | collective-permute-start | bytes 417800 | tf_op jit(solution)/shard_map/ppermute | solution.py:437
  15.8 20.5 %collective-permute-start.6 = (bf16[2,272,128]{2,1,0:T(8,128)(2,1)S(1)}, bf16[2,272,128]{2,1,0:T(8,128)(2,1)S(1)}, u32[]{:S(2)}, u32[]{:S(2)}) collective-permute-start(bf16[2,272,128]{2,1,0:T(8,128)(2,1)S(1)} %get-tuple-element.95), channel_id=1, source_target_pairs={{0,4},{1,11},{2,6},{3,9},{4,0},{5,15},{6,2},{7,13},{8,12},{9,3},{1... | collective-permute-start | bytes 417800 | tf_op jit(solution)/shard_map/ppermute | solution.py:437
  15.9 20.5 %collective-permute-start.7 = (bf16[2,272,128]{2,1,0:T(8,128)(2,1)S(1)}, bf16[2,272,128]{2,1,0:T(8,128)(2,1)S(1)}, u32[]{:S(2)}, u32[]{:S(2)}) collective-permute-start(bf16[2,272,128]{2,1,0:T(8,128)(2,1)S(1)} %get-tuple-element.96), channel_id=1, source_target_pairs={{0,12},{1,7},{2,14},{3,5},{4,8},{5,3},{6,10},{7,1},{8,4},{9,15},{1... | collective-permute-start | bytes 417800 | tf_op jit(solution)/shard_map/ppermute | solution.py:437
  23.0 13.3 %collective-permute-start.8 = (bf16[2,272,128]{2,1,0:T(8,128)(2,1)S(1)}, bf16[2,272,128]{2,1,0:T(8,128)(2,1)S(1)}, u32[]{:S(2)}, u32[]{:S(2)}) collective-permute-start(bf16[2,272,128]{2,1,0:T(8,128)(2,1)S(1)} %get-tuple-element.97), channel_id=1, source_target_pairs={{0,6},{1,13},{2,4},{3,15},{4,2},{5,9},{6,0},{7,11},{8,14},{9,5},{1... | collective-permute-start | bytes 417800 | tf_op jit(solution)/shard_map/ppermute | solution.py:437
  23.0 13.3 %collective-permute-start.9 = (bf16[2,272,128]{2,1,0:T(8,128)(2,1)S(1)}, bf16[2,272,128]{2,1,0:T(8,128)(2,1)S(1)}, u32[]{:S(2)}, u32[]{:S(2)}) collective-permute-start(bf16[2,272,128]{2,1,0:T(8,128)(2,1)S(1)} %get-tuple-element.98), channel_id=1, source_target_pairs={{0,14},{1,15},{2,12},{3,13},{4,10},{5,11},{6,8},{7,9},{8,6},{9,7},... | collective-permute-start | bytes 417800 | tf_op jit(solution)/shard_map/ppermute | solution.py:437
  40.1 2.6 %collective-permute-start.10 = (bf16[8,32,1024]{2,1,0:T(8,128)(2,1)S(1)}, bf16[8,32,1024]{2,1,0:T(8,128)(2,1)S(1)}, u32[]{:S(2)}, u32[]{:S(2)}) collective-permute-start(bf16[8,32,1024]{2,1,0:T(8,128)(2,1)S(1)} %get-tuple-element.101), channel_id=1, source_target_pairs={{0,1},{1,0},{2,3},{3,2},{4,5},{5,4},{6,7},{7,6},{8,9},{9,8},{10,11... | collective-permute-start | bytes 1572872 | tf_op jit(solution)/shard_map/ppermute | solution.py:367
  42.6 2.0 %collective-permute-start.16 = (bf16[8,32,640]{2,1,0:T(8,128)(2,1)S(1)}, bf16[8,32,640]{2,1,0:T(8,128)(2,1)S(1)}, u32[]{:S(2)}, u32[]{:S(2)}) collective-permute-start(bf16[8,32,640]{2,1,0:T(8,128)(2,1)S(1)} %get-tuple-element.118), channel_id=1, source_target_pairs={{0,1},{1,0},{2,3},{3,2},{4,5},{5,4},{6,7},{7,6},{8,9},{9,8},{10,11... | collective-permute-start | bytes 983048 | tf_op jit(solution)/shard_map/ppermute | solution.py:367
  42.7 21.7 %copy-start = (bf16[512,512]{1,0:T(8,128)(2,1)S(1)}, bf16[512,512]{1,0:T(8,128)(2,1)}, u32[]{:S(2)}) copy-start(bf16[512,512]{1,0:T(8,128)(2,1)} %w_src_ref.1) | copy-start | bytes 1572868
  42.7 21.7 %copy-start.1 = (bf16[512,512]{1,0:T(8,128)(2,1)S(1)}, bf16[512,512]{1,0:T(8,128)(2,1)}, u32[]{:S(2)}) copy-start(bf16[512,512]{1,0:T(8,128)(2,1)} %w_dst_ref.1) | copy-start | bytes 1572868
  42.9 13.3 %collective-permute-start.11 = (bf16[4,32,1024]{2,1,0:T(8,128)(2,1)S(1)}, bf16[4,32,1024]{2,1,0:T(8,128)(2,1)S(1)}, u32[]{:S(2)}, u32[]{:S(2)}) collective-permute-start(bf16[4,32,1024]{2,1,0:T(8,128)(2,1)S(1)} %get-tuple-element.103), channel_id=1, source_target_pairs={{0,2},{1,3},{2,0},{3,1},{4,6},{5,7},{6,4},{7,5},{8,10},{9,11},{10,... | collective-permute-start | bytes 786440 | tf_op jit(solution)/shard_map/ppermute | solution.py:367
  44.7 11.6 %collective-permute-start.17 = (bf16[4,32,640]{2,1,0:T(8,128)(2,1)S(1)}, bf16[4,32,640]{2,1,0:T(8,128)(2,1)S(1)}, u32[]{:S(2)}, u32[]{:S(2)}) collective-permute-start(bf16[4,32,640]{2,1,0:T(8,128)(2,1)S(1)} %get-tuple-element.122), channel_id=1, source_target_pairs={{0,4},{1,5},{2,6},{3,7},{4,0},{5,1},{6,2},{7,3},{8,12},{9,13},{10,... | collective-permute-start | bytes 491528 | tf_op jit(solution)/shard_map/ppermute | solution.py:367
  47.6 4.2 %collective-permute-start.12 = (bf16[64,512]{1,0:T(8,128)(2,1)S(1)}, bf16[64,512]{1,0:T(8,128)(2,1)S(1)}, u32[]{:S(2)}, u32[]{:S(2)}) collective-permute-start(bf16[64,512]{1,0:T(8,128)(2,1)S(1)} %get-tuple-element.104), channel_id=1, source_target_pairs={{1,0},{2,1},{3,2},{4,3},{5,4},{6,5},{7,6},{8,7},{9,8},{10,9},{11,1... | collective-permute-start | bytes 196616 | tf_op jit(solution)/shard_map/ppermute | solution.py:581
  49.8 6.4 %collective-permute-start.13 = (bf16[64,512]{1,0:T(8,128)(2,1)S(1)}, bf16[64,512]{1,0:T(8,128)(2,1)S(1)}, u32[]{:S(2)}, u32[]{:S(2)}) collective-permute-start(bf16[64,512]{1,0:T(8,128)(2,1)S(1)} %get-tuple-element.105), channel_id=1, source_target_pairs={{0,1},{1,2},{2,3},{3,4},{4,5},{5,6},{6,7},{7,8},{8,9},{9,10},{10,1... | collective-permute-start | bytes 196616 | tf_op jit(solution)/shard_map/ppermute | solution.py:582
  56.2 5.0 %collective-permute-start.14 = (bf16[2,32,1024]{2,1,0:T(8,128)(2,1)S(1)}, bf16[2,32,1024]{2,1,0:T(8,128)(2,1)S(1)}, u32[]{:S(2)}, u32[]{:S(2)}) collective-permute-start(bf16[2,32,1024]{2,1,0:T(8,128)(2,1)S(1)} %get-tuple-element.111), channel_id=1, source_target_pairs={{0,4},{1,5},{2,6},{3,7},{4,0},{5,1},{6,2},{7,3},{8,12},{9,13},{10,... | collective-permute-start | bytes 393224 | tf_op jit(solution)/shard_map/ppermute | solution.py:367
  56.4 5.7 %collective-permute-start.18 = (bf16[2,32,640]{2,1,0:T(8,128)(2,1)S(1)}, bf16[2,32,640]{2,1,0:T(8,128)(2,1)S(1)}, u32[]{:S(2)}, u32[]{:S(2)}) collective-permute-start(bf16[2,32,640]{2,1,0:T(8,128)(2,1)S(1)} %get-tuple-element.126), channel_id=1, source_target_pairs={{0,2},{1,3},{2,0},{3,1},{4,6},{5,7},{6,4},{7,5},{8,10},{9,11},{10,... | collective-permute-start | bytes 245768 | tf_op jit(solution)/shard_map/ppermute | solution.py:367
  61.3 6.8 %collective-permute-start.15 = (bf16[1,32,1024]{2,1,0:T(8,128)(2,1)S(1)}, bf16[1,32,1024]{2,1,0:T(8,128)(2,1)S(1)}, u32[]{:S(2)}, u32[]{:S(2)}) collective-permute-start(bf16[1,32,1024]{2,1,0:T(8,128)(2,1)S(1)} %get-tuple-element.113), channel_id=1, source_target_pairs={{0,8},{1,9},{2,10},{3,11},{4,12},{5,13},{6,14},{7,15},{8,0},{9,1},... | collective-permute-start | bytes 196616 | tf_op jit(solution)/shard_map/ppermute | solution.py:367
  62.1 6.0 %collective-permute-start.19 = (bf16[1,32,640]{2,1,0:T(8,128)(2,1)S(1)}, bf16[1,32,640]{2,1,0:T(8,128)(2,1)S(1)}, u32[]{:S(2)}, u32[]{:S(2)}) collective-permute-start(bf16[1,32,640]{2,1,0:T(8,128)(2,1)S(1)} %get-tuple-element.130), channel_id=1, source_target_pairs={{0,8},{1,9},{2,10},{3,11},{4,12},{5,13},{6,14},{7,15},{8,0},{9,1},... | collective-permute-start | bytes 122888 | tf_op jit(solution)/shard_map/ppermute | solution.py:367

commit v13 on v12

--- a/solution.py
+++ b/solution.py
@@ -435,8 +435,6 @@
         for turn in range(1, 2 * quarter):
             route = [(i, i ^ (2 * turns[turn][i % 2])) for i in range(slabs)]
             came.append(lax.ppermute(messages[turn], "space", route))
-        for turn in range(1, quarter - 1):
-            came[turn], below, above, me = lax.optimization_barrier((came[turn], below, above, me))
         ids = [(2 * first + j, 2 * second + j) for first, second in turns for j in range(2)]
         near, far = tuple(ids[: 2 * quarter]), tuple(ids[2 * quarter :])
         came_near, came_far = came[:quarter], came[quarter:]

time: 69.1 us -> 69.1 us (level)
  starting transfers between devices: 27 us -> 30.3 us
  waiting for transfers between devices: 17.7 us -> 14.4 us
    ppermute x7, waiting for transfers between devices: 5.11 us -> 1.79 us  [on_device(): came.append(lax.ppermute(messages[turn], 'space', route))]
    ppermute x9, starting transfers between devices: 9.96 us -> 12.1 us  [swap(): lax.ppermute(block, 'space', [(i, i ^ 1 << bit) for i in range(slabs)])]
    ppermute x7, starting transfers between devices: 9.18 us -> 10.4 us  [on_device(): came.append(lax.ppermute(messages[turn], 'space', route))]
where the time goes in v13:
time: 69.1 us; the launch traced here: 68.8 us
  starting transfers between devices  30.3 us (44%)
  Pallas kernels  21.5 us (31%)
  waiting for transfers between devices  14.4 us (21%)
  local copies, waits for them, and re-layouts  1.78 us (3%)
  between operations  0.82 us (1%)
    ppermute x9, starting transfers between devices, swap(): lax.ppermute(block, 'space', [(i, i ^ 1 << bit) for i in range(slabs)])  12.1 us
    ppermute x7, starting transfers between devices, on_device(): came.append(lax.ppermute(messages[turn], 'space', route))  10.4 us
    ppermute x9, waiting for transfers between devices, swap(): lax.ppermute(block, 'space', [(i, i ^ 1 << bit) for i in range(slabs)])  6.03 us
    pallas_call x1, Pallas kernels, on_device(): pl.pallas_call(functools.partial(edge_kernel, half, linked, near, far), o...  5.82 us
    ppermute x1, starting transfers between devices, on_device(): above = lax.ppermute(low, 'space', down)  5.61 us
    pallas_call x1, Pallas kernels, on_device(): pl.pallas_call(functools.partial(near_kernel, half), out_shape=(pltpu.HBM...  4.78 us
    ppermute x1, waiting for transfers between devices, on_device(): from_below = lax.ppermute(upper, 'space', up)  4.4 us
    pallas_call x1, Pallas kernels, on_device(): pl.pallas_call(functools.partial(grad_kernel, half, factor), out_shape=(c...  3.75 us
  transfers between devices with their start and end apart: 20, of which 6 were waited for; matrix products, arithmetic and copies ran while one was open for 3% of the time, Pallas kernels for 21%

profile of v13, /device:TPU:0, one launch (start us, length us, event | category | flops | bytes accessed | tf_op | source)
XLA Modules:
  0.0 68.8 jit_solution(8895361965048059722)
XLA Ops:
  0.7 2.5 %pack.1 = (bf16[8,272,128]{2,1,0:T(8,128)(2,1)S(1)}, bf16[8,272,128]{2,1,0:T(8,128)(2,1)S(1)}, bf16[64,512]{1,0:T(8,128)(2,1)S(1)}, bf16[64,512]{1,0:T(8,128)(2,1)S(1)}) custom-call(s32[1]{0:T(128)} %bitcast.me_ref, bf16[256,512]{1,0:T(8,128)(2,1)} %feats_hbm.1, bf16[529,16,128]{2,1,0:T(8,128)(2,1)} %bitcast.16), custom_call_target="tpu_custom_call" | custom-call | tf_op jit(solution)/shard_map/pack/pallas_call | solution.py:398
  3.2 0.5 collective-permute-start
  3.8 5.6 %collective-permute-start.2 = (bf16[64,512]{1,0:T(8,128)(2,1)S(1)}, bf16[64,512]{1,0:T(8,128)(2,1)S(1)}, u32[]{:S(2)}, u32[]{:S(2)}) collective-permute-start(bf16[64,512]{1,0:T(8,128)(2,1)S(1)} %get-tuple-element.63), channel_id=1, source_target_pairs={{1,0},{2,1},{3,2},{4,3},{5,4},{6,5},{7,6},{8,7},{9,8},{10,9},{11,1... | collective-permute-start | bytes 196616 | tf_op jit(solution)/shard_map/ppermute | solution.py:417
  9.4 1.7 %constant_dynamic-slice_fusion = bf16[1,1,64,529]{2,1,3,0:T(2,128)(2,1)S(1)} fusion(bf16[1,16,128,529]{2,1,3,0:T(8,128)(2,1)} %param.12, s32[]{:T(128)S(6)} %select_n.4, s32[]{:T(128)S(6)} %add.7), kind=kLoop, calls=%fused_computation.1 | loop fusion | bytes 135432 | tf_op jit(solution)/shard_map/slice | solution.py:418
  11.1 0.2 collective-permute-done.1.below_ref
  11.3 0.1 join.1
  11.4 0.7 %collective-permute-start.3 = (bf16[2,272,128]{2,1,0:T(8,128)(2,1)S(1)}, bf16[2,272,128]{2,1,0:T(8,128)(2,1)S(1)}, u32[]{:S(2)}, u32[]{:S(2)}) collective-permute-start(bf16[2,272,128]{2,1,0:T(8,128)(2,1)S(1)} %get-tuple-element.75), channel_id=1, source_target_pairs={{0,8},{1,3},{2,10},{3,1},{4,12},{5,7},{6,14},{7,5},{8,0},{9,11},{1... | collective-permute-start | bytes 417800 | tf_op jit(solution)/shard_map/ppermute | solution.py:437
  12.1 0.6 collective-permute-start.4
  12.7 3.1 %collective-permute-start.5 = (bf16[2,272,128]{2,1,0:T(8,128)(2,1)S(1)}, bf16[2,272,128]{2,1,0:T(8,128)(2,1)S(1)}, u32[]{:S(2)}, u32[]{:S(2)}) collective-permute-start(bf16[2,272,128]{2,1,0:T(8,128)(2,1)S(1)} %get-tuple-element.77), channel_id=1, source_target_pairs={{0,10},{1,5},{2,8},{3,7},{4,14},{5,1},{6,12},{7,3},{8,2},{9,13},{1... | collective-permute-start | bytes 417800 | tf_op jit(solution)/shard_map/ppermute | solution.py:437
  15.9 2.1 %collective-permute-start.7 = (bf16[2,272,128]{2,1,0:T(8,128)(2,1)S(1)}, bf16[2,272,128]{2,1,0:T(8,128)(2,1)S(1)}, u32[]{:S(2)}, u32[]{:S(2)}) collective-permute-start(bf16[2,272,128]{2,1,0:T(8,128)(2,1)S(1)} %get-tuple-element.80), channel_id=1, source_target_pairs={{0,12},{1,7},{2,14},{3,5},{4,8},{5,3},{6,10},{7,1},{8,4},{9,15},{1... | collective-permute-start | bytes 417800 | tf_op jit(solution)/shard_map/ppermute | solution.py:437
  17.9 5.8 %edges.1 = (bf16[640,1152]{1,0:T(8,128)(2,1)}, f32[512,1152]{1,0:T(8,128)}, bf16[512,384]{1,0:T(8,128)(2,1)}, bf16[512,640]{1,0:T(8,128)(2,1)S(1)}, bf16[512,512...) custom-call(s32[1]{0:T(128)} %bitcast.me_ref, bf16[256,512]{1,0:T(8,128)(2,1)} %feats_hbm.1, bf16[512,512]{1,0:T(8,128)(2,1)} %w_src_ref.1, ...), custom_call_target="tpu_custom_call" | custom-call | flops 30198988800 | bytes 8388608 | tf_op jit(solution)/shard_map/edges/pallas_call | solution.py:452
  23.8 0.8 %collective-permute-start.8 = (bf16[2,272,128]{2,1,0:T(8,128)(2,1)S(1)}, bf16[2,272,128]{2,1,0:T(8,128)(2,1)S(1)}, u32[]{:S(2)}, u32[]{:S(2)}) collective-permute-start(bf16[2,272,128]{2,1,0:T(8,128)(2,1)S(1)} %get-tuple-element.81), channel_id=1, source_target_pairs={{0,6},{1,13},{2,4},{3,15},{4,2},{5,9},{6,0},{7,11},{8,14},{9,5},{1... | collective-permute-start | bytes 417800 | tf_op jit(solution)/shard_map/ppermute | solution.py:437
  24.6 3.0 %collective-permute-start.9 = (bf16[2,272,128]{2,1,0:T(8,128)(2,1)S(1)}, bf16[2,272,128]{2,1,0:T(8,128)(2,1)S(1)}, u32[]{:S(2)}, u32[]{:S(2)}) collective-permute-start(bf16[2,272,128]{2,1,0:T(8,128)(2,1)S(1)} %get-tuple-element.82), channel_id=1, source_target_pairs={{0,14},{1,15},{2,12},{3,13},{4,10},{5,11},{6,8},{7,9},{8,6},{9,7},... | collective-permute-start | bytes 417800 | tf_op jit(solution)/shard_map/ppermute | solution.py:437
  27.6 4.8 %near.1 = (f32[640,512]{1,0:T(8,128)}, f32[512,544]{1,0:T(8,128)}) custom-call(bf16[544,128]{1,0:T(8,128)(2,1)S(1)} %pad.4.own_ref, bf16[512,544]{1,0:T(8,128)(2,1)S(1)} %get-tuple-element.66.w_out_ref, bf16[512,640]{1,0:T(8,128)(2,1)S(1)} %get-tuple-element.71.hidden_ref, f32[512,1152]{1,0:T(8,128)} %get-tuple-element.67.slope_hbm, ...), custom_call_target="tpu_custom_call" | custom-call | flops 7130316800 | bytes 6291456 | tf_op jit(solution)/shard_map/near/pallas_call | solution.py:491
  32.4 1.8 %collective-permute-done.8.rest_2_ = bf16[2,272,128]{2,1,0:T(8,128)(2,1)S(1)} collective-permute-done((bf16[2,272,128]{2,1,0:T(8,128)(2,1)S(1)}, bf16[2,272,128]{2,1,0:T(8,128)(2,1)S(1)}, u32[]{:S(2)}, u32[]{:S(2)}) %collective-permute-start.8) | collective-permute-done | bytes 139296 | tf_op jit(solution)/shard_map/ppermute | solution.py:437
  34.2 3.7 %grads.1 = (f32[8,32,1024]{2,1,0:T(8,128)S(1)}, bf16[8,32,1024]{2,1,0:T(8,128)(2,1)S(1)}, f32[512,512]{1,0:T(8,128)S(1)}, bf16[64,512]{1,0:T(8,128)(2,1)S(1)}, b...) custom-call(s32[1]{0:T(128)} %bitcast.me_ref, bf16[512,544]{1,0:T(8,128)(2,1)S(1)} %get-tuple-element.66.w_out_ref, ...), custom_call_target="tpu_custom_call" | custom-call | tf_op jit(solution)/shard_map/grads/pallas_call | solution.py:515
  38.0 1.9 %outer.1 = (f32[8,32,640]{2,1,0:T(8,128)S(1)}, bf16[8,32,640]{2,1,0:T(8,128)(2,1)S(1)}) custom-call(s32[1]{0:T(128)} %bitcast.me_ref, bf16[512,512]{1,0:T(8,128)(2,1)S(1)} %get-tuple-element.98.hidden_ref, bf16[544,512]{1,0:T(8,128)(2,1)S(1)} %get-tuple-element.99.g_ref, f32[512,544]{1,0:T(8,128)} %get-tuple-element.100.near_hbm), custom_call_target="tpu_custom_call" | custom-call | flops 12834570240 | bytes 4194304 | tf_op jit(solution)/shard_map/outer/pallas_call | solution.py:539
  40.0 0.6 collective-permute-start.16
  40.6 0.1 fold.6
  40.7 1.9 %collective-permute-start.11 = (bf16[4,32,1024]{2,1,0:T(8,128)(2,1)S(1)}, bf16[4,32,1024]{2,1,0:T(8,128)(2,1)S(1)}, u32[]{:S(2)}, u32[]{:S(2)}) collective-permute-start(bf16[4,32,1024]{2,1,0:T(8,128)(2,1)S(1)} %get-tuple-element.87), channel_id=1, source_target_pairs={{0,2},{1,3},{2,0},{3,1},{4,6},{5,7},{6,4},{7,5},{8,10},{9,11},{10,... | collective-permute-start | bytes 786440 | tf_op jit(solution)/shard_map/ppermute | solution.py:367
  42.6 0.1 fold.9
  42.7 4.9 %collective-permute-start.17 = (bf16[4,32,640]{2,1,0:T(8,128)(2,1)S(1)}, bf16[4,32,640]{2,1,0:T(8,128)(2,1)S(1)}, u32[]{:S(2)}, u32[]{:S(2)}) collective-permute-start(bf16[4,32,640]{2,1,0:T(8,128)(2,1)S(1)} %get-tuple-element.106), channel_id=1, source_target_pairs={{0,4},{1,5},{2,6},{3,7},{4,0},{5,1},{6,2},{7,3},{8,12},{9,13},{10,... | collective-permute-start | bytes 491528 | tf_op jit(solution)/shard_map/ppermute | solution.py:367
  47.6 2.2 %collective-permute-start.12 = (bf16[64,512]{1,0:T(8,128)(2,1)S(1)}, bf16[64,512]{1,0:T(8,128)(2,1)S(1)}, u32[]{:S(2)}, u32[]{:S(2)}) collective-permute-start(bf16[64,512]{1,0:T(8,128)(2,1)S(1)} %get-tuple-element.88), channel_id=1, source_target_pairs={{1,0},{2,1},{3,2},{4,3},{5,4},{6,5},{7,6},{8,7},{9,8},{10,9},{11,1... | collective-permute-start | bytes 196616 | tf_op jit(solution)/shard_map/ppermute | solution.py:579
  49.8 2.0 %collective-permute-done.12.from_above_ref = bf16[64,512]{1,0:T(8,128)(2,1)S(1)} collective-permute-done((bf16[64,512]{1,0:T(8,128)(2,1)S(1)}, bf16[64,512]{1,0:T(8,128)(2,1)S(1)}, u32[]{:S(2)}, u32[]{:S(2)}) %collective-permute-start.12) | collective-permute-done | bytes 65568 | tf_op jit(solution)/shard_map/ppermute | solution.py:579
  51.7 4.4 %collective-permute-done.13.from_below_ref = bf16[64,512]{1,0:T(8,128)(2,1)S(1)} collective-permute-done((bf16[64,512]{1,0:T(8,128)(2,1)S(1)}, bf16[64,512]{1,0:T(8,128)(2,1)S(1)}, u32[]{:S(2)}, u32[]{:S(2)}) %collective-permute-start.13) | collective-permute-done | bytes 65568 | tf_op jit(solution)/shard_map/ppermute | solution.py:580
  56.4 1.0 %collective-permute-start.18 = (bf16[2,32,640]{2,1,0:T(8,128)(2,1)S(1)}, bf16[2,32,640]{2,1,0:T(8,128)(2,1)S(1)}, u32[]{:S(2)}, u32[]{:S(2)}) collective-permute-start(bf16[2,32,640]{2,1,0:T(8,128)(2,1)S(1)} %get-tuple-element.110), channel_id=1, source_target_pairs={{0,2},{1,3},{2,0},{3,1},{4,6},{5,7},{6,4},{7,5},{8,10},{9,11},{10,... | collective-permute-start | bytes 245768 | tf_op jit(solution)/shard_map/ppermute | solution.py:367
  57.4 3.8 %collective-permute-done.14.came_ref = bf16[2,32,1024]{2,1,0:T(8,128)(2,1)S(1)} collective-permute-done((bf16[2,32,1024]{2,1,0:T(8,128)(2,1)S(1)}, bf16[2,32,1024]{2,1,0:T(8,128)(2,1)S(1)}, u32[]{:S(2)}, u32[]{:S(2)}) %collective-permute-start.14) | collective-permute-done | bytes 131104 | tf_op jit(solution)/shard_map/ppermute | solution.py:367
  61.3 0.8 %collective-permute-start.15 = (bf16[1,32,1024]{2,1,0:T(8,128)(2,1)S(1)}, bf16[1,32,1024]{2,1,0:T(8,128)(2,1)S(1)}, u32[]{:S(2)}, u32[]{:S(2)}) collective-permute-start(bf16[1,32,1024]{2,1,0:T(8,128)(2,1)S(1)} %get-tuple-element.97), channel_id=1, source_target_pairs={{0,8},{1,9},{2,10},{3,11},{4,12},{5,13},{6,14},{7,15},{8,0},{9,1},... | collective-permute-start | bytes 196616 | tf_op jit(solution)/shard_map/ppermute | solution.py:367
  62.1 2.3 %collective-permute-start.19 = (bf16[1,32,640]{2,1,0:T(8,128)(2,1)S(1)}, bf16[1,32,640]{2,1,0:T(8,128)(2,1)S(1)}, u32[]{:S(2)}, u32[]{:S(2)}) collective-permute-start(bf16[1,32,640]{2,1,0:T(8,128)(2,1)S(1)} %get-tuple-element.114), channel_id=1, source_target_pairs={{0,8},{1,9},{2,10},{3,11},{4,12},{5,13},{6,14},{7,15},{8,0},{9,1},... | collective-permute-start | bytes 122888 | tf_op jit(solution)/shard_map/ppermute | solution.py:367
  64.4 1.5 %rims.1 = f32[256,512]{1,0:T(8,128)} custom-call(f32[512,512]{1,0:T(8,128)S(1)} %get-tuple-element.83.sums_ref, bf16[64,512]{1,0:T(8,128)(2,1)S(1)} %collective-permute-done.13.from_below_ref, bf16[64,512]{1,0:T(8,128)(2,1)S(1)} %collective-permute-done.12.from_above_ref, bf16[512,512]{1,0:T(8,128)(2,1)S(1)} %copy-done, bf16[512,512]{1,0:T(8,128)(2,1)S(1)} %copy-done.1), custom_call_target="tpu_custom_call" | custom-call | flops 24159191040 | bytes 4194304 | tf_op jit(solution)/shard_map/rims/pallas_call | solution.py:593
  65.9 2.2 %collective-permute-done.19.refs_3_ = bf16[1,32,640]{2,1,0:T(8,128)(2,1)S(1)} collective-permute-done((bf16[1,32,640]{2,1,0:T(8,128)(2,1)S(1)}, bf16[1,32,640]{2,1,0:T(8,128)(2,1)S(1)}, u32[]{:S(2)}, u32[]{:S(2)}) %collective-permute-start.19) | collective-permute-done | bytes 40992 | tf_op jit(solution)/shard_map/ppermute | solution.py:367
  68.1 0.7 %totals.1 = (f32[32,512]{1,0:T(8,128)}, f32[32,512]{1,0:T(8,128)}, f32[32,529]{1,0:T(8,128)}) custom-call(f32[1,32,1024]{2,1,0:T(8,128)S(1)} %get-tuple-element.96.refs_0_, bf16[1,32,1024]{2,1,0:T(8,128)(2,1)S(1)} %collective-permute-done.15.refs_1_, f32[1,32,640]{2,1,0:T(8,128)S(1)} %get-tuple-element.113.refs_2_, ...), custom_call_target="tpu_custom_call" | custom-call | tf_op jit(solution)/shard_map/totals/pallas_call | solution.py:602
  (35 shorter events, 0.5 us)
Async XLA Ops:
  0.6 17.3 %copy-start.2 = (s32[2048]{0:T(1024)S(1)}, s32[2048]{0:T(1024)}, u32[]{:S(2)}) copy-start(s32[2048]{0:T(1024)} %param.13) | copy-start | bytes 24580
  0.6 17.3 %copy-start.3 = (s32[2048]{0:T(1024)S(1)}, s32[2048]{0:T(1024)}, u32[]{:S(2)}) copy-start(s32[2048]{0:T(1024)} %param.14) | copy-start | bytes 24580
  0.7 17.3 %copy-start.4 = (s32[2048]{0:T(1024)S(1)}, s32[2048]{0:T(1024)}, u32[]{:S(2)}) copy-start(s32[2048]{0:T(1024)} %param.15) | copy-start | bytes 24580
  3.2 8.1 %collective-permute-start = (bf16[8,272,128]{2,1,0:T(8,128)(2,1)S(1)}, bf16[8,272,128]{2,1,0:T(8,128)(2,1)S(1)}, u32[]{:S(2)}, u32[]{:S(2)}) collective-permute-start(bf16[8,272,128]{2,1,0:T(8,128)(2,1)S(1)} %get-tuple-element.61), channel_id=1, source_target_pairs={{0,1},{1,0},{2,3},{3,2},{4,5},{5,4},{6,7},{7,6},{8,9},{9,8},{10,11... | collective-permute-start | bytes 1671176 | tf_op jit(solution)/shard_map/ppermute | solution.py:367
  3.7 7.6 %collective-permute-start.1 = (bf16[64,512]{1,0:T(8,128)(2,1)S(1)}, bf16[64,512]{1,0:T(8,128)(2,1)S(1)}, u32[]{:S(2)}, u32[]{:S(2)}) collective-permute-start(bf16[64,512]{1,0:T(8,128)(2,1)S(1)} %get-tuple-element.62), channel_id=1, source_target_pairs={{0,1},{1,2},{2,3},{3,4},{4,5},{5,6},{6,7},{7,8},{8,9},{9,10},{10,1... | collective-permute-start | bytes 196616 | tf_op jit(solution)/shard_map/ppermute | solution.py:416
  3.8 7.6 %collective-permute-start.2 = (bf16[64,512]{1,0:T(8,128)(2,1)S(1)}, bf16[64,512]{1,0:T(8,128)(2,1)S(1)}, u32[]{:S(2)}, u32[]{:S(2)}) collective-permute-start(bf16[64,512]{1,0:T(8,128)(2,1)S(1)} %get-tuple-element.63), channel_id=1, source_target_pairs={{1,0},{2,1},{3,2},{4,3},{5,4},{6,5},{7,6},{8,7},{9,8},{10,9},{11,1... | collective-permute-start | bytes 196616 | tf_op jit(solution)/shard_map/ppermute | solution.py:417
  11.4 12.4 %collective-permute-start.3 = (bf16[2,272,128]{2,1,0:T(8,128)(2,1)S(1)}, bf16[2,272,128]{2,1,0:T(8,128)(2,1)S(1)}, u32[]{:S(2)}, u32[]{:S(2)}) collective-permute-start(bf16[2,272,128]{2,1,0:T(8,128)(2,1)S(1)} %get-tuple-element.75), channel_id=1, source_target_pairs={{0,8},{1,3},{2,10},{3,1},{4,12},{5,7},{6,14},{7,5},{8,0},{9,11},{1... | collective-permute-start | bytes 417800 | tf_op jit(solution)/shard_map/ppermute | solution.py:437
  12.1 12.5 %collective-permute-start.4 = (bf16[2,272,128]{2,1,0:T(8,128)(2,1)S(1)}, bf16[2,272,128]{2,1,0:T(8,128)(2,1)S(1)}, u32[]{:S(2)}, u32[]{:S(2)}) collective-permute-start(bf16[2,272,128]{2,1,0:T(8,128)(2,1)S(1)} %get-tuple-element.76), channel_id=1, source_target_pairs={{0,2},{1,9},{2,0},{3,11},{4,6},{5,13},{6,4},{7,15},{8,10},{9,1},{1... | collective-permute-start | bytes 417800 | tf_op jit(solution)/shard_map/ppermute | solution.py:437
  12.7 14.9 %collective-permute-start.5 = (bf16[2,272,128]{2,1,0:T(8,128)(2,1)S(1)}, bf16[2,272,128]{2,1,0:T(8,128)(2,1)S(1)}, u32[]{:S(2)}, u32[]{:S(2)}) collective-permute-start(bf16[2,272,128]{2,1,0:T(8,128)(2,1)S(1)} %get-tuple-element.77), channel_id=1, source_target_pairs={{0,10},{1,5},{2,8},{3,7},{4,14},{5,1},{6,12},{7,3},{8,2},{9,13},{1... | collective-permute-start | bytes 417800 | tf_op jit(solution)/shard_map/ppermute | solution.py:437
  15.8 16.6 %collective-permute-start.6 = (bf16[2,272,128]{2,1,0:T(8,128)(2,1)S(1)}, bf16[2,272,128]{2,1,0:T(8,128)(2,1)S(1)}, u32[]{:S(2)}, u32[]{:S(2)}) collective-permute-start(bf16[2,272,128]{2,1,0:T(8,128)(2,1)S(1)} %get-tuple-element.79), channel_id=1, source_target_pairs={{0,4},{1,11},{2,6},{3,9},{4,0},{5,15},{6,2},{7,13},{8,12},{9,3},{1... | collective-permute-start | bytes 417800 | tf_op jit(solution)/shard_map/ppermute | solution.py:437
  15.9 16.6 %collective-permute-start.7 = (bf16[2,272,128]{2,1,0:T(8,128)(2,1)S(1)}, bf16[2,272,128]{2,1,0:T(8,128)(2,1)S(1)}, u32[]{:S(2)}, u32[]{:S(2)}) collective-permute-start(bf16[2,272,128]{2,1,0:T(8,128)(2,1)S(1)} %get-tuple-element.80), channel_id=1, source_target_pairs={{0,12},{1,7},{2,14},{3,5},{4,8},{5,3},{6,10},{7,1},{8,4},{9,15},{1... | collective-permute-start | bytes 417800 | tf_op jit(solution)/shard_map/ppermute | solution.py:437
  23.8 10.4 %collective-permute-start.8 = (bf16[2,272,128]{2,1,0:T(8,128)(2,1)S(1)}, bf16[2,272,128]{2,1,0:T(8,128)(2,1)S(1)}, u32[]{:S(2)}, u32[]{:S(2)}) collective-permute-start(bf16[2,272,128]{2,1,0:T(8,128)(2,1)S(1)} %get-tuple-element.81), channel_id=1, source_target_pairs={{0,6},{1,13},{2,4},{3,15},{4,2},{5,9},{6,0},{7,11},{8,14},{9,5},{1... | collective-permute-start | bytes 417800 | tf_op jit(solution)/shard_map/ppermute | solution.py:437
  24.6 9.6 %collective-permute-start.9 = (bf16[2,272,128]{2,1,0:T(8,128)(2,1)S(1)}, bf16[2,272,128]{2,1,0:T(8,128)(2,1)S(1)}, u32[]{:S(2)}, u32[]{:S(2)}) collective-permute-start(bf16[2,272,128]{2,1,0:T(8,128)(2,1)S(1)} %get-tuple-element.82), channel_id=1, source_target_pairs={{0,14},{1,15},{2,12},{3,13},{4,10},{5,11},{6,8},{7,9},{8,6},{9,7},... | collective-permute-start | bytes 417800 | tf_op jit(solution)/shard_map/ppermute | solution.py:437
  38.0 2.6 %collective-permute-start.10 = (bf16[8,32,1024]{2,1,0:T(8,128)(2,1)S(1)}, bf16[8,32,1024]{2,1,0:T(8,128)(2,1)S(1)}, u32[]{:S(2)}, u32[]{:S(2)}) collective-permute-start(bf16[8,32,1024]{2,1,0:T(8,128)(2,1)S(1)} %get-tuple-element.85), channel_id=1, source_target_pairs={{0,1},{1,0},{2,3},{3,2},{4,5},{5,4},{6,7},{7,6},{8,9},{9,8},{10,11... | collective-permute-start | bytes 1572872 | tf_op jit(solution)/shard_map/ppermute | solution.py:367
  40.0 2.6 %collective-permute-start.16 = (bf16[8,32,640]{2,1,0:T(8,128)(2,1)S(1)}, bf16[8,32,640]{2,1,0:T(8,128)(2,1)S(1)}, u32[]{:S(2)}, u32[]{:S(2)}) collective-permute-start(bf16[8,32,640]{2,1,0:T(8,128)(2,1)S(1)} %get-tuple-element.102), channel_id=1, source_target_pairs={{0,1},{1,0},{2,3},{3,2},{4,5},{5,4},{6,7},{7,6},{8,9},{9,8},{10,11... | collective-permute-start | bytes 983048 | tf_op jit(solution)/shard_map/ppermute | solution.py:367
  40.6 23.8 %copy-start = (bf16[512,512]{1,0:T(8,128)(2,1)S(1)}, bf16[512,512]{1,0:T(8,128)(2,1)}, u32[]{:S(2)}) copy-start(bf16[512,512]{1,0:T(8,128)(2,1)} %w_src_ref.1) | copy-start | bytes 1572868
  40.6 23.8 %copy-start.1 = (bf16[512,512]{1,0:T(8,128)(2,1)S(1)}, bf16[512,512]{1,0:T(8,128)(2,1)}, u32[]{:S(2)}) copy-start(bf16[512,512]{1,0:T(8,128)(2,1)} %w_dst_ref.1) | copy-start | bytes 1572868
  40.7 15.4 %collective-permute-start.11 = (bf16[4,32,1024]{2,1,0:T(8,128)(2,1)S(1)}, bf16[4,32,1024]{2,1,0:T(8,128)(2,1)S(1)}, u32[]{:S(2)}, u32[]{:S(2)}) collective-permute-start(bf16[4,32,1024]{2,1,0:T(8,128)(2,1)S(1)} %get-tuple-element.87), channel_id=1, source_target_pairs={{0,2},{1,3},{2,0},{3,1},{4,6},{5,7},{6,4},{7,5},{8,10},{9,11},{10,... | collective-permute-start | bytes 786440 | tf_op jit(solution)/shard_map/ppermute | solution.py:367
  42.7 13.6 %collective-permute-start.17 = (bf16[4,32,640]{2,1,0:T(8,128)(2,1)S(1)}, bf16[4,32,640]{2,1,0:T(8,128)(2,1)S(1)}, u32[]{:S(2)}, u32[]{:S(2)}) collective-permute-start(bf16[4,32,640]{2,1,0:T(8,128)(2,1)S(1)} %get-tuple-element.106), channel_id=1, source_target_pairs={{0,4},{1,5},{2,6},{3,7},{4,0},{5,1},{6,2},{7,3},{8,12},{9,13},{10,... | collective-permute-start | bytes 491528 | tf_op jit(solution)/shard_map/ppermute | solution.py:367
  47.6 4.2 %collective-permute-start.12 = (bf16[64,512]{1,0:T(8,128)(2,1)S(1)}, bf16[64,512]{1,0:T(8,128)(2,1)S(1)}, u32[]{:S(2)}, u32[]{:S(2)}) collective-permute-start(bf16[64,512]{1,0:T(8,128)(2,1)S(1)} %get-tuple-element.88), channel_id=1, source_target_pairs={{1,0},{2,1},{3,2},{4,3},{5,4},{6,5},{7,6},{8,7},{9,8},{10,9},{11,1... | collective-permute-start | bytes 196616 | tf_op jit(solution)/shard_map/ppermute | solution.py:579
  49.8 6.4 %collective-permute-start.13 = (bf16[64,512]{1,0:T(8,128)(2,1)S(1)}, bf16[64,512]{1,0:T(8,128)(2,1)S(1)}, u32[]{:S(2)}, u32[]{:S(2)}) collective-permute-start(bf16[64,512]{1,0:T(8,128)(2,1)S(1)} %get-tuple-element.89), channel_id=1, source_target_pairs={{0,1},{1,2},{2,3},{3,4},{4,5},{5,6},{6,7},{7,8},{8,9},{9,10},{10,1... | collective-permute-start | bytes 196616 | tf_op jit(solution)/shard_map/ppermute | solution.py:580
  56.2 5.0 %collective-permute-start.14 = (bf16[2,32,1024]{2,1,0:T(8,128)(2,1)S(1)}, bf16[2,32,1024]{2,1,0:T(8,128)(2,1)S(1)}, u32[]{:S(2)}, u32[]{:S(2)}) collective-permute-start(bf16[2,32,1024]{2,1,0:T(8,128)(2,1)S(1)} %get-tuple-element.95), channel_id=1, source_target_pairs={{0,4},{1,5},{2,6},{3,7},{4,0},{5,1},{6,2},{7,3},{8,12},{9,13},{10,... | collective-permute-start | bytes 393224 | tf_op jit(solution)/shard_map/ppermute | solution.py:367
  56.4 5.7 %collective-permute-start.18 = (bf16[2,32,640]{2,1,0:T(8,128)(2,1)S(1)}, bf16[2,32,640]{2,1,0:T(8,128)(2,1)S(1)}, u32[]{:S(2)}, u32[]{:S(2)}) collective-permute-start(bf16[2,32,640]{2,1,0:T(8,128)(2,1)S(1)} %get-tuple-element.110), channel_id=1, source_target_pairs={{0,2},{1,3},{2,0},{3,1},{4,6},{5,7},{6,4},{7,5},{8,10},{9,11},{10,... | collective-permute-start | bytes 245768 | tf_op jit(solution)/shard_map/ppermute | solution.py:367
  61.3 6.8 %collective-permute-start.15 = (bf16[1,32,1024]{2,1,0:T(8,128)(2,1)S(1)}, bf16[1,32,1024]{2,1,0:T(8,128)(2,1)S(1)}, u32[]{:S(2)}, u32[]{:S(2)}) collective-permute-start(bf16[1,32,1024]{2,1,0:T(8,128)(2,1)S(1)} %get-tuple-element.97), channel_id=1, source_target_pairs={{0,8},{1,9},{2,10},{3,11},{4,12},{5,13},{6,14},{7,15},{8,0},{9,1},... | collective-permute-start | bytes 196616 | tf_op jit(solution)/shard_map/ppermute | solution.py:367
  62.1 6.0 %collective-permute-start.19 = (bf16[1,32,640]{2,1,0:T(8,128)(2,1)S(1)}, bf16[1,32,640]{2,1,0:T(8,128)(2,1)S(1)}, u32[]{:S(2)}, u32[]{:S(2)}) collective-permute-start(bf16[1,32,640]{2,1,0:T(8,128)(2,1)S(1)} %get-tuple-element.114), channel_id=1, source_target_pairs={{0,8},{1,9},{2,10},{3,11},{4,12},{5,13},{6,14},{7,15},{8,0},{9,1},... | collective-permute-start | bytes 122888 | tf_op jit(solution)/shard_map/ppermute | solution.py:367

commit v14 on v13

--- a/solution.py
+++ b/solution.py
@@ -581,7 +581,7 @@
     crossed = swap(send, 0, slabs)
     crossed_o = swap(send_o, 0, slabs)
     for (bit, place), (bit_o, place_o) in zip(paths[0][1:], paths[1][1:]):
-        if bit == 2:
+        if bit == 3:
             keep, crossed, from_above, from_below = lax.optimization_barrier((keep, crossed, from_above, from_below))
         keep, send = fold(bit, place, keep, crossed)
         crossed = swap(send, bit, slabs)

time: 69.1 us -> 70 us (1.013)
  starting transfers between devices: 30.3 us -> 34.5 us
  waiting for transfers between devices: 14.4 us -> 11.1 us
    ppermute x9, starting transfers between devices: 12.1 us -> 17.8 us  [swap(): lax.ppermute(block, 'space', [(i, i ^ 1 << bit) for i in range(slabs)])]
    ppermute x9, waiting for transfers between devices: 6.03 us -> 2.75 us  [swap(): lax.ppermute(block, 'space', [(i, i ^ 1 << bit) for i in range(slabs)])]
    ppermute x1, starting transfers between devices: 2.17 us -> 0.71 us  [on_device(): from_above = lax.ppermute(lower, 'space', down)]
where the time goes in v14:
time: 70 us; the launch traced here: 69.7 us
  starting transfers between devices  34.5 us (49%)
  Pallas kernels  21.5 us (31%)
  waiting for transfers between devices  11.1 us (16%)
  local copies, waits for them, and re-layouts  1.78 us (3%)
  between operations  0.82 us (1%)
    ppermute x9, starting transfers between devices, swap(): lax.ppermute(block, 'space', [(i, i ^ 1 << bit) for i in range(slabs)])  17.8 us
    ppermute x7, starting transfers between devices, on_device(): came.append(lax.ppermute(messages[turn], 'space', route))  10.4 us
    pallas_call x1, Pallas kernels, on_device(): pl.pallas_call(functools.partial(edge_kernel, half, linked, near, far), o...  5.82 us
    ppermute x1, starting transfers between devices, on_device(): above = lax.ppermute(low, 'space', down)  5.61 us
    pallas_call x1, Pallas kernels, on_device(): pl.pallas_call(functools.partial(near_kernel, half), out_shape=(pltpu.HBM...  4.79 us
    ppermute x1, waiting for transfers between devices, on_device(): from_below = lax.ppermute(upper, 'space', up)  4.49 us
    pallas_call x1, Pallas kernels, on_device(): pl.pallas_call(functools.partial(grad_kernel, half, factor), out_shape=(c...  3.75 us
    ppermute x9, waiting for transfers between devices, swap(): lax.ppermute(block, 'space', [(i, i ^ 1 << bit) for i in range(slabs)])  2.75 us
  transfers between devices with their start and end apart: 20, of which 6 were waited for; matrix products, arithmetic and copies ran while one was open for 3% of the time, Pallas kernels for 21%

profile of v14, /device:TPU:0, one launch (start us, length us, event | category | flops | bytes accessed | tf_op | source)
XLA Modules:
  0.0 69.7 jit_solution(5542990536787027808)
XLA Ops:
  0.7 2.5 %pack.1 = (bf16[8,272,128]{2,1,0:T(8,128)(2,1)S(1)}, bf16[8,272,128]{2,1,0:T(8,128)(2,1)S(1)}, bf16[64,512]{1,0:T(8,128)(2,1)S(1)}, bf16[64,512]{1,0:T(8,128)(2,1)S(1)}) custom-call(s32[1]{0:T(128)} %bitcast.me_ref, bf16[256,512]{1,0:T(8,128)(2,1)} %feats_hbm.1, bf16[529,16,128]{2,1,0:T(8,128)(2,1)} %bitcast.16), custom_call_target="tpu_custom_call" | custom-call | tf_op jit(solution)/shard_map/pack/pallas_call | solution.py:398
  3.2 0.5 collective-permute-start
  3.8 5.6 %collective-permute-start.2 = (bf16[64,512]{1,0:T(8,128)(2,1)S(1)}, bf16[64,512]{1,0:T(8,128)(2,1)S(1)}, u32[]{:S(2)}, u32[]{:S(2)}) collective-permute-start(bf16[64,512]{1,0:T(8,128)(2,1)S(1)} %get-tuple-element.63), channel_id=1, source_target_pairs={{1,0},{2,1},{3,2},{4,3},{5,4},{6,5},{7,6},{8,7},{9,8},{10,9},{11,1... | collective-permute-start | bytes 196616 | tf_op jit(solution)/shard_map/ppermute | solution.py:417
  9.4 1.7 %constant_dynamic-slice_fusion = bf16[1,1,64,529]{2,1,3,0:T(2,128)(2,1)S(1)} fusion(bf16[1,16,128,529]{2,1,3,0:T(8,128)(2,1)} %param.12, s32[]{:T(128)S(6)} %select_n.4, s32[]{:T(128)S(6)} %add.7), kind=kLoop, calls=%fused_computation.1 | loop fusion | bytes 135432 | tf_op jit(solution)/shard_map/slice | solution.py:418
  11.1 0.2 collective-permute-done.1.below_ref
  11.3 0.1 join.1
  11.4 0.7 collective-permute-start.3
  12.1 0.6 collective-permute-start.4
  12.7 3.1 %collective-permute-start.5 = (bf16[2,272,128]{2,1,0:T(8,128)(2,1)S(1)}, bf16[2,272,128]{2,1,0:T(8,128)(2,1)S(1)}, u32[]{:S(2)}, u32[]{:S(2)}) collective-permute-start(bf16[2,272,128]{2,1,0:T(8,128)(2,1)S(1)} %get-tuple-element.77), channel_id=1, source_target_pairs={{0,10},{1,5},{2,8},{3,7},{4,14},{5,1},{6,12},{7,3},{8,2},{9,13},{1... | collective-permute-start | bytes 417800 | tf_op jit(solution)/shard_map/ppermute | solution.py:437
  15.9 2.1 %collective-permute-start.7 = (bf16[2,272,128]{2,1,0:T(8,128)(2,1)S(1)}, bf16[2,272,128]{2,1,0:T(8,128)(2,1)S(1)}, u32[]{:S(2)}, u32[]{:S(2)}) collective-permute-start(bf16[2,272,128]{2,1,0:T(8,128)(2,1)S(1)} %get-tuple-element.80), channel_id=1, source_target_pairs={{0,12},{1,7},{2,14},{3,5},{4,8},{5,3},{6,10},{7,1},{8,4},{9,15},{1... | collective-permute-start | bytes 417800 | tf_op jit(solution)/shard_map/ppermute | solution.py:437
  17.9 5.8 %edges.1 = (bf16[640,1152]{1,0:T(8,128)(2,1)}, f32[512,1152]{1,0:T(8,128)}, bf16[512,384]{1,0:T(8,128)(2,1)}, bf16[512,640]{1,0:T(8,128)(2,1)S(1)}, bf16[512,512...) custom-call(s32[1]{0:T(128)} %bitcast.me_ref, bf16[256,512]{1,0:T(8,128)(2,1)} %feats_hbm.1, bf16[512,512]{1,0:T(8,128)(2,1)} %w_src_ref.1, ...), custom_call_target="tpu_custom_call" | custom-call | flops 30198988800 | bytes 8388608 | tf_op jit(solution)/shard_map/edges/pallas_call | solution.py:452
  23.8 0.8 %collective-permute-start.8 = (bf16[2,272,128]{2,1,0:T(8,128)(2,1)S(1)}, bf16[2,272,128]{2,1,0:T(8,128)(2,1)S(1)}, u32[]{:S(2)}, u32[]{:S(2)}) collective-permute-start(bf16[2,272,128]{2,1,0:T(8,128)(2,1)S(1)} %get-tuple-element.81), channel_id=1, source_target_pairs={{0,6},{1,13},{2,4},{3,15},{4,2},{5,9},{6,0},{7,11},{8,14},{9,5},{1... | collective-permute-start | bytes 417800 | tf_op jit(solution)/shard_map/ppermute | solution.py:437
  24.6 3.0 %collective-permute-start.9 = (bf16[2,272,128]{2,1,0:T(8,128)(2,1)S(1)}, bf16[2,272,128]{2,1,0:T(8,128)(2,1)S(1)}, u32[]{:S(2)}, u32[]{:S(2)}) collective-permute-start(bf16[2,272,128]{2,1,0:T(8,128)(2,1)S(1)} %get-tuple-element.82), channel_id=1, source_target_pairs={{0,14},{1,15},{2,12},{3,13},{4,10},{5,11},{6,8},{7,9},{8,6},{9,7},... | collective-permute-start | bytes 417800 | tf_op jit(solution)/shard_map/ppermute | solution.py:437
  27.6 4.8 %near.1 = (f32[640,512]{1,0:T(8,128)}, f32[512,544]{1,0:T(8,128)}) custom-call(bf16[544,128]{1,0:T(8,128)(2,1)S(1)} %pad.4.own_ref, bf16[512,544]{1,0:T(8,128)(2,1)S(1)} %get-tuple-element.66.w_out_ref, bf16[512,640]{1,0:T(8,128)(2,1)S(1)} %get-tuple-element.71.hidden_ref, f32[512,1152]{1,0:T(8,128)} %get-tuple-element.67.slope_hbm, ...), custom_call_target="tpu_custom_call" | custom-call | flops 7130316800 | bytes 6291456 | tf_op jit(solution)/shard_map/near/pallas_call | solution.py:491
  32.4 1.8 %collective-permute-done.8.rest_2_ = bf16[2,272,128]{2,1,0:T(8,128)(2,1)S(1)} collective-permute-done((bf16[2,272,128]{2,1,0:T(8,128)(2,1)S(1)}, bf16[2,272,128]{2,1,0:T(8,128)(2,1)S(1)}, u32[]{:S(2)}, u32[]{:S(2)}) %collective-permute-start.8) | collective-permute-done | bytes 139296 | tf_op jit(solution)/shard_map/ppermute | solution.py:437
  34.2 3.8 %grads.1 = (f32[8,32,1024]{2,1,0:T(8,128)S(1)}, bf16[8,32,1024]{2,1,0:T(8,128)(2,1)S(1)}, f32[512,512]{1,0:T(8,128)S(1)}, bf16[64,512]{1,0:T(8,128)(2,1)S(1)}, b...) custom-call(s32[1]{0:T(128)} %bitcast.me_ref, bf16[512,544]{1,0:T(8,128)(2,1)S(1)} %get-tuple-element.66.w_out_ref, ...), custom_call_target="tpu_custom_call" | custom-call | tf_op jit(solution)/shard_map/grads/pallas_call | solution.py:515
  38.0 1.9 %outer.1 = (f32[8,32,640]{2,1,0:T(8,128)S(1)}, bf16[8,32,640]{2,1,0:T(8,128)(2,1)S(1)}) custom-call(s32[1]{0:T(128)} %bitcast.me_ref, bf16[512,512]{1,0:T(8,128)(2,1)S(1)} %get-tuple-element.98.hidden_ref, bf16[544,512]{1,0:T(8,128)(2,1)S(1)} %get-tuple-element.99.g_ref, f32[512,544]{1,0:T(8,128)} %get-tuple-element.100.near_hbm), custom_call_target="tpu_custom_call" | custom-call | flops 12834570240 | bytes 4194304 | tf_op jit(solution)/shard_map/outer/pallas_call | solution.py:539
  40.0 0.6 collective-permute-start.16
  40.6 0.1 fold.6
  40.7 1.9 %collective-permute-start.11 = (bf16[4,32,1024]{2,1,0:T(8,128)(2,1)S(1)}, bf16[4,32,1024]{2,1,0:T(8,128)(2,1)S(1)}, u32[]{:S(2)}, u32[]{:S(2)}) collective-permute-start(bf16[4,32,1024]{2,1,0:T(8,128)(2,1)S(1)} %get-tuple-element.87), channel_id=1, source_target_pairs={{0,2},{1,3},{2,0},{3,1},{4,6},{5,7},{6,4},{7,5},{8,10},{9,11},{10,... | collective-permute-start | bytes 786440 | tf_op jit(solution)/shard_map/ppermute | solution.py:367
  42.6 0.1 fold.9
  42.7 4.9 %collective-permute-start.17 = (bf16[4,32,640]{2,1,0:T(8,128)(2,1)S(1)}, bf16[4,32,640]{2,1,0:T(8,128)(2,1)S(1)}, u32[]{:S(2)}, u32[]{:S(2)}) collective-permute-start(bf16[4,32,640]{2,1,0:T(8,128)(2,1)S(1)} %get-tuple-element.106), channel_id=1, source_target_pairs={{0,4},{1,5},{2,6},{3,7},{4,0},{5,1},{6,2},{7,3},{8,12},{9,13},{10,... | collective-permute-start | bytes 491528 | tf_op jit(solution)/shard_map/ppermute | solution.py:367
  47.6 1.5 %collective-permute-done.11.came_ref = bf16[4,32,1024]{2,1,0:T(8,128)(2,1)S(1)} collective-permute-done((bf16[4,32,1024]{2,1,0:T(8,128)(2,1)S(1)}, bf16[4,32,1024]{2,1,0:T(8,128)(2,1)S(1)}, u32[]{:S(2)}, u32[]{:S(2)}) %collective-permute-start.11) | collective-permute-done | bytes 262176 | tf_op jit(solution)/shard_map/ppermute | solution.py:367
  49.2 5.0 %collective-permute-start.12 = (bf16[2,32,1024]{2,1,0:T(8,128)(2,1)S(1)}, bf16[2,32,1024]{2,1,0:T(8,128)(2,1)S(1)}, u32[]{:S(2)}, u32[]{:S(2)}) collective-permute-start(bf16[2,32,1024]{2,1,0:T(8,128)(2,1)S(1)} %get-tuple-element.89), channel_id=1, source_target_pairs={{0,4},{1,5},{2,6},{3,7},{4,0},{5,1},{6,2},{7,3},{8,12},{9,13},{10,... | collective-permute-start | bytes 393224 | tf_op jit(solution)/shard_map/ppermute | solution.py:367
  54.2 1.8 %collective-permute-start.18 = (bf16[2,32,640]{2,1,0:T(8,128)(2,1)S(1)}, bf16[2,32,640]{2,1,0:T(8,128)(2,1)S(1)}, u32[]{:S(2)}, u32[]{:S(2)}) collective-permute-start(bf16[2,32,640]{2,1,0:T(8,128)(2,1)S(1)} %get-tuple-element.110), channel_id=1, source_target_pairs={{0,2},{1,3},{2,0},{3,1},{4,6},{5,7},{6,4},{7,5},{8,10},{9,11},{10,... | collective-permute-start | bytes 245768 | tf_op jit(solution)/shard_map/ppermute | solution.py:367
  56.0 0.7 %collective-permute-start.13 = (bf16[64,512]{1,0:T(8,128)(2,1)S(1)}, bf16[64,512]{1,0:T(8,128)(2,1)S(1)}, u32[]{:S(2)}, u32[]{:S(2)}) collective-permute-start(bf16[64,512]{1,0:T(8,128)(2,1)S(1)} %get-tuple-element.90), channel_id=1, source_target_pairs={{1,0},{2,1},{3,2},{4,3},{5,4},{6,5},{7,6},{8,7},{9,8},{10,9},{11,1... | collective-permute-start | bytes 196616 | tf_op jit(solution)/shard_map/ppermute | solution.py:579
  56.7 1.9 %collective-permute-done.13.from_above_ref = bf16[64,512]{1,0:T(8,128)(2,1)S(1)} collective-permute-done((bf16[64,512]{1,0:T(8,128)(2,1)S(1)}, bf16[64,512]{1,0:T(8,128)(2,1)S(1)}, u32[]{:S(2)}, u32[]{:S(2)}) %collective-permute-start.13) | collective-permute-done | bytes 65568 | tf_op jit(solution)/shard_map/ppermute | solution.py:579
  58.6 4.5 %collective-permute-done.14.from_below_ref = bf16[64,512]{1,0:T(8,128)(2,1)S(1)} collective-permute-done((bf16[64,512]{1,0:T(8,128)(2,1)S(1)}, bf16[64,512]{1,0:T(8,128)(2,1)S(1)}, u32[]{:S(2)}, u32[]{:S(2)}) %collective-permute-start.14) | collective-permute-done | bytes 65568 | tf_op jit(solution)/shard_map/ppermute | solution.py:580
  63.3 3.0 %collective-permute-start.19 = (bf16[1,32,640]{2,1,0:T(8,128)(2,1)S(1)}, bf16[1,32,640]{2,1,0:T(8,128)(2,1)S(1)}, u32[]{:S(2)}, u32[]{:S(2)}) collective-permute-start(bf16[1,32,640]{2,1,0:T(8,128)(2,1)S(1)} %get-tuple-element.114), channel_id=1, source_target_pairs={{0,8},{1,9},{2,10},{3,11},{4,12},{5,13},{6,14},{7,15},{8,0},{9,1},... | collective-permute-start | bytes 122888 | tf_op jit(solution)/shard_map/ppermute | solution.py:367
  66.2 1.5 %rims.1 = f32[256,512]{1,0:T(8,128)} custom-call(f32[512,512]{1,0:T(8,128)S(1)} %get-tuple-element.83.sums_ref, bf16[64,512]{1,0:T(8,128)(2,1)S(1)} %collective-permute-done.14.from_below_ref, bf16[64,512]{1,0:T(8,128)(2,1)S(1)} %collective-permute-done.13.from_above_ref, bf16[512,512]{1,0:T(8,128)(2,1)S(1)} %copy-done, bf16[512,512]{1,0:T(8,128)(2,1)S(1)} %copy-done.1), custom_call_target="tpu_custom_call" | custom-call | flops 24159191040 | bytes 4194304 | tf_op jit(solution)/shard_map/rims/pallas_call | solution.py:593
  67.8 1.2 %collective-permute-done.19.refs_3_ = bf16[1,32,640]{2,1,0:T(8,128)(2,1)S(1)} collective-permute-done((bf16[1,32,640]{2,1,0:T(8,128)(2,1)S(1)}, bf16[1,32,640]{2,1,0:T(8,128)(2,1)S(1)}, u32[]{:S(2)}, u32[]{:S(2)}) %collective-permute-start.19) | collective-permute-done | bytes 40992 | tf_op jit(solution)/shard_map/ppermute | solution.py:367
  69.0 0.7 totals.1
  (35 shorter events, 0.5 us)
Async XLA Ops:
  0.6 17.3 %copy-start.2 = (s32[2048]{0:T(1024)S(1)}, s32[2048]{0:T(1024)}, u32[]{:S(2)}) copy-start(s32[2048]{0:T(1024)} %param.13) | copy-start | bytes 24580
  0.6 17.3 %copy-start.3 = (s32[2048]{0:T(1024)S(1)}, s32[2048]{0:T(1024)}, u32[]{:S(2)}) copy-start(s32[2048]{0:T(1024)} %param.14) | copy-start | bytes 24580
  0.7 17.3 %copy-start.4 = (s32[2048]{0:T(1024)S(1)}, s32[2048]{0:T(1024)}, u32[]{:S(2)}) copy-start(s32[2048]{0:T(1024)} %param.15) | copy-start | bytes 24580
  3.2 8.1 %collective-permute-start = (bf16[8,272,128]{2,1,0:T(8,128)(2,1)S(1)}, bf16[8,272,128]{2,1,0:T(8,128)(2,1)S(1)}, u32[]{:S(2)}, u32[]{:S(2)}) collective-permute-start(bf16[8,272,128]{2,1,0:T(8,128)(2,1)S(1)} %get-tuple-element.61), channel_id=1, source_target_pairs={{0,1},{1,0},{2,3},{3,2},{4,5},{5,4},{6,7},{7,6},{8,9},{9,8},{10,11... | collective-permute-start | bytes 1671176 | tf_op jit(solution)/shard_map/ppermute | solution.py:367
  3.7 7.6 %collective-permute-start.1 = (bf16[64,512]{1,0:T(8,128)(2,1)S(1)}, bf16[64,512]{1,0:T(8,128)(2,1)S(1)}, u32[]{:S(2)}, u32[]{:S(2)}) collective-permute-start(bf16[64,512]{1,0:T(8,128)(2,1)S(1)} %get-tuple-element.62), channel_id=1, source_target_pairs={{0,1},{1,2},{2,3},{3,4},{4,5},{5,6},{6,7},{7,8},{8,9},{9,10},{10,1... | collective-permute-start | bytes 196616 | tf_op jit(solution)/shard_map/ppermute | solution.py:416
  3.8 7.6 %collective-permute-start.2 = (bf16[64,512]{1,0:T(8,128)(2,1)S(1)}, bf16[64,512]{1,0:T(8,128)(2,1)S(1)}, u32[]{:S(2)}, u32[]{:S(2)}) collective-permute-start(bf16[64,512]{1,0:T(8,128)(2,1)S(1)} %get-tuple-element.63), channel_id=1, source_target_pairs={{1,0},{2,1},{3,2},{4,3},{5,4},{6,5},{7,6},{8,7},{9,8},{10,9},{11,1... | collective-permute-start | bytes 196616 | tf_op jit(solution)/shard_map/ppermute | solution.py:417
  11.4 12.4 %collective-permute-start.3 = (bf16[2,272,128]{2,1,0:T(8,128)(2,1)S(1)}, bf16[2,272,128]{2,1,0:T(8,128)(2,1)S(1)}, u32[]{:S(2)}, u32[]{:S(2)}) collective-permute-start(bf16[2,272,128]{2,1,0:T(8,128)(2,1)S(1)} %get-tuple-element.75), channel_id=1, source_target_pairs={{0,8},{1,3},{2,10},{3,1},{4,12},{5,7},{6,14},{7,5},{8,0},{9,11},{1... | collective-permute-start | bytes 417800 | tf_op jit(solution)/shard_map/ppermute | solution.py:437
  12.1 12.5 %collective-permute-start.4 = (bf16[2,272,128]{2,1,0:T(8,128)(2,1)S(1)}, bf16[2,272,128]{2,1,0:T(8,128)(2,1)S(1)}, u32[]{:S(2)}, u32[]{:S(2)}) collective-permute-start(bf16[2,272,128]{2,1,0:T(8,128)(2,1)S(1)} %get-tuple-element.76), channel_id=1, source_target_pairs={{0,2},{1,9},{2,0},{3,11},{4,6},{5,13},{6,4},{7,15},{8,10},{9,1},{1... | collective-permute-start | bytes 417800 | tf_op jit(solution)/shard_map/ppermute | solution.py:437
  12.7 14.9 %collective-permute-start.5 = (bf16[2,272,128]{2,1,0:T(8,128)(2,1)S(1)}, bf16[2,272,128]{2,1,0:T(8,128)(2,1)S(1)}, u32[]{:S(2)}, u32[]{:S(2)}) collective-permute-start(bf16[2,272,128]{2,1,0:T(8,128)(2,1)S(1)} %get-tuple-element.77), channel_id=1, source_target_pairs={{0,10},{1,5},{2,8},{3,7},{4,14},{5,1},{6,12},{7,3},{8,2},{9,13},{1... | collective-permute-start | bytes 417800 | tf_op jit(solution)/shard_map/ppermute | solution.py:437
  15.8 16.6 %collective-permute-start.6 = (bf16[2,272,128]{2,1,0:T(8,128)(2,1)S(1)}, bf16[2,272,128]{2,1,0:T(8,128)(2,1)S(1)}, u32[]{:S(2)}, u32[]{:S(2)}) collective-permute-start(bf16[2,272,128]{2,1,0:T(8,128)(2,1)S(1)} %get-tuple-element.79), channel_id=1, source_target_pairs={{0,4},{1,11},{2,6},{3,9},{4,0},{5,15},{6,2},{7,13},{8,12},{9,3},{1... | collective-permute-start | bytes 417800 | tf_op jit(solution)/shard_map/ppermute | solution.py:437
  15.9 16.6 %collective-permute-start.7 = (bf16[2,272,128]{2,1,0:T(8,128)(2,1)S(1)}, bf16[2,272,128]{2,1,0:T(8,128)(2,1)S(1)}, u32[]{:S(2)}, u32[]{:S(2)}) collective-permute-start(bf16[2,272,128]{2,1,0:T(8,128)(2,1)S(1)} %get-tuple-element.80), channel_id=1, source_target_pairs={{0,12},{1,7},{2,14},{3,5},{4,8},{5,3},{6,10},{7,1},{8,4},{9,15},{1... | collective-permute-start | bytes 417800 | tf_op jit(solution)/shard_map/ppermute | solution.py:437
  23.8 10.4 %collective-permute-start.8 = (bf16[2,272,128]{2,1,0:T(8,128)(2,1)S(1)}, bf16[2,272,128]{2,1,0:T(8,128)(2,1)S(1)}, u32[]{:S(2)}, u32[]{:S(2)}) collective-permute-start(bf16[2,272,128]{2,1,0:T(8,128)(2,1)S(1)} %get-tuple-element.81), channel_id=1, source_target_pairs={{0,6},{1,13},{2,4},{3,15},{4,2},{5,9},{6,0},{7,11},{8,14},{9,5},{1... | collective-permute-start | bytes 417800 | tf_op jit(solution)/shard_map/ppermute | solution.py:437
  24.6 9.6 %collective-permute-start.9 = (bf16[2,272,128]{2,1,0:T(8,128)(2,1)S(1)}, bf16[2,272,128]{2,1,0:T(8,128)(2,1)S(1)}, u32[]{:S(2)}, u32[]{:S(2)}) collective-permute-start(bf16[2,272,128]{2,1,0:T(8,128)(2,1)S(1)} %get-tuple-element.82), channel_id=1, source_target_pairs={{0,14},{1,15},{2,12},{3,13},{4,10},{5,11},{6,8},{7,9},{8,6},{9,7},... | collective-permute-start | bytes 417800 | tf_op jit(solution)/shard_map/ppermute | solution.py:437
  38.0 2.6 %collective-permute-start.10 = (bf16[8,32,1024]{2,1,0:T(8,128)(2,1)S(1)}, bf16[8,32,1024]{2,1,0:T(8,128)(2,1)S(1)}, u32[]{:S(2)}, u32[]{:S(2)}) collective-permute-start(bf16[8,32,1024]{2,1,0:T(8,128)(2,1)S(1)} %get-tuple-element.85), channel_id=1, source_target_pairs={{0,1},{1,0},{2,3},{3,2},{4,5},{5,4},{6,7},{7,6},{8,9},{9,8},{10,11... | collective-permute-start | bytes 1572872 | tf_op jit(solution)/shard_map/ppermute | solution.py:367
  40.0 2.6 %collective-permute-start.16 = (bf16[8,32,640]{2,1,0:T(8,128)(2,1)S(1)}, bf16[8,32,640]{2,1,0:T(8,128)(2,1)S(1)}, u32[]{:S(2)}, u32[]{:S(2)}) collective-permute-start(bf16[8,32,640]{2,1,0:T(8,128)(2,1)S(1)} %get-tuple-element.102), channel_id=1, source_target_pairs={{0,1},{1,0},{2,3},{3,2},{4,5},{5,4},{6,7},{7,6},{8,9},{9,8},{10,11... | collective-permute-start | bytes 983048 | tf_op jit(solution)/shard_map/ppermute | solution.py:367
  40.6 25.7 %copy-start = (bf16[512,512]{1,0:T(8,128)(2,1)S(1)}, bf16[512,512]{1,0:T(8,128)(2,1)}, u32[]{:S(2)}) copy-start(bf16[512,512]{1,0:T(8,128)(2,1)} %w_src_ref.1) | copy-start | bytes 1572868
  40.6 25.7 %copy-start.1 = (bf16[512,512]{1,0:T(8,128)(2,1)S(1)}, bf16[512,512]{1,0:T(8,128)(2,1)}, u32[]{:S(2)}) copy-start(bf16[512,512]{1,0:T(8,128)(2,1)} %w_dst_ref.1) | copy-start | bytes 1572868
  40.7 8.4 %collective-permute-start.11 = (bf16[4,32,1024]{2,1,0:T(8,128)(2,1)S(1)}, bf16[4,32,1024]{2,1,0:T(8,128)(2,1)S(1)}, u32[]{:S(2)}, u32[]{:S(2)}) collective-permute-start(bf16[4,32,1024]{2,1,0:T(8,128)(2,1)S(1)} %get-tuple-element.87), channel_id=1, source_target_pairs={{0,2},{1,3},{2,0},{3,1},{4,6},{5,7},{6,4},{7,5},{8,10},{9,11},{10,... | collective-permute-start | bytes 786440 | tf_op jit(solution)/shard_map/ppermute | solution.py:367
  42.7 11.5 %collective-permute-start.17 = (bf16[4,32,640]{2,1,0:T(8,128)(2,1)S(1)}, bf16[4,32,640]{2,1,0:T(8,128)(2,1)S(1)}, u32[]{:S(2)}, u32[]{:S(2)}) collective-permute-start(bf16[4,32,640]{2,1,0:T(8,128)(2,1)S(1)} %get-tuple-element.106), channel_id=1, source_target_pairs={{0,4},{1,5},{2,6},{3,7},{4,0},{5,1},{6,2},{7,3},{8,12},{9,13},{10,... | collective-permute-start | bytes 491528 | tf_op jit(solution)/shard_map/ppermute | solution.py:367
  49.2 13.9 %collective-permute-start.12 = (bf16[2,32,1024]{2,1,0:T(8,128)(2,1)S(1)}, bf16[2,32,1024]{2,1,0:T(8,128)(2,1)S(1)}, u32[]{:S(2)}, u32[]{:S(2)}) collective-permute-start(bf16[2,32,1024]{2,1,0:T(8,128)(2,1)S(1)} %get-tuple-element.89), channel_id=1, source_target_pairs={{0,4},{1,5},{2,6},{3,7},{4,0},{5,1},{6,2},{7,3},{8,12},{9,13},{10,... | collective-permute-start | bytes 393224 | tf_op jit(solution)/shard_map/ppermute | solution.py:367
  54.2 9.0 %collective-permute-start.18 = (bf16[2,32,640]{2,1,0:T(8,128)(2,1)S(1)}, bf16[2,32,640]{2,1,0:T(8,128)(2,1)S(1)}, u32[]{:S(2)}, u32[]{:S(2)}) collective-permute-start(bf16[2,32,640]{2,1,0:T(8,128)(2,1)S(1)} %get-tuple-element.110), channel_id=1, source_target_pairs={{0,2},{1,3},{2,0},{3,1},{4,6},{5,7},{6,4},{7,5},{8,10},{9,11},{10,... | collective-permute-start | bytes 245768 | tf_op jit(solution)/shard_map/ppermute | solution.py:367
  56.0 2.6 %collective-permute-start.13 = (bf16[64,512]{1,0:T(8,128)(2,1)S(1)}, bf16[64,512]{1,0:T(8,128)(2,1)S(1)}, u32[]{:S(2)}, u32[]{:S(2)}) collective-permute-start(bf16[64,512]{1,0:T(8,128)(2,1)S(1)} %get-tuple-element.90), channel_id=1, source_target_pairs={{1,0},{2,1},{3,2},{4,3},{5,4},{6,5},{7,6},{8,7},{9,8},{10,9},{11,1... | collective-permute-start | bytes 196616 | tf_op jit(solution)/shard_map/ppermute | solution.py:579
  56.7 6.4 %collective-permute-start.14 = (bf16[64,512]{1,0:T(8,128)(2,1)S(1)}, bf16[64,512]{1,0:T(8,128)(2,1)S(1)}, u32[]{:S(2)}, u32[]{:S(2)}) collective-permute-start(bf16[64,512]{1,0:T(8,128)(2,1)S(1)} %get-tuple-element.91), channel_id=1, source_target_pairs={{0,1},{1,2},{2,3},{3,4},{4,5},{5,6},{6,7},{7,8},{8,9},{9,10},{10,1... | collective-permute-start | bytes 196616 | tf_op jit(solution)/shard_map/ppermute | solution.py:580
  63.1 5.9 %collective-permute-start.15 = (bf16[1,32,1024]{2,1,0:T(8,128)(2,1)S(1)}, bf16[1,32,1024]{2,1,0:T(8,128)(2,1)S(1)}, u32[]{:S(2)}, u32[]{:S(2)}) collective-permute-start(bf16[1,32,1024]{2,1,0:T(8,128)(2,1)S(1)} %get-tuple-element.97), channel_id=1, source_target_pairs={{0,8},{1,9},{2,10},{3,11},{4,12},{5,13},{6,14},{7,15},{8,0},{9,1},... | collective-permute-start | bytes 196616 | tf_op jit(solution)/shard_map/ppermute | solution.py:367
  63.3 5.8 %collective-permute-start.19 = (bf16[1,32,640]{2,1,0:T(8,128)(2,1)S(1)}, bf16[1,32,640]{2,1,0:T(8,128)(2,1)S(1)}, u32[]{:S(2)}, u32[]{:S(2)}) collective-permute-start(bf16[1,32,640]{2,1,0:T(8,128)(2,1)S(1)} %get-tuple-element.114), channel_id=1, source_target_pairs={{0,8},{1,9},{2,10},{3,11},{4,12},{5,13},{6,14},{7,15},{8,0},{9,1},... | collective-permute-start | bytes 122888 | tf_op jit(solution)/shard_map/ppermute | solution.py:367

commit v15 on v13

--- a/solution.py
+++ b/solution.py
@@ -436,8 +436,8 @@
             route = [(i, i ^ (2 * turns[turn][i % 2])) for i in range(slabs)]
             came.append(lax.ppermute(messages[turn], "space", route))
         ids = [(2 * first + j, 2 * second + j) for first, second in turns for j in range(2)]
-        near, far = tuple(ids[: 2 * quarter]), tuple(ids[2 * quarter :])
-        came_near, came_far = came[:quarter], came[quarter:]
+        near, far = tuple(ids[: 2 * quarter + 2]), tuple(ids[2 * quarter + 2 :])
+        came_near, came_far = came[: quarter + 1], came[quarter + 1 :]
     else:
         packed = jnp.stack([even, odd], axis=1).reshape(slabs, rows, LANES)
         near, far = (), tuple(range(slabs))

time: 69.1 us -> 68.9 us (level)
  Pallas kernels: 21.5 us -> 22.2 us
    pallas_call x1, Pallas kernels: 4.78 us -> 5.77 us  [on_device(): pl.pallas_call(functools.partial(near_kernel, half), out_shape=(pltpu.HBM...]
    ppermute x7, waiting for transfers between devices: 1.79 us -> 0.95 us  [on_device(): came.append(lax.ppermute(messages[turn], 'space', route))]
  transfers between devices with their start and end apart: 20 -> 20, of which waited for: 6 -> 7; matrix products, arithmetic and copies ran while one was open for 3% -> 3% of each run, Pallas kernels for 21% -> 22%
where the time goes in v15:
time: 68.9 us; the launch traced here: 68.6 us
  starting transfers between devices  29.8 us (43%)
  Pallas kernels  22.2 us (32%)
  waiting for transfers between devices  14.1 us (20%)
  local copies, waits for them, and re-layouts  1.78 us (3%)
  between operations  0.83 us (1%)
    ppermute x9, starting transfers between devices, swap(): lax.ppermute(block, 'space', [(i, i ^ 1 << bit) for i in range(slabs)])  11.6 us
    ppermute x7, starting transfers between devices, on_device(): came.append(lax.ppermute(messages[turn], 'space', route))  10.4 us
    ppermute x9, waiting for transfers between devices, swap(): lax.ppermute(block, 'space', [(i, i ^ 1 << bit) for i in range(slabs)])  6.55 us
    pallas_call x1, Pallas kernels, on_device(): pl.pallas_call(functools.partial(near_kernel, half), out_shape=(pltpu.HBM...  5.77 us
    pallas_call x1, Pallas kernels, on_device(): pl.pallas_call(functools.partial(edge_kernel, half, linked, near, far), o...  5.66 us
    ppermute x1, starting transfers between devices, on_device(): above = lax.ppermute(low, 'space', down)  5.61 us
    ppermute x1, waiting for transfers between devices, on_device(): from_below = lax.ppermute(upper, 'space', up)  4.4 us
    pallas_call x1, Pallas kernels, on_device(): pl.pallas_call(functools.partial(grad_kernel, half, factor), out_shape=(c...  3.65 us
  transfers between devices with their start and end apart: 20, of which 7 were waited for; matrix products, arithmetic and copies ran while one was open for 3% of the time, Pallas kernels for 22%

profile of v15, /device:TPU:0, one launch (start us, length us, event | category | flops | bytes accessed | tf_op | source)
XLA Modules:
  0.0 68.6 jit_solution(10678677708357219604)
XLA Ops:
  0.7 2.5 %pack.1 = (bf16[8,272,128]{2,1,0:T(8,128)(2,1)S(1)}, bf16[8,272,128]{2,1,0:T(8,128)(2,1)S(1)}, bf16[64,512]{1,0:T(8,128)(2,1)S(1)}, bf16[64,512]{1,0:T(8,128)(2,1)S(1)}) custom-call(s32[1]{0:T(128)} %bitcast.me_ref, bf16[256,512]{1,0:T(8,128)(2,1)} %feats_hbm.1, bf16[529,16,128]{2,1,0:T(8,128)(2,1)} %bitcast.16), custom_call_target="tpu_custom_call" | custom-call | tf_op jit(solution)/shard_map/pack/pallas_call | solution.py:398
  3.2 0.5 collective-permute-start
  3.8 5.6 %collective-permute-start.2 = (bf16[64,512]{1,0:T(8,128)(2,1)S(1)}, bf16[64,512]{1,0:T(8,128)(2,1)S(1)}, u32[]{:S(2)}, u32[]{:S(2)}) collective-permute-start(bf16[64,512]{1,0:T(8,128)(2,1)S(1)} %get-tuple-element.63), channel_id=1, source_target_pairs={{1,0},{2,1},{3,2},{4,3},{5,4},{6,5},{7,6},{8,7},{9,8},{10,9},{11,1... | collective-permute-start | bytes 196616 | tf_op jit(solution)/shard_map/ppermute | solution.py:417
  9.4 1.7 %constant_dynamic-slice_fusion = bf16[1,1,64,529]{2,1,3,0:T(2,128)(2,1)S(1)} fusion(bf16[1,16,128,529]{2,1,3,0:T(8,128)(2,1)} %param.12, s32[]{:T(128)S(6)} %select_n.4, s32[]{:T(128)S(6)} %add.7), kind=kLoop, calls=%fused_computation.1 | loop fusion | bytes 135432 | tf_op jit(solution)/shard_map/slice | solution.py:418
  11.1 0.2 collective-permute-done.1.below_ref
  11.4 0.7 %collective-permute-start.3 = (bf16[2,272,128]{2,1,0:T(8,128)(2,1)S(1)}, bf16[2,272,128]{2,1,0:T(8,128)(2,1)S(1)}, u32[]{:S(2)}, u32[]{:S(2)}) collective-permute-start(bf16[2,272,128]{2,1,0:T(8,128)(2,1)S(1)} %get-tuple-element.75), channel_id=1, source_target_pairs={{0,8},{1,3},{2,10},{3,1},{4,12},{5,7},{6,14},{7,5},{8,0},{9,11},{1... | collective-permute-start | bytes 417800 | tf_op jit(solution)/shard_map/ppermute | solution.py:437
  12.1 0.6 collective-permute-start.4
  12.7 3.1 %collective-permute-start.5 = (bf16[2,272,128]{2,1,0:T(8,128)(2,1)S(1)}, bf16[2,272,128]{2,1,0:T(8,128)(2,1)S(1)}, u32[]{:S(2)}, u32[]{:S(2)}) collective-permute-start(bf16[2,272,128]{2,1,0:T(8,128)(2,1)S(1)} %get-tuple-element.77), channel_id=1, source_target_pairs={{0,10},{1,5},{2,8},{3,7},{4,14},{5,1},{6,12},{7,3},{8,2},{9,13},{1... | collective-permute-start | bytes 417800 | tf_op jit(solution)/shard_map/ppermute | solution.py:437
  15.9 2.1 %collective-permute-start.7 = (bf16[2,272,128]{2,1,0:T(8,128)(2,1)S(1)}, bf16[2,272,128]{2,1,0:T(8,128)(2,1)S(1)}, u32[]{:S(2)}, u32[]{:S(2)}) collective-permute-start(bf16[2,272,128]{2,1,0:T(8,128)(2,1)S(1)} %get-tuple-element.80), channel_id=1, source_target_pairs={{0,12},{1,7},{2,14},{3,5},{4,8},{5,3},{6,10},{7,1},{8,4},{9,15},{1... | collective-permute-start | bytes 417800 | tf_op jit(solution)/shard_map/ppermute | solution.py:437
  17.9 5.7 %edges.1 = (bf16[640,1152]{1,0:T(8,128)(2,1)}, f32[512,1152]{1,0:T(8,128)}, bf16[512,384]{1,0:T(8,128)(2,1)}, bf16[512,768]{1,0:T(8,128)(2,1)S(1)}, bf16[512,384...) custom-call(s32[1]{0:T(128)} %bitcast.me_ref, bf16[256,512]{1,0:T(8,128)(2,1)} %feats_hbm.1, bf16[512,512]{1,0:T(8,128)(2,1)} %w_src_ref.1, ...), custom_call_target="tpu_custom_call" | custom-call | flops 30198988800 | bytes 8388608 | tf_op jit(solution)/shard_map/edges/pallas_call | solution.py:452
  23.6 0.8 %collective-permute-start.8 = (bf16[2,272,128]{2,1,0:T(8,128)(2,1)S(1)}, bf16[2,272,128]{2,1,0:T(8,128)(2,1)S(1)}, u32[]{:S(2)}, u32[]{:S(2)}) collective-permute-start(bf16[2,272,128]{2,1,0:T(8,128)(2,1)S(1)} %get-tuple-element.81), channel_id=1, source_target_pairs={{0,6},{1,13},{2,4},{3,15},{4,2},{5,9},{6,0},{7,11},{8,14},{9,5},{1... | collective-permute-start | bytes 417800 | tf_op jit(solution)/shard_map/ppermute | solution.py:437
  24.4 3.0 %collective-permute-start.9 = (bf16[2,272,128]{2,1,0:T(8,128)(2,1)S(1)}, bf16[2,272,128]{2,1,0:T(8,128)(2,1)S(1)}, u32[]{:S(2)}, u32[]{:S(2)}) collective-permute-start(bf16[2,272,128]{2,1,0:T(8,128)(2,1)S(1)} %get-tuple-element.82), channel_id=1, source_target_pairs={{0,14},{1,15},{2,12},{3,13},{4,10},{5,11},{6,8},{7,9},{8,6},{9,7},... | collective-permute-start | bytes 417800 | tf_op jit(solution)/shard_map/ppermute | solution.py:437
  27.5 5.8 %near.1 = (f32[640,512]{1,0:T(8,128)}, f32[512,544]{1,0:T(8,128)}) custom-call(bf16[544,128]{1,0:T(8,128)(2,1)S(1)} %pad.4.own_ref, bf16[512,544]{1,0:T(8,128)(2,1)S(1)} %get-tuple-element.66.w_out_ref, bf16[512,768]{1,0:T(8,128)(2,1)S(1)} %get-tuple-element.71.hidden_ref, f32[512,1152]{1,0:T(8,128)} %get-tuple-element.67.slope_hbm, ...), custom_call_target="tpu_custom_call" | custom-call | flops 8556380160 | bytes 6291456 | tf_op jit(solution)/shard_map/near/pallas_call | solution.py:491
  33.2 0.9 %collective-permute-done.8.rest_1_ = bf16[2,272,128]{2,1,0:T(8,128)(2,1)S(1)} collective-permute-done((bf16[2,272,128]{2,1,0:T(8,128)(2,1)S(1)}, bf16[2,272,128]{2,1,0:T(8,128)(2,1)S(1)}, u32[]{:S(2)}, u32[]{:S(2)}) %collective-permute-start.8) | collective-permute-done | bytes 139296 | tf_op jit(solution)/shard_map/ppermute | solution.py:437
  34.2 3.6 %grads.1 = (f32[8,32,1024]{2,1,0:T(8,128)S(1)}, bf16[8,32,1024]{2,1,0:T(8,128)(2,1)S(1)}, f32[512,512]{1,0:T(8,128)S(1)}, bf16[64,512]{1,0:T(8,128)(2,1)S(1)}, b...) custom-call(s32[1]{0:T(128)} %bitcast.me_ref, bf16[512,544]{1,0:T(8,128)(2,1)S(1)} %get-tuple-element.66.w_out_ref, ...), custom_call_target="tpu_custom_call" | custom-call | tf_op jit(solution)/shard_map/grads/pallas_call | solution.py:515
  37.8 1.6 %collective-permute-start.10 = (bf16[8,32,1024]{2,1,0:T(8,128)(2,1)S(1)}, bf16[8,32,1024]{2,1,0:T(8,128)(2,1)S(1)}, u32[]{:S(2)}, u32[]{:S(2)}) collective-permute-start(bf16[8,32,1024]{2,1,0:T(8,128)(2,1)S(1)} %get-tuple-element.85), channel_id=1, source_target_pairs={{0,1},{1,0},{2,3},{3,2},{4,5},{5,4},{6,7},{7,6},{8,9},{9,8},{10,11... | collective-permute-start | bytes 1572872 | tf_op jit(solution)/shard_map/ppermute | solution.py:367
  39.4 1.9 %outer.1 = (f32[8,32,640]{2,1,0:T(8,128)S(1)}, bf16[8,32,640]{2,1,0:T(8,128)(2,1)S(1)}) custom-call(s32[1]{0:T(128)} %bitcast.me_ref, bf16[512,384]{1,0:T(8,128)(2,1)S(1)} %get-tuple-element.98.hidden_ref, bf16[544,384]{1,0:T(8,128)(2,1)S(1)} %get-tuple-element.99.g_ref, f32[512,544]{1,0:T(8,128)} %get-tuple-element.100.near_hbm), custom_call_target="tpu_custom_call" | custom-call | flops 12834570240 | bytes 4194304 | tf_op jit(solution)/shard_map/outer/pallas_call | solution.py:539
  41.5 0.1 fold.6
  41.6 0.9 %collective-permute-start.11 = (bf16[4,32,1024]{2,1,0:T(8,128)(2,1)S(1)}, bf16[4,32,1024]{2,1,0:T(8,128)(2,1)S(1)}, u32[]{:S(2)}, u32[]{:S(2)}) collective-permute-start(bf16[4,32,1024]{2,1,0:T(8,128)(2,1)S(1)} %get-tuple-element.87), channel_id=1, source_target_pairs={{0,2},{1,3},{2,0},{3,1},{4,6},{5,7},{6,4},{7,5},{8,10},{9,11},{10,... | collective-permute-start | bytes 786440 | tf_op jit(solution)/shard_map/ppermute | solution.py:367
  42.5 0.5 collective-permute-done.16.came_ref
  43.1 0.1 fold.9
  43.1 4.3 %collective-permute-start.17 = (bf16[4,32,640]{2,1,0:T(8,128)(2,1)S(1)}, bf16[4,32,640]{2,1,0:T(8,128)(2,1)S(1)}, u32[]{:S(2)}, u32[]{:S(2)}) collective-permute-start(bf16[4,32,640]{2,1,0:T(8,128)(2,1)S(1)} %get-tuple-element.106), channel_id=1, source_target_pairs={{0,4},{1,5},{2,6},{3,7},{4,0},{5,1},{6,2},{7,3},{8,12},{9,13},{10,... | collective-permute-start | bytes 491528 | tf_op jit(solution)/shard_map/ppermute | solution.py:367
  47.5 2.2 %collective-permute-start.12 = (bf16[64,512]{1,0:T(8,128)(2,1)S(1)}, bf16[64,512]{1,0:T(8,128)(2,1)S(1)}, u32[]{:S(2)}, u32[]{:S(2)}) collective-permute-start(bf16[64,512]{1,0:T(8,128)(2,1)S(1)} %get-tuple-element.88), channel_id=1, source_target_pairs={{1,0},{2,1},{3,2},{4,3},{5,4},{6,5},{7,6},{8,7},{9,8},{10,9},{11,1... | collective-permute-start | bytes 196616 | tf_op jit(solution)/shard_map/ppermute | solution.py:579
  49.6 2.0 %collective-permute-done.12.from_above_ref = bf16[64,512]{1,0:T(8,128)(2,1)S(1)} collective-permute-done((bf16[64,512]{1,0:T(8,128)(2,1)S(1)}, bf16[64,512]{1,0:T(8,128)(2,1)S(1)}, u32[]{:S(2)}, u32[]{:S(2)}) %collective-permute-start.12) | collective-permute-done | bytes 65568 | tf_op jit(solution)/shard_map/ppermute | solution.py:579
  51.6 4.4 %collective-permute-done.13.from_below_ref = bf16[64,512]{1,0:T(8,128)(2,1)S(1)} collective-permute-done((bf16[64,512]{1,0:T(8,128)(2,1)S(1)}, bf16[64,512]{1,0:T(8,128)(2,1)S(1)}, u32[]{:S(2)}, u32[]{:S(2)}) %collective-permute-start.13) | collective-permute-done | bytes 65568 | tf_op jit(solution)/shard_map/ppermute | solution.py:580
  56.2 1.0 %collective-permute-start.18 = (bf16[2,32,640]{2,1,0:T(8,128)(2,1)S(1)}, bf16[2,32,640]{2,1,0:T(8,128)(2,1)S(1)}, u32[]{:S(2)}, u32[]{:S(2)}) collective-permute-start(bf16[2,32,640]{2,1,0:T(8,128)(2,1)S(1)} %get-tuple-element.110), channel_id=1, source_target_pairs={{0,2},{1,3},{2,0},{3,1},{4,6},{5,7},{6,4},{7,5},{8,10},{9,11},{10,... | collective-permute-start | bytes 245768 | tf_op jit(solution)/shard_map/ppermute | solution.py:367
  57.3 3.9 %collective-permute-done.14.came_ref = bf16[2,32,1024]{2,1,0:T(8,128)(2,1)S(1)} collective-permute-done((bf16[2,32,1024]{2,1,0:T(8,128)(2,1)S(1)}, bf16[2,32,1024]{2,1,0:T(8,128)(2,1)S(1)}, u32[]{:S(2)}, u32[]{:S(2)}) %collective-permute-start.14) | collective-permute-done | bytes 131104 | tf_op jit(solution)/shard_map/ppermute | solution.py:367
  61.2 0.8 %collective-permute-start.15 = (bf16[1,32,1024]{2,1,0:T(8,128)(2,1)S(1)}, bf16[1,32,1024]{2,1,0:T(8,128)(2,1)S(1)}, u32[]{:S(2)}, u32[]{:S(2)}) collective-permute-start(bf16[1,32,1024]{2,1,0:T(8,128)(2,1)S(1)} %get-tuple-element.97), channel_id=1, source_target_pairs={{0,8},{1,9},{2,10},{3,11},{4,12},{5,13},{6,14},{7,15},{8,0},{9,1},... | collective-permute-start | bytes 196616 | tf_op jit(solution)/shard_map/ppermute | solution.py:367
  62.0 2.3 %collective-permute-start.19 = (bf16[1,32,640]{2,1,0:T(8,128)(2,1)S(1)}, bf16[1,32,640]{2,1,0:T(8,128)(2,1)S(1)}, u32[]{:S(2)}, u32[]{:S(2)}) collective-permute-start(bf16[1,32,640]{2,1,0:T(8,128)(2,1)S(1)} %get-tuple-element.114), channel_id=1, source_target_pairs={{0,8},{1,9},{2,10},{3,11},{4,12},{5,13},{6,14},{7,15},{8,0},{9,1},... | collective-permute-start | bytes 122888 | tf_op jit(solution)/shard_map/ppermute | solution.py:367
  64.2 1.5 %rims.1 = f32[256,512]{1,0:T(8,128)} custom-call(f32[512,512]{1,0:T(8,128)S(1)} %get-tuple-element.83.sums_ref, bf16[64,512]{1,0:T(8,128)(2,1)S(1)} %collective-permute-done.13.from_below_ref, bf16[64,512]{1,0:T(8,128)(2,1)S(1)} %collective-permute-done.12.from_above_ref, bf16[512,512]{1,0:T(8,128)(2,1)S(1)} %copy-done, bf16[512,512]{1,0:T(8,128)(2,1)S(1)} %copy-done.1), custom_call_target="tpu_custom_call" | custom-call | flops 24159191040 | bytes 4194304 | tf_op jit(solution)/shard_map/rims/pallas_call | solution.py:593
  65.8 2.2 %collective-permute-done.19.refs_3_ = bf16[1,32,640]{2,1,0:T(8,128)(2,1)S(1)} collective-permute-done((bf16[1,32,640]{2,1,0:T(8,128)(2,1)S(1)}, bf16[1,32,640]{2,1,0:T(8,128)(2,1)S(1)}, u32[]{:S(2)}, u32[]{:S(2)}) %collective-permute-start.19) | collective-permute-done | bytes 40992 | tf_op jit(solution)/shard_map/ppermute | solution.py:367
  67.9 0.7 %totals.1 = (f32[32,512]{1,0:T(8,128)}, f32[32,512]{1,0:T(8,128)}, f32[32,529]{1,0:T(8,128)}) custom-call(f32[1,32,1024]{2,1,0:T(8,128)S(1)} %get-tuple-element.96.refs_0_, bf16[1,32,1024]{2,1,0:T(8,128)(2,1)S(1)} %collective-permute-done.15.refs_1_, f32[1,32,640]{2,1,0:T(8,128)S(1)} %get-tuple-element.113.refs_2_, ...), custom_call_target="tpu_custom_call" | custom-call | tf_op jit(solution)/shard_map/totals/pallas_call | solution.py:602
  (35 shorter events, 0.6 us)
Async XLA Ops:
  0.6 17.3 %copy-start.2 = (s32[2048]{0:T(1024)S(1)}, s32[2048]{0:T(1024)}, u32[]{:S(2)}) copy-start(s32[2048]{0:T(1024)} %param.13) | copy-start | bytes 24580
  0.6 17.3 %copy-start.3 = (s32[2048]{0:T(1024)S(1)}, s32[2048]{0:T(1024)}, u32[]{:S(2)}) copy-start(s32[2048]{0:T(1024)} %param.14) | copy-start | bytes 24580
  0.7 17.3 %copy-start.4 = (s32[2048]{0:T(1024)S(1)}, s32[2048]{0:T(1024)}, u32[]{:S(2)}) copy-start(s32[2048]{0:T(1024)} %param.15) | copy-start | bytes 24580
  3.2 8.1 %collective-permute-start = (bf16[8,272,128]{2,1,0:T(8,128)(2,1)S(1)}, bf16[8,272,128]{2,1,0:T(8,128)(2,1)S(1)}, u32[]{:S(2)}, u32[]{:S(2)}) collective-permute-start(bf16[8,272,128]{2,1,0:T(8,128)(2,1)S(1)} %get-tuple-element.61), channel_id=1, source_target_pairs={{0,1},{1,0},{2,3},{3,2},{4,5},{5,4},{6,7},{7,6},{8,9},{9,8},{10,11... | collective-permute-start | bytes 1671176 | tf_op jit(solution)/shard_map/ppermute | solution.py:367
  3.7 7.6 %collective-permute-start.1 = (bf16[64,512]{1,0:T(8,128)(2,1)S(1)}, bf16[64,512]{1,0:T(8,128)(2,1)S(1)}, u32[]{:S(2)}, u32[]{:S(2)}) collective-permute-start(bf16[64,512]{1,0:T(8,128)(2,1)S(1)} %get-tuple-element.62), channel_id=1, source_target_pairs={{0,1},{1,2},{2,3},{3,4},{4,5},{5,6},{6,7},{7,8},{8,9},{9,10},{10,1... | collective-permute-start | bytes 196616 | tf_op jit(solution)/shard_map/ppermute | solution.py:416
  3.8 7.6 %collective-permute-start.2 = (bf16[64,512]{1,0:T(8,128)(2,1)S(1)}, bf16[64,512]{1,0:T(8,128)(2,1)S(1)}, u32[]{:S(2)}, u32[]{:S(2)}) collective-permute-start(bf16[64,512]{1,0:T(8,128)(2,1)S(1)} %get-tuple-element.63), channel_id=1, source_target_pairs={{1,0},{2,1},{3,2},{4,3},{5,4},{6,5},{7,6},{8,7},{9,8},{10,9},{11,1... | collective-permute-start | bytes 196616 | tf_op jit(solution)/shard_map/ppermute | solution.py:417
  11.4 12.2 %collective-permute-start.3 = (bf16[2,272,128]{2,1,0:T(8,128)(2,1)S(1)}, bf16[2,272,128]{2,1,0:T(8,128)(2,1)S(1)}, u32[]{:S(2)}, u32[]{:S(2)}) collective-permute-start(bf16[2,272,128]{2,1,0:T(8,128)(2,1)S(1)} %get-tuple-element.75), channel_id=1, source_target_pairs={{0,8},{1,3},{2,10},{3,1},{4,12},{5,7},{6,14},{7,5},{8,0},{9,11},{1... | collective-permute-start | bytes 417800 | tf_op jit(solution)/shard_map/ppermute | solution.py:437
  12.1 12.3 %collective-permute-start.4 = (bf16[2,272,128]{2,1,0:T(8,128)(2,1)S(1)}, bf16[2,272,128]{2,1,0:T(8,128)(2,1)S(1)}, u32[]{:S(2)}, u32[]{:S(2)}) collective-permute-start(bf16[2,272,128]{2,1,0:T(8,128)(2,1)S(1)} %get-tuple-element.76), channel_id=1, source_target_pairs={{0,2},{1,9},{2,0},{3,11},{4,6},{5,13},{6,4},{7,15},{8,10},{9,1},{1... | collective-permute-start | bytes 417800 | tf_op jit(solution)/shard_map/ppermute | solution.py:437
  12.7 14.7 %collective-permute-start.5 = (bf16[2,272,128]{2,1,0:T(8,128)(2,1)S(1)}, bf16[2,272,128]{2,1,0:T(8,128)(2,1)S(1)}, u32[]{:S(2)}, u32[]{:S(2)}) collective-permute-start(bf16[2,272,128]{2,1,0:T(8,128)(2,1)S(1)} %get-tuple-element.77), channel_id=1, source_target_pairs={{0,10},{1,5},{2,8},{3,7},{4,14},{5,1},{6,12},{7,3},{8,2},{9,13},{1... | collective-permute-start | bytes 417800 | tf_op jit(solution)/shard_map/ppermute | solution.py:437
  15.8 11.6 %collective-permute-start.6 = (bf16[2,272,128]{2,1,0:T(8,128)(2,1)S(1)}, bf16[2,272,128]{2,1,0:T(8,128)(2,1)S(1)}, u32[]{:S(2)}, u32[]{:S(2)}) collective-permute-start(bf16[2,272,128]{2,1,0:T(8,128)(2,1)S(1)} %get-tuple-element.78), channel_id=1, source_target_pairs={{0,4},{1,11},{2,6},{3,9},{4,0},{5,15},{6,2},{7,13},{8,12},{9,3},{1... | collective-permute-start | bytes 417800 | tf_op jit(solution)/shard_map/ppermute | solution.py:437
  15.9 17.4 %collective-permute-start.7 = (bf16[2,272,128]{2,1,0:T(8,128)(2,1)S(1)}, bf16[2,272,128]{2,1,0:T(8,128)(2,1)S(1)}, u32[]{:S(2)}, u32[]{:S(2)}) collective-permute-start(bf16[2,272,128]{2,1,0:T(8,128)(2,1)S(1)} %get-tuple-element.80), channel_id=1, source_target_pairs={{0,12},{1,7},{2,14},{3,5},{4,8},{5,3},{6,10},{7,1},{8,4},{9,15},{1... | collective-permute-start | bytes 417800 | tf_op jit(solution)/shard_map/ppermute | solution.py:437
  23.6 10.6 %collective-permute-start.8 = (bf16[2,272,128]{2,1,0:T(8,128)(2,1)S(1)}, bf16[2,272,128]{2,1,0:T(8,128)(2,1)S(1)}, u32[]{:S(2)}, u32[]{:S(2)}) collective-permute-start(bf16[2,272,128]{2,1,0:T(8,128)(2,1)S(1)} %get-tuple-element.81), channel_id=1, source_target_pairs={{0,6},{1,13},{2,4},{3,15},{4,2},{5,9},{6,0},{7,11},{8,14},{9,5},{1... | collective-permute-start | bytes 417800 | tf_op jit(solution)/shard_map/ppermute | solution.py:437
  24.4 9.8 %collective-permute-start.9 = (bf16[2,272,128]{2,1,0:T(8,128)(2,1)S(1)}, bf16[2,272,128]{2,1,0:T(8,128)(2,1)S(1)}, u32[]{:S(2)}, u32[]{:S(2)}) collective-permute-start(bf16[2,272,128]{2,1,0:T(8,128)(2,1)S(1)} %get-tuple-element.82), channel_id=1, source_target_pairs={{0,14},{1,15},{2,12},{3,13},{4,10},{5,11},{6,8},{7,9},{8,6},{9,7},... | collective-permute-start | bytes 417800 | tf_op jit(solution)/shard_map/ppermute | solution.py:437
  37.8 3.6 %collective-permute-start.10 = (bf16[8,32,1024]{2,1,0:T(8,128)(2,1)S(1)}, bf16[8,32,1024]{2,1,0:T(8,128)(2,1)S(1)}, u32[]{:S(2)}, u32[]{:S(2)}) collective-permute-start(bf16[8,32,1024]{2,1,0:T(8,128)(2,1)S(1)} %get-tuple-element.85), channel_id=1, source_target_pairs={{0,1},{1,0},{2,3},{3,2},{4,5},{5,4},{6,7},{7,6},{8,9},{9,8},{10,11... | collective-permute-start | bytes 1572872 | tf_op jit(solution)/shard_map/ppermute | solution.py:367
  41.4 1.7 %collective-permute-start.16 = (bf16[8,32,640]{2,1,0:T(8,128)(2,1)S(1)}, bf16[8,32,640]{2,1,0:T(8,128)(2,1)S(1)}, u32[]{:S(2)}, u32[]{:S(2)}) collective-permute-start(bf16[8,32,640]{2,1,0:T(8,128)(2,1)S(1)} %get-tuple-element.102), channel_id=1, source_target_pairs={{0,1},{1,0},{2,3},{3,2},{4,5},{5,4},{6,7},{7,6},{8,9},{9,8},{10,11... | collective-permute-start | bytes 983048 | tf_op jit(solution)/shard_map/ppermute | solution.py:367
  41.4 22.8 %copy-start = (bf16[512,512]{1,0:T(8,128)(2,1)S(1)}, bf16[512,512]{1,0:T(8,128)(2,1)}, u32[]{:S(2)}) copy-start(bf16[512,512]{1,0:T(8,128)(2,1)} %w_src_ref.1) | copy-start | bytes 1572868
  41.5 22.8 %copy-start.1 = (bf16[512,512]{1,0:T(8,128)(2,1)S(1)}, bf16[512,512]{1,0:T(8,128)(2,1)}, u32[]{:S(2)}) copy-start(bf16[512,512]{1,0:T(8,128)(2,1)} %w_dst_ref.1) | copy-start | bytes 1572868
  41.6 14.4 %collective-permute-start.11 = (bf16[4,32,1024]{2,1,0:T(8,128)(2,1)S(1)}, bf16[4,32,1024]{2,1,0:T(8,128)(2,1)S(1)}, u32[]{:S(2)}, u32[]{:S(2)}) collective-permute-start(bf16[4,32,1024]{2,1,0:T(8,128)(2,1)S(1)} %get-tuple-element.87), channel_id=1, source_target_pairs={{0,2},{1,3},{2,0},{3,1},{4,6},{5,7},{6,4},{7,5},{8,10},{9,11},{10,... | collective-permute-start | bytes 786440 | tf_op jit(solution)/shard_map/ppermute | solution.py:367
  43.1 13.0 %collective-permute-start.17 = (bf16[4,32,640]{2,1,0:T(8,128)(2,1)S(1)}, bf16[4,32,640]{2,1,0:T(8,128)(2,1)S(1)}, u32[]{:S(2)}, u32[]{:S(2)}) collective-permute-start(bf16[4,32,640]{2,1,0:T(8,128)(2,1)S(1)} %get-tuple-element.106), channel_id=1, source_target_pairs={{0,4},{1,5},{2,6},{3,7},{4,0},{5,1},{6,2},{7,3},{8,12},{9,13},{10,... | collective-permute-start | bytes 491528 | tf_op jit(solution)/shard_map/ppermute | solution.py:367
  47.5 4.2 %collective-permute-start.12 = (bf16[64,512]{1,0:T(8,128)(2,1)S(1)}, bf16[64,512]{1,0:T(8,128)(2,1)S(1)}, u32[]{:S(2)}, u32[]{:S(2)}) collective-permute-start(bf16[64,512]{1,0:T(8,128)(2,1)S(1)} %get-tuple-element.88), channel_id=1, source_target_pairs={{1,0},{2,1},{3,2},{4,3},{5,4},{6,5},{7,6},{8,7},{9,8},{10,9},{11,1... | collective-permute-start | bytes 196616 | tf_op jit(solution)/shard_map/ppermute | solution.py:579
  49.6 6.4 %collective-permute-start.13 = (bf16[64,512]{1,0:T(8,128)(2,1)S(1)}, bf16[64,512]{1,0:T(8,128)(2,1)S(1)}, u32[]{:S(2)}, u32[]{:S(2)}) collective-permute-start(bf16[64,512]{1,0:T(8,128)(2,1)S(1)} %get-tuple-element.89), channel_id=1, source_target_pairs={{0,1},{1,2},{2,3},{3,4},{4,5},{5,6},{6,7},{7,8},{8,9},{9,10},{10,1... | collective-permute-start | bytes 196616 | tf_op jit(solution)/shard_map/ppermute | solution.py:580
  56.1 5.0 %collective-permute-start.14 = (bf16[2,32,1024]{2,1,0:T(8,128)(2,1)S(1)}, bf16[2,32,1024]{2,1,0:T(8,128)(2,1)S(1)}, u32[]{:S(2)}, u32[]{:S(2)}) collective-permute-start(bf16[2,32,1024]{2,1,0:T(8,128)(2,1)S(1)} %get-tuple-element.95), channel_id=1, source_target_pairs={{0,4},{1,5},{2,6},{3,7},{4,0},{5,1},{6,2},{7,3},{8,12},{9,13},{10,... | collective-permute-start | bytes 393224 | tf_op jit(solution)/shard_map/ppermute | solution.py:367
  56.2 5.7 %collective-permute-start.18 = (bf16[2,32,640]{2,1,0:T(8,128)(2,1)S(1)}, bf16[2,32,640]{2,1,0:T(8,128)(2,1)S(1)}, u32[]{:S(2)}, u32[]{:S(2)}) collective-permute-start(bf16[2,32,640]{2,1,0:T(8,128)(2,1)S(1)} %get-tuple-element.110), channel_id=1, source_target_pairs={{0,2},{1,3},{2,0},{3,1},{4,6},{5,7},{6,4},{7,5},{8,10},{9,11},{10,... | collective-permute-start | bytes 245768 | tf_op jit(solution)/shard_map/ppermute | solution.py:367
  61.2 6.8 %collective-permute-start.15 = (bf16[1,32,1024]{2,1,0:T(8,128)(2,1)S(1)}, bf16[1,32,1024]{2,1,0:T(8,128)(2,1)S(1)}, u32[]{:S(2)}, u32[]{:S(2)}) collective-permute-start(bf16[1,32,1024]{2,1,0:T(8,128)(2,1)S(1)} %get-tuple-element.97), channel_id=1, source_target_pairs={{0,8},{1,9},{2,10},{3,11},{4,12},{5,13},{6,14},{7,15},{8,0},{9,1},... | collective-permute-start | bytes 196616 | tf_op jit(solution)/shard_map/ppermute | solution.py:367
  62.0 6.0 %collective-permute-start.19 = (bf16[1,32,640]{2,1,0:T(8,128)(2,1)S(1)}, bf16[1,32,640]{2,1,0:T(8,128)(2,1)S(1)}, u32[]{:S(2)}, u32[]{:S(2)}) collective-permute-start(bf16[1,32,640]{2,1,0:T(8,128)(2,1)S(1)} %get-tuple-element.114), channel_id=1, source_target_pairs={{0,8},{1,9},{2,10},{3,11},{4,12},{5,13},{6,14},{7,15},{8,0},{9,1},... | collective-permute-start | bytes 122888 | tf_op jit(solution)/shard_map/ppermute | solution.py:367

commit v16 on v15

--- a/solution.py
+++ b/solution.py
@@ -97,13 +97,18 @@
         copy.wait()
 
 
-def by_core(pair, me):
-    return pair[0] + (me % 2) * (pair[1] - pair[0])
+def inner(slab, slabs):
+    bits = slabs.bit_length() - 1
+    return ((slab >> (bits - 1)) ^ (slab >> (bits - 2))) & 1
+
+
+def by_place(pair, me, slabs):
+    return pair[0] + inner(me, slabs) * (pair[1] - pair[0])
 
 
 def join_kernel(turns, me_ref, even_ref, other_ref, *message_refs):
     for pair, message_ref in zip(turns, message_refs):
-        k = by_core(pair, me_ref[0])
+        k = by_place(pair, me_ref[0], 2 * even_ref.shape[0])
         message_ref[0] = even_ref[k]
         message_ref[1] = other_ref[k]
 
@@ -130,7 +135,7 @@
         rows = []
         for tile in range(len(ids) // per):
             here = ids[tile * per : (tile + 1) * per]
-            pieces = [ref[pl.ds(me ^ by_core(i, me) if linked else i, 1), :] for i in here]
+            pieces = [ref[pl.ds(me ^ by_place(i, me, ref.shape[0]) if linked else i, 1), :] for i in here]
             rows.append(jnp.concatenate([piece[:, :half] for piece in pieces], axis=1))
         return rows
 
@@ -394,7 +399,7 @@
 
     rows = round_up(pl.cdiv(entries, groups), PACK)
     stages = 4
-    linked = slabs <= 16
+    linked = slabs == 16
     even, odd, low, top = pl.pallas_call(
         functools.partial(pack_kernel, rows, half, linked),
         out_shape=(
@@ -421,8 +426,8 @@
         other = swap(odd, 0, slabs)
         other, below, above, own = lax.optimization_barrier((other, below, above, own))
         quarter = slabs // 4
-        mixed = [pair for k in range(1, quarter) for pair in ((quarter + k - 1, k), (k, quarter + k - 1))]
-        turns = [(0, 0), *mixed, (2 * quarter - 1, 2 * quarter - 1)]
+        turns = [(0, 0), (1, 6), (2, 4), (3, 5), (6, 7), (7, 1), (4, 2), (5, 3)]
+        kept = (0, 1, 6, 7)
         messages = pl.pallas_call(
             functools.partial(join_kernel, turns),
             out_shape=(jax.ShapeDtypeStruct((2, rows, LANES), BF16),) * (slabs // 2),
@@ -433,9 +438,10 @@
         )(me, even, other)
         came = [messages[0]]
         for turn in range(1, 2 * quarter):
-            route = [(i, i ^ (2 * turns[turn][i % 2])) for i in range(slabs)]
+            route = [(i, i ^ (2 * turns[turn][inner(i, slabs)])) for i in range(slabs)]
             came.append(lax.ppermute(messages[turn], "space", route))
-        ids = [(2 * first + j, 2 * second + j) for first, second in turns for j in range(2)]
+        sources = [pair if pair[0] in kept else pair[::-1] for pair in turns]
+        ids = [(2 * first + j, 2 * second + j) for first, second in sources for j in range(2)]
         near, far = tuple(ids[: 2 * quarter + 2]), tuple(ids[2 * quarter + 2 :])
         came_near, came_far = came[: quarter + 1], came[quarter + 1 :]
     else:

time: 68.9 us -> 73.9 us (1.073)
  waiting for transfers between devices: 14.1 us -> 19.9 us
  starting transfers between devices: 29.8 us -> 28.8 us
    ppermute x7, waiting for transfers between devices: 0.95 us -> 6.97 us  [on_device(): came.append(lax.ppermute(messages[turn], 'space', route))]
    ppermute x9, starting transfers between devices: 11.6 us -> 9.83 us  [swap(): lax.ppermute(block, 'space', [(i, i ^ 1 << bit) for i in range(slabs)])]
    ppermute x7, starting transfers between devices: 10.4 us -> 11.2 us  [on_device(): came.append(lax.ppermute(messages[turn], 'space', route))]
  transfers between devices with their start and end apart: 20 -> 20, of which waited for: 7 -> 6; matrix products, arithmetic and copies ran while one was open for 3% -> 2% of each run, Pallas kernels for 22% -> 21%
where the time goes in v16:
time: 73.9 us; the launch traced here: 73.6 us
  starting transfers between devices  28.8 us (39%)
  Pallas kernels  22.2 us (30%)
  waiting for transfers between devices  19.9 us (27%)
  local copies, waits for them, and re-layouts  1.78 us (2%)
  between operations  0.85 us (1%)
    ppermute x7, starting transfers between devices, on_device(): came.append(lax.ppermute(messages[turn], 'space', route))  11.2 us
    ppermute x9, starting transfers between devices, swap(): lax.ppermute(block, 'space', [(i, i ^ 1 << bit) for i in range(slabs)])  9.83 us
    ppermute x7, waiting for transfers between devices, on_device(): came.append(lax.ppermute(messages[turn], 'space', route))  6.97 us
    ppermute x9, waiting for transfers between devices, swap(): lax.ppermute(block, 'space', [(i, i ^ 1 << bit) for i in range(slabs)])  6.41 us
    pallas_call x1, Pallas kernels, on_device(): pl.pallas_call(functools.partial(near_kernel, half), out_shape=(pltpu.HBM...  5.77 us
    pallas_call x1, Pallas kernels, on_device(): pl.pallas_call(functools.partial(edge_kernel, half, linked, near, far), o...  5.72 us
    ppermute x1, starting transfers between devices, on_device(): above = lax.ppermute(low, 'space', down)  5.61 us
    ppermute x1, waiting for transfers between devices, on_device(): from_below = lax.ppermute(upper, 'space', up)  3.84 us
  transfers between devices with their start and end apart: 20, of which 6 were waited for; matrix products, arithmetic and copies ran while one was open for 2% of the time, Pallas kernels for 21%

profile of v16, /device:TPU:0, one launch (start us, length us, event | category | flops | bytes accessed | tf_op | source)
XLA Modules:
  0.0 73.6 jit_solution(16873084776148276528)
XLA Ops:
  0.7 2.5 %pack.1 = (bf16[8,272,128]{2,1,0:T(8,128)(2,1)S(1)}, bf16[8,272,128]{2,1,0:T(8,128)(2,1)S(1)}, bf16[64,512]{1,0:T(8,128)(2,1)S(1)}, bf16[64,512]{1,0:T(8,128)(2,1)S(1)}) custom-call(s32[1]{0:T(128)} %bitcast.me_ref, bf16[256,512]{1,0:T(8,128)(2,1)} %feats_hbm.1, bf16[529,16,128]{2,1,0:T(8,128)(2,1)} %bitcast.16), custom_call_target="tpu_custom_call" | custom-call | tf_op jit(solution)/shard_map/pack/pallas_call | solution.py:403
  3.2 0.5 collective-permute-start
  3.8 5.6 %collective-permute-start.2 = (bf16[64,512]{1,0:T(8,128)(2,1)S(1)}, bf16[64,512]{1,0:T(8,128)(2,1)S(1)}, u32[]{:S(2)}, u32[]{:S(2)}) collective-permute-start(bf16[64,512]{1,0:T(8,128)(2,1)S(1)} %get-tuple-element.63), channel_id=1, source_target_pairs={{1,0},{2,1},{3,2},{4,3},{5,4},{6,5},{7,6},{8,7},{9,8},{10,9},{11,1... | collective-permute-start | bytes 196616 | tf_op jit(solution)/shard_map/ppermute | solution.py:422
  9.4 1.7 %constant_dynamic-slice_fusion = bf16[1,1,64,529]{2,1,3,0:T(2,128)(2,1)S(1)} fusion(bf16[1,16,128,529]{2,1,3,0:T(8,128)(2,1)} %param.12, s32[]{:T(128)S(6)} %select_n.4, s32[]{:T(128)S(6)} %add.7), kind=kLoop, calls=%fused_computation.1 | loop fusion | bytes 135432 | tf_op jit(solution)/shard_map/slice | solution.py:423
  11.1 0.2 collective-permute-done.1.below_ref
  11.3 0.1 join.1
  11.5 1.2 %collective-permute-start.4 = (bf16[2,272,128]{2,1,0:T(8,128)(2,1)S(1)}, bf16[2,272,128]{2,1,0:T(8,128)(2,1)S(1)}, u32[]{:S(2)}, u32[]{:S(2)}) collective-permute-start(bf16[2,272,128]{2,1,0:T(8,128)(2,1)S(1)} %get-tuple-element.76), channel_id=1, source_target_pairs={{0,4},{1,5},{2,6},{3,7},{4,12},{5,13},{6,14},{7,15},{8,0},{9,1},{1... | collective-permute-start | bytes 417800 | tf_op jit(solution)/shard_map/ppermute | solution.py:442
  12.6 2.5 %collective-permute-start.5 = (bf16[2,272,128]{2,1,0:T(8,128)(2,1)S(1)}, bf16[2,272,128]{2,1,0:T(8,128)(2,1)S(1)}, u32[]{:S(2)}, u32[]{:S(2)}) collective-permute-start(bf16[2,272,128]{2,1,0:T(8,128)(2,1)S(1)} %get-tuple-element.77), channel_id=1, source_target_pairs={{0,6},{1,7},{2,4},{3,5},{4,14},{5,15},{6,12},{7,13},{8,2},{9,3},{1... | collective-permute-start | bytes 417800 | tf_op jit(solution)/shard_map/ppermute | solution.py:442
  15.1 2.2 %collective-permute-start.6 = (bf16[2,272,128]{2,1,0:T(8,128)(2,1)S(1)}, bf16[2,272,128]{2,1,0:T(8,128)(2,1)S(1)}, u32[]{:S(2)}, u32[]{:S(2)}) collective-permute-start(bf16[2,272,128]{2,1,0:T(8,128)(2,1)S(1)} %get-tuple-element.78), channel_id=1, source_target_pairs={{0,12},{1,13},{2,14},{3,15},{4,10},{5,11},{6,8},{7,9},{8,6},{9,7},... | collective-permute-start | bytes 417800 | tf_op jit(solution)/shard_map/ppermute | solution.py:442
  17.3 1.7 %collective-permute-start.7 = (bf16[2,272,128]{2,1,0:T(8,128)(2,1)S(1)}, bf16[2,272,128]{2,1,0:T(8,128)(2,1)S(1)}, u32[]{:S(2)}, u32[]{:S(2)}) collective-permute-start(bf16[2,272,128]{2,1,0:T(8,128)(2,1)S(1)} %get-tuple-element.80), channel_id=1, source_target_pairs={{0,14},{1,15},{2,12},{3,13},{4,6},{5,7},{6,4},{7,5},{8,10},{9,11},... | collective-permute-start | bytes 417800 | tf_op jit(solution)/shard_map/ppermute | solution.py:442
  19.0 5.7 %edges.1 = (bf16[640,1152]{1,0:T(8,128)(2,1)}, f32[512,1152]{1,0:T(8,128)}, bf16[512,384]{1,0:T(8,128)(2,1)}, bf16[512,768]{1,0:T(8,128)(2,1)S(1)}, bf16[512,384...) custom-call(s32[1]{0:T(128)} %bitcast.me_ref, bf16[256,512]{1,0:T(8,128)(2,1)} %feats_hbm.1, bf16[512,512]{1,0:T(8,128)(2,1)} %w_src_ref.1, ...), custom_call_target="tpu_custom_call" | custom-call | flops 30198988800 | bytes 8388608 | tf_op jit(solution)/shard_map/edges/pallas_call | solution.py:458
  24.8 3.6 %collective-permute-start.9 = (bf16[2,272,128]{2,1,0:T(8,128)(2,1)S(1)}, bf16[2,272,128]{2,1,0:T(8,128)(2,1)S(1)}, u32[]{:S(2)}, u32[]{:S(2)}) collective-permute-start(bf16[2,272,128]{2,1,0:T(8,128)(2,1)S(1)} %get-tuple-element.82), channel_id=1, source_target_pairs={{0,10},{1,11},{2,8},{3,9},{4,2},{5,3},{6,0},{7,1},{8,14},{9,15},{1... | collective-permute-start | bytes 417800 | tf_op jit(solution)/shard_map/ppermute | solution.py:442
  28.4 7.0 %collective-permute-done.5.rest_3_ = bf16[2,272,128]{2,1,0:T(8,128)(2,1)S(1)} collective-permute-done((bf16[2,272,128]{2,1,0:T(8,128)(2,1)S(1)}, bf16[2,272,128]{2,1,0:T(8,128)(2,1)S(1)}, u32[]{:S(2)}, u32[]{:S(2)}) %collective-permute-start.5) | collective-permute-done | bytes 139296 | tf_op jit(solution)/shard_map/ppermute | solution.py:442
  35.4 5.8 %near.1 = (f32[640,512]{1,0:T(8,128)}, f32[512,544]{1,0:T(8,128)}) custom-call(bf16[544,128]{1,0:T(8,128)(2,1)S(1)} %pad.4.own_ref, bf16[512,544]{1,0:T(8,128)(2,1)S(1)} %get-tuple-element.66.w_out_ref, bf16[512,768]{1,0:T(8,128)(2,1)S(1)} %get-tuple-element.71.hidden_ref, f32[512,1152]{1,0:T(8,128)} %get-tuple-element.67.slope_hbm, ...), custom_call_target="tpu_custom_call" | custom-call | flops 8556380160 | bytes 6291456 | tf_op jit(solution)/shard_map/near/pallas_call | solution.py:497
  41.2 3.7 %grads.1 = (f32[8,32,1024]{2,1,0:T(8,128)S(1)}, bf16[8,32,1024]{2,1,0:T(8,128)(2,1)S(1)}, f32[512,512]{1,0:T(8,128)S(1)}, bf16[64,512]{1,0:T(8,128)(2,1)S(1)}, b...) custom-call(s32[1]{0:T(128)} %bitcast.me_ref, bf16[512,544]{1,0:T(8,128)(2,1)S(1)} %get-tuple-element.66.w_out_ref, ...), custom_call_target="tpu_custom_call" | custom-call | tf_op jit(solution)/shard_map/grads/pallas_call | solution.py:521
  44.8 0.1 collective-permute-start.10
  44.9 1.9 %outer.1 = (f32[8,32,640]{2,1,0:T(8,128)S(1)}, bf16[8,32,640]{2,1,0:T(8,128)(2,1)S(1)}) custom-call(s32[1]{0:T(128)} %bitcast.me_ref, bf16[512,384]{1,0:T(8,128)(2,1)S(1)} %get-tuple-element.98.hidden_ref, bf16[544,384]{1,0:T(8,128)(2,1)S(1)} %get-tuple-element.99.g_ref, f32[512,544]{1,0:T(8,128)} %get-tuple-element.100.near_hbm), custom_call_target="tpu_custom_call" | custom-call | flops 12834570240 | bytes 4194304 | tf_op jit(solution)/shard_map/outer/pallas_call | solution.py:545
  46.8 0.6 collective-permute-start.16
  47.4 0.1 fold.6
  47.5 1.1 %collective-permute-start.11 = (bf16[4,32,1024]{2,1,0:T(8,128)(2,1)S(1)}, bf16[4,32,1024]{2,1,0:T(8,128)(2,1)S(1)}, u32[]{:S(2)}, u32[]{:S(2)}) collective-permute-start(bf16[4,32,1024]{2,1,0:T(8,128)(2,1)S(1)} %get-tuple-element.87), channel_id=1, source_target_pairs={{0,2},{1,3},{2,0},{3,1},{4,6},{5,7},{6,4},{7,5},{8,10},{9,11},{10,... | collective-permute-start | bytes 786440 | tf_op jit(solution)/shard_map/ppermute | solution.py:372
  48.7 0.1 fold.9
  48.8 3.4 %collective-permute-start.17 = (bf16[4,32,640]{2,1,0:T(8,128)(2,1)S(1)}, bf16[4,32,640]{2,1,0:T(8,128)(2,1)S(1)}, u32[]{:S(2)}, u32[]{:S(2)}) collective-permute-start(bf16[4,32,640]{2,1,0:T(8,128)(2,1)S(1)} %get-tuple-element.106), channel_id=1, source_target_pairs={{0,4},{1,5},{2,6},{3,7},{4,0},{5,1},{6,2},{7,3},{8,12},{9,13},{10,... | collective-permute-start | bytes 491528 | tf_op jit(solution)/shard_map/ppermute | solution.py:372
  52.1 2.1 %collective-permute-start.12 = (bf16[64,512]{1,0:T(8,128)(2,1)S(1)}, bf16[64,512]{1,0:T(8,128)(2,1)S(1)}, u32[]{:S(2)}, u32[]{:S(2)}) collective-permute-start(bf16[64,512]{1,0:T(8,128)(2,1)S(1)} %get-tuple-element.88), channel_id=1, source_target_pairs={{1,0},{2,1},{3,2},{4,3},{5,4},{6,5},{7,6},{8,7},{9,8},{10,9},{11,1... | collective-permute-start | bytes 196616 | tf_op jit(solution)/shard_map/ppermute | solution.py:585
  54.2 2.5 %collective-permute-done.12.from_above_ref = bf16[64,512]{1,0:T(8,128)(2,1)S(1)} collective-permute-done((bf16[64,512]{1,0:T(8,128)(2,1)S(1)}, bf16[64,512]{1,0:T(8,128)(2,1)S(1)}, u32[]{:S(2)}, u32[]{:S(2)}) %collective-permute-start.12) | collective-permute-done | bytes 65568 | tf_op jit(solution)/shard_map/ppermute | solution.py:585
  56.8 3.8 %collective-permute-done.13.from_below_ref = bf16[64,512]{1,0:T(8,128)(2,1)S(1)} collective-permute-done((bf16[64,512]{1,0:T(8,128)(2,1)S(1)}, bf16[64,512]{1,0:T(8,128)(2,1)S(1)}, u32[]{:S(2)}, u32[]{:S(2)}) %collective-permute-start.13) | collective-permute-done | bytes 65568 | tf_op jit(solution)/shard_map/ppermute | solution.py:586
  60.8 1.1 %collective-permute-start.18 = (bf16[2,32,640]{2,1,0:T(8,128)(2,1)S(1)}, bf16[2,32,640]{2,1,0:T(8,128)(2,1)S(1)}, u32[]{:S(2)}, u32[]{:S(2)}) collective-permute-start(bf16[2,32,640]{2,1,0:T(8,128)(2,1)S(1)} %get-tuple-element.110), channel_id=1, source_target_pairs={{0,2},{1,3},{2,0},{3,1},{4,6},{5,7},{6,4},{7,5},{8,10},{9,11},{10,... | collective-permute-start | bytes 245768 | tf_op jit(solution)/shard_map/ppermute | solution.py:372
  61.9 3.8 %collective-permute-done.14.came_ref = bf16[2,32,1024]{2,1,0:T(8,128)(2,1)S(1)} collective-permute-done((bf16[2,32,1024]{2,1,0:T(8,128)(2,1)S(1)}, bf16[2,32,1024]{2,1,0:T(8,128)(2,1)S(1)}, u32[]{:S(2)}, u32[]{:S(2)}) %collective-permute-start.14) | collective-permute-done | bytes 131104 | tf_op jit(solution)/shard_map/ppermute | solution.py:372
  65.8 1.0 %collective-permute-start.15 = (bf16[1,32,1024]{2,1,0:T(8,128)(2,1)S(1)}, bf16[1,32,1024]{2,1,0:T(8,128)(2,1)S(1)}, u32[]{:S(2)}, u32[]{:S(2)}) collective-permute-start(bf16[1,32,1024]{2,1,0:T(8,128)(2,1)S(1)} %get-tuple-element.97), channel_id=1, source_target_pairs={{0,8},{1,9},{2,10},{3,11},{4,12},{5,13},{6,14},{7,15},{8,0},{9,1},... | collective-permute-start | bytes 196616 | tf_op jit(solution)/shard_map/ppermute | solution.py:372
  66.8 2.0 %collective-permute-start.19 = (bf16[1,32,640]{2,1,0:T(8,128)(2,1)S(1)}, bf16[1,32,640]{2,1,0:T(8,128)(2,1)S(1)}, u32[]{:S(2)}, u32[]{:S(2)}) collective-permute-start(bf16[1,32,640]{2,1,0:T(8,128)(2,1)S(1)} %get-tuple-element.114), channel_id=1, source_target_pairs={{0,8},{1,9},{2,10},{3,11},{4,12},{5,13},{6,14},{7,15},{8,0},{9,1},... | collective-permute-start | bytes 122888 | tf_op jit(solution)/shard_map/ppermute | solution.py:372
  68.8 1.5 %rims.1 = f32[256,512]{1,0:T(8,128)} custom-call(f32[512,512]{1,0:T(8,128)S(1)} %get-tuple-element.83.sums_ref, bf16[64,512]{1,0:T(8,128)(2,1)S(1)} %collective-permute-done.13.from_below_ref, bf16[64,512]{1,0:T(8,128)(2,1)S(1)} %collective-permute-done.12.from_above_ref, bf16[512,512]{1,0:T(8,128)(2,1)S(1)} %copy-done, bf16[512,512]{1,0:T(8,128)(2,1)S(1)} %copy-done.1), custom_call_target="tpu_custom_call" | custom-call | flops 24159191040 | bytes 4194304 | tf_op jit(solution)/shard_map/rims/pallas_call | solution.py:599
  70.4 2.6 %collective-permute-done.19.refs_3_ = bf16[1,32,640]{2,1,0:T(8,128)(2,1)S(1)} collective-permute-done((bf16[1,32,640]{2,1,0:T(8,128)(2,1)S(1)}, bf16[1,32,640]{2,1,0:T(8,128)(2,1)S(1)}, u32[]{:S(2)}, u32[]{:S(2)}) %collective-permute-start.19) | collective-permute-done | bytes 40992 | tf_op jit(solution)/shard_map/ppermute | solution.py:372
  72.9 0.7 totals.1
  (35 shorter events, 0.5 us)
Async XLA Ops:
  0.6 18.4 %copy-start.2 = (s32[2048]{0:T(1024)S(1)}, s32[2048]{0:T(1024)}, u32[]{:S(2)}) copy-start(s32[2048]{0:T(1024)} %param.13) | copy-start | bytes 24580
  0.6 18.4 %copy-start.3 = (s32[2048]{0:T(1024)S(1)}, s32[2048]{0:T(1024)}, u32[]{:S(2)}) copy-start(s32[2048]{0:T(1024)} %param.14) | copy-start | bytes 24580
  0.7 18.4 %copy-start.4 = (s32[2048]{0:T(1024)S(1)}, s32[2048]{0:T(1024)}, u32[]{:S(2)}) copy-start(s32[2048]{0:T(1024)} %param.15) | copy-start | bytes 24580
  3.2 8.1 %collective-permute-start = (bf16[8,272,128]{2,1,0:T(8,128)(2,1)S(1)}, bf16[8,272,128]{2,1,0:T(8,128)(2,1)S(1)}, u32[]{:S(2)}, u32[]{:S(2)}) collective-permute-start(bf16[8,272,128]{2,1,0:T(8,128)(2,1)S(1)} %get-tuple-element.61), channel_id=1, source_target_pairs={{0,1},{1,0},{2,3},{3,2},{4,5},{5,4},{6,7},{7,6},{8,9},{9,8},{10,11... | collective-permute-start | bytes 1671176 | tf_op jit(solution)/shard_map/ppermute | solution.py:372
  3.7 7.6 %collective-permute-start.1 = (bf16[64,512]{1,0:T(8,128)(2,1)S(1)}, bf16[64,512]{1,0:T(8,128)(2,1)S(1)}, u32[]{:S(2)}, u32[]{:S(2)}) collective-permute-start(bf16[64,512]{1,0:T(8,128)(2,1)S(1)} %get-tuple-element.62), channel_id=1, source_target_pairs={{0,1},{1,2},{2,3},{3,4},{4,5},{5,6},{6,7},{7,8},{8,9},{9,10},{10,1... | collective-permute-start | bytes 196616 | tf_op jit(solution)/shard_map/ppermute | solution.py:421
  3.8 7.6 %collective-permute-start.2 = (bf16[64,512]{1,0:T(8,128)(2,1)S(1)}, bf16[64,512]{1,0:T(8,128)(2,1)S(1)}, u32[]{:S(2)}, u32[]{:S(2)}) collective-permute-start(bf16[64,512]{1,0:T(8,128)(2,1)S(1)} %get-tuple-element.63), channel_id=1, source_target_pairs={{1,0},{2,1},{3,2},{4,3},{5,4},{6,5},{7,6},{8,7},{9,8},{10,9},{11,1... | collective-permute-start | bytes 196616 | tf_op jit(solution)/shard_map/ppermute | solution.py:422
  11.4 13.4 %collective-permute-start.3 = (bf16[2,272,128]{2,1,0:T(8,128)(2,1)S(1)}, bf16[2,272,128]{2,1,0:T(8,128)(2,1)S(1)}, u32[]{:S(2)}, u32[]{:S(2)}) collective-permute-start(bf16[2,272,128]{2,1,0:T(8,128)(2,1)S(1)} %get-tuple-element.75), channel_id=1, source_target_pairs={{0,2},{1,3},{2,0},{3,1},{4,8},{5,9},{6,10},{7,11},{8,4},{9,5},{10,... | collective-permute-start | bytes 417800 | tf_op jit(solution)/shard_map/ppermute | solution.py:442
  11.5 13.3 %collective-permute-start.4 = (bf16[2,272,128]{2,1,0:T(8,128)(2,1)S(1)}, bf16[2,272,128]{2,1,0:T(8,128)(2,1)S(1)}, u32[]{:S(2)}, u32[]{:S(2)}) collective-permute-start(bf16[2,272,128]{2,1,0:T(8,128)(2,1)S(1)} %get-tuple-element.76), channel_id=1, source_target_pairs={{0,4},{1,5},{2,6},{3,7},{4,12},{5,13},{6,14},{7,15},{8,0},{9,1},{1... | collective-permute-start | bytes 417800 | tf_op jit(solution)/shard_map/ppermute | solution.py:442
  12.6 22.7 %collective-permute-start.5 = (bf16[2,272,128]{2,1,0:T(8,128)(2,1)S(1)}, bf16[2,272,128]{2,1,0:T(8,128)(2,1)S(1)}, u32[]{:S(2)}, u32[]{:S(2)}) collective-permute-start(bf16[2,272,128]{2,1,0:T(8,128)(2,1)S(1)} %get-tuple-element.77), channel_id=1, source_target_pairs={{0,6},{1,7},{2,4},{3,5},{4,14},{5,15},{6,12},{7,13},{8,2},{9,3},{1... | collective-permute-start | bytes 417800 | tf_op jit(solution)/shard_map/ppermute | solution.py:442
  15.1 20.2 %collective-permute-start.6 = (bf16[2,272,128]{2,1,0:T(8,128)(2,1)S(1)}, bf16[2,272,128]{2,1,0:T(8,128)(2,1)S(1)}, u32[]{:S(2)}, u32[]{:S(2)}) collective-permute-start(bf16[2,272,128]{2,1,0:T(8,128)(2,1)S(1)} %get-tuple-element.78), channel_id=1, source_target_pairs={{0,12},{1,13},{2,14},{3,15},{4,10},{5,11},{6,8},{7,9},{8,6},{9,7},... | collective-permute-start | bytes 417800 | tf_op jit(solution)/shard_map/ppermute | solution.py:442
  17.3 23.8 %collective-permute-start.7 = (bf16[2,272,128]{2,1,0:T(8,128)(2,1)S(1)}, bf16[2,272,128]{2,1,0:T(8,128)(2,1)S(1)}, u32[]{:S(2)}, u32[]{:S(2)}) collective-permute-start(bf16[2,272,128]{2,1,0:T(8,128)(2,1)S(1)} %get-tuple-element.80), channel_id=1, source_target_pairs={{0,14},{1,15},{2,12},{3,13},{4,6},{5,7},{6,4},{7,5},{8,10},{9,11},... | collective-permute-start | bytes 417800 | tf_op jit(solution)/shard_map/ppermute | solution.py:442
  24.8 16.4 %collective-permute-start.8 = (bf16[2,272,128]{2,1,0:T(8,128)(2,1)S(1)}, bf16[2,272,128]{2,1,0:T(8,128)(2,1)S(1)}, u32[]{:S(2)}, u32[]{:S(2)}) collective-permute-start(bf16[2,272,128]{2,1,0:T(8,128)(2,1)S(1)} %get-tuple-element.81), channel_id=1, source_target_pairs={{0,8},{1,9},{2,10},{3,11},{4,0},{5,1},{6,2},{7,3},{8,12},{9,13},{1... | collective-permute-start | bytes 417800 | tf_op jit(solution)/shard_map/ppermute | solution.py:442
  24.8 16.3 %collective-permute-start.9 = (bf16[2,272,128]{2,1,0:T(8,128)(2,1)S(1)}, bf16[2,272,128]{2,1,0:T(8,128)(2,1)S(1)}, u32[]{:S(2)}, u32[]{:S(2)}) collective-permute-start(bf16[2,272,128]{2,1,0:T(8,128)(2,1)S(1)} %get-tuple-element.82), channel_id=1, source_target_pairs={{0,10},{1,11},{2,8},{3,9},{4,2},{5,3},{6,0},{7,1},{8,14},{9,15},{1... | collective-permute-start | bytes 417800 | tf_op jit(solution)/shard_map/ppermute | solution.py:442
  44.8 2.6 %collective-permute-start.10 = (bf16[8,32,1024]{2,1,0:T(8,128)(2,1)S(1)}, bf16[8,32,1024]{2,1,0:T(8,128)(2,1)S(1)}, u32[]{:S(2)}, u32[]{:S(2)}) collective-permute-start(bf16[8,32,1024]{2,1,0:T(8,128)(2,1)S(1)} %get-tuple-element.85), channel_id=1, source_target_pairs={{0,1},{1,0},{2,3},{3,2},{4,5},{5,4},{6,7},{7,6},{8,9},{9,8},{10,11... | collective-permute-start | bytes 1572872 | tf_op jit(solution)/shard_map/ppermute | solution.py:372
  46.8 1.8 %collective-permute-start.16 = (bf16[8,32,640]{2,1,0:T(8,128)(2,1)S(1)}, bf16[8,32,640]{2,1,0:T(8,128)(2,1)S(1)}, u32[]{:S(2)}, u32[]{:S(2)}) collective-permute-start(bf16[8,32,640]{2,1,0:T(8,128)(2,1)S(1)} %get-tuple-element.102), channel_id=1, source_target_pairs={{0,1},{1,0},{2,3},{3,2},{4,5},{5,4},{6,7},{7,6},{8,9},{9,8},{10,11... | collective-permute-start | bytes 983048 | tf_op jit(solution)/shard_map/ppermute | solution.py:372
  47.4 21.5 %copy-start = (bf16[512,512]{1,0:T(8,128)(2,1)S(1)}, bf16[512,512]{1,0:T(8,128)(2,1)}, u32[]{:S(2)}) copy-start(bf16[512,512]{1,0:T(8,128)(2,1)} %w_src_ref.1) | copy-start | bytes 1572868
  47.4 21.5 %copy-start.1 = (bf16[512,512]{1,0:T(8,128)(2,1)S(1)}, bf16[512,512]{1,0:T(8,128)(2,1)}, u32[]{:S(2)}) copy-start(bf16[512,512]{1,0:T(8,128)(2,1)} %w_dst_ref.1) | copy-start | bytes 1572868
  47.5 13.1 %collective-permute-start.11 = (bf16[4,32,1024]{2,1,0:T(8,128)(2,1)S(1)}, bf16[4,32,1024]{2,1,0:T(8,128)(2,1)S(1)}, u32[]{:S(2)}, u32[]{:S(2)}) collective-permute-start(bf16[4,32,1024]{2,1,0:T(8,128)(2,1)S(1)} %get-tuple-element.87), channel_id=1, source_target_pairs={{0,2},{1,3},{2,0},{3,1},{4,6},{5,7},{6,4},{7,5},{8,10},{9,11},{10,... | collective-permute-start | bytes 786440 | tf_op jit(solution)/shard_map/ppermute | solution.py:372
  48.8 12.0 %collective-permute-start.17 = (bf16[4,32,640]{2,1,0:T(8,128)(2,1)S(1)}, bf16[4,32,640]{2,1,0:T(8,128)(2,1)S(1)}, u32[]{:S(2)}, u32[]{:S(2)}) collective-permute-start(bf16[4,32,640]{2,1,0:T(8,128)(2,1)S(1)} %get-tuple-element.106), channel_id=1, source_target_pairs={{0,4},{1,5},{2,6},{3,7},{4,0},{5,1},{6,2},{7,3},{8,12},{9,13},{10,... | collective-permute-start | bytes 491528 | tf_op jit(solution)/shard_map/ppermute | solution.py:372
  52.1 4.6 %collective-permute-start.12 = (bf16[64,512]{1,0:T(8,128)(2,1)S(1)}, bf16[64,512]{1,0:T(8,128)(2,1)S(1)}, u32[]{:S(2)}, u32[]{:S(2)}) collective-permute-start(bf16[64,512]{1,0:T(8,128)(2,1)S(1)} %get-tuple-element.88), channel_id=1, source_target_pairs={{1,0},{2,1},{3,2},{4,3},{5,4},{6,5},{7,6},{8,7},{9,8},{10,9},{11,1... | collective-permute-start | bytes 196616 | tf_op jit(solution)/shard_map/ppermute | solution.py:585
  54.2 6.4 %collective-permute-start.13 = (bf16[64,512]{1,0:T(8,128)(2,1)S(1)}, bf16[64,512]{1,0:T(8,128)(2,1)S(1)}, u32[]{:S(2)}, u32[]{:S(2)}) collective-permute-start(bf16[64,512]{1,0:T(8,128)(2,1)S(1)} %get-tuple-element.89), channel_id=1, source_target_pairs={{0,1},{1,2},{2,3},{3,4},{4,5},{5,6},{6,7},{7,8},{8,9},{9,10},{10,1... | collective-permute-start | bytes 196616 | tf_op jit(solution)/shard_map/ppermute | solution.py:586
  60.7 5.0 %collective-permute-start.14 = (bf16[2,32,1024]{2,1,0:T(8,128)(2,1)S(1)}, bf16[2,32,1024]{2,1,0:T(8,128)(2,1)S(1)}, u32[]{:S(2)}, u32[]{:S(2)}) collective-permute-start(bf16[2,32,1024]{2,1,0:T(8,128)(2,1)S(1)} %get-tuple-element.95), channel_id=1, source_target_pairs={{0,4},{1,5},{2,6},{3,7},{4,0},{5,1},{6,2},{7,3},{8,12},{9,13},{10,... | collective-permute-start | bytes 393224 | tf_op jit(solution)/shard_map/ppermute | solution.py:372
  60.8 6.0 %collective-permute-start.18 = (bf16[2,32,640]{2,1,0:T(8,128)(2,1)S(1)}, bf16[2,32,640]{2,1,0:T(8,128)(2,1)S(1)}, u32[]{:S(2)}, u32[]{:S(2)}) collective-permute-start(bf16[2,32,640]{2,1,0:T(8,128)(2,1)S(1)} %get-tuple-element.110), channel_id=1, source_target_pairs={{0,2},{1,3},{2,0},{3,1},{4,6},{5,7},{6,4},{7,5},{8,10},{9,11},{10,... | collective-permute-start | bytes 245768 | tf_op jit(solution)/shard_map/ppermute | solution.py:372
  65.8 7.2 %collective-permute-start.15 = (bf16[1,32,1024]{2,1,0:T(8,128)(2,1)S(1)}, bf16[1,32,1024]{2,1,0:T(8,128)(2,1)S(1)}, u32[]{:S(2)}, u32[]{:S(2)}) collective-permute-start(bf16[1,32,1024]{2,1,0:T(8,128)(2,1)S(1)} %get-tuple-element.97), channel_id=1, source_target_pairs={{0,8},{1,9},{2,10},{3,11},{4,12},{5,13},{6,14},{7,15},{8,0},{9,1},... | collective-permute-start | bytes 196616 | tf_op jit(solution)/shard_map/ppermute | solution.py:372
  66.8 6.1 %collective-permute-start.19 = (bf16[1,32,640]{2,1,0:T(8,128)(2,1)S(1)}, bf16[1,32,640]{2,1,0:T(8,128)(2,1)S(1)}, u32[]{:S(2)}, u32[]{:S(2)}) collective-permute-start(bf16[1,32,640]{2,1,0:T(8,128)(2,1)S(1)} %get-tuple-element.114), channel_id=1, source_target_pairs={{0,8},{1,9},{2,10},{3,11},{4,12},{5,13},{6,14},{7,15},{8,0},{9,1},... | collective-permute-start | bytes 122888 | tf_op jit(solution)/shard_map/ppermute | solution.py:372
